TPU v7x, 256 devices: a whole 4x4x8 slice. The times are simulated.
256 devices in a mesh: row: 16 (over z_hi, x, core), col: 16 (over z_lo, y).
Axes of the slice: x: 4, y: 4, z: 8 (z_hi: 2, z_lo: 4; z = z_hi * 4 + z_lo), core: 2. Of those that a mesh axis runs over, the one named last changes fastest.
Arguments:
- features: bfloat16 [32768, 768], P(('row', 'col')), may hold values from -6 to 6
- self_weight: bfloat16 [768, 768], replicated, may hold values from -0.21875 to 0.21875
- rel_weight: bfloat16 [768, 5, 768], replicated, may hold values from -0.21875 to 0.21875
- bias: float32 [768], replicated, may hold values from -3 to 3
- blocks: bfloat16 [16, 16, 5, 8, 128, 128], P('row', 'col'), may hold values from -0.083496094 to 0.083496094
- block_rows: int32 [16, 16, 5, 8], P('row', 'col'), may hold values from 0 to 15
- block_cols: int32 [16, 16, 5, 8], P('row', 'col'), may hold values from 0 to 15
- block_counts: int32 [16, 16, 5], P('row', 'col'), may hold values from 1 to 8, as said below
Outputs:
- layer_out: bfloat16 [32768, 768], P(('row', 'col'))
Inputs may be any that keep to these rules, and one draw needn't show every extreme that they name: The live slots of a tile and relation are its first block_counts slots; the others are ignored. `block_rows`: pairs of destination and source blocks may repeat within a tile.
All inputs are finite; a program needn't handle non-finite values.
Results may differ from a plain program's by a relative error of at most 0.014.
Values may be sent and summed in bfloat16 or wider, within the bound.
No kernel may reach another device: no remote copies, remote signals or barrier semaphores. Data moves between devices by JAX's collectives and lax.ppermute only.
A program may use at most 128 MiB of HBM per device.

v0:
```python
import functools

import jax
import jax.numpy as jnp
from jax import lax
from jax.experimental import pallas as pl
from jax.experimental.pallas import tpu as pltpu
from jax.sharding import PartitionSpec as P

X, CORES, Z, Y = 4, 2, 4, 4
SPLIT = 512
UNROLL, QUAD = 4, 4


def row_shift(value, dz, dx, dc):
    pairs = []
    for index in range(16):
        z, x, c = index // 8, index // 2 % 4, index % 2
        pairs.append((index, (z ^ dz) * 8 + (x + dx) % X * 2 + (c ^ dc)))
    return lax.ppermute(value, "row", pairs)


def col_shift(value, dz, dy):
    pairs = []
    for index in range(16):
        z, y = index // 4, index % 4
        pairs.append((index, (z + dz) % Z * 4 + (y + dy) % Y))
    return lax.ppermute(value, "col", pairs)


def rows_at(index, size):
    return pl.ds(pl.multiple_of(index * size, size), size)


def stage_kernel(group, first, last, codes_ref, starts_ref, blocks_ref, weight_ref, group_ref, *refs):
    if not first:
        refs = refs[1:]
    total, refs = refs[0], refs[1:]
    if last:
        y_refs, z_refs, refs = refs[:Y], refs[Y : Y + Z], refs[Y + Z :]
    (picked,) = refs
    relations = weight_ref.shape[0]
    size = blocks_ref.shape[-1]
    if first:
        total[...] = jnp.zeros_like(total)
    base = starts_ref[group * relations]
    length = starts_ref[(group + 1) * relations] - base

    def pick(step, carry):
        for u in range(UNROLL):
            n = jnp.minimum(step * UNROLL + u, length - 1)
            code = codes_ref[base + n]
            product = jnp.dot(
                blocks_ref[code // 64],
                group_ref[rows_at(code // 16 % 4, size), :],
                preferred_element_type=jnp.float32,
            )
            picked[rows_at(n, size), :] = product.astype(picked.dtype)
        return carry

    lax.fori_loop(0, (length + UNROLL - 1) // UNROLL, pick, 0)

    def spread(relation, carry):
        start = starts_ref[group * relations + relation]
        end = starts_ref[group * relations + relation + 1]

        def quad(step, carry):
            begin = start + step * QUAD
            for count in range(1, QUAD + 1):
                enough = (end - begin >= count) if count == QUAD else (end - begin == count)

                @pl.when(enough)
                def _():
                    moved = jnp.dot(
                        picked[pl.ds(pl.multiple_of((begin - base) * size, size), count * size), :],
                        weight_ref[relation],
                        preferred_element_type=jnp.float32,
                    )
                    for part in range(count):
                        target = rows_at(codes_ref[begin + part] % 16, size)
                        total[target, :] += moved[part * size : (part + 1) * size]

            return carry

        return lax.fori_loop(0, (end - start + QUAD - 1) // QUAD, quad, carry)

    lax.fori_loop(0, relations, spread, 0)
    if last:
        for d in range(Y):
            for e in range(Z):
                rows = pl.ds((d * Z + e) * size, size)
                y_refs[d][e] = total[rows, :SPLIT].astype(jnp.bfloat16)
                z_refs[e][d] = total[rows, SPLIT:].astype(jnp.bfloat16)


def plan_kernel(
    slots, me_ref, rows_ref, cols_ref, counts_ref, codes_ref, starts_ref
):
    relations = counts_ref.shape[2]
    row_me, col_me = me_ref[0], me_ref[1]

    def place_of(relation, slot):
        source = cols_ref[0, 0, relation, slot]
        z, c = (source // 8) ^ (row_me // 8), (source % 2) ^ (row_me % 2)
        return z * 2 + c, source // 2 % X

    for index in range(4 * relations + 1):
        starts_ref[index] = 0
    for relation in range(relations):

        def count(slot, carry):
            group, _ = place_of(relation, slot)
            index = group * relations + relation + 1
            starts_ref[index] = starts_ref[index] + 1
            return carry

        lax.fori_loop(0, counts_ref[0, 0, relation], count, 0)
    for index in range(1, 4 * relations + 1):
        starts_ref[index] = starts_ref[index] + starts_ref[index - 1]
    for relation in range(relations):

        def put(slot, carry):
            group, place = place_of(relation, slot)
            target = rows_ref[0, 0, relation, slot]
            y = (target % Y - col_me % Y + Y) % Y
            z = (target // Y - col_me // Y + Z) % Z
            index = group * relations + relation
            at = starts_ref[index]
            codes_ref[at] = (relation * slots + slot) * 64 + place * 16 + y * Z + z
            starts_ref[index] = at + 1
            return carry

        lax.fori_loop(0, counts_ref[0, 0, relation], put, 0)
    for index in range(4 * relations - 1, 0, -1):
        starts_ref[index] = starts_ref[index - 1]
    starts_ref[0] = 0


def plan(me, block_rows, block_cols, block_counts):
    relations, slots = block_rows.shape[2:]
    smem = pl.BlockSpec(memory_space=pltpu.SMEM)
    many = relations * slots
    return pl.pallas_call(
        functools.partial(plan_kernel, slots),
        out_shape=[
            jax.ShapeDtypeStruct((many,), jnp.int32),
            jax.ShapeDtypeStruct((4 * relations + 1,), jnp.int32),
        ],
        in_specs=[smem] * 4,
        out_specs=[smem] * 2,
        compiler_params=pltpu.CompilerParams(vmem_limit_bytes=1 << 20),
        name="plan",
    )(me, block_rows, block_cols, block_counts)


def tile_stage(group, tables, blocks, weights, value, total):
    many, size, _ = blocks.shape
    width = weights.shape[-1]
    first, last = group == 0, group == 3
    vmem = pl.BlockSpec(memory_space=pltpu.VMEM)
    smem = pl.BlockSpec(memory_space=pltpu.SMEM)
    out_shape = [jax.ShapeDtypeStruct((Y * Z * size, width), jnp.float32)]
    if last:
        out_shape += [jax.ShapeDtypeStruct((Z, size, SPLIT), jnp.bfloat16)] * Y
        out_shape += [jax.ShapeDtypeStruct((Y, size, width - SPLIT), jnp.bfloat16)] * Z
    args = [*tables, blocks, weights, value]
    if not first:
        args.append(total)
    return pl.pallas_call(
        functools.partial(stage_kernel, group, first, last),
        out_shape=out_shape,
        in_specs=[smem] * 2 + [vmem] * (len(args) - 2),
        out_specs=[vmem] * len(out_shape),
        scratch_shapes=[pltpu.VMEM((many * size, width), jnp.bfloat16)],
        input_output_aliases={} if first else {len(args) - 1: 0},
        compiler_params=pltpu.CompilerParams(vmem_limit_bytes=24 << 20),
        cost_estimate=pl.CostEstimate(flops=1 << 30, bytes_accessed=4 << 20, transcendentals=0),
        name="tile",
    )(*args)


def merge_kernel(own_ref, *refs):
    ins, (keep_ref, *send_refs) = refs[:3], refs[3:]
    for e in range(len(send_refs) + 1):
        summed = own_ref[e].astype(jnp.float32)
        for ref in ins:
            summed += ref[e].astype(jnp.float32)
        if e == 0:
            keep_ref[...] = summed
        else:
            send_refs[e - 1][...] = summed.astype(jnp.bfloat16)


def merge(own, ins):
    vmem = pl.BlockSpec(memory_space=pltpu.VMEM)
    count, rows, columns = own.shape
    return pl.pallas_call(
        merge_kernel,
        out_shape=[jax.ShapeDtypeStruct((rows, columns), jnp.float32)]
        + [jax.ShapeDtypeStruct((rows, columns), jnp.bfloat16)] * (count - 1),
        in_specs=[vmem] * 4,
        out_specs=[vmem] * count,
        compiler_params=pltpu.CompilerParams(vmem_limit_bytes=4 << 20),
        name="merge",
    )(own, *ins)


X_GROUPS = [[z * 8 + x * 2 + c for x in range(X)] for z in range(2) for c in range(CORES)]
Y_GROUPS = [[z * Y + y for y in range(Y)] for z in range(Z)]
Z_GROUPS = [[z * Y + y for z in range(Z)] for y in range(Y)]


def along_x(value):
    copies = jnp.broadcast_to(value[None], (X, *value.shape))
    got = lax.all_to_all(copies, "row", 0, 0, axis_index_groups=X_GROUPS)
    return got.reshape(X * value.shape[0], value.shape[1])


def gather_groups(features, self_weight, tables, blocks, weights):
    stage = lambda index, value, total, tables: tile_stage(index, tables, blocks, weights, value, total)
    far = row_shift(features, 1, 0, 0)
    near = along_x(features)
    self_term = jnp.dot(features, self_weight, preferred_element_type=jnp.float32)
    far, self_term, tables = lax.optimization_barrier((far, self_term, tables))
    rest = along_x(far)
    near_other = row_shift(near, 0, 0, 1)
    (total,) = stage(0, near, None, tables)
    (total,) = stage(1, near_other, total, tables)
    rest, total = lax.optimization_barrier((rest, total))
    rest_other = row_shift(rest, 0, 0, 1)
    (total,) = stage(2, rest, total, tables)
    return self_term, stage(3, rest_other, total, tables)[1:]


def scatter_sum(y_parts, z_parts):
    y_in = [col_shift(y_parts[d], 0, d) for d in (1, 3, 2)]
    z_in = [col_shift(z_parts[e], e, 0) for e in (1, 3, 2)]
    y_own, *y_send = merge(y_parts[0], y_in)
    z_in, y_send = lax.optimization_barrier((z_in, y_send))
    z_own, *z_send = merge(z_parts[0], z_in)
    z_last = [col_shift(z_send[d - 1], 0, d) for d in (1, 3, 2)]
    y_last = [col_shift(y_send[e - 1], e, 0) for e in (1, 3, 2)]
    y_own += sum(part.astype(jnp.float32) for part in y_last)
    y_own, z_last = lax.optimization_barrier((y_own, z_last))
    z_own += sum(part.astype(jnp.float32) for part in z_last)
    return y_own, z_own


def per_device(
    features, self_weight, rel_weight, bias, blocks, block_rows, block_cols, block_counts
):
    relations, slots, size, _ = blocks.shape[2:]
    me = jnp.stack([lax.axis_index("row"), lax.axis_index("col")])
    weights = jnp.transpose(rel_weight, (1, 0, 2))
    blocks = blocks.reshape(relations * slots, size, size)
    tables = plan(me, block_rows, block_cols, block_counts)
    self_term, parts = gather_groups(features, self_weight, tables, blocks, weights)
    y_parts, z_parts = parts[:Y], parts[Y:]
    y_own, z_own = scatter_sum(y_parts, z_parts)
    owned = jnp.concatenate([y_own, z_own], axis=1)
    return jnp.maximum(self_term + owned + bias, 0.0).astype(jnp.bfloat16)


def solution(mesh):
    return jax.shard_map(
        per_device,
        mesh=mesh,
        in_specs=(
            P(("row", "col"), None),
            P(),
            P(),
            P(),
            P("row", "col", None, None, None, None),
            P("row", "col", None, None),
            P("row", "col", None, None),
            P("row", "col", None),
        ),
        out_specs=P(("row", "col"), None),
        check_vma=False,
    )
```

profile of v0, /device:TPU:198, one launch (start us, length us, event | category | flops | bytes accessed | tf_op | source)
XLA Modules:
  0.0 108.8 jit_solution(10665921864432968428)
XLA Ops:
  0.0 2.0 %broadcast_in_dim.5 = bf16[4,128,768]{2,1,0:T(8,128)(2,1)} broadcast(bf16[128,768]{1,0:T(8,128)(2,1)} %param.8), dimensions={1,2} | broadcast | bytes 983040 | tf_op jit(solution)/shard_map/broadcast_in_dim | solution.py:214
  2.0 4.8 %all-to-all-start.1 = ((bf16[4,128,768]{2,1,0:T(8,128)(2,1)}), bf16[4,128,768]{2,1,0:T(8,128)(2,1)S(1)}, u32[]{:S(2)}, u32[]{:S(2)}) async-start(bf16[4,128,768]{2,1,0:T(8,128)(2,1)} %broadcast_in_dim.5), calls=%async_computation.1 | async-start | bytes 1572864 | tf_op jit(solution)/shard_map/all_to_all | solution.py:215
  7.3 9.7 %all-to-all-done.1 = bf16[4,128,768]{2,1,0:T(8,128)(2,1)S(1)} async-done(((bf16[4,128,768]{2,1,0:T(8,128)(2,1)}), bf16[4,128,768]{2,1,0:T(8,128)(2,1)S(1)}, u32[]{:S(2)}, u32[]{:S(2)}) %all-to-all-start.1) | async-done | bytes 786464 | tf_op jit(solution)/shard_map/all_to_all | solution.py:215
  19.1 2.2 %plan.1 = (s32[40]{0:T(128)S(1)}, s32[21]{0:T(128)S(1)}) custom-call(s32[2]{0:T(128)S(1)} %pad_add_fusion.me_ref, s32[1,1,5,8]{3,2,1,0:T(8,128)S(1)} %copy.12.rows_ref, s32[1,1,5,8]{3,2,1,0:T(8,128)S(1)} %copy.13.cols_ref, s32[1,1,5]{2,1,0:T(1,128)S(1)} %copy-done.6), custom_call_target="tpu_custom_call" | custom-call | tf_op jit(solution)/shard_map/plan/pallas_call | solution.py:143
  21.3 2.0 %fusion.3 = f32[128,768]{1,0:T(8,128)} fusion(bf16[128,768]{1,0:T(8,128)(2,1)} %param.8, bf16[768,768]{1,0:T(8,128)(2,1)S(1)} %copy-done), kind=kOutput, calls=%fused_computation.7 | convolution fusion | flops 150994944 | bytes 1769472 | tf_op jit(solution)/shard_map/dot_general | solution.py:223
  24.3 6.1 %all-to-all-start = ((bf16[4,128,768]{2,1,0:T(8,128)(2,1)}), bf16[4,128,768]{2,1,0:T(8,128)(2,1)}, u32[]{:S(2)}, u32[]{:S(2)}) async-start(bf16[4,128,768]{2,1,0:T(8,128)(2,1)} %broadcast_in_dim.4), calls=%async_computation | async-start | bytes 1572864 | tf_op jit(solution)/shard_map/all_to_all | solution.py:215
  30.4 2.7 %copy-done.3 = bf16[768,5,768]{2,0,1:T(8,128)(2,1)S(1)} copy-done((bf16[768,5,768]{2,0,1:T(8,128)(2,1)S(1)}, bf16[768,5,768]{2,0,1:T(8,128)(2,1)}, u32[]{:S(2)}) %copy-start.3) | copy-done | bytes 5898264
  33.1 2.3 %tile.4.refs_0_ = f32[2048,768]{1,0:T(8,128)S(1)} custom-call(s32[40]{0:T(128)S(1)} %get-tuple-element.42.codes_ref, s32[21]{0:T(128)S(1)} %get-tuple-element.43.starts_ref, bf16[40,128,128]{2,1,0:T(8,128)(2,1)S(1)} %bitcast.12, bf16[5,768,768]{2,1,0:T(8,128)(2,1)S(1)} %bitcast.8, bf16[512,768]{1,0:T(8,128)(2,1)S(1)} %bitcast.17), custom_call_target="tpu_custom_call" | custom-call | flops 1073741824 | bytes 4194304 | tf_op jit(solution)/shard_map/tile/pallas_call | solution.py:169
  35.4 2.6 %tile.5.refs_0_ = f32[2048,768]{1,0:T(8,128)S(1)} custom-call(s32[40]{0:T(128)S(1)} %get-tuple-element.42.codes_ref, s32[21]{0:T(128)S(1)} %get-tuple-element.43.starts_ref, bf16[40,128,128]{2,1,0:T(8,128)(2,1)S(1)} %bitcast.13, bf16[5,768,768]{2,1,0:T(8,128)(2,1)S(1)} %bitcast.9, ...), custom_call_target="tpu_custom_call", output_to_operand_aliasing={{}: (5, {})} | custom-call | flops 1073741824 | bytes 4194304 | tf_op jit(solution)/shard_map/tile/pallas_call | solution.py:169
  38.0 2.6 %copy-done.1 = f32[2048,768]{1,0:T(8,128)} copy-done((f32[2048,768]{1,0:T(8,128)}, f32[2048,768]{1,0:T(8,128)S(1)}, u32[]{:S(2)}) %copy-start.1) | copy-done | bytes 6291480
  42.0 2.8 %copy-done.2 = f32[2048,768]{1,0:T(8,128)S(1)} copy-done((f32[2048,768]{1,0:T(8,128)S(1)}, f32[2048,768]{1,0:T(8,128)}, u32[]{:S(2)}) %copy-start.2) | copy-done | bytes 6291480
  44.8 2.7 %copy-done.4 = bf16[768,5,768]{2,0,1:T(8,128)(2,1)S(1)} copy-done((bf16[768,5,768]{2,0,1:T(8,128)(2,1)S(1)}, bf16[768,5,768]{2,0,1:T(8,128)(2,1)}, u32[]{:S(2)}) %copy-start.4) | copy-done | bytes 5898264
  47.5 2.3 %tile.6.refs_0_ = f32[2048,768]{1,0:T(8,128)S(1)} custom-call(s32[40]{0:T(128)S(1)} %get-tuple-element.42.codes_ref, s32[21]{0:T(128)S(1)} %get-tuple-element.43.starts_ref, bf16[40,128,128]{2,1,0:T(8,128)(2,1)S(1)} %bitcast.14, bf16[5,768,768]{2,1,0:T(8,128)(2,1)S(1)} %bitcast.10, ...), custom_call_target="tpu_custom_call", output_to_operand_aliasing={{}: (5, {})} | custom-call | flops 1073741824 | bytes 4194304 | tf_op jit(solution)/shard_map/tile/pallas_call | solution.py:169
  49.8 2.5 %tile.7 = (f32[2048,768]{1,0:T(8,128)S(1)}, bf16[4,128,512]{2,1,0:T(8,128)(2,1)S(1)}, bf16[4,128,512]{2,1,0:T(8,128)(2,1)S(1)}, bf16[4,128,512]{2,1,0:T(8,128)(2...) custom-call(s32[40]{0:T(128)S(1)} %get-tuple-element.42.codes_ref, ...), custom_call_target="tpu_custom_call", output_to_operand_aliasing={{0}: (5, {})} | custom-call | flops 1073741824 | bytes 4194304 | tf_op jit(solution)/shard_map/tile/pallas_call | solution.py:169
  52.4 2.7 %collective-permute-start.3 = (bf16[4,128,512]{2,1,0:T(8,128)(2,1)S(1)}, bf16[4,128,512]{2,1,0:T(8,128)(2,1)S(1)}, u32[]{:S(2)}, u32[]{:S(2)}) collective-permute-start(bf16[4,128,512]{2,1,0:T(8,128)(2,1)S(1)} %get-tuple-element.48), channel_id=1, source_target_pairs={{0,1},{1,2},{2,3},{3,0},{4,5},{5,6},{6,7},{7,4},{8,9},{9,10},{10,1... | collective-permute-start | bytes 1572872 | tf_op jit(solution)/shard_map/ppermute | solution.py:28
  55.9 3.2 %collective-permute-start.5 = (bf16[4,128,512]{2,1,0:T(8,128)(2,1)S(1)}, bf16[4,128,512]{2,1,0:T(8,128)(2,1)S(1)}, u32[]{:S(2)}, u32[]{:S(2)}) collective-permute-start(bf16[4,128,512]{2,1,0:T(8,128)(2,1)S(1)} %get-tuple-element.50), channel_id=1, source_target_pairs={{0,2},{1,3},{2,0},{3,1},{4,6},{5,7},{6,4},{7,5},{8,10},{9,11},{10,... | collective-permute-start | bytes 1572872 | tf_op jit(solution)/shard_map/ppermute | solution.py:28
  59.8 1.4 %collective-permute-start.7 = (bf16[4,128,256]{2,1,0:T(8,128)(2,1)S(1)}, bf16[4,128,256]{2,1,0:T(8,128)(2,1)S(1)}, u32[]{:S(2)}, u32[]{:S(2)}) collective-permute-start(bf16[4,128,256]{2,1,0:T(8,128)(2,1)S(1)} %get-tuple-element.53), channel_id=1, source_target_pairs={{0,12},{1,13},{2,14},{3,15},{4,0},{5,1},{6,2},{7,3},{8,4},{9,5},{1... | collective-permute-start | bytes 786440 | tf_op jit(solution)/shard_map/ppermute | solution.py:28
  61.2 7.4 %collective-permute-done.3.refs_0_ = bf16[4,128,512]{2,1,0:T(8,128)(2,1)S(1)} collective-permute-done((bf16[4,128,512]{2,1,0:T(8,128)(2,1)S(1)}, bf16[4,128,512]{2,1,0:T(8,128)(2,1)S(1)}, u32[]{:S(2)}, u32[]{:S(2)}) %collective-permute-start.3) | collective-permute-done | bytes 524320 | tf_op jit(solution)/shard_map/ppermute | solution.py:28
  68.5 13.7 %collective-permute-start.8 = (bf16[4,128,256]{2,1,0:T(8,128)(2,1)S(1)}, bf16[4,128,256]{2,1,0:T(8,128)(2,1)S(1)}, u32[]{:S(2)}, u32[]{:S(2)}) collective-permute-start(bf16[4,128,256]{2,1,0:T(8,128)(2,1)S(1)} %get-tuple-element.54), channel_id=1, source_target_pairs={{0,8},{1,9},{2,10},{3,11},{4,12},{5,13},{6,14},{7,15},{8,0},{9,1},... | collective-permute-start | bytes 786440 | tf_op jit(solution)/shard_map/ppermute | solution.py:28
  82.5 9.0 %collective-permute-done.8.refs_2_ = bf16[4,128,256]{2,1,0:T(8,128)(2,1)S(1)} collective-permute-done((bf16[4,128,256]{2,1,0:T(8,128)(2,1)S(1)}, bf16[4,128,256]{2,1,0:T(8,128)(2,1)S(1)}, u32[]{:S(2)}, u32[]{:S(2)}) %collective-permute-start.8) | collective-permute-done | bytes 262176 | tf_op jit(solution)/shard_map/ppermute | solution.py:28
  91.5 2.0 %collective-permute-start.10 = (bf16[128,512]{1,0:T(8,128)(2,1)S(1)}, bf16[128,512]{1,0:T(8,128)(2,1)S(1)}, u32[]{:S(2)}, u32[]{:S(2)}) collective-permute-start(bf16[128,512]{1,0:T(8,128)(2,1)S(1)} %get-tuple-element.59), channel_id=1, source_target_pairs={{0,12},{1,13},{2,14},{3,15},{4,0},{5,1},{6,2},{7,3},{8,4},{9,5},{1... | collective-permute-start | bytes 393224 | tf_op jit(solution)/shard_map/ppermute | solution.py:28
  93.6 5.2 %collective-permute-start.11 = (bf16[128,512]{1,0:T(8,128)(2,1)S(1)}, bf16[128,512]{1,0:T(8,128)(2,1)S(1)}, u32[]{:S(2)}, u32[]{:S(2)}) collective-permute-start(bf16[128,512]{1,0:T(8,128)(2,1)S(1)} %get-tuple-element.60), channel_id=1, source_target_pairs={{0,8},{1,9},{2,10},{3,11},{4,12},{5,13},{6,14},{7,15},{8,0},{9,1},... | collective-permute-start | bytes 393224 | tf_op jit(solution)/shard_map/ppermute | solution.py:28
  99.0 3.2 %collective-permute-start.13 = (bf16[128,256]{1,0:T(8,128)(2,1)S(1)}, bf16[128,256]{1,0:T(8,128)(2,1)S(1)}, u32[]{:S(2)}, u32[]{:S(2)}) collective-permute-start(bf16[128,256]{1,0:T(8,128)(2,1)S(1)} %get-tuple-element.66), channel_id=1, source_target_pairs={{0,3},{1,0},{2,1},{3,2},{4,7},{5,4},{6,5},{7,6},{8,11},{9,8},{10,9... | collective-permute-start | bytes 196616 | tf_op jit(solution)/shard_map/ppermute | solution.py:28
  104.7 3.3 %collective-permute-done.14 = bf16[128,256]{1,0:T(8,128)(2,1)S(1)} collective-permute-done((bf16[128,256]{1,0:T(8,128)(2,1)S(1)}, bf16[128,256]{1,0:T(8,128)(2,1)S(1)}, u32[]{:S(2)}, u32[]{:S(2)}) %collective-permute-start.14) | collective-permute-done | bytes 65568 | tf_op jit(solution)/shard_map/ppermute | solution.py:28
  (44 shorter events, 10.3 us)
Async XLA Ops:
  0.0 21.3 %copy-start = (bf16[768,768]{1,0:T(8,128)(2,1)S(1)}, bf16[768,768]{1,0:T(8,128)(2,1)}, u32[]{:S(2)}) copy-start(bf16[768,768]{1,0:T(8,128)(2,1)} %param.9) | copy-start | bytes 3538948
  0.0 30.4 %copy-start.5 = (bf16[1,1,5,8,128,128]{5,4,3,2,1,0:T(8,128)(2,1)S(1)}, bf16[1,1,5,8,128,128]{5,4,3,2,1,0:T(8,128)(2,1)}, u32[]{:S(2)}) copy-start(bf16[1,1,5,8,128,128]{5,4,3,2,1,0:T(8,128)(2,1)} %param.12) | copy-start | bytes 3932164
  2.0 15.0 %all-to-all-start.1 = ((bf16[4,128,768]{2,1,0:T(8,128)(2,1)}), bf16[4,128,768]{2,1,0:T(8,128)(2,1)S(1)}, u32[]{:S(2)}, u32[]{:S(2)}) async-start(bf16[4,128,768]{2,1,0:T(8,128)(2,1)} %broadcast_in_dim.5), calls=%async_computation.1 | async-start | bytes 1572864 | tf_op jit(solution)/shard_map/all_to_all | solution.py:215
  6.8 16.6 %collective-permute-start = (bf16[128,768]{1,0:T(8,128)(2,1)}, bf16[128,768]{1,0:T(8,128)(2,1)S(1)}, u32[]{:S(2)}, u32[]{:S(2)}) collective-permute-start(bf16[128,768]{1,0:T(8,128)(2,1)} %param.8), channel_id=1, source_target_pairs={{0,128},{16,144},{32,160},{48,176},{64,192},{80,208},{96,224},{112... | collective-permute-start | bytes 589832 | tf_op jit(solution)/shard_map/ppermute | solution.py:20
  17.0 18.3 %collective-permute-start.1 = (bf16[512,768]{1,0:T(8,128)(2,1)S(1)}, bf16[512,768]{1,0:T(8,128)(2,1)}, u32[]{:S(2)}, u32[]{:S(2)}) collective-permute-start(bf16[512,768]{1,0:T(8,128)(2,1)S(1)} %bitcast.16), channel_id=1, source_target_pairs={{0,16},{16,0},{32,48},{48,32},{64,80},{80,64},{96,112},{112,96},{1... | collective-permute-start | bytes 2359304 | tf_op jit(solution)/shard_map/ppermute | solution.py:20
  24.3 17.6 %all-to-all-start = ((bf16[4,128,768]{2,1,0:T(8,128)(2,1)}), bf16[4,128,768]{2,1,0:T(8,128)(2,1)}, u32[]{:S(2)}, u32[]{:S(2)}) async-start(bf16[4,128,768]{2,1,0:T(8,128)(2,1)} %broadcast_in_dim.4), calls=%async_computation | async-start | bytes 1572864 | tf_op jit(solution)/shard_map/all_to_all | solution.py:215
  30.4 2.7 %copy-start.3 = (bf16[768,5,768]{2,0,1:T(8,128)(2,1)S(1)}, bf16[768,5,768]{2,0,1:T(8,128)(2,1)}, u32[]{:S(2)}) copy-start(bf16[768,5,768]{2,0,1:T(8,128)(2,1)} %param.10) | copy-start | bytes 17694724
  41.9 7.9 %collective-permute-start.2 = (bf16[512,768]{1,0:T(8,128)(2,1)}, bf16[512,768]{1,0:T(8,128)(2,1)S(1)}, u32[]{:S(2)}, u32[]{:S(2)}) collective-permute-start(bf16[512,768]{1,0:T(8,128)(2,1)} %bitcast.4.group_ref), channel_id=1, source_target_pairs={{0,16},{16,0},{32,48},{48,32},{64,80},{80,64},{96,112},{112,96},{1... | collective-permute-start | bytes 2359304 | tf_op jit(solution)/shard_map/ppermute | solution.py:20
  42.0 2.8 %copy-start.2 = (f32[2048,768]{1,0:T(8,128)S(1)}, f32[2048,768]{1,0:T(8,128)}, u32[]{:S(2)}) copy-start(f32[2048,768]{1,0:T(8,128)} %copy-done.1) | copy-start | bytes 18874372
  44.8 2.7 %copy-start.4 = (bf16[768,5,768]{2,0,1:T(8,128)(2,1)S(1)}, bf16[768,5,768]{2,0,1:T(8,128)(2,1)}, u32[]{:S(2)}) copy-start(bf16[768,5,768]{2,0,1:T(8,128)(2,1)} %param.10) | copy-start | bytes 17694724
  49.8 58.2 %copy-start.7 = (f32[128,768]{1,0:T(8,128)S(1)}, f32[128,768]{1,0:T(8,128)}, u32[]{:S(2)}) copy-start(f32[128,768]{1,0:T(8,128)} %fusion.3) | copy-start | bytes 1179652
  49.8 58.2 %copy-start.8 = (f32[768]{0:T(1024)S(1)}, f32[768]{0:T(1024)}, u32[]{:S(2)}) copy-start(f32[768]{0:T(1024)} %param.11) | copy-start | bytes 9220
  52.4 16.2 %collective-permute-start.3 = (bf16[4,128,512]{2,1,0:T(8,128)(2,1)S(1)}, bf16[4,128,512]{2,1,0:T(8,128)(2,1)S(1)}, u32[]{:S(2)}, u32[]{:S(2)}) collective-permute-start(bf16[4,128,512]{2,1,0:T(8,128)(2,1)S(1)} %get-tuple-element.48), channel_id=1, source_target_pairs={{0,1},{1,2},{2,3},{3,0},{4,5},{5,6},{6,7},{7,4},{8,9},{9,10},{10,1... | collective-permute-start | bytes 1572872 | tf_op jit(solution)/shard_map/ppermute | solution.py:28
  55.1 27.2 %collective-permute-start.4 = (bf16[4,128,512]{2,1,0:T(8,128)(2,1)S(1)}, bf16[4,128,512]{2,1,0:T(8,128)(2,1)S(1)}, u32[]{:S(2)}, u32[]{:S(2)}) collective-permute-start(bf16[4,128,512]{2,1,0:T(8,128)(2,1)S(1)} %get-tuple-element.49), channel_id=1, source_target_pairs={{0,3},{1,0},{2,1},{3,2},{4,7},{5,4},{6,5},{7,6},{8,11},{9,8},{10,9... | collective-permute-start | bytes 1572872 | tf_op jit(solution)/shard_map/ppermute | solution.py:28
  55.9 26.4 %collective-permute-start.5 = (bf16[4,128,512]{2,1,0:T(8,128)(2,1)S(1)}, bf16[4,128,512]{2,1,0:T(8,128)(2,1)S(1)}, u32[]{:S(2)}, u32[]{:S(2)}) collective-permute-start(bf16[4,128,512]{2,1,0:T(8,128)(2,1)S(1)} %get-tuple-element.50), channel_id=1, source_target_pairs={{0,2},{1,3},{2,0},{3,1},{4,6},{5,7},{6,4},{7,5},{8,10},{9,11},{10,... | collective-permute-start | bytes 1572872 | tf_op jit(solution)/shard_map/ppermute | solution.py:28
  59.1 23.4 %collective-permute-start.6 = (bf16[4,128,256]{2,1,0:T(8,128)(2,1)S(1)}, bf16[4,128,256]{2,1,0:T(8,128)(2,1)S(1)}, u32[]{:S(2)}, u32[]{:S(2)}) collective-permute-start(bf16[4,128,256]{2,1,0:T(8,128)(2,1)S(1)} %get-tuple-element.52), channel_id=1, source_target_pairs={{0,4},{1,5},{2,6},{3,7},{4,8},{5,9},{6,10},{7,11},{8,12},{9,13},{1... | collective-permute-start | bytes 786440 | tf_op jit(solution)/shard_map/ppermute | solution.py:28
  59.8 22.7 %collective-permute-start.7 = (bf16[4,128,256]{2,1,0:T(8,128)(2,1)S(1)}, bf16[4,128,256]{2,1,0:T(8,128)(2,1)S(1)}, u32[]{:S(2)}, u32[]{:S(2)}) collective-permute-start(bf16[4,128,256]{2,1,0:T(8,128)(2,1)S(1)} %get-tuple-element.53), channel_id=1, source_target_pairs={{0,12},{1,13},{2,14},{3,15},{4,0},{5,1},{6,2},{7,3},{8,4},{9,5},{1... | collective-permute-start | bytes 786440 | tf_op jit(solution)/shard_map/ppermute | solution.py:28
  68.5 23.0 %collective-permute-start.8 = (bf16[4,128,256]{2,1,0:T(8,128)(2,1)S(1)}, bf16[4,128,256]{2,1,0:T(8,128)(2,1)S(1)}, u32[]{:S(2)}, u32[]{:S(2)}) collective-permute-start(bf16[4,128,256]{2,1,0:T(8,128)(2,1)S(1)} %get-tuple-element.54), channel_id=1, source_target_pairs={{0,8},{1,9},{2,10},{3,11},{4,12},{5,13},{6,14},{7,15},{8,0},{9,1},... | collective-permute-start | bytes 786440 | tf_op jit(solution)/shard_map/ppermute | solution.py:28
  91.5 10.7 %collective-permute-start.9 = (bf16[128,512]{1,0:T(8,128)(2,1)S(1)}, bf16[128,512]{1,0:T(8,128)(2,1)S(1)}, u32[]{:S(2)}, u32[]{:S(2)}) collective-permute-start(bf16[128,512]{1,0:T(8,128)(2,1)S(1)} %get-tuple-element.58), channel_id=1, source_target_pairs={{0,4},{1,5},{2,6},{3,7},{4,8},{5,9},{6,10},{7,11},{8,12},{9,13},{1... | collective-permute-start | bytes 393224 | tf_op jit(solution)/shard_map/ppermute | solution.py:28
  91.5 10.7 %collective-permute-start.10 = (bf16[128,512]{1,0:T(8,128)(2,1)S(1)}, bf16[128,512]{1,0:T(8,128)(2,1)S(1)}, u32[]{:S(2)}, u32[]{:S(2)}) collective-permute-start(bf16[128,512]{1,0:T(8,128)(2,1)S(1)} %get-tuple-element.59), channel_id=1, source_target_pairs={{0,12},{1,13},{2,14},{3,15},{4,0},{5,1},{6,2},{7,3},{8,4},{9,5},{1... | collective-permute-start | bytes 393224 | tf_op jit(solution)/shard_map/ppermute | solution.py:28
  93.6 9.6 %collective-permute-start.11 = (bf16[128,512]{1,0:T(8,128)(2,1)S(1)}, bf16[128,512]{1,0:T(8,128)(2,1)S(1)}, u32[]{:S(2)}, u32[]{:S(2)}) collective-permute-start(bf16[128,512]{1,0:T(8,128)(2,1)S(1)} %get-tuple-element.60), channel_id=1, source_target_pairs={{0,8},{1,9},{2,10},{3,11},{4,12},{5,13},{6,14},{7,15},{8,0},{9,1},... | collective-permute-start | bytes 393224 | tf_op jit(solution)/shard_map/ppermute | solution.py:28
  98.9 5.6 %collective-permute-start.12 = (bf16[128,256]{1,0:T(8,128)(2,1)S(1)}, bf16[128,256]{1,0:T(8,128)(2,1)S(1)}, u32[]{:S(2)}, u32[]{:S(2)}) collective-permute-start(bf16[128,256]{1,0:T(8,128)(2,1)S(1)} %get-tuple-element.65), channel_id=1, source_target_pairs={{0,1},{1,2},{2,3},{3,0},{4,5},{5,6},{6,7},{7,4},{8,9},{9,10},{10,1... | collective-permute-start | bytes 196616 | tf_op jit(solution)/shard_map/ppermute | solution.py:28
  99.0 5.7 %collective-permute-start.13 = (bf16[128,256]{1,0:T(8,128)(2,1)S(1)}, bf16[128,256]{1,0:T(8,128)(2,1)S(1)}, u32[]{:S(2)}, u32[]{:S(2)}) collective-permute-start(bf16[128,256]{1,0:T(8,128)(2,1)S(1)} %get-tuple-element.66), channel_id=1, source_target_pairs={{0,3},{1,0},{2,1},{3,2},{4,7},{5,4},{6,5},{7,6},{8,11},{9,8},{10,9... | collective-permute-start | bytes 196616 | tf_op jit(solution)/shard_map/ppermute | solution.py:28
  102.2 5.8 %collective-permute-start.14 = (bf16[128,256]{1,0:T(8,128)(2,1)S(1)}, bf16[128,256]{1,0:T(8,128)(2,1)S(1)}, u32[]{:S(2)}, u32[]{:S(2)}) collective-permute-start(bf16[128,256]{1,0:T(8,128)(2,1)S(1)} %get-tuple-element.67), channel_id=1, source_target_pairs={{0,2},{1,3},{2,0},{3,1},{4,6},{5,7},{6,4},{7,5},{8,10},{9,11},{10,... | collective-permute-start | bytes 196616 | tf_op jit(solution)/shard_map/ppermute | solution.py:28
  (2 other events, 3.3 us)
where the time goes:
time: 111 us; the launch traced here: 109 us
  starting transfers between devices  44.5 us (40%)
  waiting for transfers between devices  33.1 us (30%)
  local copies, waits for them, and re-layouts  15.8 us (14%)
  Pallas kernels  12.3 us (11%)
  matrix products  2.05 us (2%)
    ppermute x12, starting transfers between devices, col_shift(): return lax.ppermute(value, 'col', pairs)  33 us
    ppermute x12, waiting for transfers between devices, col_shift(): return lax.ppermute(value, 'col', pairs)  22.1 us
    unnamed x20, local copies, waits for them, and re-layouts  12.8 us
    all_to_all x2, waiting for transfers between devices, along_x(): got = lax.all_to_all(copies, 'row', 0, 0, axis_index_groups=X_GROUPS)  11 us
    all_to_all x2, starting transfers between devices, along_x(): got = lax.all_to_all(copies, 'row', 0, 0, axis_index_groups=X_GROUPS)  10.9 us
    pallas_call x4, Pallas kernels, tile_stage(): pl.pallas_call(functools.partial(stage_kernel, group, first, last), out_s...  9.73 us
    broadcast_in_dim x2, local copies, waits for them, and re-layouts, along_x(): copies = jnp.broadcast_to(value[None], (X, *value.shape))  2.97 us
  transfers between devices with their start and end apart: 17, of which 8 were waited for; matrix products, arithmetic and copies ran while one was open for 4% of the time, Pallas kernels for 9%

commit v1 on v0

--- a/solution.py
+++ b/solution.py
@@ -102,7 +102,8 @@
     def place_of(relation, slot):
         source = cols_ref[0, 0, relation, slot]
         z, c = (source // 8) ^ (row_me // 8), (source % 2) ^ (row_me % 2)
-        return z * 2 + c, source // 2 % X
+        x = (row_me // 2 - source // 2 + 2 * X) % X
+        return c * 2 + z, jnp.where(x == 2, 3, jnp.where(x == 3, 2, x))
 
     for index in range(4 * relations + 1):
         starts_ref[index] = 0
@@ -173,7 +174,7 @@
         out_specs=[vmem] * len(out_shape),
         scratch_shapes=[pltpu.VMEM((many * size, width), jnp.bfloat16)],
         input_output_aliases={} if first else {len(args) - 1: 0},
-        compiler_params=pltpu.CompilerParams(vmem_limit_bytes=24 << 20),
+        compiler_params=pltpu.CompilerParams(vmem_limit_bytes=14 << 20),
         cost_estimate=pl.CostEstimate(flops=1 << 30, bytes_accessed=4 << 20, transcendentals=0),
         name="tile",
     )(*args)
@@ -205,31 +206,23 @@
     )(own, *ins)
 
 
-X_GROUPS = [[z * 8 + x * 2 + c for x in range(X)] for z in range(2) for c in range(CORES)]
-Y_GROUPS = [[z * Y + y for y in range(Y)] for z in range(Z)]
-Z_GROUPS = [[z * Y + y for z in range(Z)] for y in range(Y)]
-
-
-def along_x(value):
-    copies = jnp.broadcast_to(value[None], (X, *value.shape))
-    got = lax.all_to_all(copies, "row", 0, 0, axis_index_groups=X_GROUPS)
-    return got.reshape(X * value.shape[0], value.shape[1])
-
-
 def gather_groups(features, self_weight, tables, blocks, weights):
-    stage = lambda index, value, total, tables: tile_stage(index, tables, blocks, weights, value, total)
     far = row_shift(features, 1, 0, 0)
-    near = along_x(features)
+    near_parts = [features] + [row_shift(features, 0, d, 0) for d in (1, 3, 2)]
     self_term = jnp.dot(features, self_weight, preferred_element_type=jnp.float32)
     far, self_term, tables = lax.optimization_barrier((far, self_term, tables))
-    rest = along_x(far)
+    stage = lambda index, value, total: tile_stage(index, tables, blocks, weights, value, total)
+    far_parts = [far] + [row_shift(far, 0, d, 0) for d in (1, 3, 2)]
+
+    near = jnp.concatenate(near_parts, axis=0)
     near_other = row_shift(near, 0, 0, 1)
-    (total,) = stage(0, near, None, tables)
-    (total,) = stage(1, near_other, total, tables)
-    rest, total = lax.optimization_barrier((rest, total))
+    (total,) = stage(0, near, None)
+    far_parts[-1], total = lax.optimization_barrier((far_parts[-1], total))
+    rest = jnp.concatenate(far_parts, axis=0)
     rest_other = row_shift(rest, 0, 0, 1)
-    (total,) = stage(2, rest, total, tables)
-    return self_term, stage(3, rest_other, total, tables)[1:]
+    (total,) = stage(1, rest, total)
+    (total,) = stage(2, near_other, total)
+    return self_term, stage(3, rest_other, total)[1:]
 
 
 def scatter_sum(y_parts, z_parts):

time: 111 us -> 92.4 us (0.83)
  the two profiles are of different devices: /device:TPU:198 before, /device:TPU:4 now
where the time goes in v1:
time: 92.4 us; the launch traced here: 91.9 us
  starting transfers between devices  47.7 us (52%)
  waiting for transfers between devices  24 us (26%)
  Pallas kernels  10.7 us (12%)
  local copies, waits for them, and re-layouts  7.06 us (8%)
  matrix products  1.25 us (1%)
    ppermute x12, starting transfers between devices, col_shift(): return lax.ppermute(value, 'col', pairs)  32.1 us
    ppermute x12, waiting for transfers between devices, col_shift(): return lax.ppermute(value, 'col', pairs)  22.8 us
    ppermute x9, starting transfers between devices, row_shift(): return lax.ppermute(value, 'row', pairs)  15.6 us
    pallas_call x4, Pallas kernels, tile_stage(): pl.pallas_call(functools.partial(stage_kernel, group, first, last), out_s...  8.26 us
    unnamed x18, local copies, waits for them, and re-layouts  7.03 us
    pallas_call x1, Pallas kernels, plan(): pl.pallas_call(functools.partial(plan_kernel, slots), out_shape=[jax.Shap...  2.09 us
  transfers between devices with their start and end apart: 21, of which 7 were waited for; matrix products, arithmetic and copies ran while one was open for 4% of the time, Pallas kernels for 9%

profile of v1, /device:TPU:4, one launch (start us, length us, event | category | flops | bytes accessed | tf_op | source)
XLA Modules:
  0.0 91.9 jit_solution(12370862487083048202)
XLA Ops:
  0.5 1.5 %collective-permute-start.4 = (bf16[128,768]{1,0:T(8,128)(2,1)}, bf16[128,768]{1,0:T(8,128)(2,1)S(1)}, u32[]{:S(2)}, u32[]{:S(2)}) collective-permute-start(bf16[128,768]{1,0:T(8,128)(2,1)} %param.8), channel_id=1, source_target_pairs={{0,32},{16,48},{32,64},{48,80},{64,96},{80,112},{96,0},{112,16},{1... | collective-permute-start | bytes 589832 | tf_op jit(solution)/shard_map/ppermute | solution.py:20
  2.0 7.2 %collective-permute-start = (bf16[128,768]{1,0:T(8,128)(2,1)}, bf16[128,768]{1,0:T(8,128)(2,1)S(1)}, u32[]{:S(2)}, u32[]{:S(2)}) collective-permute-start(bf16[128,768]{1,0:T(8,128)(2,1)} %param.8), channel_id=1, source_target_pairs={{0,128},{16,144},{32,160},{48,176},{64,192},{80,208},{96,224},{112... | collective-permute-start | bytes 589832 | tf_op jit(solution)/shard_map/ppermute | solution.py:20
  9.2 1.2 %collective-permute-start.6 = (bf16[128,768]{1,0:T(8,128)(2,1)}, bf16[128,768]{1,0:T(8,128)(2,1)S(1)}, u32[]{:S(2)}, u32[]{:S(2)}) collective-permute-start(bf16[128,768]{1,0:T(8,128)(2,1)} %param.8), channel_id=1, source_target_pairs={{0,64},{16,80},{32,96},{48,112},{64,0},{80,16},{96,32},{112,48},{1... | collective-permute-start | bytes 589832 | tf_op jit(solution)/shard_map/ppermute | solution.py:20
  11.8 1.3 %fusion.3 = f32[128,768]{1,0:T(8,128)S(1)} fusion(bf16[128,768]{1,0:T(8,128)(2,1)} %param.8, bf16[768,768]{1,0:T(8,128)(2,1)S(1)} %copy-done), kind=kOutput, calls=%fused_computation.15 | convolution fusion | flops 150994944 | bytes 1769472 | tf_op jit(solution)/shard_map/dot_general | solution.py:212
  13.8 2.1 %plan.1 = (s32[40]{0:T(128)S(1)}, s32[21]{0:T(128)S(1)}) custom-call(s32[2]{0:T(128)S(1)} %pad_add_fusion.me_ref, s32[1,1,5,8]{3,2,1,0:T(8,128)S(1)} %copy.12.rows_ref, s32[1,1,5,8]{3,2,1,0:T(8,128)S(1)} %copy.13.cols_ref, s32[1,1,5]{2,1,0:T(1,128)S(1)} %copy-done.3), custom_call_target="tpu_custom_call" | custom-call | tf_op jit(solution)/shard_map/plan/pallas_call | solution.py:144
  16.9 2.9 %collective-permute-start.3 = (bf16[128,768]{1,0:T(8,128)(2,1)S(1)}, bf16[128,768]{1,0:T(8,128)(2,1)S(1)}, u32[]{:S(2)}, u32[]{:S(2)}) collective-permute-start(bf16[128,768]{1,0:T(8,128)(2,1)S(1)} %collective-permute-done), channel_id=1, source_target_pairs={{0,64},{16,80},{32,96},{48,112},{64,0},{80,16},{96,32},{112,48},{1... | collective-permute-start | bytes 589832 | tf_op jit(solution)/shard_map/ppermute | solution.py:20
  20.1 1.7 %collective-permute-start.1 = (bf16[128,768]{1,0:T(8,128)(2,1)S(1)}, bf16[128,768]{1,0:T(8,128)(2,1)S(1)}, u32[]{:S(2)}, u32[]{:S(2)}) collective-permute-start(bf16[128,768]{1,0:T(8,128)(2,1)S(1)} %collective-permute-done), channel_id=1, source_target_pairs={{0,32},{16,48},{32,64},{48,80},{64,96},{80,112},{96,0},{112,16},{1... | collective-permute-start | bytes 589832 | tf_op jit(solution)/shard_map/ppermute | solution.py:20
  22.0 2.7 %copy-done.1 = bf16[768,5,768]{2,0,1:T(8,128)(2,1)S(1)} copy-done((bf16[768,5,768]{2,0,1:T(8,128)(2,1)S(1)}, bf16[768,5,768]{2,0,1:T(8,128)(2,1)}, u32[]{:S(2)}) %copy-start.1) | copy-done | bytes 5898264
  24.7 1.3 %copy-done.2 = bf16[1,1,5,8,128,128]{5,4,3,2,1,0:T(8,128)(2,1)S(1)} copy-done((bf16[1,1,5,8,128,128]{5,4,3,2,1,0:T(8,128)(2,1)S(1)}, bf16[1,1,5,8,128,128]{5,4,3,2,1,0:T(8,128)(2,1)}, u32[]{:S(2)}) %copy-start.2) | copy-done | bytes 1310744
  26.0 2.3 %tile.4.refs_0_ = f32[2048,768]{1,0:T(8,128)S(1)} custom-call(s32[40]{0:T(128)S(1)} %get-tuple-element.42.codes_ref, s32[21]{0:T(128)S(1)} %get-tuple-element.43.starts_ref, bf16[40,128,128]{2,1,0:T(8,128)(2,1)S(1)} %bitcast.10, bf16[5,768,768]{2,1,0:T(8,128)(2,1)S(1)} %bitcast.6, bf16[512,768]{1,0:T(8,128)(2,1)S(1)} %constant_dynamic-update-slice_fusion.group_ref), custom_call_target="tpu_custom_call" | custom-call | flops 1073741824 | bytes 4194304 | tf_op jit(solution)/shard_map/tile/pallas_call | solution.py:170
  29.6 1.7 %tile.5.refs_0_ = f32[2048,768]{1,0:T(8,128)S(1)} custom-call(s32[40]{0:T(128)S(1)} %get-tuple-element.42.codes_ref, s32[21]{0:T(128)S(1)} %get-tuple-element.43.starts_ref, bf16[40,128,128]{2,1,0:T(8,128)(2,1)S(1)} %bitcast.11, bf16[5,768,768]{2,1,0:T(8,128)(2,1)S(1)} %bitcast.7, ...), custom_call_target="tpu_custom_call", output_to_operand_aliasing={{}: (5, {})} | custom-call | flops 1073741824 | bytes 4194304 | tf_op jit(solution)/shard_map/tile/pallas_call | solution.py:170
  31.4 1.9 %tile.6.refs_0_ = f32[2048,768]{1,0:T(8,128)S(1)} custom-call(s32[40]{0:T(128)S(1)} %get-tuple-element.42.codes_ref, s32[21]{0:T(128)S(1)} %get-tuple-element.43.starts_ref, bf16[40,128,128]{2,1,0:T(8,128)(2,1)S(1)} %bitcast.12, bf16[5,768,768]{2,1,0:T(8,128)(2,1)S(1)} %bitcast.8, ...), custom_call_target="tpu_custom_call", output_to_operand_aliasing={{}: (5, {})} | custom-call | flops 1073741824 | bytes 4194304 | tf_op jit(solution)/shard_map/tile/pallas_call | solution.py:170
  33.3 2.3 %tile.7 = (f32[2048,768]{1,0:T(8,128)S(1)}, bf16[4,128,512]{2,1,0:T(8,128)(2,1)S(1)}, bf16[4,128,512]{2,1,0:T(8,128)(2,1)S(1)}, bf16[4,128,512]{2,1,0:T(8,128)(2...) custom-call(s32[40]{0:T(128)S(1)} %get-tuple-element.42.codes_ref, ...), custom_call_target="tpu_custom_call", output_to_operand_aliasing={{0}: (5, {})} | custom-call | flops 1073741824 | bytes 4194304 | tf_op jit(solution)/shard_map/tile/pallas_call | solution.py:170
  35.7 4.4 %collective-permute-start.9 = (bf16[4,128,512]{2,1,0:T(8,128)(2,1)S(1)}, bf16[4,128,512]{2,1,0:T(8,128)(2,1)S(1)}, u32[]{:S(2)}, u32[]{:S(2)}) collective-permute-start(bf16[4,128,512]{2,1,0:T(8,128)(2,1)S(1)} %get-tuple-element.48), channel_id=1, source_target_pairs={{0,1},{1,2},{2,3},{3,0},{4,5},{5,6},{6,7},{7,4},{8,9},{9,10},{10,1... | collective-permute-start | bytes 1572872 | tf_op jit(solution)/shard_map/ppermute | solution.py:28
  40.6 1.7 %collective-permute-start.11 = (bf16[4,128,512]{2,1,0:T(8,128)(2,1)S(1)}, bf16[4,128,512]{2,1,0:T(8,128)(2,1)S(1)}, u32[]{:S(2)}, u32[]{:S(2)}) collective-permute-start(bf16[4,128,512]{2,1,0:T(8,128)(2,1)S(1)} %get-tuple-element.50), channel_id=1, source_target_pairs={{0,2},{1,3},{2,0},{3,1},{4,6},{5,7},{6,4},{7,5},{8,10},{9,11},{10,... | collective-permute-start | bytes 1572872 | tf_op jit(solution)/shard_map/ppermute | solution.py:28
  42.3 3.0 %collective-permute-start.12 = (bf16[4,128,256]{2,1,0:T(8,128)(2,1)S(1)}, bf16[4,128,256]{2,1,0:T(8,128)(2,1)S(1)}, u32[]{:S(2)}, u32[]{:S(2)}) collective-permute-start(bf16[4,128,256]{2,1,0:T(8,128)(2,1)S(1)} %get-tuple-element.52), channel_id=1, source_target_pairs={{0,4},{1,5},{2,6},{3,7},{4,8},{5,9},{6,10},{7,11},{8,12},{9,13},{1... | collective-permute-start | bytes 786440 | tf_op jit(solution)/shard_map/ppermute | solution.py:28
  46.1 7.9 %collective-permute-done.9.refs_0_ = bf16[4,128,512]{2,1,0:T(8,128)(2,1)S(1)} collective-permute-done((bf16[4,128,512]{2,1,0:T(8,128)(2,1)S(1)}, bf16[4,128,512]{2,1,0:T(8,128)(2,1)S(1)}, u32[]{:S(2)}, u32[]{:S(2)}) %collective-permute-start.9) | collective-permute-done | bytes 524320 | tf_op jit(solution)/shard_map/ppermute | solution.py:28
  54.8 9.5 %collective-permute-done.11.refs_2_ = bf16[4,128,512]{2,1,0:T(8,128)(2,1)S(1)} collective-permute-done((bf16[4,128,512]{2,1,0:T(8,128)(2,1)S(1)}, bf16[4,128,512]{2,1,0:T(8,128)(2,1)S(1)}, u32[]{:S(2)}, u32[]{:S(2)}) %collective-permute-start.11) | collective-permute-done | bytes 524320 | tf_op jit(solution)/shard_map/ppermute | solution.py:28
  64.5 2.6 %collective-permute-done.14.refs_2_ = bf16[4,128,256]{2,1,0:T(8,128)(2,1)S(1)} collective-permute-done((bf16[4,128,256]{2,1,0:T(8,128)(2,1)S(1)}, bf16[4,128,256]{2,1,0:T(8,128)(2,1)S(1)}, u32[]{:S(2)}, u32[]{:S(2)}) %collective-permute-start.14) | collective-permute-done | bytes 262176 | tf_op jit(solution)/shard_map/ppermute | solution.py:28
  67.1 10.6 %collective-permute-start.15 = (bf16[128,512]{1,0:T(8,128)(2,1)S(1)}, bf16[128,512]{1,0:T(8,128)(2,1)S(1)}, u32[]{:S(2)}, u32[]{:S(2)}) collective-permute-start(bf16[128,512]{1,0:T(8,128)(2,1)S(1)} %get-tuple-element.58), channel_id=1, source_target_pairs={{0,4},{1,5},{2,6},{3,7},{4,8},{5,9},{6,10},{7,11},{8,12},{9,13},{1... | collective-permute-start | bytes 393224 | tf_op jit(solution)/shard_map/ppermute | solution.py:28
  77.7 2.8 %collective-permute-start.16 = (bf16[128,512]{1,0:T(8,128)(2,1)S(1)}, bf16[128,512]{1,0:T(8,128)(2,1)S(1)}, u32[]{:S(2)}, u32[]{:S(2)}) collective-permute-start(bf16[128,512]{1,0:T(8,128)(2,1)S(1)} %get-tuple-element.59), channel_id=1, source_target_pairs={{0,12},{1,13},{2,14},{3,15},{4,0},{5,1},{6,2},{7,3},{8,4},{9,5},{1... | collective-permute-start | bytes 393224 | tf_op jit(solution)/shard_map/ppermute | solution.py:28
  82.0 2.5 %collective-permute-start.19 = (bf16[128,256]{1,0:T(8,128)(2,1)S(1)}, bf16[128,256]{1,0:T(8,128)(2,1)S(1)}, u32[]{:S(2)}, u32[]{:S(2)}) collective-permute-start(bf16[128,256]{1,0:T(8,128)(2,1)S(1)} %get-tuple-element.66), channel_id=1, source_target_pairs={{0,3},{1,0},{2,1},{3,2},{4,7},{5,4},{6,5},{7,6},{8,11},{9,8},{10,9... | collective-permute-start | bytes 196616 | tf_op jit(solution)/shard_map/ppermute | solution.py:28
  84.5 4.3 %collective-permute-start.20 = (bf16[128,256]{1,0:T(8,128)(2,1)S(1)}, bf16[128,256]{1,0:T(8,128)(2,1)S(1)}, u32[]{:S(2)}, u32[]{:S(2)}) collective-permute-start(bf16[128,256]{1,0:T(8,128)(2,1)S(1)} %get-tuple-element.67), channel_id=1, source_target_pairs={{0,2},{1,3},{2,0},{3,1},{4,6},{5,7},{6,4},{7,5},{8,10},{9,11},{10,... | collective-permute-start | bytes 196616 | tf_op jit(solution)/shard_map/ppermute | solution.py:28
  88.9 2.1 %collective-permute-done.20 = bf16[128,256]{1,0:T(8,128)(2,1)S(1)} collective-permute-done((bf16[128,256]{1,0:T(8,128)(2,1)S(1)}, bf16[128,256]{1,0:T(8,128)(2,1)S(1)}, u32[]{:S(2)}, u32[]{:S(2)}) %collective-permute-start.20) | collective-permute-done | bytes 65568 | tf_op jit(solution)/shard_map/ppermute | solution.py:28
  (50 shorter events, 9.9 us)
Async XLA Ops:
  0.0 11.8 %copy-start = (bf16[768,768]{1,0:T(8,128)(2,1)S(1)}, bf16[768,768]{1,0:T(8,128)(2,1)}, u32[]{:S(2)}) copy-start(bf16[768,768]{1,0:T(8,128)(2,1)} %param.9) | copy-start | bytes 3538948
  0.0 21.8 %collective-permute-start.5 = (bf16[128,768]{1,0:T(8,128)(2,1)}, bf16[128,768]{1,0:T(8,128)(2,1)S(1)}, u32[]{:S(2)}, u32[]{:S(2)}) collective-permute-start(bf16[128,768]{1,0:T(8,128)(2,1)} %param.8), channel_id=1, source_target_pairs={{0,96},{16,112},{32,0},{48,16},{64,32},{80,48},{96,64},{112,80},{1... | collective-permute-start | bytes 589832 | tf_op jit(solution)/shard_map/ppermute | solution.py:20
  0.5 19.5 %collective-permute-start.4 = (bf16[128,768]{1,0:T(8,128)(2,1)}, bf16[128,768]{1,0:T(8,128)(2,1)S(1)}, u32[]{:S(2)}, u32[]{:S(2)}) collective-permute-start(bf16[128,768]{1,0:T(8,128)(2,1)} %param.8), channel_id=1, source_target_pairs={{0,32},{16,48},{32,64},{48,80},{64,96},{80,112},{96,0},{112,16},{1... | collective-permute-start | bytes 589832 | tf_op jit(solution)/shard_map/ppermute | solution.py:20
  2.0 14.8 %collective-permute-start = (bf16[128,768]{1,0:T(8,128)(2,1)}, bf16[128,768]{1,0:T(8,128)(2,1)S(1)}, u32[]{:S(2)}, u32[]{:S(2)}) collective-permute-start(bf16[128,768]{1,0:T(8,128)(2,1)} %param.8), channel_id=1, source_target_pairs={{0,128},{16,144},{32,160},{48,176},{64,192},{80,208},{96,224},{112... | collective-permute-start | bytes 589832 | tf_op jit(solution)/shard_map/ppermute | solution.py:20
  9.2 12.6 %collective-permute-start.6 = (bf16[128,768]{1,0:T(8,128)(2,1)}, bf16[128,768]{1,0:T(8,128)(2,1)S(1)}, u32[]{:S(2)}, u32[]{:S(2)}) collective-permute-start(bf16[128,768]{1,0:T(8,128)(2,1)} %param.8), channel_id=1, source_target_pairs={{0,64},{16,80},{32,96},{48,112},{64,0},{80,16},{96,32},{112,48},{1... | collective-permute-start | bytes 589832 | tf_op jit(solution)/shard_map/ppermute | solution.py:20
  16.9 11.4 %collective-permute-start.3 = (bf16[128,768]{1,0:T(8,128)(2,1)S(1)}, bf16[128,768]{1,0:T(8,128)(2,1)S(1)}, u32[]{:S(2)}, u32[]{:S(2)}) collective-permute-start(bf16[128,768]{1,0:T(8,128)(2,1)S(1)} %collective-permute-done), channel_id=1, source_target_pairs={{0,64},{16,80},{32,96},{48,112},{64,0},{80,16},{96,32},{112,48},{1... | collective-permute-start | bytes 589832 | tf_op jit(solution)/shard_map/ppermute | solution.py:20
  19.8 9.7 %collective-permute-start.2 = (bf16[128,768]{1,0:T(8,128)(2,1)S(1)}, bf16[128,768]{1,0:T(8,128)(2,1)S(1)}, u32[]{:S(2)}, u32[]{:S(2)}) collective-permute-start(bf16[128,768]{1,0:T(8,128)(2,1)S(1)} %collective-permute-done), channel_id=1, source_target_pairs={{0,96},{16,112},{32,0},{48,16},{64,32},{80,48},{96,64},{112,80},{1... | collective-permute-start | bytes 589832 | tf_op jit(solution)/shard_map/ppermute | solution.py:20
  20.1 8.7 %collective-permute-start.1 = (bf16[128,768]{1,0:T(8,128)(2,1)S(1)}, bf16[128,768]{1,0:T(8,128)(2,1)S(1)}, u32[]{:S(2)}, u32[]{:S(2)}) collective-permute-start(bf16[128,768]{1,0:T(8,128)(2,1)S(1)} %collective-permute-done), channel_id=1, source_target_pairs={{0,32},{16,48},{32,64},{48,80},{64,96},{80,112},{96,0},{112,16},{1... | collective-permute-start | bytes 589832 | tf_op jit(solution)/shard_map/ppermute | solution.py:20
  21.9 9.5 %collective-permute-start.8 = (bf16[512,768]{1,0:T(8,128)(2,1)S(1)}, bf16[512,768]{1,0:T(8,128)(2,1)S(1)}, u32[]{:S(2)}, u32[]{:S(2)}) collective-permute-start(bf16[512,768]{1,0:T(8,128)(2,1)S(1)} %constant_dynamic-update-slice_fusion.group_ref), channel_id=1, source_target_pairs={{0,16},{16,0},{32,48},{48,32},{64,80},{80,64},{96,112},{112,96},{1... | collective-permute-start | bytes 2359304 | tf_op jit(solution)/shard_map/ppermute | solution.py:20
  22.0 2.7 %copy-start.1 = (bf16[768,5,768]{2,0,1:T(8,128)(2,1)S(1)}, bf16[768,5,768]{2,0,1:T(8,128)(2,1)}, u32[]{:S(2)}) copy-start(bf16[768,5,768]{2,0,1:T(8,128)(2,1)} %param.10) | copy-start | bytes 17694724
  29.5 3.8 %collective-permute-start.7 = (bf16[512,768]{1,0:T(8,128)(2,1)S(1)}, bf16[512,768]{1,0:T(8,128)(2,1)S(1)}, u32[]{:S(2)}, u32[]{:S(2)}) collective-permute-start(bf16[512,768]{1,0:T(8,128)(2,1)S(1)} %constant_dynamic-update-slice_fusion.4.group_ref), channel_id=1, source_target_pairs={{0,16},{16,0},{32,48},{48,32},{64,80},{80,64},{96,112},{112,96},{1... | collective-permute-start | bytes 2359304 | tf_op jit(solution)/shard_map/ppermute | solution.py:20
  33.3 57.8 %copy-start.4 = (f32[768]{0:T(1024)S(1)}, f32[768]{0:T(1024)}, u32[]{:S(2)}) copy-start(f32[768]{0:T(1024)} %param.11) | copy-start | bytes 9220
  35.7 18.3 %collective-permute-start.9 = (bf16[4,128,512]{2,1,0:T(8,128)(2,1)S(1)}, bf16[4,128,512]{2,1,0:T(8,128)(2,1)S(1)}, u32[]{:S(2)}, u32[]{:S(2)}) collective-permute-start(bf16[4,128,512]{2,1,0:T(8,128)(2,1)S(1)} %get-tuple-element.48), channel_id=1, source_target_pairs={{0,1},{1,2},{2,3},{3,0},{4,5},{5,6},{6,7},{7,4},{8,9},{9,10},{10,1... | collective-permute-start | bytes 1572872 | tf_op jit(solution)/shard_map/ppermute | solution.py:28
  40.1 14.7 %collective-permute-start.10 = (bf16[4,128,512]{2,1,0:T(8,128)(2,1)S(1)}, bf16[4,128,512]{2,1,0:T(8,128)(2,1)S(1)}, u32[]{:S(2)}, u32[]{:S(2)}) collective-permute-start(bf16[4,128,512]{2,1,0:T(8,128)(2,1)S(1)} %get-tuple-element.49), channel_id=1, source_target_pairs={{0,3},{1,0},{2,1},{3,2},{4,7},{5,4},{6,5},{7,6},{8,11},{9,8},{10,9... | collective-permute-start | bytes 1572872 | tf_op jit(solution)/shard_map/ppermute | solution.py:28
  40.6 23.7 %collective-permute-start.11 = (bf16[4,128,512]{2,1,0:T(8,128)(2,1)S(1)}, bf16[4,128,512]{2,1,0:T(8,128)(2,1)S(1)}, u32[]{:S(2)}, u32[]{:S(2)}) collective-permute-start(bf16[4,128,512]{2,1,0:T(8,128)(2,1)S(1)} %get-tuple-element.50), channel_id=1, source_target_pairs={{0,2},{1,3},{2,0},{3,1},{4,6},{5,7},{6,4},{7,5},{8,10},{9,11},{10,... | collective-permute-start | bytes 1572872 | tf_op jit(solution)/shard_map/ppermute | solution.py:28
  42.3 22.2 %collective-permute-start.12 = (bf16[4,128,256]{2,1,0:T(8,128)(2,1)S(1)}, bf16[4,128,256]{2,1,0:T(8,128)(2,1)S(1)}, u32[]{:S(2)}, u32[]{:S(2)}) collective-permute-start(bf16[4,128,256]{2,1,0:T(8,128)(2,1)S(1)} %get-tuple-element.52), channel_id=1, source_target_pairs={{0,4},{1,5},{2,6},{3,7},{4,8},{5,9},{6,10},{7,11},{8,12},{9,13},{1... | collective-permute-start | bytes 786440 | tf_op jit(solution)/shard_map/ppermute | solution.py:28
  45.3 19.2 %collective-permute-start.13 = (bf16[4,128,256]{2,1,0:T(8,128)(2,1)S(1)}, bf16[4,128,256]{2,1,0:T(8,128)(2,1)S(1)}, u32[]{:S(2)}, u32[]{:S(2)}) collective-permute-start(bf16[4,128,256]{2,1,0:T(8,128)(2,1)S(1)} %get-tuple-element.53), channel_id=1, source_target_pairs={{0,12},{1,13},{2,14},{3,15},{4,0},{5,1},{6,2},{7,3},{8,4},{9,5},{1... | collective-permute-start | bytes 786440 | tf_op jit(solution)/shard_map/ppermute | solution.py:28
  54.0 13.1 %collective-permute-start.14 = (bf16[4,128,256]{2,1,0:T(8,128)(2,1)S(1)}, bf16[4,128,256]{2,1,0:T(8,128)(2,1)S(1)}, u32[]{:S(2)}, u32[]{:S(2)}) collective-permute-start(bf16[4,128,256]{2,1,0:T(8,128)(2,1)S(1)} %get-tuple-element.54), channel_id=1, source_target_pairs={{0,8},{1,9},{2,10},{3,11},{4,12},{5,13},{6,14},{7,15},{8,0},{9,1},... | collective-permute-start | bytes 786440 | tf_op jit(solution)/shard_map/ppermute | solution.py:28
  67.1 17.4 %collective-permute-start.15 = (bf16[128,512]{1,0:T(8,128)(2,1)S(1)}, bf16[128,512]{1,0:T(8,128)(2,1)S(1)}, u32[]{:S(2)}, u32[]{:S(2)}) collective-permute-start(bf16[128,512]{1,0:T(8,128)(2,1)S(1)} %get-tuple-element.58), channel_id=1, source_target_pairs={{0,4},{1,5},{2,6},{3,7},{4,8},{5,9},{6,10},{7,11},{8,12},{9,13},{1... | collective-permute-start | bytes 393224 | tf_op jit(solution)/shard_map/ppermute | solution.py:28
  77.7 11.1 %collective-permute-start.16 = (bf16[128,512]{1,0:T(8,128)(2,1)S(1)}, bf16[128,512]{1,0:T(8,128)(2,1)S(1)}, u32[]{:S(2)}, u32[]{:S(2)}) collective-permute-start(bf16[128,512]{1,0:T(8,128)(2,1)S(1)} %get-tuple-element.59), channel_id=1, source_target_pairs={{0,12},{1,13},{2,14},{3,15},{4,0},{5,1},{6,2},{7,3},{8,4},{9,5},{1... | collective-permute-start | bytes 393224 | tf_op jit(solution)/shard_map/ppermute | solution.py:28
  80.5 8.3 %collective-permute-start.17 = (bf16[128,512]{1,0:T(8,128)(2,1)S(1)}, bf16[128,512]{1,0:T(8,128)(2,1)S(1)}, u32[]{:S(2)}, u32[]{:S(2)}) collective-permute-start(bf16[128,512]{1,0:T(8,128)(2,1)S(1)} %get-tuple-element.60), channel_id=1, source_target_pairs={{0,8},{1,9},{2,10},{3,11},{4,12},{5,13},{6,14},{7,15},{8,0},{9,1},... | collective-permute-start | bytes 393224 | tf_op jit(solution)/shard_map/ppermute | solution.py:28
  81.2 7.7 %collective-permute-start.18 = (bf16[128,256]{1,0:T(8,128)(2,1)S(1)}, bf16[128,256]{1,0:T(8,128)(2,1)S(1)}, u32[]{:S(2)}, u32[]{:S(2)}) collective-permute-start(bf16[128,256]{1,0:T(8,128)(2,1)S(1)} %get-tuple-element.65), channel_id=1, source_target_pairs={{0,1},{1,2},{2,3},{3,0},{4,5},{5,6},{6,7},{7,4},{8,9},{9,10},{10,1... | collective-permute-start | bytes 196616 | tf_op jit(solution)/shard_map/ppermute | solution.py:28
  82.0 6.9 %collective-permute-start.19 = (bf16[128,256]{1,0:T(8,128)(2,1)S(1)}, bf16[128,256]{1,0:T(8,128)(2,1)S(1)}, u32[]{:S(2)}, u32[]{:S(2)}) collective-permute-start(bf16[128,256]{1,0:T(8,128)(2,1)S(1)} %get-tuple-element.66), channel_id=1, source_target_pairs={{0,3},{1,0},{2,1},{3,2},{4,7},{5,4},{6,5},{7,6},{8,11},{9,8},{10,9... | collective-permute-start | bytes 196616 | tf_op jit(solution)/shard_map/ppermute | solution.py:28
  84.5 6.5 %collective-permute-start.20 = (bf16[128,256]{1,0:T(8,128)(2,1)S(1)}, bf16[128,256]{1,0:T(8,128)(2,1)S(1)}, u32[]{:S(2)}, u32[]{:S(2)}) collective-permute-start(bf16[128,256]{1,0:T(8,128)(2,1)S(1)} %get-tuple-element.67), channel_id=1, source_target_pairs={{0,2},{1,3},{2,0},{3,1},{4,6},{5,7},{6,4},{7,5},{8,10},{9,11},{10,... | collective-permute-start | bytes 196616 | tf_op jit(solution)/shard_map/ppermute | solution.py:28
  (2 other events, 2.0 us)

commit v2 on v1

v2 whole, which is shorter than its diff:
```python
import functools

import jax
import jax.numpy as jnp
from jax import lax
from jax.experimental import pallas as pl
from jax.experimental.pallas import tpu as pltpu
from jax.sharding import PartitionSpec as P

Z, Y = 4, 4
SPLIT = 512
UNROLL, QUAD = 4, 4


def row_swap(value, dz, dx, dc):
    return lax.ppermute(value, "row", [(at, at ^ (dz * 8 + dx * 2 + dc)) for at in range(16)])


def col_swap(value, dz, dy):
    return lax.ppermute(value, "col", [(at, at ^ (dz * Y + dy)) for at in range(16)])


def rows_at(index, size):
    return pl.ds(pl.multiple_of(index * size, size), size)


def stage_kernel(group, first, last, codes_ref, starts_ref, blocks_ref, weight_ref, group_ref, *refs):
    if not first:
        refs = refs[1:]
    total, refs = refs[0], refs[1:]
    if last:
        y_refs, z_refs, refs = refs[:Y], refs[Y : Y + 2], refs[Y + 2 :]
    (picked,) = refs
    relations = weight_ref.shape[0]
    size = blocks_ref.shape[-1]
    if first:
        total[...] = jnp.zeros_like(total)
    base = starts_ref[group * relations]
    length = starts_ref[(group + 1) * relations] - base

    def pick(step, carry):
        for u in range(UNROLL):
            n = jnp.minimum(step * UNROLL + u, length - 1)
            code = codes_ref[base + n]
            product = jnp.dot(
                blocks_ref[code // 64],
                group_ref[rows_at(code // 16 % 4, size), :],
                preferred_element_type=jnp.float32,
            )
            picked[rows_at(n, size), :] = product.astype(picked.dtype)
        return carry

    lax.fori_loop(0, (length + UNROLL - 1) // UNROLL, pick, 0)

    def spread(relation, carry):
        start = starts_ref[group * relations + relation]
        end = starts_ref[group * relations + relation + 1]

        def quad(step, carry):
            begin = start + step * QUAD
            for count in range(1, QUAD + 1):
                enough = (end - begin >= count) if count == QUAD else (end - begin == count)

                @pl.when(enough)
                def _():
                    moved = jnp.dot(
                        picked[pl.ds(pl.multiple_of((begin - base) * size, size), count * size), :],
                        weight_ref[relation],
                        preferred_element_type=jnp.float32,
                    )
                    for part in range(count):
                        target = rows_at(codes_ref[begin + part] % 16, size)
                        total[target, :] += moved[part * size : (part + 1) * size]

            return carry

        return lax.fori_loop(0, (end - start + QUAD - 1) // QUAD, quad, carry)

    lax.fori_loop(0, relations, spread, 0)
    if last:
        for d in range(Y):
            for e in range(Z):
                rows = pl.ds((d * Z + e) * size, size)
                y_refs[d][e] = total[rows, :SPLIT].astype(jnp.bfloat16)
                z_refs[e % 2][e // 2, d] = total[rows, SPLIT:].astype(jnp.bfloat16)


def plan_kernel(relations, me_ref, table_ref, codes_ref, starts_ref):
    slots = table_ref.shape[0] // relations
    row_me, col_me = me_ref[0] >> 4, me_ref[0] & 15
    for index in range(4 * relations + 1):
        starts_ref[index] = 0

    def parts(at):
        packed = table_ref[at]
        source = (packed >> 4 & 15) ^ row_me
        target = (packed & 15) ^ col_me
        return packed >> 8, (source & 1) * 2 + (source >> 3), source >> 1 & 3, (target & 3) * 4 + (target >> 2)

    def per_slot(act):
        for relation in range(relations):
            live = table_ref[relation * slots] >> 8

            def body(slot, carry):
                at = relation * slots + slot
                _, group, place, target = parts(at)
                act(group * relations + relation, at, place, target)
                return carry

            lax.fori_loop(0, live, body, 0)

    def count(index, at, place, target):
        starts_ref[index + 1] = starts_ref[index + 1] + 1

    def put(index, at, place, target):
        spot = starts_ref[index]
        codes_ref[spot] = at * 64 + place * 16 + target
        starts_ref[index] = spot + 1

    per_slot(count)
    for index in range(1, 4 * relations + 1):
        starts_ref[index] = starts_ref[index] + starts_ref[index - 1]
    per_slot(put)
    for index in range(4 * relations - 1, 0, -1):
        starts_ref[index] = starts_ref[index - 1]
    starts_ref[0] = 0


def plan(me, block_rows, block_cols, block_counts):
    relations, slots = block_rows.shape[2:]
    smem = pl.BlockSpec(memory_space=pltpu.SMEM)
    many = relations * slots
    table = (block_rows + block_cols * 16 + block_counts[..., None] * 256).reshape(many)
    return pl.pallas_call(
        functools.partial(plan_kernel, relations),
        out_shape=[
            jax.ShapeDtypeStruct((many,), jnp.int32),
            jax.ShapeDtypeStruct((4 * relations + 1,), jnp.int32),
        ],
        in_specs=[smem] * 2,
        out_specs=[smem] * 2,
        compiler_params=pltpu.CompilerParams(vmem_limit_bytes=1 << 20),
        name="plan",
    )(me, table)


def tile_stage(group, tables, blocks, weights, value, total):
    many, size, _ = blocks.shape
    width = weights.shape[-1]
    first, last = group == 0, group == 3
    vmem = pl.BlockSpec(memory_space=pltpu.VMEM)
    smem = pl.BlockSpec(memory_space=pltpu.SMEM)
    out_shape = [jax.ShapeDtypeStruct((Y * Z * size, width), jnp.float32)]
    if last:
        out_shape += [jax.ShapeDtypeStruct((Z, size, SPLIT), jnp.bfloat16)] * Y
        out_shape += [jax.ShapeDtypeStruct((Z // 2, Y, size, width - SPLIT), jnp.bfloat16)] * 2
    args = [*tables, blocks, weights, value]
    if not first:
        args.append(total)
    return pl.pallas_call(
        functools.partial(stage_kernel, group, first, last),
        out_shape=out_shape,
        in_specs=[smem] * 2 + [vmem] * (len(args) - 2),
        out_specs=[vmem] * len(out_shape),
        scratch_shapes=[pltpu.VMEM((many * size, width), jnp.bfloat16)],
        input_output_aliases={} if first else {len(args) - 1: 0},
        compiler_params=pltpu.CompilerParams(vmem_limit_bytes=14 << 20),
        cost_estimate=pl.CostEstimate(flops=1 << 30, bytes_accessed=4 << 20, transcendentals=0),
        name="tile",
    )(*args)


def small(function, out_shape, *args):
    def kernel(*refs):
        function(refs[: len(args)], refs[len(args) :])

    vmem = pl.BlockSpec(memory_space=pltpu.VMEM)
    return pl.pallas_call(
        kernel,
        out_shape=out_shape,
        in_specs=[vmem] * len(args),
        out_specs=[vmem] * len(out_shape),
        compiler_params=pltpu.CompilerParams(vmem_limit_bytes=4 << 20),
        name="merge",
    )(*args)


def merge_y(ins, outs):
    for e in range(Z):
        summed = sum(ref[e].astype(jnp.float32) for ref in ins)
        outs[e][...] = summed.astype(outs[e].dtype)


def merge_z_near(ins, outs):
    own, got = ins
    outs[0][...] = own[0].astype(jnp.float32) + got[0].astype(jnp.float32)
    outs[1][...] = (own[1].astype(jnp.float32) + got[1].astype(jnp.float32)).astype(jnp.bfloat16)


def merge_z_far(ins, outs):
    kept, got = ins
    for d in range(Y):
        summed = kept[d] + got[d].astype(jnp.float32)
        if d == 0 or d == 3:
            outs[d // 3][...] = summed
        else:
            outs[2][d - 1] = summed.astype(jnp.bfloat16)


def merge_z_last(ins, outs):
    here, across, got = ins
    outs[0][...] = here[...] + got[0].astype(jnp.float32)
    outs[1][...] = (across[...] + got[1].astype(jnp.float32)).astype(jnp.bfloat16)


def gather_groups(features, self_weight, to_plan, blocks, weights):
    far = row_swap(features, 1, 0, 0)
    near_parts = [features] + [row_swap(features, 0, d, 0) for d in (1, 2, 3)]
    self_term = jnp.dot(features, self_weight, preferred_element_type=jnp.float32)
    far, self_term, to_plan = lax.optimization_barrier((far, self_term, to_plan))
    tables = plan(*to_plan)
    stage = lambda index, value, total: tile_stage(index, tables, blocks, weights, value, total)
    far_parts = [far] + [row_swap(far, 0, d, 0) for d in (1, 2, 3)]
    near = jnp.concatenate(near_parts, axis=0)
    near_other = row_swap(near, 0, 0, 1)
    (total,) = stage(0, near, None)
    far_parts[-1], total = lax.optimization_barrier((far_parts[-1], total))
    rest = jnp.concatenate(far_parts, axis=0)
    rest_other = row_swap(rest, 0, 0, 1)
    (total,) = stage(1, rest, total)
    (total,) = stage(2, near_other, total)
    return self_term, stage(3, rest_other, total)[1:]


def scatter_sum(parts):
    y_parts, (z_here, z_there) = parts[:Y], parts[Y:]
    f32, bf16 = jnp.float32, jnp.bfloat16
    many, size, columns = z_here.shape[1:]
    piece = (size, columns)
    z_near = col_swap(z_there, 1, 0)
    y_in = [col_swap(y_parts[d], 0, d) for d in (2, 1, 3)]
    shapes = [jax.ShapeDtypeStruct((many, *piece), f32), jax.ShapeDtypeStruct((many, *piece), bf16)]
    z_kept, z_send = small(merge_z_near, shapes, z_here, z_near)
    z_far = col_swap(z_send, 2, 0)
    shapes = [jax.ShapeDtypeStruct(piece, f32)] * 2 + [jax.ShapeDtypeStruct((2, *piece), bf16)]
    z_own, z_across, z_send = small(merge_z_far, shapes, z_kept, z_far)
    z_got = col_swap(z_send, 0, 1)
    y_in, z_across = lax.optimization_barrier((y_in, z_across))
    piece_y = y_parts[0].shape[1:]
    shapes = [jax.ShapeDtypeStruct(piece_y, f32)] + [jax.ShapeDtypeStruct(piece_y, bf16)] * 3
    y_own, *y_send = small(merge_y, shapes, y_parts[0], *y_in)
    y_last = [col_swap(y_send[e - 1], e, 0) for e in (2, 3, 1)]
    shapes = [jax.ShapeDtypeStruct(piece, f32), jax.ShapeDtypeStruct(piece, bf16)]
    z_own, z_send = small(merge_z_last, shapes, z_own, z_across, z_got)
    z_own += col_swap(z_send, 0, 3).astype(f32)
    y_last, z_own = lax.optimization_barrier((y_last, z_own))
    y_own += sum(part.astype(f32) for part in y_last)
    return y_own, z_own


def per_device(
    features, self_weight, rel_weight, bias, blocks, block_rows, block_cols, block_counts
):
    relations, slots, size, _ = blocks.shape[2:]
    me = (lax.axis_index("row") * 16 + lax.axis_index("col")).reshape(1)
    weights = jnp.transpose(rel_weight, (1, 0, 2))
    blocks = blocks.reshape(relations * slots, size, size)
    to_plan = (me, block_rows, block_cols, block_counts)
    self_term, parts = gather_groups(features, self_weight, to_plan, blocks, weights)
    y_own, z_own = scatter_sum(parts)
    owned = jnp.concatenate([y_own, z_own], axis=1)
    return jnp.maximum(self_term + owned + bias, 0.0).astype(jnp.bfloat16)


def solution(mesh):
    return jax.shard_map(
        per_device,
        mesh=mesh,
        in_specs=(
            P(("row", "col"), None),
            P(),
            P(),
            P(),
            P("row", "col", None, None, None, None),
            P("row", "col", None, None),
            P("row", "col", None, None),
            P("row", "col", None),
        ),
        out_specs=P(("row", "col"), None),
        check_vma=False,
    )
```

time: 92.4 us -> 92.1 us (level)
  starting transfers between devices: 47.7 us -> 44.8 us
  waiting for transfers between devices: 24 us -> 26.7 us
  local copies, waits for them, and re-layouts: 7.06 us -> 5.15 us
  other arithmetic: 0.92 us -> 2.26 us
    ppermute x21 -> x19, starting transfers between devices: 47.7 us -> 44.8 us  [the longest x10 28.5 us: col_swap(): lax.ppermute(value, 'col', [(at, at ^ dz * Y + dy) for at in range(16)])]
    ppermute x21 -> x19, waiting for transfers between devices: 24 us -> 26.7 us  [the longest x10 25.8 us: col_swap(): lax.ppermute(value, 'col', [(at, at ^ dz * Y + dy) for at in range(16)])]
    unnamed x18 -> x14, local copies, waits for them, and re-layouts: 7.03 us -> 5.04 us
    pallas_call x3 -> x5, Pallas kernels: 2.47 us -> 1.95 us  [the longest x1 1.51 us: plan(): pl.pallas_call(functools.partial(plan_kernel, relations), out_shape=[jax....]
  transfers between devices with their start and end apart: 21 -> 19, of which waited for: 7 -> 6; matrix products, arithmetic and copies ran while one was open for 4% -> 4% of each run, Pallas kernels for 9% -> 10%
where the time goes in v2:
time: 92.1 us; the launch traced here: 91.4 us
  starting transfers between devices  44.8 us (49%)
  waiting for transfers between devices  26.7 us (29%)
  Pallas kernels  11 us (12%)
  local copies, waits for them, and re-layouts  5.15 us (6%)
  other arithmetic  2.26 us (2%)
  matrix products  1.25 us (1%)
    ppermute x10, starting transfers between devices, col_swap(): lax.ppermute(value, 'col', [(at, at ^ dz * Y + dy) for at in range(16)])  28.5 us
    ppermute x10, waiting for transfers between devices, col_swap(): lax.ppermute(value, 'col', [(at, at ^ dz * Y + dy) for at in range(16)])  25.8 us
    ppermute x9, starting transfers between devices, row_swap(): lax.ppermute(value, 'row', [(at, at ^ dz * 8 + dx * 2 + dc) for at in ran...  16.3 us
    pallas_call x4, Pallas kernels, tile_stage(): pl.pallas_call(functools.partial(stage_kernel, group, first, last), out_s...  9.02 us
    unnamed x14, local copies, waits for them, and re-layouts  5.04 us
  transfers between devices with their start and end apart: 19, of which 6 were waited for; matrix products, arithmetic and copies ran while one was open for 4% of the time, Pallas kernels for 10%

profile of v2, /device:TPU:4, one launch (start us, length us, event | category | flops | bytes accessed | tf_op | source)
XLA Modules:
  0.0 91.4 jit_solution(11291018899058054952)
XLA Ops:
  0.0 2.2 %collective-permute-start.5 = (bf16[128,768]{1,0:T(8,128)(2,1)}, bf16[128,768]{1,0:T(8,128)(2,1)S(1)}, u32[]{:S(2)}, u32[]{:S(2)}) collective-permute-start(bf16[128,768]{1,0:T(8,128)(2,1)} %param.8), channel_id=1, source_target_pairs={{0,64},{16,80},{32,96},{48,112},{64,0},{80,16},{96,32},{112,48},{1... | collective-permute-start | bytes 589832 | tf_op jit(solution)/shard_map/ppermute | solution.py:16
  2.6 7.2 %collective-permute-start = (bf16[128,768]{1,0:T(8,128)(2,1)}, bf16[128,768]{1,0:T(8,128)(2,1)S(1)}, u32[]{:S(2)}, u32[]{:S(2)}) collective-permute-start(bf16[128,768]{1,0:T(8,128)(2,1)} %param.8), channel_id=1, source_target_pairs={{0,128},{16,144},{32,160},{48,176},{64,192},{80,208},{96,224},{112... | collective-permute-start | bytes 589832 | tf_op jit(solution)/shard_map/ppermute | solution.py:16
  9.8 1.5 %collective-permute-start.6 = (bf16[128,768]{1,0:T(8,128)(2,1)}, bf16[128,768]{1,0:T(8,128)(2,1)S(1)}, u32[]{:S(2)}, u32[]{:S(2)}) collective-permute-start(bf16[128,768]{1,0:T(8,128)(2,1)} %param.8), channel_id=1, source_target_pairs={{0,96},{16,112},{32,64},{48,80},{64,32},{80,48},{96,0},{112,16},{1... | collective-permute-start | bytes 589832 | tf_op jit(solution)/shard_map/ppermute | solution.py:16
  14.5 1.5 %collective-permute-start.3 = (bf16[128,768]{1,0:T(8,128)(2,1)S(1)}, bf16[128,768]{1,0:T(8,128)(2,1)S(1)}, u32[]{:S(2)}, u32[]{:S(2)}) collective-permute-start(bf16[128,768]{1,0:T(8,128)(2,1)S(1)} %collective-permute-done), channel_id=1, source_target_pairs={{0,96},{16,112},{32,64},{48,80},{64,32},{80,48},{96,0},{112,16},{1... | collective-permute-start | bytes 589832 | tf_op jit(solution)/shard_map/ppermute | solution.py:16
  18.4 1.7 %collective-permute-start.1 = (bf16[128,768]{1,0:T(8,128)(2,1)S(1)}, bf16[128,768]{1,0:T(8,128)(2,1)S(1)}, u32[]{:S(2)}, u32[]{:S(2)}) collective-permute-start(bf16[128,768]{1,0:T(8,128)(2,1)S(1)} %collective-permute-done), channel_id=1, source_target_pairs={{0,32},{16,48},{32,0},{48,16},{64,96},{80,112},{96,64},{112,80},{1... | collective-permute-start | bytes 589832 | tf_op jit(solution)/shard_map/ppermute | solution.py:16
  20.3 1.5 %plan.1 = (s32[40]{0:T(128)S(1)}, s32[21]{0:T(128)S(1)}) custom-call(s32[1]{0:T(128)} %bitcast.me_ref, s32[40]{0:T(128)S(1)} %reshape.22.table_ref), custom_call_target="tpu_custom_call" | custom-call | tf_op jit(solution)/shard_map/plan/pallas_call | solution.py:134
  21.9 2.7 %copy-done.1 = bf16[768,5,768]{2,0,1:T(8,128)(2,1)S(1)} copy-done((bf16[768,5,768]{2,0,1:T(8,128)(2,1)S(1)}, bf16[768,5,768]{2,0,1:T(8,128)(2,1)}, u32[]{:S(2)}) %copy-start.1) | copy-done | bytes 5898264
  24.5 1.3 %copy-done.2 = bf16[1,1,5,8,128,128]{5,4,3,2,1,0:T(8,128)(2,1)S(1)} copy-done((bf16[1,1,5,8,128,128]{5,4,3,2,1,0:T(8,128)(2,1)S(1)}, bf16[1,1,5,8,128,128]{5,4,3,2,1,0:T(8,128)(2,1)}, u32[]{:S(2)}) %copy-start.2) | copy-done | bytes 1310744
  25.9 2.1 %tile.4.refs_0_ = f32[2048,768]{1,0:T(8,128)S(1)} custom-call(s32[40]{0:T(128)S(1)} %get-tuple-element.45.codes_ref, s32[21]{0:T(128)S(1)} %get-tuple-element.46.starts_ref, bf16[40,128,128]{2,1,0:T(8,128)(2,1)S(1)} %bitcast.11, bf16[5,768,768]{2,1,0:T(8,128)(2,1)S(1)} %bitcast.7, bf16[512,768]{1,0:T(8,128)(2,1)S(1)} %constant_dynamic-update-slice_fusion.group_ref), custom_call_target="tpu_custom_call" | custom-call | flops 1073741824 | bytes 4194304 | tf_op jit(solution)/shard_map/tile/pallas_call | solution.py:160
  28.9 1.7 %tile.5.refs_0_ = f32[2048,768]{1,0:T(8,128)S(1)} custom-call(s32[40]{0:T(128)S(1)} %get-tuple-element.45.codes_ref, s32[21]{0:T(128)S(1)} %get-tuple-element.46.starts_ref, bf16[40,128,128]{2,1,0:T(8,128)(2,1)S(1)} %bitcast.12, bf16[5,768,768]{2,1,0:T(8,128)(2,1)S(1)} %bitcast.8, ...), custom_call_target="tpu_custom_call", output_to_operand_aliasing={{}: (5, {})} | custom-call | flops 1073741824 | bytes 4194304 | tf_op jit(solution)/shard_map/tile/pallas_call | solution.py:160
  30.6 3.1 %tile.6.refs_0_ = f32[2048,768]{1,0:T(8,128)S(1)} custom-call(s32[40]{0:T(128)S(1)} %get-tuple-element.45.codes_ref, s32[21]{0:T(128)S(1)} %get-tuple-element.46.starts_ref, bf16[40,128,128]{2,1,0:T(8,128)(2,1)S(1)} %bitcast.13, bf16[5,768,768]{2,1,0:T(8,128)(2,1)S(1)} %bitcast.9, ...), custom_call_target="tpu_custom_call", output_to_operand_aliasing={{}: (5, {})} | custom-call | flops 1073741824 | bytes 4194304 | tf_op jit(solution)/shard_map/tile/pallas_call | solution.py:160
  33.8 2.0 %tile.7 = (f32[2048,768]{1,0:T(8,128)S(1)}, bf16[4,128,512]{2,1,0:T(8,128)(2,1)S(1)}, bf16[4,128,512]{2,1,0:T(8,128)(2,1)S(1)}, bf16[4,128,512]{2,1,0:T(8,128)(2...) custom-call(s32[40]{0:T(128)S(1)} %get-tuple-element.45.codes_ref, ...), custom_call_target="tpu_custom_call", output_to_operand_aliasing={{0}: (5, {})} | custom-call | flops 1073741824 | bytes 4194304 | tf_op jit(solution)/shard_map/tile/pallas_call | solution.py:160
  35.8 5.1 %collective-permute-start.12 = (bf16[2,4,128,256]{3,2,1,0:T(8,128)(2,1)S(1)}, bf16[2,4,128,256]{3,2,1,0:T(8,128)(2,1)S(1)}, u32[]{:S(2)}, u32[]{:S(2)}) collective-permute-start(bf16[2,4,128,256]{3,2,1,0:T(8,128)(2,1)S(1)} %get-tuple-element.55), channel_id=1, source_target_pairs={{0,4},{1,5},{2,6},{3,7},{4,0},{5,1},{6,2},{7,3},{8,12},{9,13},{10,... | collective-permute-start | bytes 1572872 | tf_op jit(solution)/shard_map/ppermute | solution.py:20
  40.9 1.8 %collective-permute-start.9 = (bf16[4,128,512]{2,1,0:T(8,128)(2,1)S(1)}, bf16[4,128,512]{2,1,0:T(8,128)(2,1)S(1)}, u32[]{:S(2)}, u32[]{:S(2)}) collective-permute-start(bf16[4,128,512]{2,1,0:T(8,128)(2,1)S(1)} %get-tuple-element.51), channel_id=1, source_target_pairs={{0,2},{1,3},{2,0},{3,1},{4,6},{5,7},{6,4},{7,5},{8,10},{9,11},{10,... | collective-permute-start | bytes 1572872 | tf_op jit(solution)/shard_map/ppermute | solution.py:20
  42.8 2.6 %collective-permute-start.10 = (bf16[4,128,512]{2,1,0:T(8,128)(2,1)S(1)}, bf16[4,128,512]{2,1,0:T(8,128)(2,1)S(1)}, u32[]{:S(2)}, u32[]{:S(2)}) collective-permute-start(bf16[4,128,512]{2,1,0:T(8,128)(2,1)S(1)} %get-tuple-element.52), channel_id=1, source_target_pairs={{0,1},{1,0},{2,3},{3,2},{4,5},{5,4},{6,7},{7,6},{8,9},{9,8},{10,11... | collective-permute-start | bytes 1572872 | tf_op jit(solution)/shard_map/ppermute | solution.py:20
  45.4 2.5 %collective-permute-start.11 = (bf16[4,128,512]{2,1,0:T(8,128)(2,1)S(1)}, bf16[4,128,512]{2,1,0:T(8,128)(2,1)S(1)}, u32[]{:S(2)}, u32[]{:S(2)}) collective-permute-start(bf16[4,128,512]{2,1,0:T(8,128)(2,1)S(1)} %get-tuple-element.53), channel_id=1, source_target_pairs={{0,3},{1,2},{2,1},{3,0},{4,7},{5,6},{6,5},{7,4},{8,11},{9,10},{10,... | collective-permute-start | bytes 1572872 | tf_op jit(solution)/shard_map/ppermute | solution.py:20
  48.0 3.5 %collective-permute-done.12.refs_1_ = bf16[2,4,128,256]{3,2,1,0:T(8,128)(2,1)S(1)} collective-permute-done((bf16[2,4,128,256]{3,2,1,0:T(8,128)(2,1)S(1)}, bf16[2,4,128,256]{3,2,1,0:T(8,128)(2,1)S(1)}, u32[]{:S(2)}, u32[]{:S(2)}) %collective-permute-start.12) | collective-permute-done | bytes 524320 | tf_op jit(solution)/shard_map/ppermute | solution.py:20
  51.6 6.7 %collective-permute-start.13 = (bf16[4,128,256]{2,1,0:T(8,128)(2,1)S(1)}, bf16[4,128,256]{2,1,0:T(8,128)(2,1)S(1)}, u32[]{:S(2)}, u32[]{:S(2)}) collective-permute-start(bf16[4,128,256]{2,1,0:T(8,128)(2,1)S(1)} %get-tuple-element.57), channel_id=1, source_target_pairs={{0,8},{1,9},{2,10},{3,11},{4,12},{5,13},{6,14},{7,15},{8,0},{9,1},... | collective-permute-start | bytes 786440 | tf_op jit(solution)/shard_map/ppermute | solution.py:20
  58.2 10.5 %collective-permute-done.13.refs_1_ = bf16[4,128,256]{2,1,0:T(8,128)(2,1)S(1)} collective-permute-done((bf16[4,128,256]{2,1,0:T(8,128)(2,1)S(1)}, bf16[4,128,256]{2,1,0:T(8,128)(2,1)S(1)}, u32[]{:S(2)}, u32[]{:S(2)}) %collective-permute-start.13) | collective-permute-done | bytes 262176 | tf_op jit(solution)/shard_map/ppermute | solution.py:20
  68.8 1.8 %collective-permute-start.17 = (bf16[2,128,256]{2,1,0:T(8,128)(2,1)S(1)}, bf16[2,128,256]{2,1,0:T(8,128)(2,1)S(1)}, u32[]{:S(2)}, u32[]{:S(2)}) collective-permute-start(bf16[2,128,256]{2,1,0:T(8,128)(2,1)S(1)} %get-tuple-element.68), channel_id=1, source_target_pairs={{0,1},{1,0},{2,3},{3,2},{4,5},{5,4},{6,7},{7,6},{8,9},{9,8},{10,11... | collective-permute-start | bytes 393224 | tf_op jit(solution)/shard_map/ppermute | solution.py:20
  70.6 3.3 %collective-permute-done.17.refs_2_ = bf16[2,128,256]{2,1,0:T(8,128)(2,1)S(1)} collective-permute-done((bf16[2,128,256]{2,1,0:T(8,128)(2,1)S(1)}, bf16[2,128,256]{2,1,0:T(8,128)(2,1)S(1)}, u32[]{:S(2)}, u32[]{:S(2)}) %collective-permute-start.17) | collective-permute-done | bytes 131104 | tf_op jit(solution)/shard_map/ppermute | solution.py:20
  73.9 4.3 %collective-permute-start.18 = (bf16[128,256]{1,0:T(8,128)(2,1)S(1)}, bf16[128,256]{1,0:T(8,128)(2,1)S(1)}, u32[]{:S(2)}, u32[]{:S(2)}) collective-permute-start(bf16[128,256]{1,0:T(8,128)(2,1)S(1)} %get-tuple-element.70), channel_id=1, source_target_pairs={{0,3},{1,2},{2,1},{3,0},{4,7},{5,6},{6,5},{7,4},{8,11},{9,10},{10,... | collective-permute-start | bytes 196616 | tf_op jit(solution)/shard_map/ppermute | solution.py:20
  78.6 2.6 %collective-permute-start.15 = (bf16[128,512]{1,0:T(8,128)(2,1)S(1)}, bf16[128,512]{1,0:T(8,128)(2,1)S(1)}, u32[]{:S(2)}, u32[]{:S(2)}) collective-permute-start(bf16[128,512]{1,0:T(8,128)(2,1)S(1)} %get-tuple-element.64), channel_id=1, source_target_pairs={{0,12},{1,13},{2,14},{3,15},{4,8},{5,9},{6,10},{7,11},{8,4},{9,5},... | collective-permute-start | bytes 393224 | tf_op jit(solution)/shard_map/ppermute | solution.py:20
  82.1 7.2 %collective-permute-done.14 = bf16[128,512]{1,0:T(8,128)(2,1)S(1)} collective-permute-done((bf16[128,512]{1,0:T(8,128)(2,1)S(1)}, bf16[128,512]{1,0:T(8,128)(2,1)S(1)}, u32[]{:S(2)}, u32[]{:S(2)}) %collective-permute-start.14) | collective-permute-done | bytes 131104 | tf_op jit(solution)/shard_map/ppermute | solution.py:20
  (46 shorter events, 10.5 us)
Async XLA Ops:
  0.0 12.3 %copy-start = (bf16[768,768]{1,0:T(8,128)(2,1)S(1)}, bf16[768,768]{1,0:T(8,128)(2,1)}, u32[]{:S(2)}) copy-start(bf16[768,768]{1,0:T(8,128)(2,1)} %param.9) | copy-start | bytes 3538948
  0.0 20.1 %collective-permute-start.5 = (bf16[128,768]{1,0:T(8,128)(2,1)}, bf16[128,768]{1,0:T(8,128)(2,1)S(1)}, u32[]{:S(2)}, u32[]{:S(2)}) collective-permute-start(bf16[128,768]{1,0:T(8,128)(2,1)} %param.8), channel_id=1, source_target_pairs={{0,64},{16,80},{32,96},{48,112},{64,0},{80,16},{96,32},{112,48},{1... | collective-permute-start | bytes 589832 | tf_op jit(solution)/shard_map/ppermute | solution.py:16
  2.2 16.2 %collective-permute-start.4 = (bf16[128,768]{1,0:T(8,128)(2,1)}, bf16[128,768]{1,0:T(8,128)(2,1)S(1)}, u32[]{:S(2)}, u32[]{:S(2)}) collective-permute-start(bf16[128,768]{1,0:T(8,128)(2,1)} %param.8), channel_id=1, source_target_pairs={{0,32},{16,48},{32,0},{48,16},{64,96},{80,112},{96,64},{112,80},{1... | collective-permute-start | bytes 589832 | tf_op jit(solution)/shard_map/ppermute | solution.py:16
  2.6 11.9 %collective-permute-start = (bf16[128,768]{1,0:T(8,128)(2,1)}, bf16[128,768]{1,0:T(8,128)(2,1)S(1)}, u32[]{:S(2)}, u32[]{:S(2)}) collective-permute-start(bf16[128,768]{1,0:T(8,128)(2,1)} %param.8), channel_id=1, source_target_pairs={{0,128},{16,144},{32,160},{48,176},{64,192},{80,208},{96,224},{112... | collective-permute-start | bytes 589832 | tf_op jit(solution)/shard_map/ppermute | solution.py:16
  9.8 10.4 %collective-permute-start.6 = (bf16[128,768]{1,0:T(8,128)(2,1)}, bf16[128,768]{1,0:T(8,128)(2,1)S(1)}, u32[]{:S(2)}, u32[]{:S(2)}) collective-permute-start(bf16[128,768]{1,0:T(8,128)(2,1)} %param.8), channel_id=1, source_target_pairs={{0,96},{16,112},{32,64},{48,80},{64,32},{80,48},{96,0},{112,16},{1... | collective-permute-start | bytes 589832 | tf_op jit(solution)/shard_map/ppermute | solution.py:16
  14.5 13.5 %collective-permute-start.3 = (bf16[128,768]{1,0:T(8,128)(2,1)S(1)}, bf16[128,768]{1,0:T(8,128)(2,1)S(1)}, u32[]{:S(2)}, u32[]{:S(2)}) collective-permute-start(bf16[128,768]{1,0:T(8,128)(2,1)S(1)} %collective-permute-done), channel_id=1, source_target_pairs={{0,96},{16,112},{32,64},{48,80},{64,32},{80,48},{96,0},{112,16},{1... | collective-permute-start | bytes 589832 | tf_op jit(solution)/shard_map/ppermute | solution.py:16
  16.0 12.1 %collective-permute-start.2 = (bf16[128,768]{1,0:T(8,128)(2,1)S(1)}, bf16[128,768]{1,0:T(8,128)(2,1)S(1)}, u32[]{:S(2)}, u32[]{:S(2)}) collective-permute-start(bf16[128,768]{1,0:T(8,128)(2,1)S(1)} %collective-permute-done), channel_id=1, source_target_pairs={{0,64},{16,80},{32,96},{48,112},{64,0},{80,16},{96,32},{112,48},{1... | collective-permute-start | bytes 589832 | tf_op jit(solution)/shard_map/ppermute | solution.py:16
  18.4 9.6 %collective-permute-start.1 = (bf16[128,768]{1,0:T(8,128)(2,1)S(1)}, bf16[128,768]{1,0:T(8,128)(2,1)S(1)}, u32[]{:S(2)}, u32[]{:S(2)}) collective-permute-start(bf16[128,768]{1,0:T(8,128)(2,1)S(1)} %collective-permute-done), channel_id=1, source_target_pairs={{0,32},{16,48},{32,0},{48,16},{64,96},{80,112},{96,64},{112,80},{1... | collective-permute-start | bytes 589832 | tf_op jit(solution)/shard_map/ppermute | solution.py:16
  20.2 10.4 %collective-permute-start.8 = (bf16[512,768]{1,0:T(8,128)(2,1)S(1)}, bf16[512,768]{1,0:T(8,128)(2,1)S(1)}, u32[]{:S(2)}, u32[]{:S(2)}) collective-permute-start(bf16[512,768]{1,0:T(8,128)(2,1)S(1)} %constant_dynamic-update-slice_fusion.group_ref), channel_id=1, source_target_pairs={{0,16},{16,0},{32,48},{48,32},{64,80},{80,64},{96,112},{112,96},{1... | collective-permute-start | bytes 2359304 | tf_op jit(solution)/shard_map/ppermute | solution.py:16
  21.9 2.7 %copy-start.1 = (bf16[768,5,768]{2,0,1:T(8,128)(2,1)S(1)}, bf16[768,5,768]{2,0,1:T(8,128)(2,1)}, u32[]{:S(2)}) copy-start(bf16[768,5,768]{2,0,1:T(8,128)(2,1)} %param.10) | copy-start | bytes 17694724
  24.5 1.3 %copy-start.2 = (bf16[1,1,5,8,128,128]{5,4,3,2,1,0:T(8,128)(2,1)S(1)}, bf16[1,1,5,8,128,128]{5,4,3,2,1,0:T(8,128)(2,1)}, u32[]{:S(2)}) copy-start(bf16[1,1,5,8,128,128]{5,4,3,2,1,0:T(8,128)(2,1)} %param.12) | copy-start | bytes 3932164
  28.1 5.7 %collective-permute-start.7 = (bf16[512,768]{1,0:T(8,128)(2,1)S(1)}, bf16[512,768]{1,0:T(8,128)(2,1)S(1)}, u32[]{:S(2)}, u32[]{:S(2)}) collective-permute-start(bf16[512,768]{1,0:T(8,128)(2,1)S(1)} %constant_dynamic-update-slice_fusion.4.group_ref), channel_id=1, source_target_pairs={{0,16},{16,0},{32,48},{48,32},{64,80},{80,64},{96,112},{112,96},{1... | collective-permute-start | bytes 2359304 | tf_op jit(solution)/shard_map/ppermute | solution.py:16
  33.7 56.9 %copy-start.3 = (f32[768]{0:T(1024)S(1)}, f32[768]{0:T(1024)}, u32[]{:S(2)}) copy-start(f32[768]{0:T(1024)} %param.11) | copy-start | bytes 9220
  35.8 15.6 %collective-permute-start.12 = (bf16[2,4,128,256]{3,2,1,0:T(8,128)(2,1)S(1)}, bf16[2,4,128,256]{3,2,1,0:T(8,128)(2,1)S(1)}, u32[]{:S(2)}, u32[]{:S(2)}) collective-permute-start(bf16[2,4,128,256]{3,2,1,0:T(8,128)(2,1)S(1)} %get-tuple-element.55), channel_id=1, source_target_pairs={{0,4},{1,5},{2,6},{3,7},{4,0},{5,1},{6,2},{7,3},{8,12},{9,13},{10,... | collective-permute-start | bytes 1572872 | tf_op jit(solution)/shard_map/ppermute | solution.py:20
  40.9 29.7 %collective-permute-start.9 = (bf16[4,128,512]{2,1,0:T(8,128)(2,1)S(1)}, bf16[4,128,512]{2,1,0:T(8,128)(2,1)S(1)}, u32[]{:S(2)}, u32[]{:S(2)}) collective-permute-start(bf16[4,128,512]{2,1,0:T(8,128)(2,1)S(1)} %get-tuple-element.51), channel_id=1, source_target_pairs={{0,2},{1,3},{2,0},{3,1},{4,6},{5,7},{6,4},{7,5},{8,10},{9,11},{10,... | collective-permute-start | bytes 1572872 | tf_op jit(solution)/shard_map/ppermute | solution.py:20
  42.8 27.8 %collective-permute-start.10 = (bf16[4,128,512]{2,1,0:T(8,128)(2,1)S(1)}, bf16[4,128,512]{2,1,0:T(8,128)(2,1)S(1)}, u32[]{:S(2)}, u32[]{:S(2)}) collective-permute-start(bf16[4,128,512]{2,1,0:T(8,128)(2,1)S(1)} %get-tuple-element.52), channel_id=1, source_target_pairs={{0,1},{1,0},{2,3},{3,2},{4,5},{5,4},{6,7},{7,6},{8,9},{9,8},{10,11... | collective-permute-start | bytes 1572872 | tf_op jit(solution)/shard_map/ppermute | solution.py:20
  45.4 25.2 %collective-permute-start.11 = (bf16[4,128,512]{2,1,0:T(8,128)(2,1)S(1)}, bf16[4,128,512]{2,1,0:T(8,128)(2,1)S(1)}, u32[]{:S(2)}, u32[]{:S(2)}) collective-permute-start(bf16[4,128,512]{2,1,0:T(8,128)(2,1)S(1)} %get-tuple-element.53), channel_id=1, source_target_pairs={{0,3},{1,2},{2,1},{3,0},{4,7},{5,6},{6,5},{7,4},{8,11},{9,10},{10,... | collective-permute-start | bytes 1572872 | tf_op jit(solution)/shard_map/ppermute | solution.py:20
  51.6 17.2 %collective-permute-start.13 = (bf16[4,128,256]{2,1,0:T(8,128)(2,1)S(1)}, bf16[4,128,256]{2,1,0:T(8,128)(2,1)S(1)}, u32[]{:S(2)}, u32[]{:S(2)}) collective-permute-start(bf16[4,128,256]{2,1,0:T(8,128)(2,1)S(1)} %get-tuple-element.57), channel_id=1, source_target_pairs={{0,8},{1,9},{2,10},{3,11},{4,12},{5,13},{6,14},{7,15},{8,0},{9,1},... | collective-permute-start | bytes 786440 | tf_op jit(solution)/shard_map/ppermute | solution.py:20
  68.8 5.1 %collective-permute-start.17 = (bf16[2,128,256]{2,1,0:T(8,128)(2,1)S(1)}, bf16[2,128,256]{2,1,0:T(8,128)(2,1)S(1)}, u32[]{:S(2)}, u32[]{:S(2)}) collective-permute-start(bf16[2,128,256]{2,1,0:T(8,128)(2,1)S(1)} %get-tuple-element.68), channel_id=1, source_target_pairs={{0,1},{1,0},{2,3},{3,2},{4,5},{5,4},{6,7},{7,6},{8,9},{9,8},{10,11... | collective-permute-start | bytes 393224 | tf_op jit(solution)/shard_map/ppermute | solution.py:20
  73.9 8.2 %collective-permute-start.18 = (bf16[128,256]{1,0:T(8,128)(2,1)S(1)}, bf16[128,256]{1,0:T(8,128)(2,1)S(1)}, u32[]{:S(2)}, u32[]{:S(2)}) collective-permute-start(bf16[128,256]{1,0:T(8,128)(2,1)S(1)} %get-tuple-element.70), channel_id=1, source_target_pairs={{0,3},{1,2},{2,1},{3,0},{4,7},{5,6},{6,5},{7,4},{8,11},{9,10},{10,... | collective-permute-start | bytes 196616 | tf_op jit(solution)/shard_map/ppermute | solution.py:20
  78.5 10.7 %collective-permute-start.14 = (bf16[128,512]{1,0:T(8,128)(2,1)S(1)}, bf16[128,512]{1,0:T(8,128)(2,1)S(1)}, u32[]{:S(2)}, u32[]{:S(2)}) collective-permute-start(bf16[128,512]{1,0:T(8,128)(2,1)S(1)} %get-tuple-element.63), channel_id=1, source_target_pairs={{0,8},{1,9},{2,10},{3,11},{4,12},{5,13},{6,14},{7,15},{8,0},{9,1},... | collective-permute-start | bytes 393224 | tf_op jit(solution)/shard_map/ppermute | solution.py:20
  78.6 10.7 %collective-permute-start.15 = (bf16[128,512]{1,0:T(8,128)(2,1)S(1)}, bf16[128,512]{1,0:T(8,128)(2,1)S(1)}, u32[]{:S(2)}, u32[]{:S(2)}) collective-permute-start(bf16[128,512]{1,0:T(8,128)(2,1)S(1)} %get-tuple-element.64), channel_id=1, source_target_pairs={{0,12},{1,13},{2,14},{3,15},{4,8},{5,9},{6,10},{7,11},{8,4},{9,5},... | collective-permute-start | bytes 393224 | tf_op jit(solution)/shard_map/ppermute | solution.py:20
  81.2 9.3 %collective-permute-start.16 = (bf16[128,512]{1,0:T(8,128)(2,1)S(1)}, bf16[128,512]{1,0:T(8,128)(2,1)S(1)}, u32[]{:S(2)}, u32[]{:S(2)}) collective-permute-start(bf16[128,512]{1,0:T(8,128)(2,1)S(1)} %get-tuple-element.65), channel_id=1, source_target_pairs={{0,4},{1,5},{2,6},{3,7},{4,0},{5,1},{6,2},{7,3},{8,12},{9,13},{10,... | collective-permute-start | bytes 393224 | tf_op jit(solution)/shard_map/ppermute | solution.py:20

commit v3 on v2

--- a/solution.py
+++ b/solution.py
@@ -85,25 +85,25 @@
                 z_refs[e % 2][e // 2, d] = total[rows, SPLIT:].astype(jnp.bfloat16)
 
 
-def plan_kernel(relations, me_ref, table_ref, codes_ref, starts_ref):
-    slots = table_ref.shape[0] // relations
-    row_me, col_me = me_ref[0] >> 4, me_ref[0] & 15
+def plan_kernel(table_ref, codes_ref, starts_ref):
+    relations, slots = table_ref.shape
+    row_me, col_me = lax.axis_index("row"), lax.axis_index("col")
     for index in range(4 * relations + 1):
         starts_ref[index] = 0
 
-    def parts(at):
-        packed = table_ref[at]
+    def parts(relation, slot):
+        packed = table_ref[relation, slot]
         source = (packed >> 4 & 15) ^ row_me
         target = (packed & 15) ^ col_me
-        return packed >> 8, (source & 1) * 2 + (source >> 3), source >> 1 & 3, (target & 3) * 4 + (target >> 2)
+        return packed >> 8, (source >> 3) * 2 + (source & 1), source >> 1 & 3, (target & 3) * 4 + (target >> 2)
 
     def per_slot(act):
         for relation in range(relations):
-            live = table_ref[relation * slots] >> 8
+            live = table_ref[relation, 0] >> 8
 
             def body(slot, carry):
                 at = relation * slots + slot
-                _, group, place, target = parts(at)
+                _, group, place, target = parts(relation, slot)
                 act(group * relations + relation, at, place, target)
                 return carry
 
@@ -126,22 +126,22 @@
     starts_ref[0] = 0
 
 
-def plan(me, block_rows, block_cols, block_counts):
+def plan(block_rows, block_cols, block_counts):
     relations, slots = block_rows.shape[2:]
     smem = pl.BlockSpec(memory_space=pltpu.SMEM)
     many = relations * slots
-    table = (block_rows + block_cols * 16 + block_counts[..., None] * 256).reshape(many)
+    table = (block_rows + block_cols * 16 + block_counts[..., None] * 256)[0, 0]
     return pl.pallas_call(
-        functools.partial(plan_kernel, relations),
+        plan_kernel,
         out_shape=[
             jax.ShapeDtypeStruct((many,), jnp.int32),
             jax.ShapeDtypeStruct((4 * relations + 1,), jnp.int32),
         ],
-        in_specs=[smem] * 2,
+        in_specs=[smem],
         out_specs=[smem] * 2,
         compiler_params=pltpu.CompilerParams(vmem_limit_bytes=1 << 20),
         name="plan",
-    )(me, table)
+    )(table)
 
 
 def tile_stage(group, tables, blocks, weights, value, total):
@@ -213,26 +213,43 @@
     outs[1][...] = (across[...] + got[1].astype(jnp.float32)).astype(jnp.bfloat16)
 
 
-def gather_groups(features, self_weight, to_plan, blocks, weights):
+def load_kernel(blocks_ref, weights_ref, blocks_out, weights_out):
+    blocks_out[...] = blocks_ref[...]
+    weights_out[...] = weights_ref[...]
+
+
+def load(blocks, weights):
+    vmem = pl.BlockSpec(memory_space=pltpu.VMEM)
+    return pl.pallas_call(
+        load_kernel,
+        out_shape=[jax.ShapeDtypeStruct(a.shape, a.dtype) for a in (blocks, weights)],
+        in_specs=[vmem] * 2,
+        out_specs=[vmem] * 2,
+        compiler_params=pltpu.CompilerParams(vmem_limit_bytes=2 << 20),
+        name="load",
+    )(blocks, weights)
+
+
+def gather_groups(features, to_plan, blocks, weights):
     far = row_swap(features, 1, 0, 0)
     near_parts = [features] + [row_swap(features, 0, d, 0) for d in (1, 2, 3)]
-    self_term = jnp.dot(features, self_weight, preferred_element_type=jnp.float32)
-    far, self_term, to_plan = lax.optimization_barrier((far, self_term, to_plan))
+    blocks, weights = load(blocks, weights)
+    far, blocks, weights, to_plan = lax.optimization_barrier((far, blocks, weights, to_plan))
     tables = plan(*to_plan)
     stage = lambda index, value, total: tile_stage(index, tables, blocks, weights, value, total)
     far_parts = [far] + [row_swap(far, 0, d, 0) for d in (1, 2, 3)]
     near = jnp.concatenate(near_parts, axis=0)
     near_other = row_swap(near, 0, 0, 1)
     (total,) = stage(0, near, None)
+    (total,) = stage(1, near_other, total)
     far_parts[-1], total = lax.optimization_barrier((far_parts[-1], total))
     rest = jnp.concatenate(far_parts, axis=0)
     rest_other = row_swap(rest, 0, 0, 1)
-    (total,) = stage(1, rest, total)
-    (total,) = stage(2, near_other, total)
-    return self_term, stage(3, rest_other, total)[1:]
-
-
-def scatter_sum(parts):
+    (total,) = stage(2, rest, total)
+    return stage(3, rest_other, total)[1:]
+
+
+def scatter_sum(parts, features, self_weight):
     y_parts, (z_here, z_there) = parts[:Y], parts[Y:]
     f32, bf16 = jnp.float32, jnp.bfloat16
     many, size, columns = z_here.shape[1:]
@@ -242,6 +259,9 @@
     shapes = [jax.ShapeDtypeStruct((many, *piece), f32), jax.ShapeDtypeStruct((many, *piece), bf16)]
     z_kept, z_send = small(merge_z_near, shapes, z_here, z_near)
     z_far = col_swap(z_send, 2, 0)
+    features, z_kept = lax.optimization_barrier((features, z_kept))
+    self_term = jnp.dot(features, self_weight, preferred_element_type=jnp.float32)
+    self_term, z_far = lax.optimization_barrier((self_term, z_far))
     shapes = [jax.ShapeDtypeStruct(piece, f32)] * 2 + [jax.ShapeDtypeStruct((2, *piece), bf16)]
     z_own, z_across, z_send = small(merge_z_far, shapes, z_kept, z_far)
     z_got = col_swap(z_send, 0, 1)
@@ -251,23 +271,23 @@
     y_own, *y_send = small(merge_y, shapes, y_parts[0], *y_in)
     y_last = [col_swap(y_send[e - 1], e, 0) for e in (2, 3, 1)]
     shapes = [jax.ShapeDtypeStruct(piece, f32), jax.ShapeDtypeStruct(piece, bf16)]
+    z_got, y_own = lax.optimization_barrier((z_got, y_own))
     z_own, z_send = small(merge_z_last, shapes, z_own, z_across, z_got)
     z_own += col_swap(z_send, 0, 3).astype(f32)
     y_last, z_own = lax.optimization_barrier((y_last, z_own))
     y_own += sum(part.astype(f32) for part in y_last)
-    return y_own, z_own
+    return y_own, z_own, self_term
 
 
 def per_device(
     features, self_weight, rel_weight, bias, blocks, block_rows, block_cols, block_counts
 ):
     relations, slots, size, _ = blocks.shape[2:]
-    me = (lax.axis_index("row") * 16 + lax.axis_index("col")).reshape(1)
     weights = jnp.transpose(rel_weight, (1, 0, 2))
     blocks = blocks.reshape(relations * slots, size, size)
-    to_plan = (me, block_rows, block_cols, block_counts)
-    self_term, parts = gather_groups(features, self_weight, to_plan, blocks, weights)
-    y_own, z_own = scatter_sum(parts)
+    to_plan = (block_rows, block_cols, block_counts)
+    parts = gather_groups(features, to_plan, blocks, weights)
+    y_own, z_own, self_term = scatter_sum(parts, features, self_weight)
     owned = jnp.concatenate([y_own, z_own], axis=1)
     return jnp.maximum(self_term + owned + bias, 0.0).astype(jnp.bfloat16)
 

time: 92.1 us -> 86.6 us (0.940); the launches traced: 91.4 us -> 84.9 us
  starting transfers between devices: 44.8 us -> 35.2 us
  waiting for transfers between devices: 26.7 us -> 35 us
  Pallas kernels: 11 us -> 8.73 us
  other arithmetic: 2.26 us -> 0.89 us
    ppermute x10, starting transfers between devices: 28.5 us -> 19.4 us  [col_swap(): lax.ppermute(value, 'col', [(at, at ^ dz * Y + dy) for at in range(16)])]
    ppermute x9, waiting for transfers between devices: 0.96 us -> 5.38 us  [row_swap(): lax.ppermute(value, 'row', [(at, at ^ dz * 8 + dx * 2 + dc) for at in ran...]
    ppermute x10, waiting for transfers between devices: 25.8 us -> 29.6 us  [col_swap(): lax.ppermute(value, 'col', [(at, at ^ dz * Y + dy) for at in range(16)])]
    pallas_call x4, Pallas kernels: 9.02 us -> 6.4 us  [tile_stage(): pl.pallas_call(functools.partial(stage_kernel, group, first, last), out_s...]
    dot_general x1, matrix products: 1.25 us -> 0.33 us  [scatter_sum(): jnp.dot(features, self_weight, preferred_element_type=jnp.float32)]
    unnamed x14 -> x22, local copies, waits for them, and re-layouts: 5.04 us -> 4.55 us
    pallas_call x1 -> x2, Pallas kernels: 1.51 us -> 1.9 us  [the longest x1 1.43 us: plan(): pl.pallas_call(plan_kernel, out_shape=[jax.ShapeDtypeStruct((many,), jnp....]
  transfers between devices with their start and end apart: 19 -> 19, of which waited for: 6 -> 9; matrix products, arithmetic and copies ran while one was open for 4% -> 1% of each run, Pallas kernels for 10% -> 8%
where the time goes in v3:
time: 86.6 us; the launch traced here: 84.9 us
  starting transfers between devices  35.2 us (41%)
  waiting for transfers between devices  35 us (40%)
  Pallas kernels  8.73 us (10%)
  local copies, waits for them, and re-layouts  4.58 us (5%)
  other arithmetic  0.89 us (1%)
    ppermute x10, waiting for transfers between devices, col_swap(): lax.ppermute(value, 'col', [(at, at ^ dz * Y + dy) for at in range(16)])  29.6 us
    ppermute x10, starting transfers between devices, col_swap(): lax.ppermute(value, 'col', [(at, at ^ dz * Y + dy) for at in range(16)])  19.4 us
    ppermute x9, starting transfers between devices, row_swap(): lax.ppermute(value, 'row', [(at, at ^ dz * 8 + dx * 2 + dc) for at in ran...  15.7 us
    pallas_call x4, Pallas kernels, tile_stage(): pl.pallas_call(functools.partial(stage_kernel, group, first, last), out_s...  6.4 us
    ppermute x9, waiting for transfers between devices, row_swap(): lax.ppermute(value, 'row', [(at, at ^ dz * 8 + dx * 2 + dc) for at in ran...  5.38 us
    unnamed x22, local copies, waits for them, and re-layouts  4.55 us
  transfers between devices with their start and end apart: 19, of which 9 were waited for; matrix products, arithmetic and copies ran while one was open for 1% of the time, Pallas kernels for 8%

profile of v3, /device:TPU:4, one launch (start us, length us, event | category | flops | bytes accessed | tf_op | source)
XLA Modules:
  0.0 84.9 jit_solution(5731288056237683465)
XLA Ops:
  0.0 7.3 %collective-permute-start = (bf16[128,768]{1,0:T(8,128)(2,1)}, bf16[128,768]{1,0:T(8,128)(2,1)S(1)}, u32[]{:S(2)}, u32[]{:S(2)}) collective-permute-start(bf16[128,768]{1,0:T(8,128)(2,1)} %param.8), channel_id=1, source_target_pairs={{0,128},{16,144},{32,160},{48,176},{64,192},{80,208},{96,224},{112... | collective-permute-start | bytes 589832 | tf_op jit(solution)/shard_map/ppermute | solution.py:16
  7.3 1.2 %collective-permute-start.4 = (bf16[128,768]{1,0:T(8,128)(2,1)}, bf16[128,768]{1,0:T(8,128)(2,1)S(1)}, u32[]{:S(2)}, u32[]{:S(2)}) collective-permute-start(bf16[128,768]{1,0:T(8,128)(2,1)} %param.8), channel_id=1, source_target_pairs={{0,32},{16,48},{32,0},{48,16},{64,96},{80,112},{96,64},{112,80},{1... | collective-permute-start | bytes 589832 | tf_op jit(solution)/shard_map/ppermute | solution.py:16
  8.5 2.9 %collective-permute-start.5 = (bf16[128,768]{1,0:T(8,128)(2,1)}, bf16[128,768]{1,0:T(8,128)(2,1)S(1)}, u32[]{:S(2)}, u32[]{:S(2)}) collective-permute-start(bf16[128,768]{1,0:T(8,128)(2,1)} %param.8), channel_id=1, source_target_pairs={{0,64},{16,80},{32,96},{48,112},{64,0},{80,16},{96,32},{112,48},{1... | collective-permute-start | bytes 589832 | tf_op jit(solution)/shard_map/ppermute | solution.py:16
  11.4 2.7 %copy-done.1 = bf16[768,5,768]{2,0,1:T(8,128)(2,1)S(1)} copy-done((bf16[768,5,768]{2,0,1:T(8,128)(2,1)S(1)}, bf16[768,5,768]{2,0,1:T(8,128)(2,1)}, u32[]{:S(2)}) %copy-start.1) | copy-done | bytes 5898264
  14.1 1.3 %copy-done.2 = bf16[1,1,5,8,128,128]{5,4,3,2,1,0:T(8,128)(2,1)S(1)} copy-done((bf16[1,1,5,8,128,128]{5,4,3,2,1,0:T(8,128)(2,1)S(1)}, bf16[1,1,5,8,128,128]{5,4,3,2,1,0:T(8,128)(2,1)}, u32[]{:S(2)}) %copy-start.2) | copy-done | bytes 1310744
  16.9 2.7 %collective-permute-start.2 = (bf16[128,768]{1,0:T(8,128)(2,1)S(1)}, bf16[128,768]{1,0:T(8,128)(2,1)S(1)}, u32[]{:S(2)}, u32[]{:S(2)}) collective-permute-start(bf16[128,768]{1,0:T(8,128)(2,1)S(1)} %collective-permute-done), channel_id=1, source_target_pairs={{0,64},{16,80},{32,96},{48,112},{64,0},{80,16},{96,32},{112,48},{1... | collective-permute-start | bytes 589832 | tf_op jit(solution)/shard_map/ppermute | solution.py:16
  20.6 1.3 %collective-permute-done.6 = bf16[128,768]{1,0:T(8,128)(2,1)S(1)} collective-permute-done((bf16[128,768]{1,0:T(8,128)(2,1)}, bf16[128,768]{1,0:T(8,128)(2,1)S(1)}, u32[]{:S(2)}, u32[]{:S(2)}) %collective-permute-start.6) | collective-permute-done | bytes 196640 | tf_op jit(solution)/shard_map/ppermute | solution.py:16
  22.1 1.4 %plan.1 = (s32[40]{0:T(128)S(1)}, s32[21]{0:T(128)S(1)}) custom-call(s32[5,8]{1,0:T(8,128)S(1)} %fusion.4.table_ref), custom_call_target="tpu_custom_call" | custom-call | tf_op jit(solution)/shard_map/plan/pallas_call | solution.py:134
  23.6 1.8 %tile.4.refs_0_ = f32[2048,768]{1,0:T(8,128)S(1)} custom-call(s32[40]{0:T(128)S(1)} %get-tuple-element.53.codes_ref, s32[21]{0:T(128)S(1)} %get-tuple-element.54.starts_ref, bf16[40,128,128]{2,1,0:T(8,128)(2,1)S(1)} %get-tuple-element.55.blocks_ref, bf16[5,768,768]{2,1,0:T(8,128)(2,1)S(1)} %get-tuple-element.56.weight_ref, ...), custom_call_target="tpu_custom_call" | custom-call | flops 1073741824 | bytes 4194304 | tf_op jit(solution)/shard_map/tile/pallas_call | solution.py:160
  25.4 2.6 %collective-permute-done.1 = bf16[128,768]{1,0:T(8,128)(2,1)S(1)} collective-permute-done((bf16[128,768]{1,0:T(8,128)(2,1)S(1)}, bf16[128,768]{1,0:T(8,128)(2,1)S(1)}, u32[]{:S(2)}, u32[]{:S(2)}) %collective-permute-start.1) | collective-permute-done | bytes 196640 | tf_op jit(solution)/shard_map/ppermute | solution.py:16
  28.0 2.1 %tile.5.refs_0_ = f32[2048,768]{1,0:T(8,128)S(1)} custom-call(s32[40]{0:T(128)S(1)} %get-tuple-element.53.codes_ref, s32[21]{0:T(128)S(1)} %get-tuple-element.54.starts_ref, bf16[40,128,128]{2,1,0:T(8,128)(2,1)S(1)} %get-tuple-element.55.blocks_ref, bf16[5,768,768]{2,1,0:T(8,128)(2,1)S(1)} %get-tuple-element.56.weight_ref, ...), custom_call_target="tpu_custom_call", output_to_operand_aliasing={{}: (5, {})} | custom-call | flops 1073741824 | bytes 4194304 | tf_op jit(solution)/shard_map/tile/pallas_call | solution.py:160
  31.1 1.4 %collective-permute-done.8.group_ref = bf16[512,768]{1,0:T(8,128)(2,1)S(1)} collective-permute-done((bf16[512,768]{1,0:T(8,128)(2,1)S(1)}, bf16[512,768]{1,0:T(8,128)(2,1)S(1)}, u32[]{:S(2)}, u32[]{:S(2)}) %collective-permute-start.8) | collective-permute-done | bytes 786464 | tf_op jit(solution)/shard_map/ppermute | solution.py:16
  32.5 1.7 %tile.7 = (f32[2048,768]{1,0:T(8,128)S(1)}, bf16[4,128,512]{2,1,0:T(8,128)(2,1)S(1)}, bf16[4,128,512]{2,1,0:T(8,128)(2,1)S(1)}, bf16[4,128,512]{2,1,0:T(8,128)(2...) custom-call(s32[40]{0:T(128)S(1)} %get-tuple-element.53.codes_ref, ...), custom_call_target="tpu_custom_call", output_to_operand_aliasing={{0}: (5, {})} | custom-call | flops 1073741824 | bytes 4194304 | tf_op jit(solution)/shard_map/tile/pallas_call | solution.py:160
  34.3 2.4 %collective-permute-start.9 = (bf16[2,4,128,256]{3,2,1,0:T(8,128)(2,1)S(1)}, bf16[2,4,128,256]{3,2,1,0:T(8,128)(2,1)S(1)}, u32[]{:S(2)}, u32[]{:S(2)}) collective-permute-start(bf16[2,4,128,256]{3,2,1,0:T(8,128)(2,1)S(1)} %get-tuple-element.61), channel_id=1, source_target_pairs={{0,4},{1,5},{2,6},{3,7},{4,0},{5,1},{6,2},{7,3},{8,12},{9,13},{10,... | collective-permute-start | bytes 1572872 | tf_op jit(solution)/shard_map/ppermute | solution.py:20
  36.6 2.8 %collective-permute-start.12 = (bf16[4,128,512]{2,1,0:T(8,128)(2,1)S(1)}, bf16[4,128,512]{2,1,0:T(8,128)(2,1)S(1)}, u32[]{:S(2)}, u32[]{:S(2)}) collective-permute-start(bf16[4,128,512]{2,1,0:T(8,128)(2,1)S(1)} %get-tuple-element.70), channel_id=1, source_target_pairs={{0,2},{1,3},{2,0},{3,1},{4,6},{5,7},{6,4},{7,5},{8,10},{9,11},{10,... | collective-permute-start | bytes 1572872 | tf_op jit(solution)/shard_map/ppermute | solution.py:20
  39.5 1.7 %collective-permute-start.13 = (bf16[4,128,512]{2,1,0:T(8,128)(2,1)S(1)}, bf16[4,128,512]{2,1,0:T(8,128)(2,1)S(1)}, u32[]{:S(2)}, u32[]{:S(2)}) collective-permute-start(bf16[4,128,512]{2,1,0:T(8,128)(2,1)S(1)} %get-tuple-element.71), channel_id=1, source_target_pairs={{0,1},{1,0},{2,3},{3,2},{4,5},{5,4},{6,7},{7,6},{8,9},{9,8},{10,11... | collective-permute-start | bytes 1572872 | tf_op jit(solution)/shard_map/ppermute | solution.py:20
  41.1 6.7 %collective-permute-done.9.refs_1_ = bf16[2,4,128,256]{3,2,1,0:T(8,128)(2,1)S(1)} collective-permute-done((bf16[2,4,128,256]{3,2,1,0:T(8,128)(2,1)S(1)}, bf16[2,4,128,256]{3,2,1,0:T(8,128)(2,1)S(1)}, u32[]{:S(2)}, u32[]{:S(2)}) %collective-permute-start.9) | collective-permute-done | bytes 524320 | tf_op jit(solution)/shard_map/ppermute | solution.py:20
  47.9 3.3 %collective-permute-start.10 = (bf16[4,128,256]{2,1,0:T(8,128)(2,1)S(1)}, bf16[4,128,256]{2,1,0:T(8,128)(2,1)S(1)}, u32[]{:S(2)}, u32[]{:S(2)}) collective-permute-start(bf16[4,128,256]{2,1,0:T(8,128)(2,1)S(1)} %get-tuple-element.64), channel_id=1, source_target_pairs={{0,8},{1,9},{2,10},{3,11},{4,12},{5,13},{6,14},{7,15},{8,0},{9,1},... | collective-permute-start | bytes 786440 | tf_op jit(solution)/shard_map/ppermute | solution.py:20
  51.5 12.1 %collective-permute-done.10.refs_1_ = bf16[4,128,256]{2,1,0:T(8,128)(2,1)S(1)} collective-permute-done((bf16[4,128,256]{2,1,0:T(8,128)(2,1)S(1)}, bf16[4,128,256]{2,1,0:T(8,128)(2,1)S(1)}, u32[]{:S(2)}, u32[]{:S(2)}) %collective-permute-start.10) | collective-permute-done | bytes 262176 | tf_op jit(solution)/shard_map/ppermute | solution.py:20
  63.7 4.8 %collective-permute-start.11 = (bf16[2,128,256]{2,1,0:T(8,128)(2,1)S(1)}, bf16[2,128,256]{2,1,0:T(8,128)(2,1)S(1)}, u32[]{:S(2)}, u32[]{:S(2)}) collective-permute-start(bf16[2,128,256]{2,1,0:T(8,128)(2,1)S(1)} %get-tuple-element.68), channel_id=1, source_target_pairs={{0,1},{1,0},{2,3},{3,2},{4,5},{5,4},{6,7},{7,6},{8,9},{9,8},{10,11... | collective-permute-start | bytes 393224 | tf_op jit(solution)/shard_map/ppermute | solution.py:20
  68.8 3.4 %collective-permute-done.11.refs_2_ = bf16[2,128,256]{2,1,0:T(8,128)(2,1)S(1)} collective-permute-done((bf16[2,128,256]{2,1,0:T(8,128)(2,1)S(1)}, bf16[2,128,256]{2,1,0:T(8,128)(2,1)S(1)}, u32[]{:S(2)}, u32[]{:S(2)}) %collective-permute-start.11) | collective-permute-done | bytes 131104 | tf_op jit(solution)/shard_map/ppermute | solution.py:20
  73.2 1.4 %collective-permute-start.16 = (bf16[128,512]{1,0:T(8,128)(2,1)S(1)}, bf16[128,512]{1,0:T(8,128)(2,1)S(1)}, u32[]{:S(2)}, u32[]{:S(2)}) collective-permute-start(bf16[128,512]{1,0:T(8,128)(2,1)S(1)} %get-tuple-element.80), channel_id=1, source_target_pairs={{0,12},{1,13},{2,14},{3,15},{4,8},{5,9},{6,10},{7,11},{8,4},{9,5},... | collective-permute-start | bytes 393224 | tf_op jit(solution)/shard_map/ppermute | solution.py:20
  74.6 2.1 %collective-permute-start.17 = (bf16[128,512]{1,0:T(8,128)(2,1)S(1)}, bf16[128,512]{1,0:T(8,128)(2,1)S(1)}, u32[]{:S(2)}, u32[]{:S(2)}) collective-permute-start(bf16[128,512]{1,0:T(8,128)(2,1)S(1)} %get-tuple-element.81), channel_id=1, source_target_pairs={{0,4},{1,5},{2,6},{3,7},{4,0},{5,1},{6,2},{7,3},{8,12},{9,13},{10,... | collective-permute-start | bytes 393224 | tf_op jit(solution)/shard_map/ppermute | solution.py:20
  77.8 5.4 %collective-permute-done.15 = bf16[128,512]{1,0:T(8,128)(2,1)S(1)} collective-permute-done((bf16[128,512]{1,0:T(8,128)(2,1)S(1)}, bf16[128,512]{1,0:T(8,128)(2,1)S(1)}, u32[]{:S(2)}, u32[]{:S(2)}) %collective-permute-start.15) | collective-permute-done | bytes 131104 | tf_op jit(solution)/shard_map/ppermute | solution.py:20
  (54 shorter events, 8.2 us)
Async XLA Ops:
  0.0 51.2 %copy-start = (bf16[768,768]{1,0:T(8,128)(2,1)S(1)}, bf16[768,768]{1,0:T(8,128)(2,1)}, u32[]{:S(2)}) copy-start(bf16[768,768]{1,0:T(8,128)(2,1)} %param.9) | copy-start | bytes 3538948
  0.0 22.0 %copy-start.7 = (s32[1,1,5]{2,1,0:T(1,128)S(1)}, s32[1,1,5]{2,1,0:T(1,128)}, u32[]{:S(2)}) copy-start(s32[1,1,5]{2,1,0:T(1,128)} %param.15) | copy-start | bytes 64
  0.0 22.0 %copy-start.5 = (s32[1,1,5,8]{3,1,2,0:T(1,128)S(1)}, s32[1,1,5,8]{3,1,2,0:T(1,128)}, u32[]{:S(2)}) copy-start(s32[1,1,5,8]{3,1,2,0:T(1,128)} %param.13) | copy-start | bytes 484
  0.0 16.3 %collective-permute-start = (bf16[128,768]{1,0:T(8,128)(2,1)}, bf16[128,768]{1,0:T(8,128)(2,1)S(1)}, u32[]{:S(2)}, u32[]{:S(2)}) collective-permute-start(bf16[128,768]{1,0:T(8,128)(2,1)} %param.8), channel_id=1, source_target_pairs={{0,128},{16,144},{32,160},{48,176},{64,192},{80,208},{96,224},{112... | collective-permute-start | bytes 589832 | tf_op jit(solution)/shard_map/ppermute | solution.py:16
  7.3 12.4 %collective-permute-start.4 = (bf16[128,768]{1,0:T(8,128)(2,1)}, bf16[128,768]{1,0:T(8,128)(2,1)S(1)}, u32[]{:S(2)}, u32[]{:S(2)}) collective-permute-start(bf16[128,768]{1,0:T(8,128)(2,1)} %param.8), channel_id=1, source_target_pairs={{0,32},{16,48},{32,0},{48,16},{64,96},{80,112},{96,64},{112,80},{1... | collective-permute-start | bytes 589832 | tf_op jit(solution)/shard_map/ppermute | solution.py:16
  8.5 13.4 %collective-permute-start.6 = (bf16[128,768]{1,0:T(8,128)(2,1)}, bf16[128,768]{1,0:T(8,128)(2,1)S(1)}, u32[]{:S(2)}, u32[]{:S(2)}) collective-permute-start(bf16[128,768]{1,0:T(8,128)(2,1)} %param.8), channel_id=1, source_target_pairs={{0,96},{16,112},{32,64},{48,80},{64,32},{80,48},{96,0},{112,16},{1... | collective-permute-start | bytes 589832 | tf_op jit(solution)/shard_map/ppermute | solution.py:16
  8.5 12.0 %collective-permute-start.5 = (bf16[128,768]{1,0:T(8,128)(2,1)}, bf16[128,768]{1,0:T(8,128)(2,1)S(1)}, u32[]{:S(2)}, u32[]{:S(2)}) collective-permute-start(bf16[128,768]{1,0:T(8,128)(2,1)} %param.8), channel_id=1, source_target_pairs={{0,64},{16,80},{32,96},{48,112},{64,0},{80,16},{96,32},{112,48},{1... | collective-permute-start | bytes 589832 | tf_op jit(solution)/shard_map/ppermute | solution.py:16
  15.4 6.7 %copy-start.6 = (s32[1,1,5,8]{3,1,2,0:T(1,128)S(1)}, s32[1,1,5,8]{3,1,2,0:T(1,128)}, u32[]{:S(2)}) copy-start(s32[1,1,5,8]{3,1,2,0:T(1,128)} %param.14) | copy-start | bytes 484
  16.3 13.8 %collective-permute-start.3 = (bf16[128,768]{1,0:T(8,128)(2,1)S(1)}, bf16[128,768]{1,0:T(8,128)(2,1)S(1)}, u32[]{:S(2)}, u32[]{:S(2)}) collective-permute-start(bf16[128,768]{1,0:T(8,128)(2,1)S(1)} %collective-permute-done), channel_id=1, source_target_pairs={{0,96},{16,112},{32,64},{48,80},{64,32},{80,48},{96,0},{112,16},{1... | collective-permute-start | bytes 589832 | tf_op jit(solution)/shard_map/ppermute | solution.py:16
  16.9 11.1 %collective-permute-start.2 = (bf16[128,768]{1,0:T(8,128)(2,1)S(1)}, bf16[128,768]{1,0:T(8,128)(2,1)S(1)}, u32[]{:S(2)}, u32[]{:S(2)}) collective-permute-start(bf16[128,768]{1,0:T(8,128)(2,1)S(1)} %collective-permute-done), channel_id=1, source_target_pairs={{0,64},{16,80},{32,96},{48,112},{64,0},{80,16},{96,32},{112,48},{1... | collective-permute-start | bytes 589832 | tf_op jit(solution)/shard_map/ppermute | solution.py:16
  19.7 8.3 %collective-permute-start.1 = (bf16[128,768]{1,0:T(8,128)(2,1)S(1)}, bf16[128,768]{1,0:T(8,128)(2,1)S(1)}, u32[]{:S(2)}, u32[]{:S(2)}) collective-permute-start(bf16[128,768]{1,0:T(8,128)(2,1)S(1)} %collective-permute-done), channel_id=1, source_target_pairs={{0,32},{16,48},{32,0},{48,16},{64,96},{80,112},{96,64},{112,80},{1... | collective-permute-start | bytes 589832 | tf_op jit(solution)/shard_map/ppermute | solution.py:16
  21.9 6.1 %collective-permute-start.7 = (bf16[512,768]{1,0:T(8,128)(2,1)S(1)}, bf16[512,768]{1,0:T(8,128)(2,1)S(1)}, u32[]{:S(2)}, u32[]{:S(2)}) collective-permute-start(bf16[512,768]{1,0:T(8,128)(2,1)S(1)} %constant_dynamic-update-slice_fusion.group_ref), channel_id=1, source_target_pairs={{0,16},{16,0},{32,48},{48,32},{64,80},{80,64},{96,112},{112,96},{1... | collective-permute-start | bytes 2359304 | tf_op jit(solution)/shard_map/ppermute | solution.py:16
  30.2 2.4 %collective-permute-start.8 = (bf16[512,768]{1,0:T(8,128)(2,1)S(1)}, bf16[512,768]{1,0:T(8,128)(2,1)S(1)}, u32[]{:S(2)}, u32[]{:S(2)}) collective-permute-start(bf16[512,768]{1,0:T(8,128)(2,1)S(1)} %constant_dynamic-update-slice_fusion.4.group_ref), channel_id=1, source_target_pairs={{0,16},{16,0},{32,48},{48,32},{64,80},{80,64},{96,112},{112,96},{1... | collective-permute-start | bytes 2359304 | tf_op jit(solution)/shard_map/ppermute | solution.py:16
  34.2 49.9 %copy-start.4 = (f32[768]{0:T(1024)S(1)}, f32[768]{0:T(1024)}, u32[]{:S(2)}) copy-start(f32[768]{0:T(1024)} %param.11) | copy-start | bytes 9220
  34.3 13.5 %collective-permute-start.9 = (bf16[2,4,128,256]{3,2,1,0:T(8,128)(2,1)S(1)}, bf16[2,4,128,256]{3,2,1,0:T(8,128)(2,1)S(1)}, u32[]{:S(2)}, u32[]{:S(2)}) collective-permute-start(bf16[2,4,128,256]{3,2,1,0:T(8,128)(2,1)S(1)} %get-tuple-element.61), channel_id=1, source_target_pairs={{0,4},{1,5},{2,6},{3,7},{4,0},{5,1},{6,2},{7,3},{8,12},{9,13},{10,... | collective-permute-start | bytes 1572872 | tf_op jit(solution)/shard_map/ppermute | solution.py:20
  36.6 31.9 %collective-permute-start.12 = (bf16[4,128,512]{2,1,0:T(8,128)(2,1)S(1)}, bf16[4,128,512]{2,1,0:T(8,128)(2,1)S(1)}, u32[]{:S(2)}, u32[]{:S(2)}) collective-permute-start(bf16[4,128,512]{2,1,0:T(8,128)(2,1)S(1)} %get-tuple-element.70), channel_id=1, source_target_pairs={{0,2},{1,3},{2,0},{3,1},{4,6},{5,7},{6,4},{7,5},{8,10},{9,11},{10,... | collective-permute-start | bytes 1572872 | tf_op jit(solution)/shard_map/ppermute | solution.py:20
  39.5 29.0 %collective-permute-start.13 = (bf16[4,128,512]{2,1,0:T(8,128)(2,1)S(1)}, bf16[4,128,512]{2,1,0:T(8,128)(2,1)S(1)}, u32[]{:S(2)}, u32[]{:S(2)}) collective-permute-start(bf16[4,128,512]{2,1,0:T(8,128)(2,1)S(1)} %get-tuple-element.71), channel_id=1, source_target_pairs={{0,1},{1,0},{2,3},{3,2},{4,5},{5,4},{6,7},{7,6},{8,9},{9,8},{10,11... | collective-permute-start | bytes 1572872 | tf_op jit(solution)/shard_map/ppermute | solution.py:20
  41.1 27.4 %collective-permute-start.14 = (bf16[4,128,512]{2,1,0:T(8,128)(2,1)S(1)}, bf16[4,128,512]{2,1,0:T(8,128)(2,1)S(1)}, u32[]{:S(2)}, u32[]{:S(2)}) collective-permute-start(bf16[4,128,512]{2,1,0:T(8,128)(2,1)S(1)} %get-tuple-element.72), channel_id=1, source_target_pairs={{0,3},{1,2},{2,1},{3,0},{4,7},{5,6},{6,5},{7,4},{8,11},{9,10},{10,... | collective-permute-start | bytes 1572872 | tf_op jit(solution)/shard_map/ppermute | solution.py:20
  47.9 15.7 %collective-permute-start.10 = (bf16[4,128,256]{2,1,0:T(8,128)(2,1)S(1)}, bf16[4,128,256]{2,1,0:T(8,128)(2,1)S(1)}, u32[]{:S(2)}, u32[]{:S(2)}) collective-permute-start(bf16[4,128,256]{2,1,0:T(8,128)(2,1)S(1)} %get-tuple-element.64), channel_id=1, source_target_pairs={{0,8},{1,9},{2,10},{3,11},{4,12},{5,13},{6,14},{7,15},{8,0},{9,1},... | collective-permute-start | bytes 786440 | tf_op jit(solution)/shard_map/ppermute | solution.py:20
  63.7 8.5 %collective-permute-start.11 = (bf16[2,128,256]{2,1,0:T(8,128)(2,1)S(1)}, bf16[2,128,256]{2,1,0:T(8,128)(2,1)S(1)}, u32[]{:S(2)}, u32[]{:S(2)}) collective-permute-start(bf16[2,128,256]{2,1,0:T(8,128)(2,1)S(1)} %get-tuple-element.68), channel_id=1, source_target_pairs={{0,1},{1,0},{2,3},{3,2},{4,5},{5,4},{6,7},{7,6},{8,9},{9,8},{10,11... | collective-permute-start | bytes 393224 | tf_op jit(solution)/shard_map/ppermute | solution.py:20
  72.2 5.6 %collective-permute-start.18 = (bf16[128,256]{1,0:T(8,128)(2,1)S(1)}, bf16[128,256]{1,0:T(8,128)(2,1)S(1)}, u32[]{:S(2)}, u32[]{:S(2)}) collective-permute-start(bf16[128,256]{1,0:T(8,128)(2,1)S(1)} %get-tuple-element.86), channel_id=1, source_target_pairs={{0,3},{1,2},{2,1},{3,0},{4,7},{5,6},{6,5},{7,4},{8,11},{9,10},{10,... | collective-permute-start | bytes 196616 | tf_op jit(solution)/shard_map/ppermute | solution.py:20
  73.2 10.0 %collective-permute-start.15 = (bf16[128,512]{1,0:T(8,128)(2,1)S(1)}, bf16[128,512]{1,0:T(8,128)(2,1)S(1)}, u32[]{:S(2)}, u32[]{:S(2)}) collective-permute-start(bf16[128,512]{1,0:T(8,128)(2,1)S(1)} %get-tuple-element.79), channel_id=1, source_target_pairs={{0,8},{1,9},{2,10},{3,11},{4,12},{5,13},{6,14},{7,15},{8,0},{9,1},... | collective-permute-start | bytes 393224 | tf_op jit(solution)/shard_map/ppermute | solution.py:20
  73.2 10.0 %collective-permute-start.16 = (bf16[128,512]{1,0:T(8,128)(2,1)S(1)}, bf16[128,512]{1,0:T(8,128)(2,1)S(1)}, u32[]{:S(2)}, u32[]{:S(2)}) collective-permute-start(bf16[128,512]{1,0:T(8,128)(2,1)S(1)} %get-tuple-element.80), channel_id=1, source_target_pairs={{0,12},{1,13},{2,14},{3,15},{4,8},{5,9},{6,10},{7,11},{8,4},{9,5},... | collective-permute-start | bytes 393224 | tf_op jit(solution)/shard_map/ppermute | solution.py:20
  74.6 9.5 %collective-permute-start.17 = (bf16[128,512]{1,0:T(8,128)(2,1)S(1)}, bf16[128,512]{1,0:T(8,128)(2,1)S(1)}, u32[]{:S(2)}, u32[]{:S(2)}) collective-permute-start(bf16[128,512]{1,0:T(8,128)(2,1)S(1)} %get-tuple-element.81), channel_id=1, source_target_pairs={{0,4},{1,5},{2,6},{3,7},{4,0},{5,1},{6,2},{7,3},{8,12},{9,13},{10,... | collective-permute-start | bytes 393224 | tf_op jit(solution)/shard_map/ppermute | solution.py:20
  (3 other events, 4.9 us)

commit v4 on v3

--- a/solution.py
+++ b/solution.py
@@ -273,9 +273,10 @@
     shapes = [jax.ShapeDtypeStruct(piece, f32), jax.ShapeDtypeStruct(piece, bf16)]
     z_got, y_own = lax.optimization_barrier((z_got, y_own))
     z_own, z_send = small(merge_z_last, shapes, z_own, z_across, z_got)
-    z_own += col_swap(z_send, 0, 3).astype(f32)
-    y_last, z_own = lax.optimization_barrier((y_last, z_own))
+    z_last = col_swap(z_send, 0, 3)
     y_own += sum(part.astype(f32) for part in y_last)
+    z_last, y_own = lax.optimization_barrier((z_last, y_own))
+    z_own += z_last.astype(f32)
     return y_own, z_own, self_term
 
 

time: 86.6 us -> 82.1 us (0.948)
  the two profiles are of different devices: /device:TPU:4 before, /device:TPU:39 now
where the time goes in v4:
time: 82.1 us; the launch traced here: 81.9 us
  starting transfers between devices  34.8 us (42%)
  waiting for transfers between devices  28.3 us (34%)
  Pallas kernels  12.8 us (16%)
  local copies, waits for them, and re-layouts  4.58 us (6%)
  other arithmetic  0.89 us (1%)
    ppermute x10, waiting for transfers between devices, col_swap(): lax.ppermute(value, 'col', [(at, at ^ dz * Y + dy) for at in range(16)])  27.7 us
    ppermute x9, starting transfers between devices, row_swap(): lax.ppermute(value, 'row', [(at, at ^ dz * 8 + dx * 2 + dc) for at in ran...  18.2 us
    ppermute x10, starting transfers between devices, col_swap(): lax.ppermute(value, 'col', [(at, at ^ dz * Y + dy) for at in range(16)])  16.6 us
    pallas_call x4, Pallas kernels, tile_stage(): pl.pallas_call(functools.partial(stage_kernel, group, first, last), out_s...  10.1 us
    unnamed x22, local copies, waits for them, and re-layouts  4.55 us
    pallas_call x1, Pallas kernels, plan(): pl.pallas_call(plan_kernel, out_shape=[jax.ShapeDtypeStruct((many,), jnp....  1.78 us
  transfers between devices with their start and end apart: 19, of which 6 were waited for; matrix products, arithmetic and copies ran while one was open for 1% of the time, Pallas kernels for 11%

profile of v4, /device:TPU:39, one launch (start us, length us, event | category | flops | bytes accessed | tf_op | source)
XLA Modules:
  0.0 81.9 jit_solution(4375901899907185551)
XLA Ops:
  0.0 6.1 %collective-permute-start = (bf16[128,768]{1,0:T(8,128)(2,1)}, bf16[128,768]{1,0:T(8,128)(2,1)S(1)}, u32[]{:S(2)}, u32[]{:S(2)}) collective-permute-start(bf16[128,768]{1,0:T(8,128)(2,1)} %param.8), channel_id=1, source_target_pairs={{0,128},{16,144},{32,160},{48,176},{64,192},{80,208},{96,224},{112... | collective-permute-start | bytes 589832 | tf_op jit(solution)/shard_map/ppermute | solution.py:16
  7.5 1.8 %collective-permute-start.5 = (bf16[128,768]{1,0:T(8,128)(2,1)}, bf16[128,768]{1,0:T(8,128)(2,1)S(1)}, u32[]{:S(2)}, u32[]{:S(2)}) collective-permute-start(bf16[128,768]{1,0:T(8,128)(2,1)} %param.8), channel_id=1, source_target_pairs={{0,64},{16,80},{32,96},{48,112},{64,0},{80,16},{96,32},{112,48},{1... | collective-permute-start | bytes 589832 | tf_op jit(solution)/shard_map/ppermute | solution.py:16
  9.4 2.7 %copy-done.1 = bf16[768,5,768]{2,0,1:T(8,128)(2,1)S(1)} copy-done((bf16[768,5,768]{2,0,1:T(8,128)(2,1)S(1)}, bf16[768,5,768]{2,0,1:T(8,128)(2,1)}, u32[]{:S(2)}) %copy-start.1) | copy-done | bytes 5898264
  12.0 1.3 %copy-done.2 = bf16[1,1,5,8,128,128]{5,4,3,2,1,0:T(8,128)(2,1)S(1)} copy-done((bf16[1,1,5,8,128,128]{5,4,3,2,1,0:T(8,128)(2,1)S(1)}, bf16[1,1,5,8,128,128]{5,4,3,2,1,0:T(8,128)(2,1)}, u32[]{:S(2)}) %copy-start.2) | copy-done | bytes 1310744
  15.0 1.7 %collective-permute-start.2 = (bf16[128,768]{1,0:T(8,128)(2,1)S(1)}, bf16[128,768]{1,0:T(8,128)(2,1)S(1)}, u32[]{:S(2)}, u32[]{:S(2)}) collective-permute-start(bf16[128,768]{1,0:T(8,128)(2,1)S(1)} %collective-permute-done), channel_id=1, source_target_pairs={{0,64},{16,80},{32,96},{48,112},{64,0},{80,16},{96,32},{112,48},{1... | collective-permute-start | bytes 589832 | tf_op jit(solution)/shard_map/ppermute | solution.py:16
  16.7 0.9 %collective-permute-start.1 = (bf16[128,768]{1,0:T(8,128)(2,1)S(1)}, bf16[128,768]{1,0:T(8,128)(2,1)S(1)}, u32[]{:S(2)}, u32[]{:S(2)}) collective-permute-start(bf16[128,768]{1,0:T(8,128)(2,1)S(1)} %collective-permute-done), channel_id=1, source_target_pairs={{0,32},{16,48},{32,0},{48,16},{64,96},{80,112},{96,64},{112,80},{1... | collective-permute-start | bytes 589832 | tf_op jit(solution)/shard_map/ppermute | solution.py:16
  17.7 5.4 %collective-permute-start.7 = (bf16[512,768]{1,0:T(8,128)(2,1)S(1)}, bf16[512,768]{1,0:T(8,128)(2,1)S(1)}, u32[]{:S(2)}, u32[]{:S(2)}) collective-permute-start(bf16[512,768]{1,0:T(8,128)(2,1)S(1)} %constant_dynamic-update-slice_fusion.group_ref), channel_id=1, source_target_pairs={{0,16},{16,0},{32,48},{48,32},{64,80},{80,64},{96,112},{112,96},{1... | collective-permute-start | bytes 2359304 | tf_op jit(solution)/shard_map/ppermute | solution.py:16
  23.2 1.8 %plan.1 = (s32[40]{0:T(128)S(1)}, s32[21]{0:T(128)S(1)}) custom-call(s32[5,8]{1,0:T(8,128)S(1)} %fusion.4.table_ref), custom_call_target="tpu_custom_call" | custom-call | tf_op jit(solution)/shard_map/plan/pallas_call | solution.py:134
  25.0 2.9 %tile.4.refs_0_ = f32[2048,768]{1,0:T(8,128)S(1)} custom-call(s32[40]{0:T(128)S(1)} %get-tuple-element.51.codes_ref, s32[21]{0:T(128)S(1)} %get-tuple-element.52.starts_ref, bf16[40,128,128]{2,1,0:T(8,128)(2,1)S(1)} %get-tuple-element.53.blocks_ref, bf16[5,768,768]{2,1,0:T(8,128)(2,1)S(1)} %get-tuple-element.54.weight_ref, ...), custom_call_target="tpu_custom_call" | custom-call | flops 1073741824 | bytes 4194304 | tf_op jit(solution)/shard_map/tile/pallas_call | solution.py:160
  28.1 2.0 %tile.5.refs_0_ = f32[2048,768]{1,0:T(8,128)S(1)} custom-call(s32[40]{0:T(128)S(1)} %get-tuple-element.51.codes_ref, s32[21]{0:T(128)S(1)} %get-tuple-element.52.starts_ref, bf16[40,128,128]{2,1,0:T(8,128)(2,1)S(1)} %get-tuple-element.53.blocks_ref, bf16[5,768,768]{2,1,0:T(8,128)(2,1)S(1)} %get-tuple-element.54.weight_ref, ...), custom_call_target="tpu_custom_call", output_to_operand_aliasing={{}: (5, {})} | custom-call | flops 1073741824 | bytes 4194304 | tf_op jit(solution)/shard_map/tile/pallas_call | solution.py:160
  30.3 1.7 %tile.6.refs_0_ = f32[2048,768]{1,0:T(8,128)S(1)} custom-call(s32[40]{0:T(128)S(1)} %get-tuple-element.51.codes_ref, s32[21]{0:T(128)S(1)} %get-tuple-element.52.starts_ref, bf16[40,128,128]{2,1,0:T(8,128)(2,1)S(1)} %get-tuple-element.53.blocks_ref, bf16[5,768,768]{2,1,0:T(8,128)(2,1)S(1)} %get-tuple-element.54.weight_ref, ...), custom_call_target="tpu_custom_call", output_to_operand_aliasing={{}: (5, {})} | custom-call | flops 1073741824 | bytes 4194304 | tf_op jit(solution)/shard_map/tile/pallas_call | solution.py:160
  32.5 3.4 %tile.7 = (f32[2048,768]{1,0:T(8,128)S(1)}, bf16[4,128,512]{2,1,0:T(8,128)(2,1)S(1)}, bf16[4,128,512]{2,1,0:T(8,128)(2,1)S(1)}, bf16[4,128,512]{2,1,0:T(8,128)(2...) custom-call(s32[40]{0:T(128)S(1)} %get-tuple-element.51.codes_ref, ...), custom_call_target="tpu_custom_call", output_to_operand_aliasing={{0}: (5, {})} | custom-call | flops 1073741824 | bytes 4194304 | tf_op jit(solution)/shard_map/tile/pallas_call | solution.py:160
  36.3 4.7 %collective-permute-start.11 = (bf16[4,128,512]{2,1,0:T(8,128)(2,1)S(1)}, bf16[4,128,512]{2,1,0:T(8,128)(2,1)S(1)}, u32[]{:S(2)}, u32[]{:S(2)}) collective-permute-start(bf16[4,128,512]{2,1,0:T(8,128)(2,1)S(1)} %get-tuple-element.67), channel_id=1, source_target_pairs={{0,2},{1,3},{2,0},{3,1},{4,6},{5,7},{6,4},{7,5},{8,10},{9,11},{10,... | collective-permute-start | bytes 1572872 | tf_op jit(solution)/shard_map/ppermute | solution.py:20
  41.0 1.6 %collective-permute-start.12 = (bf16[4,128,512]{2,1,0:T(8,128)(2,1)S(1)}, bf16[4,128,512]{2,1,0:T(8,128)(2,1)S(1)}, u32[]{:S(2)}, u32[]{:S(2)}) collective-permute-start(bf16[4,128,512]{2,1,0:T(8,128)(2,1)S(1)} %get-tuple-element.68), channel_id=1, source_target_pairs={{0,1},{1,0},{2,3},{3,2},{4,5},{5,4},{6,7},{7,6},{8,9},{9,8},{10,11... | collective-permute-start | bytes 1572872 | tf_op jit(solution)/shard_map/ppermute | solution.py:20
  43.1 6.6 %collective-permute-done.9.refs_1_ = bf16[2,4,128,256]{3,2,1,0:T(8,128)(2,1)S(1)} collective-permute-done((bf16[2,4,128,256]{3,2,1,0:T(8,128)(2,1)S(1)}, bf16[2,4,128,256]{3,2,1,0:T(8,128)(2,1)S(1)}, u32[]{:S(2)}, u32[]{:S(2)}) %collective-permute-start.9) | collective-permute-done | bytes 524320 | tf_op jit(solution)/shard_map/ppermute | solution.py:20
  49.8 2.3 %collective-permute-start.10 = (bf16[4,128,256]{2,1,0:T(8,128)(2,1)S(1)}, bf16[4,128,256]{2,1,0:T(8,128)(2,1)S(1)}, u32[]{:S(2)}, u32[]{:S(2)}) collective-permute-start(bf16[4,128,256]{2,1,0:T(8,128)(2,1)S(1)} %get-tuple-element.62), channel_id=1, source_target_pairs={{0,8},{1,9},{2,10},{3,11},{4,12},{5,13},{6,14},{7,15},{8,0},{9,1},... | collective-permute-start | bytes 786440 | tf_op jit(solution)/shard_map/ppermute | solution.py:20
  52.5 11.1 %collective-permute-done.10.refs_1_ = bf16[4,128,256]{2,1,0:T(8,128)(2,1)S(1)} collective-permute-done((bf16[4,128,256]{2,1,0:T(8,128)(2,1)S(1)}, bf16[4,128,256]{2,1,0:T(8,128)(2,1)S(1)}, u32[]{:S(2)}, u32[]{:S(2)}) %collective-permute-start.10) | collective-permute-done | bytes 262176 | tf_op jit(solution)/shard_map/ppermute | solution.py:20
  63.9 2.1 %collective-permute-done.12.refs_2_ = bf16[4,128,512]{2,1,0:T(8,128)(2,1)S(1)} collective-permute-done((bf16[4,128,512]{2,1,0:T(8,128)(2,1)S(1)}, bf16[4,128,512]{2,1,0:T(8,128)(2,1)S(1)}, u32[]{:S(2)}, u32[]{:S(2)}) %collective-permute-start.12) | collective-permute-done | bytes 524320 | tf_op jit(solution)/shard_map/ppermute | solution.py:20
  66.2 1.1 %collective-permute-start.16 = (bf16[128,512]{1,0:T(8,128)(2,1)S(1)}, bf16[128,512]{1,0:T(8,128)(2,1)S(1)}, u32[]{:S(2)}, u32[]{:S(2)}) collective-permute-start(bf16[128,512]{1,0:T(8,128)(2,1)S(1)} %get-tuple-element.81), channel_id=1, source_target_pairs={{0,8},{1,9},{2,10},{3,11},{4,12},{5,13},{6,14},{7,15},{8,0},{9,1},... | collective-permute-start | bytes 393224 | tf_op jit(solution)/shard_map/ppermute | solution.py:20
  67.3 1.6 %collective-permute-start.17 = (bf16[128,512]{1,0:T(8,128)(2,1)S(1)}, bf16[128,512]{1,0:T(8,128)(2,1)S(1)}, u32[]{:S(2)}, u32[]{:S(2)}) collective-permute-start(bf16[128,512]{1,0:T(8,128)(2,1)S(1)} %get-tuple-element.82), channel_id=1, source_target_pairs={{0,12},{1,13},{2,14},{3,15},{4,8},{5,9},{6,10},{7,11},{8,4},{9,5},... | collective-permute-start | bytes 393224 | tf_op jit(solution)/shard_map/ppermute | solution.py:20
  69.0 0.9 %collective-permute-start.18 = (bf16[128,512]{1,0:T(8,128)(2,1)S(1)}, bf16[128,512]{1,0:T(8,128)(2,1)S(1)}, u32[]{:S(2)}, u32[]{:S(2)}) collective-permute-start(bf16[128,512]{1,0:T(8,128)(2,1)S(1)} %get-tuple-element.83), channel_id=1, source_target_pairs={{0,4},{1,5},{2,6},{3,7},{4,0},{5,1},{6,2},{7,3},{8,12},{9,13},{10,... | collective-permute-start | bytes 393224 | tf_op jit(solution)/shard_map/ppermute | solution.py:20
  69.9 3.2 %collective-permute-start.15 = (bf16[128,256]{1,0:T(8,128)(2,1)S(1)}, bf16[128,256]{1,0:T(8,128)(2,1)S(1)}, u32[]{:S(2)}, u32[]{:S(2)}) collective-permute-start(bf16[128,256]{1,0:T(8,128)(2,1)S(1)} %get-tuple-element.79), channel_id=1, source_target_pairs={{0,3},{1,2},{2,1},{3,0},{4,7},{5,6},{6,5},{7,4},{8,11},{9,10},{10,... | collective-permute-start | bytes 196616 | tf_op jit(solution)/shard_map/ppermute | solution.py:20
  73.1 2.6 %collective-permute-done.16 = bf16[128,512]{1,0:T(8,128)(2,1)S(1)} collective-permute-done((bf16[128,512]{1,0:T(8,128)(2,1)S(1)}, bf16[128,512]{1,0:T(8,128)(2,1)S(1)}, u32[]{:S(2)}, u32[]{:S(2)}) %collective-permute-start.16) | collective-permute-done | bytes 131104 | tf_op jit(solution)/shard_map/ppermute | solution.py:20
  75.7 5.3 %collective-permute-done.17 = bf16[128,512]{1,0:T(8,128)(2,1)S(1)} collective-permute-done((bf16[128,512]{1,0:T(8,128)(2,1)S(1)}, bf16[128,512]{1,0:T(8,128)(2,1)S(1)}, u32[]{:S(2)}, u32[]{:S(2)}) %collective-permute-start.17) | collective-permute-done | bytes 131104 | tf_op jit(solution)/shard_map/ppermute | solution.py:20
  (54 shorter events, 6.6 us)
Async XLA Ops:
  0.0 52.2 %copy-start = (bf16[768,768]{1,0:T(8,128)(2,1)S(1)}, bf16[768,768]{1,0:T(8,128)(2,1)}, u32[]{:S(2)}) copy-start(bf16[768,768]{1,0:T(8,128)(2,1)} %param.9) | copy-start | bytes 3538948
  0.0 23.1 %copy-start.7 = (s32[1,1,5]{2,1,0:T(1,128)S(1)}, s32[1,1,5]{2,1,0:T(1,128)}, u32[]{:S(2)}) copy-start(s32[1,1,5]{2,1,0:T(1,128)} %param.15) | copy-start | bytes 64
  0.0 23.1 %copy-start.5 = (s32[1,1,5,8]{3,1,2,0:T(1,128)S(1)}, s32[1,1,5,8]{3,1,2,0:T(1,128)}, u32[]{:S(2)}) copy-start(s32[1,1,5,8]{3,1,2,0:T(1,128)} %param.13) | copy-start | bytes 484
  0.0 14.3 %collective-permute-start = (bf16[128,768]{1,0:T(8,128)(2,1)}, bf16[128,768]{1,0:T(8,128)(2,1)S(1)}, u32[]{:S(2)}, u32[]{:S(2)}) collective-permute-start(bf16[128,768]{1,0:T(8,128)(2,1)} %param.8), channel_id=1, source_target_pairs={{0,128},{16,144},{32,160},{48,176},{64,192},{80,208},{96,224},{112... | collective-permute-start | bytes 589832 | tf_op jit(solution)/shard_map/ppermute | solution.py:16
  6.1 10.6 %collective-permute-start.4 = (bf16[128,768]{1,0:T(8,128)(2,1)}, bf16[128,768]{1,0:T(8,128)(2,1)S(1)}, u32[]{:S(2)}, u32[]{:S(2)}) collective-permute-start(bf16[128,768]{1,0:T(8,128)(2,1)} %param.8), channel_id=1, source_target_pairs={{0,32},{16,48},{32,0},{48,16},{64,96},{80,112},{96,64},{112,80},{1... | collective-permute-start | bytes 589832 | tf_op jit(solution)/shard_map/ppermute | solution.py:16
  6.7 11.0 %collective-permute-start.6 = (bf16[128,768]{1,0:T(8,128)(2,1)}, bf16[128,768]{1,0:T(8,128)(2,1)S(1)}, u32[]{:S(2)}, u32[]{:S(2)}) collective-permute-start(bf16[128,768]{1,0:T(8,128)(2,1)} %param.8), channel_id=1, source_target_pairs={{0,96},{16,112},{32,64},{48,80},{64,32},{80,48},{96,0},{112,16},{1... | collective-permute-start | bytes 589832 | tf_op jit(solution)/shard_map/ppermute | solution.py:16
  7.5 10.2 %collective-permute-start.5 = (bf16[128,768]{1,0:T(8,128)(2,1)}, bf16[128,768]{1,0:T(8,128)(2,1)S(1)}, u32[]{:S(2)}, u32[]{:S(2)}) collective-permute-start(bf16[128,768]{1,0:T(8,128)(2,1)} %param.8), channel_id=1, source_target_pairs={{0,64},{16,80},{32,96},{48,112},{64,0},{80,16},{96,32},{112,48},{1... | collective-permute-start | bytes 589832 | tf_op jit(solution)/shard_map/ppermute | solution.py:16
  13.4 9.8 %copy-start.6 = (s32[1,1,5,8]{3,1,2,0:T(1,128)S(1)}, s32[1,1,5,8]{3,1,2,0:T(1,128)}, u32[]{:S(2)}) copy-start(s32[1,1,5,8]{3,1,2,0:T(1,128)} %param.14) | copy-start | bytes 484
  14.3 15.8 %collective-permute-start.3 = (bf16[128,768]{1,0:T(8,128)(2,1)S(1)}, bf16[128,768]{1,0:T(8,128)(2,1)S(1)}, u32[]{:S(2)}, u32[]{:S(2)}) collective-permute-start(bf16[128,768]{1,0:T(8,128)(2,1)S(1)} %collective-permute-done), channel_id=1, source_target_pairs={{0,96},{16,112},{32,64},{48,80},{64,32},{80,48},{96,0},{112,16},{1... | collective-permute-start | bytes 589832 | tf_op jit(solution)/shard_map/ppermute | solution.py:16
  15.0 13.0 %collective-permute-start.2 = (bf16[128,768]{1,0:T(8,128)(2,1)S(1)}, bf16[128,768]{1,0:T(8,128)(2,1)S(1)}, u32[]{:S(2)}, u32[]{:S(2)}) collective-permute-start(bf16[128,768]{1,0:T(8,128)(2,1)S(1)} %collective-permute-done), channel_id=1, source_target_pairs={{0,64},{16,80},{32,96},{48,112},{64,0},{80,16},{96,32},{112,48},{1... | collective-permute-start | bytes 589832 | tf_op jit(solution)/shard_map/ppermute | solution.py:16
  16.7 11.3 %collective-permute-start.1 = (bf16[128,768]{1,0:T(8,128)(2,1)S(1)}, bf16[128,768]{1,0:T(8,128)(2,1)S(1)}, u32[]{:S(2)}, u32[]{:S(2)}) collective-permute-start(bf16[128,768]{1,0:T(8,128)(2,1)S(1)} %collective-permute-done), channel_id=1, source_target_pairs={{0,32},{16,48},{32,0},{48,16},{64,96},{80,112},{96,64},{112,80},{1... | collective-permute-start | bytes 589832 | tf_op jit(solution)/shard_map/ppermute | solution.py:16
  17.7 10.3 %collective-permute-start.7 = (bf16[512,768]{1,0:T(8,128)(2,1)S(1)}, bf16[512,768]{1,0:T(8,128)(2,1)S(1)}, u32[]{:S(2)}, u32[]{:S(2)}) collective-permute-start(bf16[512,768]{1,0:T(8,128)(2,1)S(1)} %constant_dynamic-update-slice_fusion.group_ref), channel_id=1, source_target_pairs={{0,16},{16,0},{32,48},{48,32},{64,80},{80,64},{96,112},{112,96},{1... | collective-permute-start | bytes 2359304 | tf_op jit(solution)/shard_map/ppermute | solution.py:16
  30.2 2.4 %collective-permute-start.8 = (bf16[512,768]{1,0:T(8,128)(2,1)S(1)}, bf16[512,768]{1,0:T(8,128)(2,1)S(1)}, u32[]{:S(2)}, u32[]{:S(2)}) collective-permute-start(bf16[512,768]{1,0:T(8,128)(2,1)S(1)} %constant_dynamic-update-slice_fusion.4.group_ref), channel_id=1, source_target_pairs={{0,16},{16,0},{32,48},{48,32},{64,80},{80,64},{96,112},{112,96},{1... | collective-permute-start | bytes 2359304 | tf_op jit(solution)/shard_map/ppermute | solution.py:16
  35.9 45.2 %copy-start.4 = (f32[768]{0:T(1024)S(1)}, f32[768]{0:T(1024)}, u32[]{:S(2)}) copy-start(f32[768]{0:T(1024)} %param.11) | copy-start | bytes 9220
  36.0 13.8 %collective-permute-start.9 = (bf16[2,4,128,256]{3,2,1,0:T(8,128)(2,1)S(1)}, bf16[2,4,128,256]{3,2,1,0:T(8,128)(2,1)S(1)}, u32[]{:S(2)}, u32[]{:S(2)}) collective-permute-start(bf16[2,4,128,256]{3,2,1,0:T(8,128)(2,1)S(1)} %get-tuple-element.59), channel_id=1, source_target_pairs={{0,4},{1,5},{2,6},{3,7},{4,0},{5,1},{6,2},{7,3},{8,12},{9,13},{10,... | collective-permute-start | bytes 1572872 | tf_op jit(solution)/shard_map/ppermute | solution.py:20
  36.3 27.6 %collective-permute-start.11 = (bf16[4,128,512]{2,1,0:T(8,128)(2,1)S(1)}, bf16[4,128,512]{2,1,0:T(8,128)(2,1)S(1)}, u32[]{:S(2)}, u32[]{:S(2)}) collective-permute-start(bf16[4,128,512]{2,1,0:T(8,128)(2,1)S(1)} %get-tuple-element.67), channel_id=1, source_target_pairs={{0,2},{1,3},{2,0},{3,1},{4,6},{5,7},{6,4},{7,5},{8,10},{9,11},{10,... | collective-permute-start | bytes 1572872 | tf_op jit(solution)/shard_map/ppermute | solution.py:20
  41.0 24.9 %collective-permute-start.12 = (bf16[4,128,512]{2,1,0:T(8,128)(2,1)S(1)}, bf16[4,128,512]{2,1,0:T(8,128)(2,1)S(1)}, u32[]{:S(2)}, u32[]{:S(2)}) collective-permute-start(bf16[4,128,512]{2,1,0:T(8,128)(2,1)S(1)} %get-tuple-element.68), channel_id=1, source_target_pairs={{0,1},{1,0},{2,3},{3,2},{4,5},{5,4},{6,7},{7,6},{8,9},{9,8},{10,11... | collective-permute-start | bytes 1572872 | tf_op jit(solution)/shard_map/ppermute | solution.py:20
  42.6 23.3 %collective-permute-start.13 = (bf16[4,128,512]{2,1,0:T(8,128)(2,1)S(1)}, bf16[4,128,512]{2,1,0:T(8,128)(2,1)S(1)}, u32[]{:S(2)}, u32[]{:S(2)}) collective-permute-start(bf16[4,128,512]{2,1,0:T(8,128)(2,1)S(1)} %get-tuple-element.69), channel_id=1, source_target_pairs={{0,3},{1,2},{2,1},{3,0},{4,7},{5,6},{6,5},{7,4},{8,11},{9,10},{10,... | collective-permute-start | bytes 1572872 | tf_op jit(solution)/shard_map/ppermute | solution.py:20
  49.8 13.7 %collective-permute-start.10 = (bf16[4,128,256]{2,1,0:T(8,128)(2,1)S(1)}, bf16[4,128,256]{2,1,0:T(8,128)(2,1)S(1)}, u32[]{:S(2)}, u32[]{:S(2)}) collective-permute-start(bf16[4,128,256]{2,1,0:T(8,128)(2,1)S(1)} %get-tuple-element.62), channel_id=1, source_target_pairs={{0,8},{1,9},{2,10},{3,11},{4,12},{5,13},{6,14},{7,15},{8,0},{9,1},... | collective-permute-start | bytes 786440 | tf_op jit(solution)/shard_map/ppermute | solution.py:20
  63.6 6.2 %collective-permute-start.14 = (bf16[2,128,256]{2,1,0:T(8,128)(2,1)S(1)}, bf16[2,128,256]{2,1,0:T(8,128)(2,1)S(1)}, u32[]{:S(2)}, u32[]{:S(2)}) collective-permute-start(bf16[2,128,256]{2,1,0:T(8,128)(2,1)S(1)} %get-tuple-element.72), channel_id=1, source_target_pairs={{0,1},{1,0},{2,3},{3,2},{4,5},{5,4},{6,7},{7,6},{8,9},{9,8},{10,11... | collective-permute-start | bytes 393224 | tf_op jit(solution)/shard_map/ppermute | solution.py:20
  66.2 9.5 %collective-permute-start.16 = (bf16[128,512]{1,0:T(8,128)(2,1)S(1)}, bf16[128,512]{1,0:T(8,128)(2,1)S(1)}, u32[]{:S(2)}, u32[]{:S(2)}) collective-permute-start(bf16[128,512]{1,0:T(8,128)(2,1)S(1)} %get-tuple-element.81), channel_id=1, source_target_pairs={{0,8},{1,9},{2,10},{3,11},{4,12},{5,13},{6,14},{7,15},{8,0},{9,1},... | collective-permute-start | bytes 393224 | tf_op jit(solution)/shard_map/ppermute | solution.py:20
  67.3 13.7 %collective-permute-start.17 = (bf16[128,512]{1,0:T(8,128)(2,1)S(1)}, bf16[128,512]{1,0:T(8,128)(2,1)S(1)}, u32[]{:S(2)}, u32[]{:S(2)}) collective-permute-start(bf16[128,512]{1,0:T(8,128)(2,1)S(1)} %get-tuple-element.82), channel_id=1, source_target_pairs={{0,12},{1,13},{2,14},{3,15},{4,8},{5,9},{6,10},{7,11},{8,4},{9,5},... | collective-permute-start | bytes 393224 | tf_op jit(solution)/shard_map/ppermute | solution.py:20
  69.0 12.1 %collective-permute-start.18 = (bf16[128,512]{1,0:T(8,128)(2,1)S(1)}, bf16[128,512]{1,0:T(8,128)(2,1)S(1)}, u32[]{:S(2)}, u32[]{:S(2)}) collective-permute-start(bf16[128,512]{1,0:T(8,128)(2,1)S(1)} %get-tuple-element.83), channel_id=1, source_target_pairs={{0,4},{1,5},{2,6},{3,7},{4,0},{5,1},{6,2},{7,3},{8,12},{9,13},{10,... | collective-permute-start | bytes 393224 | tf_op jit(solution)/shard_map/ppermute | solution.py:20
  69.9 11.3 %collective-permute-start.15 = (bf16[128,256]{1,0:T(8,128)(2,1)S(1)}, bf16[128,256]{1,0:T(8,128)(2,1)S(1)}, u32[]{:S(2)}, u32[]{:S(2)}) collective-permute-start(bf16[128,256]{1,0:T(8,128)(2,1)S(1)} %get-tuple-element.79), channel_id=1, source_target_pairs={{0,3},{1,2},{2,1},{3,0},{4,7},{5,6},{6,5},{7,4},{8,11},{9,10},{10,... | collective-permute-start | bytes 196616 | tf_op jit(solution)/shard_map/ppermute | solution.py:20
  (3 other events, 4.9 us)

commit v5 on v3

--- a/solution.py
+++ b/solution.py
@@ -8,7 +8,7 @@
 from jax.sharding import PartitionSpec as P
 
 Z, Y = 4, 4
-SPLIT = 512
+FIRST = 32
 UNROLL, QUAD = 4, 4
 
 
@@ -29,7 +29,7 @@
         refs = refs[1:]
     total, refs = refs[0], refs[1:]
     if last:
-        y_refs, z_refs, refs = refs[:Y], refs[Y : Y + 2], refs[Y + 2 :]
+        y_refs, z_refs, own_ref, refs = refs[:Y], refs[Y : Y + 2], refs[Y + 2], refs[Y + 3 :]
     (picked,) = refs
     relations = weight_ref.shape[0]
     size = blocks_ref.shape[-1]
@@ -80,9 +80,12 @@
     if last:
         for d in range(Y):
             for e in range(Z):
-                rows = pl.ds((d * Z + e) * size, size)
-                y_refs[d][e] = total[rows, :SPLIT].astype(jnp.bfloat16)
-                z_refs[e % 2][e // 2, d] = total[rows, SPLIT:].astype(jnp.bfloat16)
+                rows = total[(d * Z + e) * size : (d * Z + e + 1) * size, :].astype(jnp.bfloat16)
+                z_refs[e % 2][e // 2, d] = rows[:FIRST]
+                if e == 0:
+                    own_ref[d] = rows[FIRST:]
+                else:
+                    y_refs[d][e - 1] = rows[FIRST:]
 
 
 def plan_kernel(table_ref, codes_ref, starts_ref):
@@ -152,8 +155,9 @@
     smem = pl.BlockSpec(memory_space=pltpu.SMEM)
     out_shape = [jax.ShapeDtypeStruct((Y * Z * size, width), jnp.float32)]
     if last:
-        out_shape += [jax.ShapeDtypeStruct((Z, size, SPLIT), jnp.bfloat16)] * Y
-        out_shape += [jax.ShapeDtypeStruct((Z // 2, Y, size, width - SPLIT), jnp.bfloat16)] * 2
+        out_shape += [jax.ShapeDtypeStruct((Z - 1, size - FIRST, width), jnp.bfloat16)] * Y
+        out_shape += [jax.ShapeDtypeStruct((Z // 2, Y, FIRST, width), jnp.bfloat16)] * 2
+        out_shape += [jax.ShapeDtypeStruct((Y, size - FIRST, width), jnp.bfloat16)]
     args = [*tables, blocks, weights, value]
     if not first:
         args.append(total)
@@ -186,9 +190,8 @@
 
 
 def merge_y(ins, outs):
-    for e in range(Z):
-        summed = sum(ref[e].astype(jnp.float32) for ref in ins)
-        outs[e][...] = summed.astype(outs[e].dtype)
+    for e in range(Z - 1):
+        outs[e][...] = sum(ref[e].astype(jnp.float32) for ref in ins).astype(jnp.bfloat16)
 
 
 def merge_z_near(ins, outs):
@@ -198,13 +201,15 @@
 
 
 def merge_z_far(ins, outs):
-    kept, got = ins
+    kept, got, own = ins
     for d in range(Y):
-        summed = kept[d] + got[d].astype(jnp.float32)
+        top = kept[d] + got[d].astype(jnp.float32)
         if d == 0 or d == 3:
-            outs[d // 3][...] = summed
+            outs[d // 3][:FIRST, :] = top
+            outs[d // 3][FIRST:, :] = own[d].astype(jnp.float32)
         else:
-            outs[2][d - 1] = summed.astype(jnp.bfloat16)
+            outs[2][d - 1, :FIRST, :] = top.astype(jnp.bfloat16)
+            outs[2][d - 1, FIRST:, :] = own[d]
 
 
 def merge_z_last(ins, outs):
@@ -250,33 +255,34 @@
 
 
 def scatter_sum(parts, features, self_weight):
-    y_parts, (z_here, z_there) = parts[:Y], parts[Y:]
+    y_parts, (z_here, z_there, own) = parts[:Y], parts[Y:]
     f32, bf16 = jnp.float32, jnp.bfloat16
-    many, size, columns = z_here.shape[1:]
-    piece = (size, columns)
+    width = own.shape[-1]
     z_near = col_swap(z_there, 1, 0)
     y_in = [col_swap(y_parts[d], 0, d) for d in (2, 1, 3)]
-    shapes = [jax.ShapeDtypeStruct((many, *piece), f32), jax.ShapeDtypeStruct((many, *piece), bf16)]
+    piece = z_here.shape[1:]
+    shapes = [jax.ShapeDtypeStruct(piece, f32), jax.ShapeDtypeStruct(piece, bf16)]
     z_kept, z_send = small(merge_z_near, shapes, z_here, z_near)
     z_far = col_swap(z_send, 2, 0)
     features, z_kept = lax.optimization_barrier((features, z_kept))
-    self_term = jnp.dot(features, self_weight, preferred_element_type=jnp.float32)
+    self_term = jnp.dot(features, self_weight, preferred_element_type=f32)
     self_term, z_far = lax.optimization_barrier((self_term, z_far))
-    shapes = [jax.ShapeDtypeStruct(piece, f32)] * 2 + [jax.ShapeDtypeStruct((2, *piece), bf16)]
-    z_own, z_across, z_send = small(merge_z_far, shapes, z_kept, z_far)
-    z_got = col_swap(z_send, 0, 1)
-    y_in, z_across = lax.optimization_barrier((y_in, z_across))
-    piece_y = y_parts[0].shape[1:]
-    shapes = [jax.ShapeDtypeStruct(piece_y, f32)] + [jax.ShapeDtypeStruct(piece_y, bf16)] * 3
-    y_own, *y_send = small(merge_y, shapes, y_parts[0], *y_in)
+    block = (FIRST + own.shape[1], width)
+    shapes = [jax.ShapeDtypeStruct(block, f32)] * 2 + [jax.ShapeDtypeStruct((2, *block), bf16)]
+    here, across, send = small(merge_z_far, shapes, z_kept, z_far, own)
+    got = col_swap(send, 0, 1)
+    y_in, across = lax.optimization_barrier((y_in, across))
+    shapes = [jax.ShapeDtypeStruct(own.shape[1:], bf16)] * (Z - 1)
+    y_send = list(small(merge_y, shapes, y_parts[0], *y_in))
     y_last = [col_swap(y_send[e - 1], e, 0) for e in (2, 3, 1)]
-    shapes = [jax.ShapeDtypeStruct(piece, f32), jax.ShapeDtypeStruct(piece, bf16)]
-    z_got, y_own = lax.optimization_barrier((z_got, y_own))
-    z_own, z_send = small(merge_z_last, shapes, z_own, z_across, z_got)
-    z_own += col_swap(z_send, 0, 3).astype(f32)
-    y_last, z_own = lax.optimization_barrier((y_last, z_own))
-    y_own += sum(part.astype(f32) for part in y_last)
-    return y_own, z_own, self_term
+    y_send[0], got = lax.optimization_barrier((y_send[0], got))
+    shapes = [jax.ShapeDtypeStruct(block, f32), jax.ShapeDtypeStruct(block, bf16)]
+    here, send = small(merge_z_last, shapes, here, across, got)
+    last = col_swap(send, 0, 3)
+    y_sum = sum(part.astype(f32) for part in y_last)
+    last, y_sum = lax.optimization_barrier((last, y_sum))
+    here += last.astype(f32)
+    return jnp.concatenate([here[:FIRST], here[FIRST:] + y_sum], axis=0), self_term
 
 
 def per_device(
@@ -287,8 +293,7 @@
     blocks = blocks.reshape(relations * slots, size, size)
     to_plan = (block_rows, block_cols, block_counts)
     parts = gather_groups(features, to_plan, blocks, weights)
-    y_own, z_own, self_term = scatter_sum(parts, features, self_weight)
-    owned = jnp.concatenate([y_own, z_own], axis=1)
+    owned, self_term = scatter_sum(parts, features, self_weight)
     return jnp.maximum(self_term + owned + bias, 0.0).astype(jnp.bfloat16)
 
 

time: 86.6 us -> 80.2 us (0.926); the launches traced: 84.9 us -> 79.4 us
  waiting for transfers between devices: 35 us -> 30.6 us
  starting transfers between devices: 35.2 us -> 30.9 us
  Pallas kernels: 8.73 us -> 11.7 us
    ppermute x10, starting transfers between devices: 19.4 us -> 15.2 us  [col_swap(): lax.ppermute(value, 'col', [(at, at ^ dz * Y + dy) for at in range(16)])]
    ppermute x10, waiting for transfers between devices: 29.6 us -> 26.2 us  [col_swap(): lax.ppermute(value, 'col', [(at, at ^ dz * Y + dy) for at in range(16)])]
    pallas_call x4, Pallas kernels: 6.4 us -> 9.11 us  [tile_stage(): pl.pallas_call(functools.partial(stage_kernel, group, first, last), out_s...]
    ppermute x9, waiting for transfers between devices: 5.38 us -> 4.43 us  [row_swap(): lax.ppermute(value, 'row', [(at, at ^ dz * 8 + dx * 2 + dc) for at in ran...]
  transfers between devices with their start and end apart: 19 -> 19, of which waited for: 9 -> 8; matrix products, arithmetic and copies ran while one was open for 1% -> 1% of each run, Pallas kernels for 8% -> 11%
where the time goes in v5:
time: 80.2 us; the launch traced here: 79.4 us
  starting transfers between devices  30.9 us (39%)
  waiting for transfers between devices  30.6 us (38%)
  Pallas kernels  11.7 us (15%)
  local copies, waits for them, and re-layouts  4.59 us (6%)
  other arithmetic  0.93 us (1%)
    ppermute x10, waiting for transfers between devices, col_swap(): lax.ppermute(value, 'col', [(at, at ^ dz * Y + dy) for at in range(16)])  26.2 us
    ppermute x9, starting transfers between devices, row_swap(): lax.ppermute(value, 'row', [(at, at ^ dz * 8 + dx * 2 + dc) for at in ran...  15.7 us
    ppermute x10, starting transfers between devices, col_swap(): lax.ppermute(value, 'col', [(at, at ^ dz * Y + dy) for at in range(16)])  15.2 us
    pallas_call x4, Pallas kernels, tile_stage(): pl.pallas_call(functools.partial(stage_kernel, group, first, last), out_s...  9.11 us
    unnamed x22, local copies, waits for them, and re-layouts  4.55 us
    ppermute x9, waiting for transfers between devices, row_swap(): lax.ppermute(value, 'row', [(at, at ^ dz * 8 + dx * 2 + dc) for at in ran...  4.43 us
    pallas_call x1, Pallas kernels, plan(): pl.pallas_call(plan_kernel, out_shape=[jax.ShapeDtypeStruct((many,), jnp....  1.68 us
  transfers between devices with their start and end apart: 19, of which 8 were waited for; matrix products, arithmetic and copies ran while one was open for 1% of the time, Pallas kernels for 11%

profile of v5, /device:TPU:4, one launch (start us, length us, event | category | flops | bytes accessed | tf_op | source)
XLA Modules:
  0.0 79.4 jit_solution(7220462727424132026)
XLA Ops:
  0.0 7.3 %collective-permute-start = (bf16[128,768]{1,0:T(8,128)(2,1)}, bf16[128,768]{1,0:T(8,128)(2,1)S(1)}, u32[]{:S(2)}, u32[]{:S(2)}) collective-permute-start(bf16[128,768]{1,0:T(8,128)(2,1)} %param.8), channel_id=1, source_target_pairs={{0,128},{16,144},{32,160},{48,176},{64,192},{80,208},{96,224},{112... | collective-permute-start | bytes 589832 | tf_op jit(solution)/shard_map/ppermute | solution.py:16
  8.5 2.9 %collective-permute-start.5 = (bf16[128,768]{1,0:T(8,128)(2,1)}, bf16[128,768]{1,0:T(8,128)(2,1)S(1)}, u32[]{:S(2)}, u32[]{:S(2)}) collective-permute-start(bf16[128,768]{1,0:T(8,128)(2,1)} %param.8), channel_id=1, source_target_pairs={{0,64},{16,80},{32,96},{48,112},{64,0},{80,16},{96,32},{112,48},{1... | collective-permute-start | bytes 589832 | tf_op jit(solution)/shard_map/ppermute | solution.py:16
  11.4 2.7 %copy-done.1 = bf16[768,5,768]{2,0,1:T(8,128)(2,1)S(1)} copy-done((bf16[768,5,768]{2,0,1:T(8,128)(2,1)S(1)}, bf16[768,5,768]{2,0,1:T(8,128)(2,1)}, u32[]{:S(2)}) %copy-start.1) | copy-done | bytes 5898264
  14.1 1.3 %copy-done.2 = bf16[1,1,5,8,128,128]{5,4,3,2,1,0:T(8,128)(2,1)S(1)} copy-done((bf16[1,1,5,8,128,128]{5,4,3,2,1,0:T(8,128)(2,1)S(1)}, bf16[1,1,5,8,128,128]{5,4,3,2,1,0:T(8,128)(2,1)}, u32[]{:S(2)}) %copy-start.2) | copy-done | bytes 1310744
  16.9 2.7 %collective-permute-start.2 = (bf16[128,768]{1,0:T(8,128)(2,1)S(1)}, bf16[128,768]{1,0:T(8,128)(2,1)S(1)}, u32[]{:S(2)}, u32[]{:S(2)}) collective-permute-start(bf16[128,768]{1,0:T(8,128)(2,1)S(1)} %collective-permute-done), channel_id=1, source_target_pairs={{0,64},{16,80},{32,96},{48,112},{64,0},{80,16},{96,32},{112,48},{1... | collective-permute-start | bytes 589832 | tf_op jit(solution)/shard_map/ppermute | solution.py:16
  20.6 1.3 %collective-permute-done.6 = bf16[128,768]{1,0:T(8,128)(2,1)S(1)} collective-permute-done((bf16[128,768]{1,0:T(8,128)(2,1)}, bf16[128,768]{1,0:T(8,128)(2,1)S(1)}, u32[]{:S(2)}, u32[]{:S(2)}) %collective-permute-start.6) | collective-permute-done | bytes 196640 | tf_op jit(solution)/shard_map/ppermute | solution.py:16
  22.1 1.7 %plan.1 = (s32[40]{0:T(128)S(1)}, s32[21]{0:T(128)S(1)}) custom-call(s32[5,8]{1,0:T(8,128)S(1)} %fusion.4.table_ref), custom_call_target="tpu_custom_call" | custom-call | tf_op jit(solution)/shard_map/plan/pallas_call | solution.py:137
  24.9 3.1 %collective-permute-done.1 = bf16[128,768]{1,0:T(8,128)(2,1)S(1)} collective-permute-done((bf16[128,768]{1,0:T(8,128)(2,1)S(1)}, bf16[128,768]{1,0:T(8,128)(2,1)S(1)}, u32[]{:S(2)}, u32[]{:S(2)}) %collective-permute-start.1) | collective-permute-done | bytes 196640 | tf_op jit(solution)/shard_map/ppermute | solution.py:16
  28.0 2.9 %tile.5.refs_0_ = f32[2048,768]{1,0:T(8,128)S(1)} custom-call(s32[40]{0:T(128)S(1)} %get-tuple-element.50.codes_ref, s32[21]{0:T(128)S(1)} %get-tuple-element.51.starts_ref, bf16[40,128,128]{2,1,0:T(8,128)(2,1)S(1)} %get-tuple-element.52.blocks_ref, bf16[5,768,768]{2,1,0:T(8,128)(2,1)S(1)} %get-tuple-element.53.weight_ref, ...), custom_call_target="tpu_custom_call", output_to_operand_aliasing={{}: (5, {})} | custom-call | flops 1073741824 | bytes 4194304 | tf_op jit(solution)/shard_map/tile/pallas_call | solution.py:164
  31.1 2.4 %tile.6.refs_0_ = f32[2048,768]{1,0:T(8,128)S(1)} custom-call(s32[40]{0:T(128)S(1)} %get-tuple-element.50.codes_ref, s32[21]{0:T(128)S(1)} %get-tuple-element.51.starts_ref, bf16[40,128,128]{2,1,0:T(8,128)(2,1)S(1)} %get-tuple-element.52.blocks_ref, bf16[5,768,768]{2,1,0:T(8,128)(2,1)S(1)} %get-tuple-element.53.weight_ref, ...), custom_call_target="tpu_custom_call", output_to_operand_aliasing={{}: (5, {})} | custom-call | flops 1073741824 | bytes 4194304 | tf_op jit(solution)/shard_map/tile/pallas_call | solution.py:164
  33.5 2.7 %tile.7 = (f32[2048,768]{1,0:T(8,128)S(1)}, bf16[3,96,768]{2,1,0:T(8,128)(2,1)S(1)}, bf16[3,96,768]{2,1,0:T(8,128)(2,1)S(1)}, bf16[3,96,768]{2,1,0:T(8,128)(2,1)...) custom-call(s32[40]{0:T(128)S(1)} %get-tuple-element.50.codes_ref, ...), custom_call_target="tpu_custom_call", output_to_operand_aliasing={{0}: (5, {})} | custom-call | flops 1073741824 | bytes 4194304 | tf_op jit(solution)/shard_map/tile/pallas_call | solution.py:164
  36.4 4.6 %collective-permute-start.11 = (bf16[3,96,768]{2,1,0:T(8,128)(2,1)S(1)}, bf16[3,96,768]{2,1,0:T(8,128)(2,1)S(1)}, u32[]{:S(2)}, u32[]{:S(2)}) collective-permute-start(bf16[3,96,768]{2,1,0:T(8,128)(2,1)S(1)} %get-tuple-element.67), channel_id=1, source_target_pairs={{0,2},{1,3},{2,0},{3,1},{4,6},{5,7},{6,4},{7,5},{8,10},{9,11},{10,... | collective-permute-start | bytes 1327112 | tf_op jit(solution)/shard_map/ppermute | solution.py:20
  41.0 1.9 %collective-permute-start.12 = (bf16[3,96,768]{2,1,0:T(8,128)(2,1)S(1)}, bf16[3,96,768]{2,1,0:T(8,128)(2,1)S(1)}, u32[]{:S(2)}, u32[]{:S(2)}) collective-permute-start(bf16[3,96,768]{2,1,0:T(8,128)(2,1)S(1)} %get-tuple-element.68), channel_id=1, source_target_pairs={{0,1},{1,0},{2,3},{3,2},{4,5},{5,4},{6,7},{7,6},{8,9},{9,8},{10,11... | collective-permute-start | bytes 1327112 | tf_op jit(solution)/shard_map/ppermute | solution.py:20
  43.0 5.3 %collective-permute-done.9.refs_1_ = bf16[2,4,32,768]{3,2,1,0:T(8,128)(2,1)S(1)} collective-permute-done((bf16[2,4,32,768]{3,2,1,0:T(8,128)(2,1)S(1)}, bf16[2,4,32,768]{3,2,1,0:T(8,128)(2,1)S(1)}, u32[]{:S(2)}, u32[]{:S(2)}) %collective-permute-start.9) | collective-permute-done | bytes 393248 | tf_op jit(solution)/shard_map/ppermute | solution.py:20
  48.3 1.3 %collective-permute-start.10 = (bf16[4,32,768]{2,1,0:T(8,128)(2,1)S(1)}, bf16[4,32,768]{2,1,0:T(8,128)(2,1)S(1)}, u32[]{:S(2)}, u32[]{:S(2)}) collective-permute-start(bf16[4,32,768]{2,1,0:T(8,128)(2,1)S(1)} %get-tuple-element.61), channel_id=1, source_target_pairs={{0,8},{1,9},{2,10},{3,11},{4,12},{5,13},{6,14},{7,15},{8,0},{9,1},... | collective-permute-start | bytes 589832 | tf_op jit(solution)/shard_map/ppermute | solution.py:20
  49.9 10.1 %collective-permute-done.10.refs_1_ = bf16[4,32,768]{2,1,0:T(8,128)(2,1)S(1)} collective-permute-done((bf16[4,32,768]{2,1,0:T(8,128)(2,1)S(1)}, bf16[4,32,768]{2,1,0:T(8,128)(2,1)S(1)}, u32[]{:S(2)}, u32[]{:S(2)}) %collective-permute-start.10) | collective-permute-done | bytes 196640 | tf_op jit(solution)/shard_map/ppermute | solution.py:20
  60.1 2.0 %collective-permute-start.14 = (bf16[2,128,768]{2,1,0:T(8,128)(2,1)S(1)}, bf16[2,128,768]{2,1,0:T(8,128)(2,1)S(1)}, u32[]{:S(2)}, u32[]{:S(2)}) collective-permute-start(bf16[2,128,768]{2,1,0:T(8,128)(2,1)S(1)} %get-tuple-element.77), channel_id=1, source_target_pairs={{0,1},{1,0},{2,3},{3,2},{4,5},{5,4},{6,7},{7,6},{8,9},{9,8},{10,11... | collective-permute-start | bytes 1179656 | tf_op jit(solution)/shard_map/ppermute | solution.py:20
  62.6 2.1 %collective-permute-start.17 = (bf16[96,768]{1,0:T(8,128)(2,1)S(1)}, bf16[96,768]{1,0:T(8,128)(2,1)S(1)}, u32[]{:S(2)}, u32[]{:S(2)}) collective-permute-start(bf16[96,768]{1,0:T(8,128)(2,1)S(1)} %get-tuple-element.82), channel_id=1, source_target_pairs={{0,12},{1,13},{2,14},{3,15},{4,8},{5,9},{6,10},{7,11},{8,4},{9,5},... | collective-permute-start | bytes 442376 | tf_op jit(solution)/shard_map/ppermute | solution.py:20
  64.7 1.2 %collective-permute-start.18 = (bf16[96,768]{1,0:T(8,128)(2,1)S(1)}, bf16[96,768]{1,0:T(8,128)(2,1)S(1)}, u32[]{:S(2)}, u32[]{:S(2)}) collective-permute-start(bf16[96,768]{1,0:T(8,128)(2,1)S(1)} %get-tuple-element.76), channel_id=1, source_target_pairs={{0,4},{1,5},{2,6},{3,7},{4,0},{5,1},{6,2},{7,3},{8,12},{9,13},{10,... | collective-permute-start | bytes 442376 | tf_op jit(solution)/shard_map/ppermute | solution.py:20
  65.9 5.3 %collective-permute-done.14.refs_2_ = bf16[2,128,768]{2,1,0:T(8,128)(2,1)S(1)} collective-permute-done((bf16[2,128,768]{2,1,0:T(8,128)(2,1)S(1)}, bf16[2,128,768]{2,1,0:T(8,128)(2,1)S(1)}, u32[]{:S(2)}, u32[]{:S(2)}) %collective-permute-start.14) | collective-permute-done | bytes 393248 | tf_op jit(solution)/shard_map/ppermute | solution.py:20
  71.3 1.7 %collective-permute-start.15 = (bf16[128,768]{1,0:T(8,128)(2,1)S(1)}, bf16[128,768]{1,0:T(8,128)(2,1)S(1)}, u32[]{:S(2)}, u32[]{:S(2)}) collective-permute-start(bf16[128,768]{1,0:T(8,128)(2,1)S(1)} %get-tuple-element.80), channel_id=1, source_target_pairs={{0,3},{1,2},{2,1},{3,0},{4,7},{5,6},{6,5},{7,4},{8,11},{9,10},{10,... | collective-permute-start | bytes 589832 | tf_op jit(solution)/shard_map/ppermute | solution.py:20
  73.0 1.8 %collective-permute-done.16 = bf16[96,768]{1,0:T(8,128)(2,1)S(1)} collective-permute-done((bf16[96,768]{1,0:T(8,128)(2,1)S(1)}, bf16[96,768]{1,0:T(8,128)(2,1)S(1)}, u32[]{:S(2)}, u32[]{:S(2)}) %collective-permute-start.16) | collective-permute-done | bytes 147488 | tf_op jit(solution)/shard_map/ppermute | solution.py:20
  74.9 1.2 %collective-permute-done.18 = bf16[96,768]{1,0:T(8,128)(2,1)S(1)} collective-permute-done((bf16[96,768]{1,0:T(8,128)(2,1)S(1)}, bf16[96,768]{1,0:T(8,128)(2,1)S(1)}, u32[]{:S(2)}, u32[]{:S(2)}) %collective-permute-start.18) | collective-permute-done | bytes 147488 | tf_op jit(solution)/shard_map/ppermute | solution.py:20
  76.2 2.4 %collective-permute-done.15 = bf16[128,768]{1,0:T(8,128)(2,1)S(1)} collective-permute-done((bf16[128,768]{1,0:T(8,128)(2,1)S(1)}, bf16[128,768]{1,0:T(8,128)(2,1)S(1)}, u32[]{:S(2)}, u32[]{:S(2)}) %collective-permute-start.15) | collective-permute-done | bytes 196640 | tf_op jit(solution)/shard_map/ppermute | solution.py:20
  (56 shorter events, 7.1 us)
Async XLA Ops:
  0.0 49.6 %copy-start = (bf16[768,768]{1,0:T(8,128)(2,1)S(1)}, bf16[768,768]{1,0:T(8,128)(2,1)}, u32[]{:S(2)}) copy-start(bf16[768,768]{1,0:T(8,128)(2,1)} %param.9) | copy-start | bytes 3538948
  0.0 22.0 %copy-start.7 = (s32[1,1,5]{2,1,0:T(1,128)S(1)}, s32[1,1,5]{2,1,0:T(1,128)}, u32[]{:S(2)}) copy-start(s32[1,1,5]{2,1,0:T(1,128)} %param.15) | copy-start | bytes 64
  0.0 22.0 %copy-start.5 = (s32[1,1,5,8]{3,1,2,0:T(1,128)S(1)}, s32[1,1,5,8]{3,1,2,0:T(1,128)}, u32[]{:S(2)}) copy-start(s32[1,1,5,8]{3,1,2,0:T(1,128)} %param.13) | copy-start | bytes 484
  0.0 16.3 %collective-permute-start = (bf16[128,768]{1,0:T(8,128)(2,1)}, bf16[128,768]{1,0:T(8,128)(2,1)S(1)}, u32[]{:S(2)}, u32[]{:S(2)}) collective-permute-start(bf16[128,768]{1,0:T(8,128)(2,1)} %param.8), channel_id=1, source_target_pairs={{0,128},{16,144},{32,160},{48,176},{64,192},{80,208},{96,224},{112... | collective-permute-start | bytes 589832 | tf_op jit(solution)/shard_map/ppermute | solution.py:16
  7.3 12.4 %collective-permute-start.4 = (bf16[128,768]{1,0:T(8,128)(2,1)}, bf16[128,768]{1,0:T(8,128)(2,1)S(1)}, u32[]{:S(2)}, u32[]{:S(2)}) collective-permute-start(bf16[128,768]{1,0:T(8,128)(2,1)} %param.8), channel_id=1, source_target_pairs={{0,32},{16,48},{32,0},{48,16},{64,96},{80,112},{96,64},{112,80},{1... | collective-permute-start | bytes 589832 | tf_op jit(solution)/shard_map/ppermute | solution.py:16
  8.5 13.4 %collective-permute-start.6 = (bf16[128,768]{1,0:T(8,128)(2,1)}, bf16[128,768]{1,0:T(8,128)(2,1)S(1)}, u32[]{:S(2)}, u32[]{:S(2)}) collective-permute-start(bf16[128,768]{1,0:T(8,128)(2,1)} %param.8), channel_id=1, source_target_pairs={{0,96},{16,112},{32,64},{48,80},{64,32},{80,48},{96,0},{112,16},{1... | collective-permute-start | bytes 589832 | tf_op jit(solution)/shard_map/ppermute | solution.py:16
  8.5 12.0 %collective-permute-start.5 = (bf16[128,768]{1,0:T(8,128)(2,1)}, bf16[128,768]{1,0:T(8,128)(2,1)S(1)}, u32[]{:S(2)}, u32[]{:S(2)}) collective-permute-start(bf16[128,768]{1,0:T(8,128)(2,1)} %param.8), channel_id=1, source_target_pairs={{0,64},{16,80},{32,96},{48,112},{64,0},{80,16},{96,32},{112,48},{1... | collective-permute-start | bytes 589832 | tf_op jit(solution)/shard_map/ppermute | solution.py:16
  15.4 6.7 %copy-start.6 = (s32[1,1,5,8]{3,1,2,0:T(1,128)S(1)}, s32[1,1,5,8]{3,1,2,0:T(1,128)}, u32[]{:S(2)}) copy-start(s32[1,1,5,8]{3,1,2,0:T(1,128)} %param.14) | copy-start | bytes 484
  16.3 14.6 %collective-permute-start.3 = (bf16[128,768]{1,0:T(8,128)(2,1)S(1)}, bf16[128,768]{1,0:T(8,128)(2,1)S(1)}, u32[]{:S(2)}, u32[]{:S(2)}) collective-permute-start(bf16[128,768]{1,0:T(8,128)(2,1)S(1)} %collective-permute-done), channel_id=1, source_target_pairs={{0,96},{16,112},{32,64},{48,80},{64,32},{80,48},{96,0},{112,16},{1... | collective-permute-start | bytes 589832 | tf_op jit(solution)/shard_map/ppermute | solution.py:16
  16.9 11.1 %collective-permute-start.2 = (bf16[128,768]{1,0:T(8,128)(2,1)S(1)}, bf16[128,768]{1,0:T(8,128)(2,1)S(1)}, u32[]{:S(2)}, u32[]{:S(2)}) collective-permute-start(bf16[128,768]{1,0:T(8,128)(2,1)S(1)} %collective-permute-done), channel_id=1, source_target_pairs={{0,64},{16,80},{32,96},{48,112},{64,0},{80,16},{96,32},{112,48},{1... | collective-permute-start | bytes 589832 | tf_op jit(solution)/shard_map/ppermute | solution.py:16
  19.7 8.3 %collective-permute-start.1 = (bf16[128,768]{1,0:T(8,128)(2,1)S(1)}, bf16[128,768]{1,0:T(8,128)(2,1)S(1)}, u32[]{:S(2)}, u32[]{:S(2)}) collective-permute-start(bf16[128,768]{1,0:T(8,128)(2,1)S(1)} %collective-permute-done), channel_id=1, source_target_pairs={{0,32},{16,48},{32,0},{48,16},{64,96},{80,112},{96,64},{112,80},{1... | collective-permute-start | bytes 589832 | tf_op jit(solution)/shard_map/ppermute | solution.py:16
  21.9 6.1 %collective-permute-start.7 = (bf16[512,768]{1,0:T(8,128)(2,1)S(1)}, bf16[512,768]{1,0:T(8,128)(2,1)S(1)}, u32[]{:S(2)}, u32[]{:S(2)}) collective-permute-start(bf16[512,768]{1,0:T(8,128)(2,1)S(1)} %constant_dynamic-update-slice_fusion.group_ref), channel_id=1, source_target_pairs={{0,16},{16,0},{32,48},{48,32},{64,80},{80,64},{96,112},{112,96},{1... | collective-permute-start | bytes 2359304 | tf_op jit(solution)/shard_map/ppermute | solution.py:16
  31.0 2.5 %collective-permute-start.8 = (bf16[512,768]{1,0:T(8,128)(2,1)S(1)}, bf16[512,768]{1,0:T(8,128)(2,1)S(1)}, u32[]{:S(2)}, u32[]{:S(2)}) collective-permute-start(bf16[512,768]{1,0:T(8,128)(2,1)S(1)} %constant_dynamic-update-slice_fusion.4.group_ref), channel_id=1, source_target_pairs={{0,16},{16,0},{32,48},{48,32},{64,80},{80,64},{96,112},{112,96},{1... | collective-permute-start | bytes 2359304 | tf_op jit(solution)/shard_map/ppermute | solution.py:16
  36.3 42.4 %copy-start.4 = (f32[768]{0:T(1024)S(1)}, f32[768]{0:T(1024)}, u32[]{:S(2)}) copy-start(f32[768]{0:T(1024)} %param.11) | copy-start | bytes 9220
  36.3 11.9 %collective-permute-start.9 = (bf16[2,4,32,768]{3,2,1,0:T(8,128)(2,1)S(1)}, bf16[2,4,32,768]{3,2,1,0:T(8,128)(2,1)S(1)}, u32[]{:S(2)}, u32[]{:S(2)}) collective-permute-start(bf16[2,4,32,768]{3,2,1,0:T(8,128)(2,1)S(1)} %get-tuple-element.58), channel_id=1, source_target_pairs={{0,4},{1,5},{2,6},{3,7},{4,0},{5,1},{6,2},{7,3},{8,12},{9,13},{10,... | collective-permute-start | bytes 1179656 | tf_op jit(solution)/shard_map/ppermute | solution.py:20
  36.4 25.7 %collective-permute-start.11 = (bf16[3,96,768]{2,1,0:T(8,128)(2,1)S(1)}, bf16[3,96,768]{2,1,0:T(8,128)(2,1)S(1)}, u32[]{:S(2)}, u32[]{:S(2)}) collective-permute-start(bf16[3,96,768]{2,1,0:T(8,128)(2,1)S(1)} %get-tuple-element.67), channel_id=1, source_target_pairs={{0,2},{1,3},{2,0},{3,1},{4,6},{5,7},{6,4},{7,5},{8,10},{9,11},{10,... | collective-permute-start | bytes 1327112 | tf_op jit(solution)/shard_map/ppermute | solution.py:20
  41.0 21.1 %collective-permute-start.12 = (bf16[3,96,768]{2,1,0:T(8,128)(2,1)S(1)}, bf16[3,96,768]{2,1,0:T(8,128)(2,1)S(1)}, u32[]{:S(2)}, u32[]{:S(2)}) collective-permute-start(bf16[3,96,768]{2,1,0:T(8,128)(2,1)S(1)} %get-tuple-element.68), channel_id=1, source_target_pairs={{0,1},{1,0},{2,3},{3,2},{4,5},{5,4},{6,7},{7,6},{8,9},{9,8},{10,11... | collective-permute-start | bytes 1327112 | tf_op jit(solution)/shard_map/ppermute | solution.py:20
  42.9 19.1 %collective-permute-start.13 = (bf16[3,96,768]{2,1,0:T(8,128)(2,1)S(1)}, bf16[3,96,768]{2,1,0:T(8,128)(2,1)S(1)}, u32[]{:S(2)}, u32[]{:S(2)}) collective-permute-start(bf16[3,96,768]{2,1,0:T(8,128)(2,1)S(1)} %get-tuple-element.69), channel_id=1, source_target_pairs={{0,3},{1,2},{2,1},{3,0},{4,7},{5,6},{6,5},{7,4},{8,11},{9,10},{10,... | collective-permute-start | bytes 1327112 | tf_op jit(solution)/shard_map/ppermute | solution.py:20
  48.3 11.7 %collective-permute-start.10 = (bf16[4,32,768]{2,1,0:T(8,128)(2,1)S(1)}, bf16[4,32,768]{2,1,0:T(8,128)(2,1)S(1)}, u32[]{:S(2)}, u32[]{:S(2)}) collective-permute-start(bf16[4,32,768]{2,1,0:T(8,128)(2,1)S(1)} %get-tuple-element.61), channel_id=1, source_target_pairs={{0,8},{1,9},{2,10},{3,11},{4,12},{5,13},{6,14},{7,15},{8,0},{9,1},... | collective-permute-start | bytes 589832 | tf_op jit(solution)/shard_map/ppermute | solution.py:20
  60.1 11.1 %collective-permute-start.14 = (bf16[2,128,768]{2,1,0:T(8,128)(2,1)S(1)}, bf16[2,128,768]{2,1,0:T(8,128)(2,1)S(1)}, u32[]{:S(2)}, u32[]{:S(2)}) collective-permute-start(bf16[2,128,768]{2,1,0:T(8,128)(2,1)S(1)} %get-tuple-element.77), channel_id=1, source_target_pairs={{0,1},{1,0},{2,3},{3,2},{4,5},{5,4},{6,7},{7,6},{8,9},{9,8},{10,11... | collective-permute-start | bytes 1179656 | tf_op jit(solution)/shard_map/ppermute | solution.py:20
  62.3 12.6 %collective-permute-start.16 = (bf16[96,768]{1,0:T(8,128)(2,1)S(1)}, bf16[96,768]{1,0:T(8,128)(2,1)S(1)}, u32[]{:S(2)}, u32[]{:S(2)}) collective-permute-start(bf16[96,768]{1,0:T(8,128)(2,1)S(1)} %get-tuple-element.81), channel_id=1, source_target_pairs={{0,8},{1,9},{2,10},{3,11},{4,12},{5,13},{6,14},{7,15},{8,0},{9,1},... | collective-permute-start | bytes 442376 | tf_op jit(solution)/shard_map/ppermute | solution.py:20
  62.6 12.3 %collective-permute-start.17 = (bf16[96,768]{1,0:T(8,128)(2,1)S(1)}, bf16[96,768]{1,0:T(8,128)(2,1)S(1)}, u32[]{:S(2)}, u32[]{:S(2)}) collective-permute-start(bf16[96,768]{1,0:T(8,128)(2,1)S(1)} %get-tuple-element.82), channel_id=1, source_target_pairs={{0,12},{1,13},{2,14},{3,15},{4,8},{5,9},{6,10},{7,11},{8,4},{9,5},... | collective-permute-start | bytes 442376 | tf_op jit(solution)/shard_map/ppermute | solution.py:20
  64.7 11.4 %collective-permute-start.18 = (bf16[96,768]{1,0:T(8,128)(2,1)S(1)}, bf16[96,768]{1,0:T(8,128)(2,1)S(1)}, u32[]{:S(2)}, u32[]{:S(2)}) collective-permute-start(bf16[96,768]{1,0:T(8,128)(2,1)S(1)} %get-tuple-element.76), channel_id=1, source_target_pairs={{0,4},{1,5},{2,6},{3,7},{4,0},{5,1},{6,2},{7,3},{8,12},{9,13},{10,... | collective-permute-start | bytes 442376 | tf_op jit(solution)/shard_map/ppermute | solution.py:20
  71.3 7.3 %collective-permute-start.15 = (bf16[128,768]{1,0:T(8,128)(2,1)S(1)}, bf16[128,768]{1,0:T(8,128)(2,1)S(1)}, u32[]{:S(2)}, u32[]{:S(2)}) collective-permute-start(bf16[128,768]{1,0:T(8,128)(2,1)S(1)} %get-tuple-element.80), channel_id=1, source_target_pairs={{0,3},{1,2},{2,1},{3,0},{4,7},{5,6},{6,5},{7,4},{8,11},{9,10},{10,... | collective-permute-start | bytes 589832 | tf_op jit(solution)/shard_map/ppermute | solution.py:20
  (3 other events, 4.9 us)

commit v6 on v5

--- a/solution.py
+++ b/solution.py
@@ -98,7 +98,7 @@
         packed = table_ref[relation, slot]
         source = (packed >> 4 & 15) ^ row_me
         target = (packed & 15) ^ col_me
-        return packed >> 8, (source >> 3) * 2 + (source & 1), source >> 1 & 3, (target & 3) * 4 + (target >> 2)
+        return packed >> 8, (source >> 3) * 2 + (source & 1), (source >> 1 & 3) ^ (source >> 2 & 1), (target & 3) * 4 + (target >> 2)
 
     def per_slot(act):
         for relation in range(relations):
@@ -237,12 +237,12 @@
 
 def gather_groups(features, to_plan, blocks, weights):
     far = row_swap(features, 1, 0, 0)
-    near_parts = [features] + [row_swap(features, 0, d, 0) for d in (1, 2, 3)]
+    near_parts = [features] + [row_swap(features, 0, d, 0) for d in (1, 3, 2)]
     blocks, weights = load(blocks, weights)
     far, blocks, weights, to_plan = lax.optimization_barrier((far, blocks, weights, to_plan))
     tables = plan(*to_plan)
     stage = lambda index, value, total: tile_stage(index, tables, blocks, weights, value, total)
-    far_parts = [far] + [row_swap(far, 0, d, 0) for d in (1, 2, 3)]
+    far_parts = [far] + [row_swap(far, 0, d, 0) for d in (1, 3, 2)]
     near = jnp.concatenate(near_parts, axis=0)
     near_other = row_swap(near, 0, 0, 1)
     (total,) = stage(0, near, None)

time: 80.2 us -> 84.3 us (1.051)
  the two profiles are of different devices: /device:TPU:4 before, /device:TPU:24 now
where the time goes in v6:
time: 84.3 us; the launch traced here: 83.1 us
  waiting for transfers between devices  34.3 us (41%)
  starting transfers between devices  30.9 us (37%)
  Pallas kernels  11.8 us (14%)
  local copies, waits for them, and re-layouts  4.59 us (5%)
  other arithmetic  0.93 us (1%)
    ppermute x10, waiting for transfers between devices, col_swap(): lax.ppermute(value, 'col', [(at, at ^ dz * Y + dy) for at in range(16)])  26.6 us
    ppermute x9, starting transfers between devices, row_swap(): lax.ppermute(value, 'row', [(at, at ^ dz * 8 + dx * 2 + dc) for at in ran...  16.9 us
    ppermute x10, starting transfers between devices, col_swap(): lax.ppermute(value, 'col', [(at, at ^ dz * Y + dy) for at in range(16)])  14 us
    pallas_call x4, Pallas kernels, tile_stage(): pl.pallas_call(functools.partial(stage_kernel, group, first, last), out_s...  9.15 us
    ppermute x9, waiting for transfers between devices, row_swap(): lax.ppermute(value, 'row', [(at, at ^ dz * 8 + dx * 2 + dc) for at in ran...  7.61 us
    unnamed x22, local copies, waits for them, and re-layouts  4.55 us
    pallas_call x1, Pallas kernels, plan(): pl.pallas_call(plan_kernel, out_shape=[jax.ShapeDtypeStruct((many,), jnp....  1.69 us
  transfers between devices with their start and end apart: 19, of which 7 were waited for; matrix products, arithmetic and copies ran while one was open for 1% of the time, Pallas kernels for 12%

profile of v6, /device:TPU:24, one launch (start us, length us, event | category | flops | bytes accessed | tf_op | source)
XLA Modules:
  0.0 83.1 jit_solution(17337712768314467113)
XLA Ops:
  0.0 7.3 %collective-permute-start = (bf16[128,768]{1,0:T(8,128)(2,1)}, bf16[128,768]{1,0:T(8,128)(2,1)S(1)}, u32[]{:S(2)}, u32[]{:S(2)}) collective-permute-start(bf16[128,768]{1,0:T(8,128)(2,1)} %param.8), channel_id=1, source_target_pairs={{0,128},{16,144},{32,160},{48,176},{64,192},{80,208},{96,224},{112... | collective-permute-start | bytes 589832 | tf_op jit(solution)/shard_map/ppermute | solution.py:16
  7.3 1.5 %collective-permute-start.4 = (bf16[128,768]{1,0:T(8,128)(2,1)}, bf16[128,768]{1,0:T(8,128)(2,1)S(1)}, u32[]{:S(2)}, u32[]{:S(2)}) collective-permute-start(bf16[128,768]{1,0:T(8,128)(2,1)} %param.8), channel_id=1, source_target_pairs={{0,32},{16,48},{32,0},{48,16},{64,96},{80,112},{96,64},{112,80},{1... | collective-permute-start | bytes 589832 | tf_op jit(solution)/shard_map/ppermute | solution.py:16
  8.8 2.7 %collective-permute-start.6 = (bf16[128,768]{1,0:T(8,128)(2,1)}, bf16[128,768]{1,0:T(8,128)(2,1)S(1)}, u32[]{:S(2)}, u32[]{:S(2)}) collective-permute-start(bf16[128,768]{1,0:T(8,128)(2,1)} %param.8), channel_id=1, source_target_pairs={{0,64},{16,80},{32,96},{48,112},{64,0},{80,16},{96,32},{112,48},{1... | collective-permute-start | bytes 589832 | tf_op jit(solution)/shard_map/ppermute | solution.py:16
  12.0 2.7 %copy-done.1 = bf16[768,5,768]{2,0,1:T(8,128)(2,1)S(1)} copy-done((bf16[768,5,768]{2,0,1:T(8,128)(2,1)S(1)}, bf16[768,5,768]{2,0,1:T(8,128)(2,1)}, u32[]{:S(2)}) %copy-start.1) | copy-done | bytes 5898264
  14.7 1.3 %copy-done.2 = bf16[1,1,5,8,128,128]{5,4,3,2,1,0:T(8,128)(2,1)S(1)} copy-done((bf16[1,1,5,8,128,128]{5,4,3,2,1,0:T(8,128)(2,1)S(1)}, bf16[1,1,5,8,128,128]{5,4,3,2,1,0:T(8,128)(2,1)}, u32[]{:S(2)}) %copy-start.2) | copy-done | bytes 1310744
  16.9 1.9 %collective-permute-start.3 = (bf16[128,768]{1,0:T(8,128)(2,1)S(1)}, bf16[128,768]{1,0:T(8,128)(2,1)S(1)}, u32[]{:S(2)}, u32[]{:S(2)}) collective-permute-start(bf16[128,768]{1,0:T(8,128)(2,1)S(1)} %collective-permute-done), channel_id=1, source_target_pairs={{0,64},{16,80},{32,96},{48,112},{64,0},{80,16},{96,32},{112,48},{1... | collective-permute-start | bytes 589832 | tf_op jit(solution)/shard_map/ppermute | solution.py:16
  18.8 1.1 %collective-permute-start.2 = (bf16[128,768]{1,0:T(8,128)(2,1)S(1)}, bf16[128,768]{1,0:T(8,128)(2,1)S(1)}, u32[]{:S(2)}, u32[]{:S(2)}) collective-permute-start(bf16[128,768]{1,0:T(8,128)(2,1)S(1)} %collective-permute-done), channel_id=1, source_target_pairs={{0,96},{16,112},{32,64},{48,80},{64,32},{80,48},{96,0},{112,16},{1... | collective-permute-start | bytes 589832 | tf_op jit(solution)/shard_map/ppermute | solution.py:16
  20.7 7.6 %collective-permute-done.5 = bf16[128,768]{1,0:T(8,128)(2,1)S(1)} collective-permute-done((bf16[128,768]{1,0:T(8,128)(2,1)}, bf16[128,768]{1,0:T(8,128)(2,1)S(1)}, u32[]{:S(2)}, u32[]{:S(2)}) %collective-permute-start.5) | collective-permute-done | bytes 196640 | tf_op jit(solution)/shard_map/ppermute | solution.py:16
  28.5 1.7 %plan.1 = (s32[40]{0:T(128)S(1)}, s32[21]{0:T(128)S(1)}) custom-call(s32[5,8]{1,0:T(8,128)S(1)} %fusion.4.table_ref), custom_call_target="tpu_custom_call" | custom-call | tf_op jit(solution)/shard_map/plan/pallas_call | solution.py:137
  30.2 2.6 %tile.4.refs_0_ = f32[2048,768]{1,0:T(8,128)S(1)} custom-call(s32[40]{0:T(128)S(1)} %get-tuple-element.50.codes_ref, s32[21]{0:T(128)S(1)} %get-tuple-element.51.starts_ref, bf16[40,128,128]{2,1,0:T(8,128)(2,1)S(1)} %get-tuple-element.52.blocks_ref, bf16[5,768,768]{2,1,0:T(8,128)(2,1)S(1)} %get-tuple-element.53.weight_ref, ...), custom_call_target="tpu_custom_call" | custom-call | flops 1073741824 | bytes 4194304 | tf_op jit(solution)/shard_map/tile/pallas_call | solution.py:164
  32.9 2.4 %tile.5.refs_0_ = f32[2048,768]{1,0:T(8,128)S(1)} custom-call(s32[40]{0:T(128)S(1)} %get-tuple-element.50.codes_ref, s32[21]{0:T(128)S(1)} %get-tuple-element.51.starts_ref, bf16[40,128,128]{2,1,0:T(8,128)(2,1)S(1)} %get-tuple-element.52.blocks_ref, bf16[5,768,768]{2,1,0:T(8,128)(2,1)S(1)} %get-tuple-element.53.weight_ref, ...), custom_call_target="tpu_custom_call", output_to_operand_aliasing={{}: (5, {})} | custom-call | flops 1073741824 | bytes 4194304 | tf_op jit(solution)/shard_map/tile/pallas_call | solution.py:164
  35.4 1.1 %collective-permute-start.8 = (bf16[512,768]{1,0:T(8,128)(2,1)S(1)}, bf16[512,768]{1,0:T(8,128)(2,1)S(1)}, u32[]{:S(2)}, u32[]{:S(2)}) collective-permute-start(bf16[512,768]{1,0:T(8,128)(2,1)S(1)} %constant_dynamic-update-slice_fusion.4.group_ref), channel_id=1, source_target_pairs={{0,16},{16,0},{32,48},{48,32},{64,80},{80,64},{96,112},{112,96},{1... | collective-permute-start | bytes 2359304 | tf_op jit(solution)/shard_map/ppermute | solution.py:16
  36.5 1.9 %tile.6.refs_0_ = f32[2048,768]{1,0:T(8,128)S(1)} custom-call(s32[40]{0:T(128)S(1)} %get-tuple-element.50.codes_ref, s32[21]{0:T(128)S(1)} %get-tuple-element.51.starts_ref, bf16[40,128,128]{2,1,0:T(8,128)(2,1)S(1)} %get-tuple-element.52.blocks_ref, bf16[5,768,768]{2,1,0:T(8,128)(2,1)S(1)} %get-tuple-element.53.weight_ref, ...), custom_call_target="tpu_custom_call", output_to_operand_aliasing={{}: (5, {})} | custom-call | flops 1073741824 | bytes 4194304 | tf_op jit(solution)/shard_map/tile/pallas_call | solution.py:164
  38.5 2.2 %tile.7 = (f32[2048,768]{1,0:T(8,128)S(1)}, bf16[3,96,768]{2,1,0:T(8,128)(2,1)S(1)}, bf16[3,96,768]{2,1,0:T(8,128)(2,1)S(1)}, bf16[3,96,768]{2,1,0:T(8,128)(2,1)...) custom-call(s32[40]{0:T(128)S(1)} %get-tuple-element.50.codes_ref, ...), custom_call_target="tpu_custom_call", output_to_operand_aliasing={{0}: (5, {})} | custom-call | flops 1073741824 | bytes 4194304 | tf_op jit(solution)/shard_map/tile/pallas_call | solution.py:164
  40.7 2.1 %collective-permute-start.9 = (bf16[2,4,32,768]{3,2,1,0:T(8,128)(2,1)S(1)}, bf16[2,4,32,768]{3,2,1,0:T(8,128)(2,1)S(1)}, u32[]{:S(2)}, u32[]{:S(2)}) collective-permute-start(bf16[2,4,32,768]{3,2,1,0:T(8,128)(2,1)S(1)} %get-tuple-element.58), channel_id=1, source_target_pairs={{0,4},{1,5},{2,6},{3,7},{4,0},{5,1},{6,2},{7,3},{8,12},{9,13},{10,... | collective-permute-start | bytes 1179656 | tf_op jit(solution)/shard_map/ppermute | solution.py:20
  44.1 2.8 %collective-permute-start.13 = (bf16[3,96,768]{2,1,0:T(8,128)(2,1)S(1)}, bf16[3,96,768]{2,1,0:T(8,128)(2,1)S(1)}, u32[]{:S(2)}, u32[]{:S(2)}) collective-permute-start(bf16[3,96,768]{2,1,0:T(8,128)(2,1)S(1)} %get-tuple-element.69), channel_id=1, source_target_pairs={{0,3},{1,2},{2,1},{3,0},{4,7},{5,6},{6,5},{7,4},{8,11},{9,10},{10,... | collective-permute-start | bytes 1327112 | tf_op jit(solution)/shard_map/ppermute | solution.py:20
  46.9 5.8 %collective-permute-done.9.refs_1_ = bf16[2,4,32,768]{3,2,1,0:T(8,128)(2,1)S(1)} collective-permute-done((bf16[2,4,32,768]{3,2,1,0:T(8,128)(2,1)S(1)}, bf16[2,4,32,768]{3,2,1,0:T(8,128)(2,1)S(1)}, u32[]{:S(2)}, u32[]{:S(2)}) %collective-permute-start.9) | collective-permute-done | bytes 393248 | tf_op jit(solution)/shard_map/ppermute | solution.py:20
  52.8 2.9 %collective-permute-start.10 = (bf16[4,32,768]{2,1,0:T(8,128)(2,1)S(1)}, bf16[4,32,768]{2,1,0:T(8,128)(2,1)S(1)}, u32[]{:S(2)}, u32[]{:S(2)}) collective-permute-start(bf16[4,32,768]{2,1,0:T(8,128)(2,1)S(1)} %get-tuple-element.61), channel_id=1, source_target_pairs={{0,8},{1,9},{2,10},{3,11},{4,12},{5,13},{6,14},{7,15},{8,0},{9,1},... | collective-permute-start | bytes 589832 | tf_op jit(solution)/shard_map/ppermute | solution.py:20
  56.0 8.8 %collective-permute-done.10.refs_1_ = bf16[4,32,768]{2,1,0:T(8,128)(2,1)S(1)} collective-permute-done((bf16[4,32,768]{2,1,0:T(8,128)(2,1)S(1)}, bf16[4,32,768]{2,1,0:T(8,128)(2,1)S(1)}, u32[]{:S(2)}, u32[]{:S(2)}) %collective-permute-start.10) | collective-permute-done | bytes 196640 | tf_op jit(solution)/shard_map/ppermute | solution.py:20
  65.8 3.5 %collective-permute-start.16 = (bf16[96,768]{1,0:T(8,128)(2,1)S(1)}, bf16[96,768]{1,0:T(8,128)(2,1)S(1)}, u32[]{:S(2)}, u32[]{:S(2)}) collective-permute-start(bf16[96,768]{1,0:T(8,128)(2,1)S(1)} %get-tuple-element.81), channel_id=1, source_target_pairs={{0,8},{1,9},{2,10},{3,11},{4,12},{5,13},{6,14},{7,15},{8,0},{9,1},... | collective-permute-start | bytes 442376 | tf_op jit(solution)/shard_map/ppermute | solution.py:20
  69.9 5.2 %collective-permute-done.14.refs_2_ = bf16[2,128,768]{2,1,0:T(8,128)(2,1)S(1)} collective-permute-done((bf16[2,128,768]{2,1,0:T(8,128)(2,1)S(1)}, bf16[2,128,768]{2,1,0:T(8,128)(2,1)S(1)}, u32[]{:S(2)}, u32[]{:S(2)}) %collective-permute-start.14) | collective-permute-done | bytes 393248 | tf_op jit(solution)/shard_map/ppermute | solution.py:20
  75.4 4.2 %collective-permute-done.16 = bf16[96,768]{1,0:T(8,128)(2,1)S(1)} collective-permute-done((bf16[96,768]{1,0:T(8,128)(2,1)S(1)}, bf16[96,768]{1,0:T(8,128)(2,1)S(1)}, u32[]{:S(2)}, u32[]{:S(2)}) %collective-permute-start.16) | collective-permute-done | bytes 147488 | tf_op jit(solution)/shard_map/ppermute | solution.py:20
  79.6 1.4 %collective-permute-done.18 = bf16[96,768]{1,0:T(8,128)(2,1)S(1)} collective-permute-done((bf16[96,768]{1,0:T(8,128)(2,1)S(1)}, bf16[96,768]{1,0:T(8,128)(2,1)S(1)}, u32[]{:S(2)}, u32[]{:S(2)}) %collective-permute-start.18) | collective-permute-done | bytes 147488 | tf_op jit(solution)/shard_map/ppermute | solution.py:20
  81.0 1.2 %collective-permute-done.15 = bf16[128,768]{1,0:T(8,128)(2,1)S(1)} collective-permute-done((bf16[128,768]{1,0:T(8,128)(2,1)S(1)}, bf16[128,768]{1,0:T(8,128)(2,1)S(1)}, u32[]{:S(2)}, u32[]{:S(2)}) %collective-permute-start.15) | collective-permute-done | bytes 196640 | tf_op jit(solution)/shard_map/ppermute | solution.py:20
  (56 shorter events, 6.8 us)
Async XLA Ops:
  0.0 55.6 %copy-start = (bf16[768,768]{1,0:T(8,128)(2,1)S(1)}, bf16[768,768]{1,0:T(8,128)(2,1)}, u32[]{:S(2)}) copy-start(bf16[768,768]{1,0:T(8,128)(2,1)} %param.9) | copy-start | bytes 3538948
  0.0 28.4 %copy-start.7 = (s32[1,1,5]{2,1,0:T(1,128)S(1)}, s32[1,1,5]{2,1,0:T(1,128)}, u32[]{:S(2)}) copy-start(s32[1,1,5]{2,1,0:T(1,128)} %param.15) | copy-start | bytes 64
  0.0 28.4 %copy-start.5 = (s32[1,1,5,8]{3,1,2,0:T(1,128)S(1)}, s32[1,1,5,8]{3,1,2,0:T(1,128)}, u32[]{:S(2)}) copy-start(s32[1,1,5,8]{3,1,2,0:T(1,128)} %param.13) | copy-start | bytes 484
  0.0 16.9 %collective-permute-start = (bf16[128,768]{1,0:T(8,128)(2,1)}, bf16[128,768]{1,0:T(8,128)(2,1)S(1)}, u32[]{:S(2)}, u32[]{:S(2)}) collective-permute-start(bf16[128,768]{1,0:T(8,128)(2,1)} %param.8), channel_id=1, source_target_pairs={{0,128},{16,144},{32,160},{48,176},{64,192},{80,208},{96,224},{112... | collective-permute-start | bytes 589832 | tf_op jit(solution)/shard_map/ppermute | solution.py:16
  7.3 12.7 %collective-permute-start.4 = (bf16[128,768]{1,0:T(8,128)(2,1)}, bf16[128,768]{1,0:T(8,128)(2,1)S(1)}, u32[]{:S(2)}, u32[]{:S(2)}) collective-permute-start(bf16[128,768]{1,0:T(8,128)(2,1)} %param.8), channel_id=1, source_target_pairs={{0,32},{16,48},{32,0},{48,16},{64,96},{80,112},{96,64},{112,80},{1... | collective-permute-start | bytes 589832 | tf_op jit(solution)/shard_map/ppermute | solution.py:16
  8.8 19.5 %collective-permute-start.6 = (bf16[128,768]{1,0:T(8,128)(2,1)}, bf16[128,768]{1,0:T(8,128)(2,1)S(1)}, u32[]{:S(2)}, u32[]{:S(2)}) collective-permute-start(bf16[128,768]{1,0:T(8,128)(2,1)} %param.8), channel_id=1, source_target_pairs={{0,64},{16,80},{32,96},{48,112},{64,0},{80,16},{96,32},{112,48},{1... | collective-permute-start | bytes 589832 | tf_op jit(solution)/shard_map/ppermute | solution.py:16
  11.5 16.7 %collective-permute-start.5 = (bf16[128,768]{1,0:T(8,128)(2,1)}, bf16[128,768]{1,0:T(8,128)(2,1)S(1)}, u32[]{:S(2)}, u32[]{:S(2)}) collective-permute-start(bf16[128,768]{1,0:T(8,128)(2,1)} %param.8), channel_id=1, source_target_pairs={{0,96},{16,112},{32,64},{48,80},{64,32},{80,48},{96,0},{112,16},{1... | collective-permute-start | bytes 589832 | tf_op jit(solution)/shard_map/ppermute | solution.py:16
  16.0 12.5 %copy-start.6 = (s32[1,1,5,8]{3,1,2,0:T(1,128)S(1)}, s32[1,1,5,8]{3,1,2,0:T(1,128)}, u32[]{:S(2)}) copy-start(s32[1,1,5,8]{3,1,2,0:T(1,128)} %param.14) | copy-start | bytes 484
  16.9 18.4 %collective-permute-start.3 = (bf16[128,768]{1,0:T(8,128)(2,1)S(1)}, bf16[128,768]{1,0:T(8,128)(2,1)S(1)}, u32[]{:S(2)}, u32[]{:S(2)}) collective-permute-start(bf16[128,768]{1,0:T(8,128)(2,1)S(1)} %collective-permute-done), channel_id=1, source_target_pairs={{0,64},{16,80},{32,96},{48,112},{64,0},{80,16},{96,32},{112,48},{1... | collective-permute-start | bytes 589832 | tf_op jit(solution)/shard_map/ppermute | solution.py:16
  18.8 14.1 %collective-permute-start.2 = (bf16[128,768]{1,0:T(8,128)(2,1)S(1)}, bf16[128,768]{1,0:T(8,128)(2,1)S(1)}, u32[]{:S(2)}, u32[]{:S(2)}) collective-permute-start(bf16[128,768]{1,0:T(8,128)(2,1)S(1)} %collective-permute-done), channel_id=1, source_target_pairs={{0,96},{16,112},{32,64},{48,80},{64,32},{80,48},{96,0},{112,16},{1... | collective-permute-start | bytes 589832 | tf_op jit(solution)/shard_map/ppermute | solution.py:16
  20.0 12.9 %collective-permute-start.1 = (bf16[128,768]{1,0:T(8,128)(2,1)S(1)}, bf16[128,768]{1,0:T(8,128)(2,1)S(1)}, u32[]{:S(2)}, u32[]{:S(2)}) collective-permute-start(bf16[128,768]{1,0:T(8,128)(2,1)S(1)} %collective-permute-done), channel_id=1, source_target_pairs={{0,32},{16,48},{32,0},{48,16},{64,96},{80,112},{96,64},{112,80},{1... | collective-permute-start | bytes 589832 | tf_op jit(solution)/shard_map/ppermute | solution.py:16
  28.3 4.6 %collective-permute-start.7 = (bf16[512,768]{1,0:T(8,128)(2,1)S(1)}, bf16[512,768]{1,0:T(8,128)(2,1)S(1)}, u32[]{:S(2)}, u32[]{:S(2)}) collective-permute-start(bf16[512,768]{1,0:T(8,128)(2,1)S(1)} %constant_dynamic-update-slice_fusion.group_ref), channel_id=1, source_target_pairs={{0,16},{16,0},{32,48},{48,32},{64,80},{80,64},{96,112},{112,96},{1... | collective-permute-start | bytes 2359304 | tf_op jit(solution)/shard_map/ppermute | solution.py:16
  35.4 3.1 %collective-permute-start.8 = (bf16[512,768]{1,0:T(8,128)(2,1)S(1)}, bf16[512,768]{1,0:T(8,128)(2,1)S(1)}, u32[]{:S(2)}, u32[]{:S(2)}) collective-permute-start(bf16[512,768]{1,0:T(8,128)(2,1)S(1)} %constant_dynamic-update-slice_fusion.4.group_ref), channel_id=1, source_target_pairs={{0,16},{16,0},{32,48},{48,32},{64,80},{80,64},{96,112},{112,96},{1... | collective-permute-start | bytes 2359304 | tf_op jit(solution)/shard_map/ppermute | solution.py:16
  40.7 41.6 %copy-start.4 = (f32[768]{0:T(1024)S(1)}, f32[768]{0:T(1024)}, u32[]{:S(2)}) copy-start(f32[768]{0:T(1024)} %param.11) | copy-start | bytes 9220
  40.7 12.0 %collective-permute-start.9 = (bf16[2,4,32,768]{3,2,1,0:T(8,128)(2,1)S(1)}, bf16[2,4,32,768]{3,2,1,0:T(8,128)(2,1)S(1)}, u32[]{:S(2)}, u32[]{:S(2)}) collective-permute-start(bf16[2,4,32,768]{3,2,1,0:T(8,128)(2,1)S(1)} %get-tuple-element.58), channel_id=1, source_target_pairs={{0,4},{1,5},{2,6},{3,7},{4,0},{5,1},{6,2},{7,3},{8,12},{9,13},{10,... | collective-permute-start | bytes 1179656 | tf_op jit(solution)/shard_map/ppermute | solution.py:20
  42.8 22.8 %collective-permute-start.11 = (bf16[3,96,768]{2,1,0:T(8,128)(2,1)S(1)}, bf16[3,96,768]{2,1,0:T(8,128)(2,1)S(1)}, u32[]{:S(2)}, u32[]{:S(2)}) collective-permute-start(bf16[3,96,768]{2,1,0:T(8,128)(2,1)S(1)} %get-tuple-element.67), channel_id=1, source_target_pairs={{0,2},{1,3},{2,0},{3,1},{4,6},{5,7},{6,4},{7,5},{8,10},{9,11},{10,... | collective-permute-start | bytes 1327112 | tf_op jit(solution)/shard_map/ppermute | solution.py:20
  43.4 22.2 %collective-permute-start.12 = (bf16[3,96,768]{2,1,0:T(8,128)(2,1)S(1)}, bf16[3,96,768]{2,1,0:T(8,128)(2,1)S(1)}, u32[]{:S(2)}, u32[]{:S(2)}) collective-permute-start(bf16[3,96,768]{2,1,0:T(8,128)(2,1)S(1)} %get-tuple-element.68), channel_id=1, source_target_pairs={{0,1},{1,0},{2,3},{3,2},{4,5},{5,4},{6,7},{7,6},{8,9},{9,8},{10,11... | collective-permute-start | bytes 1327112 | tf_op jit(solution)/shard_map/ppermute | solution.py:20
  44.1 21.4 %collective-permute-start.13 = (bf16[3,96,768]{2,1,0:T(8,128)(2,1)S(1)}, bf16[3,96,768]{2,1,0:T(8,128)(2,1)S(1)}, u32[]{:S(2)}, u32[]{:S(2)}) collective-permute-start(bf16[3,96,768]{2,1,0:T(8,128)(2,1)S(1)} %get-tuple-element.69), channel_id=1, source_target_pairs={{0,3},{1,2},{2,1},{3,0},{4,7},{5,6},{6,5},{7,4},{8,11},{9,10},{10,... | collective-permute-start | bytes 1327112 | tf_op jit(solution)/shard_map/ppermute | solution.py:20
  52.8 12.0 %collective-permute-start.10 = (bf16[4,32,768]{2,1,0:T(8,128)(2,1)S(1)}, bf16[4,32,768]{2,1,0:T(8,128)(2,1)S(1)}, u32[]{:S(2)}, u32[]{:S(2)}) collective-permute-start(bf16[4,32,768]{2,1,0:T(8,128)(2,1)S(1)} %get-tuple-element.61), channel_id=1, source_target_pairs={{0,8},{1,9},{2,10},{3,11},{4,12},{5,13},{6,14},{7,15},{8,0},{9,1},... | collective-permute-start | bytes 589832 | tf_op jit(solution)/shard_map/ppermute | solution.py:20
  64.9 10.3 %collective-permute-start.14 = (bf16[2,128,768]{2,1,0:T(8,128)(2,1)S(1)}, bf16[2,128,768]{2,1,0:T(8,128)(2,1)S(1)}, u32[]{:S(2)}, u32[]{:S(2)}) collective-permute-start(bf16[2,128,768]{2,1,0:T(8,128)(2,1)S(1)} %get-tuple-element.77), channel_id=1, source_target_pairs={{0,1},{1,0},{2,3},{3,2},{4,5},{5,4},{6,7},{7,6},{8,9},{9,8},{10,11... | collective-permute-start | bytes 1179656 | tf_op jit(solution)/shard_map/ppermute | solution.py:20
  65.8 13.8 %collective-permute-start.16 = (bf16[96,768]{1,0:T(8,128)(2,1)S(1)}, bf16[96,768]{1,0:T(8,128)(2,1)S(1)}, u32[]{:S(2)}, u32[]{:S(2)}) collective-permute-start(bf16[96,768]{1,0:T(8,128)(2,1)S(1)} %get-tuple-element.81), channel_id=1, source_target_pairs={{0,8},{1,9},{2,10},{3,11},{4,12},{5,13},{6,14},{7,15},{8,0},{9,1},... | collective-permute-start | bytes 442376 | tf_op jit(solution)/shard_map/ppermute | solution.py:20
  69.3 10.3 %collective-permute-start.17 = (bf16[96,768]{1,0:T(8,128)(2,1)S(1)}, bf16[96,768]{1,0:T(8,128)(2,1)S(1)}, u32[]{:S(2)}, u32[]{:S(2)}) collective-permute-start(bf16[96,768]{1,0:T(8,128)(2,1)S(1)} %get-tuple-element.82), channel_id=1, source_target_pairs={{0,12},{1,13},{2,14},{3,15},{4,8},{5,9},{6,10},{7,11},{8,4},{9,5},... | collective-permute-start | bytes 442376 | tf_op jit(solution)/shard_map/ppermute | solution.py:20
  69.3 11.7 %collective-permute-start.18 = (bf16[96,768]{1,0:T(8,128)(2,1)S(1)}, bf16[96,768]{1,0:T(8,128)(2,1)S(1)}, u32[]{:S(2)}, u32[]{:S(2)}) collective-permute-start(bf16[96,768]{1,0:T(8,128)(2,1)S(1)} %get-tuple-element.76), channel_id=1, source_target_pairs={{0,4},{1,5},{2,6},{3,7},{4,0},{5,1},{6,2},{7,3},{8,12},{9,13},{10,... | collective-permute-start | bytes 442376 | tf_op jit(solution)/shard_map/ppermute | solution.py:20
  75.3 7.0 %collective-permute-start.15 = (bf16[128,768]{1,0:T(8,128)(2,1)S(1)}, bf16[128,768]{1,0:T(8,128)(2,1)S(1)}, u32[]{:S(2)}, u32[]{:S(2)}) collective-permute-start(bf16[128,768]{1,0:T(8,128)(2,1)S(1)} %get-tuple-element.80), channel_id=1, source_target_pairs={{0,3},{1,2},{2,1},{3,0},{4,7},{5,6},{6,5},{7,4},{8,11},{9,10},{10,... | collective-permute-start | bytes 589832 | tf_op jit(solution)/shard_map/ppermute | solution.py:20
  (3 other events, 4.9 us)

commit v7 on v5

--- a/solution.py
+++ b/solution.py
@@ -259,7 +259,7 @@
     f32, bf16 = jnp.float32, jnp.bfloat16
     width = own.shape[-1]
     z_near = col_swap(z_there, 1, 0)
-    y_in = [col_swap(y_parts[d], 0, d) for d in (2, 1, 3)]
+    y_in = [col_swap(y_parts[d], 0, d) for d in (1, 3, 2)]
     piece = z_here.shape[1:]
     shapes = [jax.ShapeDtypeStruct(piece, f32), jax.ShapeDtypeStruct(piece, bf16)]
     z_kept, z_send = small(merge_z_near, shapes, z_here, z_near)

time: 80.2 us -> 80.6 us (level)
  starting transfers between devices: 30.9 us -> 36.1 us
  Pallas kernels: 11.7 us -> 9.1 us
  waiting for transfers between devices: 30.6 us -> 28.1 us
    ppermute x10, starting transfers between devices: 15.2 us -> 20.4 us  [col_swap(): lax.ppermute(value, 'col', [(at, at ^ dz * Y + dy) for at in range(16)])]
    ppermute x10, waiting for transfers between devices: 26.2 us -> 23.4 us  [col_swap(): lax.ppermute(value, 'col', [(at, at ^ dz * Y + dy) for at in range(16)])]
    pallas_call x4, Pallas kernels: 9.11 us -> 6.68 us  [tile_stage(): pl.pallas_call(functools.partial(stage_kernel, group, first, last), out_s...]
  transfers between devices with their start and end apart: 19 -> 19, of which waited for: 8 -> 11; matrix products, arithmetic and copies ran while one was open for 1% -> 1% of each run, Pallas kernels for 11% -> 9%
where the time goes in v7:
time: 80.6 us; the launch traced here: 79.4 us
  starting transfers between devices  36.1 us (45%)
  waiting for transfers between devices  28.1 us (35%)
  Pallas kernels  9.1 us (11%)
  local copies, waits for them, and re-layouts  4.59 us (6%)
  other arithmetic  0.93 us (1%)
    ppermute x10, waiting for transfers between devices, col_swap(): lax.ppermute(value, 'col', [(at, at ^ dz * Y + dy) for at in range(16)])  23.4 us
    ppermute x10, starting transfers between devices, col_swap(): lax.ppermute(value, 'col', [(at, at ^ dz * Y + dy) for at in range(16)])  20.4 us
    ppermute x9, starting transfers between devices, row_swap(): lax.ppermute(value, 'row', [(at, at ^ dz * 8 + dx * 2 + dc) for at in ran...  15.7 us
    pallas_call x4, Pallas kernels, tile_stage(): pl.pallas_call(functools.partial(stage_kernel, group, first, last), out_s...  6.68 us
    ppermute x9, waiting for transfers between devices, row_swap(): lax.ppermute(value, 'row', [(at, at ^ dz * 8 + dx * 2 + dc) for at in ran...  4.67 us
    unnamed x22, local copies, waits for them, and re-layouts  4.55 us
  transfers between devices with their start and end apart: 19, of which 11 were waited for; matrix products, arithmetic and copies ran while one was open for 1% of the time, Pallas kernels for 9%

profile of v7, /device:TPU:4, one launch (start us, length us, event | category | flops | bytes accessed | tf_op | source)
XLA Modules:
  0.0 79.4 jit_solution(2787073583485909448)
XLA Ops:
  0.0 7.3 %collective-permute-start = (bf16[128,768]{1,0:T(8,128)(2,1)}, bf16[128,768]{1,0:T(8,128)(2,1)S(1)}, u32[]{:S(2)}, u32[]{:S(2)}) collective-permute-start(bf16[128,768]{1,0:T(8,128)(2,1)} %param.8), channel_id=1, source_target_pairs={{0,128},{16,144},{32,160},{48,176},{64,192},{80,208},{96,224},{112... | collective-permute-start | bytes 589832 | tf_op jit(solution)/shard_map/ppermute | solution.py:16
  8.5 2.9 %collective-permute-start.5 = (bf16[128,768]{1,0:T(8,128)(2,1)}, bf16[128,768]{1,0:T(8,128)(2,1)S(1)}, u32[]{:S(2)}, u32[]{:S(2)}) collective-permute-start(bf16[128,768]{1,0:T(8,128)(2,1)} %param.8), channel_id=1, source_target_pairs={{0,64},{16,80},{32,96},{48,112},{64,0},{80,16},{96,32},{112,48},{1... | collective-permute-start | bytes 589832 | tf_op jit(solution)/shard_map/ppermute | solution.py:16
  11.4 2.7 %copy-done.1 = bf16[768,5,768]{2,0,1:T(8,128)(2,1)S(1)} copy-done((bf16[768,5,768]{2,0,1:T(8,128)(2,1)S(1)}, bf16[768,5,768]{2,0,1:T(8,128)(2,1)}, u32[]{:S(2)}) %copy-start.1) | copy-done | bytes 5898264
  14.1 1.3 %copy-done.2 = bf16[1,1,5,8,128,128]{5,4,3,2,1,0:T(8,128)(2,1)S(1)} copy-done((bf16[1,1,5,8,128,128]{5,4,3,2,1,0:T(8,128)(2,1)S(1)}, bf16[1,1,5,8,128,128]{5,4,3,2,1,0:T(8,128)(2,1)}, u32[]{:S(2)}) %copy-start.2) | copy-done | bytes 1310744
  16.9 2.7 %collective-permute-start.2 = (bf16[128,768]{1,0:T(8,128)(2,1)S(1)}, bf16[128,768]{1,0:T(8,128)(2,1)S(1)}, u32[]{:S(2)}, u32[]{:S(2)}) collective-permute-start(bf16[128,768]{1,0:T(8,128)(2,1)S(1)} %collective-permute-done), channel_id=1, source_target_pairs={{0,64},{16,80},{32,96},{48,112},{64,0},{80,16},{96,32},{112,48},{1... | collective-permute-start | bytes 589832 | tf_op jit(solution)/shard_map/ppermute | solution.py:16
  20.6 1.3 %collective-permute-done.6 = bf16[128,768]{1,0:T(8,128)(2,1)S(1)} collective-permute-done((bf16[128,768]{1,0:T(8,128)(2,1)}, bf16[128,768]{1,0:T(8,128)(2,1)S(1)}, u32[]{:S(2)}, u32[]{:S(2)}) %collective-permute-start.6) | collective-permute-done | bytes 196640 | tf_op jit(solution)/shard_map/ppermute | solution.py:16
  22.1 1.5 %plan.1 = (s32[40]{0:T(128)S(1)}, s32[21]{0:T(128)S(1)}) custom-call(s32[5,8]{1,0:T(8,128)S(1)} %fusion.4.table_ref), custom_call_target="tpu_custom_call" | custom-call | tf_op jit(solution)/shard_map/plan/pallas_call | solution.py:137
  23.6 2.4 %tile.4.refs_0_ = f32[2048,768]{1,0:T(8,128)S(1)} custom-call(s32[40]{0:T(128)S(1)} %get-tuple-element.50.codes_ref, s32[21]{0:T(128)S(1)} %get-tuple-element.51.starts_ref, bf16[40,128,128]{2,1,0:T(8,128)(2,1)S(1)} %get-tuple-element.52.blocks_ref, bf16[5,768,768]{2,1,0:T(8,128)(2,1)S(1)} %get-tuple-element.53.weight_ref, ...), custom_call_target="tpu_custom_call" | custom-call | flops 1073741824 | bytes 4194304 | tf_op jit(solution)/shard_map/tile/pallas_call | solution.py:164
  26.1 1.9 %collective-permute-done.1 = bf16[128,768]{1,0:T(8,128)(2,1)S(1)} collective-permute-done((bf16[128,768]{1,0:T(8,128)(2,1)S(1)}, bf16[128,768]{1,0:T(8,128)(2,1)S(1)}, u32[]{:S(2)}, u32[]{:S(2)}) %collective-permute-start.1) | collective-permute-done | bytes 196640 | tf_op jit(solution)/shard_map/ppermute | solution.py:16
  28.0 1.4 %tile.5.refs_0_ = f32[2048,768]{1,0:T(8,128)S(1)} custom-call(s32[40]{0:T(128)S(1)} %get-tuple-element.50.codes_ref, s32[21]{0:T(128)S(1)} %get-tuple-element.51.starts_ref, bf16[40,128,128]{2,1,0:T(8,128)(2,1)S(1)} %get-tuple-element.52.blocks_ref, bf16[5,768,768]{2,1,0:T(8,128)(2,1)S(1)} %get-tuple-element.53.weight_ref, ...), custom_call_target="tpu_custom_call", output_to_operand_aliasing={{}: (5, {})} | custom-call | flops 1073741824 | bytes 4194304 | tf_op jit(solution)/shard_map/tile/pallas_call | solution.py:164
  30.4 1.4 %collective-permute-done.8.group_ref = bf16[512,768]{1,0:T(8,128)(2,1)S(1)} collective-permute-done((bf16[512,768]{1,0:T(8,128)(2,1)S(1)}, bf16[512,768]{1,0:T(8,128)(2,1)S(1)}, u32[]{:S(2)}, u32[]{:S(2)}) %collective-permute-start.8) | collective-permute-done | bytes 786464 | tf_op jit(solution)/shard_map/ppermute | solution.py:16
  31.8 2.0 %tile.7 = (f32[2048,768]{1,0:T(8,128)S(1)}, bf16[3,96,768]{2,1,0:T(8,128)(2,1)S(1)}, bf16[3,96,768]{2,1,0:T(8,128)(2,1)S(1)}, bf16[3,96,768]{2,1,0:T(8,128)(2,1)...) custom-call(s32[40]{0:T(128)S(1)} %get-tuple-element.50.codes_ref, ...), custom_call_target="tpu_custom_call", output_to_operand_aliasing={{0}: (5, {})} | custom-call | flops 1073741824 | bytes 4194304 | tf_op jit(solution)/shard_map/tile/pallas_call | solution.py:164
  33.9 3.1 %collective-permute-start.9 = (bf16[2,4,32,768]{3,2,1,0:T(8,128)(2,1)S(1)}, bf16[2,4,32,768]{3,2,1,0:T(8,128)(2,1)S(1)}, u32[]{:S(2)}, u32[]{:S(2)}) collective-permute-start(bf16[2,4,32,768]{3,2,1,0:T(8,128)(2,1)S(1)} %get-tuple-element.58), channel_id=1, source_target_pairs={{0,4},{1,5},{2,6},{3,7},{4,0},{5,1},{6,2},{7,3},{8,12},{9,13},{10,... | collective-permute-start | bytes 1179656 | tf_op jit(solution)/shard_map/ppermute | solution.py:20
  37.0 1.9 %collective-permute-start.11 = (bf16[3,96,768]{2,1,0:T(8,128)(2,1)S(1)}, bf16[3,96,768]{2,1,0:T(8,128)(2,1)S(1)}, u32[]{:S(2)}, u32[]{:S(2)}) collective-permute-start(bf16[3,96,768]{2,1,0:T(8,128)(2,1)S(1)} %get-tuple-element.67), channel_id=1, source_target_pairs={{0,1},{1,0},{2,3},{3,2},{4,5},{5,4},{6,7},{7,6},{8,9},{9,8},{10,11... | collective-permute-start | bytes 1327112 | tf_op jit(solution)/shard_map/ppermute | solution.py:20
  39.0 3.3 %collective-permute-start.12 = (bf16[3,96,768]{2,1,0:T(8,128)(2,1)S(1)}, bf16[3,96,768]{2,1,0:T(8,128)(2,1)S(1)}, u32[]{:S(2)}, u32[]{:S(2)}) collective-permute-start(bf16[3,96,768]{2,1,0:T(8,128)(2,1)S(1)} %get-tuple-element.68), channel_id=1, source_target_pairs={{0,3},{1,2},{2,1},{3,0},{4,7},{5,6},{6,5},{7,4},{8,11},{9,10},{10,... | collective-permute-start | bytes 1327112 | tf_op jit(solution)/shard_map/ppermute | solution.py:20
  42.9 4.1 %collective-permute-done.9.refs_1_ = bf16[2,4,32,768]{3,2,1,0:T(8,128)(2,1)S(1)} collective-permute-done((bf16[2,4,32,768]{3,2,1,0:T(8,128)(2,1)S(1)}, bf16[2,4,32,768]{3,2,1,0:T(8,128)(2,1)S(1)}, u32[]{:S(2)}, u32[]{:S(2)}) %collective-permute-start.9) | collective-permute-done | bytes 393248 | tf_op jit(solution)/shard_map/ppermute | solution.py:20
  47.1 1.7 %collective-permute-start.10 = (bf16[4,32,768]{2,1,0:T(8,128)(2,1)S(1)}, bf16[4,32,768]{2,1,0:T(8,128)(2,1)S(1)}, u32[]{:S(2)}, u32[]{:S(2)}) collective-permute-start(bf16[4,32,768]{2,1,0:T(8,128)(2,1)S(1)} %get-tuple-element.61), channel_id=1, source_target_pairs={{0,8},{1,9},{2,10},{3,11},{4,12},{5,13},{6,14},{7,15},{8,0},{9,1},... | collective-permute-start | bytes 589832 | tf_op jit(solution)/shard_map/ppermute | solution.py:20
  49.1 9.4 %collective-permute-done.10.refs_1_ = bf16[4,32,768]{2,1,0:T(8,128)(2,1)S(1)} collective-permute-done((bf16[4,32,768]{2,1,0:T(8,128)(2,1)S(1)}, bf16[4,32,768]{2,1,0:T(8,128)(2,1)S(1)}, u32[]{:S(2)}, u32[]{:S(2)}) %collective-permute-start.10) | collective-permute-done | bytes 196640 | tf_op jit(solution)/shard_map/ppermute | solution.py:20
  58.6 1.7 %collective-permute-start.14 = (bf16[2,128,768]{2,1,0:T(8,128)(2,1)S(1)}, bf16[2,128,768]{2,1,0:T(8,128)(2,1)S(1)}, u32[]{:S(2)}, u32[]{:S(2)}) collective-permute-start(bf16[2,128,768]{2,1,0:T(8,128)(2,1)S(1)} %get-tuple-element.77), channel_id=1, source_target_pairs={{0,1},{1,0},{2,3},{3,2},{4,5},{5,4},{6,7},{7,6},{8,9},{9,8},{10,11... | collective-permute-start | bytes 1179656 | tf_op jit(solution)/shard_map/ppermute | solution.py:20
  60.4 1.9 %collective-permute-done.13.refs_3_ = bf16[3,96,768]{2,1,0:T(8,128)(2,1)S(1)} collective-permute-done((bf16[3,96,768]{2,1,0:T(8,128)(2,1)S(1)}, bf16[3,96,768]{2,1,0:T(8,128)(2,1)S(1)}, u32[]{:S(2)}, u32[]{:S(2)}) %collective-permute-start.13) | collective-permute-done | bytes 442400 | tf_op jit(solution)/shard_map/ppermute | solution.py:20
  62.6 1.6 %collective-permute-start.16 = (bf16[96,768]{1,0:T(8,128)(2,1)S(1)}, bf16[96,768]{1,0:T(8,128)(2,1)S(1)}, u32[]{:S(2)}, u32[]{:S(2)}) collective-permute-start(bf16[96,768]{1,0:T(8,128)(2,1)S(1)} %get-tuple-element.81), channel_id=1, source_target_pairs={{0,8},{1,9},{2,10},{3,11},{4,12},{5,13},{6,14},{7,15},{8,0},{9,1},... | collective-permute-start | bytes 442376 | tf_op jit(solution)/shard_map/ppermute | solution.py:20
  66.1 3.6 %collective-permute-done.14.refs_2_ = bf16[2,128,768]{2,1,0:T(8,128)(2,1)S(1)} collective-permute-done((bf16[2,128,768]{2,1,0:T(8,128)(2,1)S(1)}, bf16[2,128,768]{2,1,0:T(8,128)(2,1)S(1)}, u32[]{:S(2)}, u32[]{:S(2)}) %collective-permute-start.14) | collective-permute-done | bytes 393248 | tf_op jit(solution)/shard_map/ppermute | solution.py:20
  69.8 4.4 %collective-permute-start.15 = (bf16[128,768]{1,0:T(8,128)(2,1)S(1)}, bf16[128,768]{1,0:T(8,128)(2,1)S(1)}, u32[]{:S(2)}, u32[]{:S(2)}) collective-permute-start(bf16[128,768]{1,0:T(8,128)(2,1)S(1)} %get-tuple-element.80), channel_id=1, source_target_pairs={{0,3},{1,2},{2,1},{3,0},{4,7},{5,6},{6,5},{7,4},{8,11},{9,10},{10,... | collective-permute-start | bytes 589832 | tf_op jit(solution)/shard_map/ppermute | solution.py:20
  76.1 2.4 %collective-permute-done.15 = bf16[128,768]{1,0:T(8,128)(2,1)S(1)} collective-permute-done((bf16[128,768]{1,0:T(8,128)(2,1)S(1)}, bf16[128,768]{1,0:T(8,128)(2,1)S(1)}, u32[]{:S(2)}, u32[]{:S(2)}) %collective-permute-start.15) | collective-permute-done | bytes 196640 | tf_op jit(solution)/shard_map/ppermute | solution.py:20
  (56 shorter events, 11.2 us)
Async XLA Ops:
  0.0 48.7 %copy-start = (bf16[768,768]{1,0:T(8,128)(2,1)S(1)}, bf16[768,768]{1,0:T(8,128)(2,1)}, u32[]{:S(2)}) copy-start(bf16[768,768]{1,0:T(8,128)(2,1)} %param.9) | copy-start | bytes 3538948
  0.0 22.0 %copy-start.7 = (s32[1,1,5]{2,1,0:T(1,128)S(1)}, s32[1,1,5]{2,1,0:T(1,128)}, u32[]{:S(2)}) copy-start(s32[1,1,5]{2,1,0:T(1,128)} %param.15) | copy-start | bytes 64
  0.0 22.0 %copy-start.5 = (s32[1,1,5,8]{3,1,2,0:T(1,128)S(1)}, s32[1,1,5,8]{3,1,2,0:T(1,128)}, u32[]{:S(2)}) copy-start(s32[1,1,5,8]{3,1,2,0:T(1,128)} %param.13) | copy-start | bytes 484
  0.0 16.3 %collective-permute-start = (bf16[128,768]{1,0:T(8,128)(2,1)}, bf16[128,768]{1,0:T(8,128)(2,1)S(1)}, u32[]{:S(2)}, u32[]{:S(2)}) collective-permute-start(bf16[128,768]{1,0:T(8,128)(2,1)} %param.8), channel_id=1, source_target_pairs={{0,128},{16,144},{32,160},{48,176},{64,192},{80,208},{96,224},{112... | collective-permute-start | bytes 589832 | tf_op jit(solution)/shard_map/ppermute | solution.py:16
  7.3 12.4 %collective-permute-start.4 = (bf16[128,768]{1,0:T(8,128)(2,1)}, bf16[128,768]{1,0:T(8,128)(2,1)S(1)}, u32[]{:S(2)}, u32[]{:S(2)}) collective-permute-start(bf16[128,768]{1,0:T(8,128)(2,1)} %param.8), channel_id=1, source_target_pairs={{0,32},{16,48},{32,0},{48,16},{64,96},{80,112},{96,64},{112,80},{1... | collective-permute-start | bytes 589832 | tf_op jit(solution)/shard_map/ppermute | solution.py:16
  8.5 13.4 %collective-permute-start.6 = (bf16[128,768]{1,0:T(8,128)(2,1)}, bf16[128,768]{1,0:T(8,128)(2,1)S(1)}, u32[]{:S(2)}, u32[]{:S(2)}) collective-permute-start(bf16[128,768]{1,0:T(8,128)(2,1)} %param.8), channel_id=1, source_target_pairs={{0,96},{16,112},{32,64},{48,80},{64,32},{80,48},{96,0},{112,16},{1... | collective-permute-start | bytes 589832 | tf_op jit(solution)/shard_map/ppermute | solution.py:16
  8.5 12.0 %collective-permute-start.5 = (bf16[128,768]{1,0:T(8,128)(2,1)}, bf16[128,768]{1,0:T(8,128)(2,1)S(1)}, u32[]{:S(2)}, u32[]{:S(2)}) collective-permute-start(bf16[128,768]{1,0:T(8,128)(2,1)} %param.8), channel_id=1, source_target_pairs={{0,64},{16,80},{32,96},{48,112},{64,0},{80,16},{96,32},{112,48},{1... | collective-permute-start | bytes 589832 | tf_op jit(solution)/shard_map/ppermute | solution.py:16
  15.4 6.7 %copy-start.6 = (s32[1,1,5,8]{3,1,2,0:T(1,128)S(1)}, s32[1,1,5,8]{3,1,2,0:T(1,128)}, u32[]{:S(2)}) copy-start(s32[1,1,5,8]{3,1,2,0:T(1,128)} %param.14) | copy-start | bytes 484
  16.3 13.1 %collective-permute-start.3 = (bf16[128,768]{1,0:T(8,128)(2,1)S(1)}, bf16[128,768]{1,0:T(8,128)(2,1)S(1)}, u32[]{:S(2)}, u32[]{:S(2)}) collective-permute-start(bf16[128,768]{1,0:T(8,128)(2,1)S(1)} %collective-permute-done), channel_id=1, source_target_pairs={{0,96},{16,112},{32,64},{48,80},{64,32},{80,48},{96,0},{112,16},{1... | collective-permute-start | bytes 589832 | tf_op jit(solution)/shard_map/ppermute | solution.py:16
  16.9 11.1 %collective-permute-start.2 = (bf16[128,768]{1,0:T(8,128)(2,1)S(1)}, bf16[128,768]{1,0:T(8,128)(2,1)S(1)}, u32[]{:S(2)}, u32[]{:S(2)}) collective-permute-start(bf16[128,768]{1,0:T(8,128)(2,1)S(1)} %collective-permute-done), channel_id=1, source_target_pairs={{0,64},{16,80},{32,96},{48,112},{64,0},{80,16},{96,32},{112,48},{1... | collective-permute-start | bytes 589832 | tf_op jit(solution)/shard_map/ppermute | solution.py:16
  19.7 8.3 %collective-permute-start.1 = (bf16[128,768]{1,0:T(8,128)(2,1)S(1)}, bf16[128,768]{1,0:T(8,128)(2,1)S(1)}, u32[]{:S(2)}, u32[]{:S(2)}) collective-permute-start(bf16[128,768]{1,0:T(8,128)(2,1)S(1)} %collective-permute-done), channel_id=1, source_target_pairs={{0,32},{16,48},{32,0},{48,16},{64,96},{80,112},{96,64},{112,80},{1... | collective-permute-start | bytes 589832 | tf_op jit(solution)/shard_map/ppermute | solution.py:16
  21.9 6.1 %collective-permute-start.7 = (bf16[512,768]{1,0:T(8,128)(2,1)S(1)}, bf16[512,768]{1,0:T(8,128)(2,1)S(1)}, u32[]{:S(2)}, u32[]{:S(2)}) collective-permute-start(bf16[512,768]{1,0:T(8,128)(2,1)S(1)} %constant_dynamic-update-slice_fusion.group_ref), channel_id=1, source_target_pairs={{0,16},{16,0},{32,48},{48,32},{64,80},{80,64},{96,112},{112,96},{1... | collective-permute-start | bytes 2359304 | tf_op jit(solution)/shard_map/ppermute | solution.py:16
  29.5 2.4 %collective-permute-start.8 = (bf16[512,768]{1,0:T(8,128)(2,1)S(1)}, bf16[512,768]{1,0:T(8,128)(2,1)S(1)}, u32[]{:S(2)}, u32[]{:S(2)}) collective-permute-start(bf16[512,768]{1,0:T(8,128)(2,1)S(1)} %constant_dynamic-update-slice_fusion.4.group_ref), channel_id=1, source_target_pairs={{0,16},{16,0},{32,48},{48,32},{64,80},{80,64},{96,112},{112,96},{1... | collective-permute-start | bytes 2359304 | tf_op jit(solution)/shard_map/ppermute | solution.py:16
  33.9 44.7 %copy-start.4 = (f32[768]{0:T(1024)S(1)}, f32[768]{0:T(1024)}, u32[]{:S(2)}) copy-start(f32[768]{0:T(1024)} %param.11) | copy-start | bytes 9220
  33.9 13.1 %collective-permute-start.9 = (bf16[2,4,32,768]{3,2,1,0:T(8,128)(2,1)S(1)}, bf16[2,4,32,768]{3,2,1,0:T(8,128)(2,1)S(1)}, u32[]{:S(2)}, u32[]{:S(2)}) collective-permute-start(bf16[2,4,32,768]{3,2,1,0:T(8,128)(2,1)S(1)} %get-tuple-element.58), channel_id=1, source_target_pairs={{0,4},{1,5},{2,6},{3,7},{4,0},{5,1},{6,2},{7,3},{8,12},{9,13},{10,... | collective-permute-start | bytes 1179656 | tf_op jit(solution)/shard_map/ppermute | solution.py:20
  37.0 23.2 %collective-permute-start.11 = (bf16[3,96,768]{2,1,0:T(8,128)(2,1)S(1)}, bf16[3,96,768]{2,1,0:T(8,128)(2,1)S(1)}, u32[]{:S(2)}, u32[]{:S(2)}) collective-permute-start(bf16[3,96,768]{2,1,0:T(8,128)(2,1)S(1)} %get-tuple-element.67), channel_id=1, source_target_pairs={{0,1},{1,0},{2,3},{3,2},{4,5},{5,4},{6,7},{7,6},{8,9},{9,8},{10,11... | collective-permute-start | bytes 1327112 | tf_op jit(solution)/shard_map/ppermute | solution.py:20
  39.0 21.4 %collective-permute-start.12 = (bf16[3,96,768]{2,1,0:T(8,128)(2,1)S(1)}, bf16[3,96,768]{2,1,0:T(8,128)(2,1)S(1)}, u32[]{:S(2)}, u32[]{:S(2)}) collective-permute-start(bf16[3,96,768]{2,1,0:T(8,128)(2,1)S(1)} %get-tuple-element.68), channel_id=1, source_target_pairs={{0,3},{1,2},{2,1},{3,0},{4,7},{5,6},{6,5},{7,4},{8,11},{9,10},{10,... | collective-permute-start | bytes 1327112 | tf_op jit(solution)/shard_map/ppermute | solution.py:20
  42.3 20.1 %collective-permute-start.13 = (bf16[3,96,768]{2,1,0:T(8,128)(2,1)S(1)}, bf16[3,96,768]{2,1,0:T(8,128)(2,1)S(1)}, u32[]{:S(2)}, u32[]{:S(2)}) collective-permute-start(bf16[3,96,768]{2,1,0:T(8,128)(2,1)S(1)} %get-tuple-element.69), channel_id=1, source_target_pairs={{0,2},{1,3},{2,0},{3,1},{4,6},{5,7},{6,4},{7,5},{8,10},{9,11},{10,... | collective-permute-start | bytes 1327112 | tf_op jit(solution)/shard_map/ppermute | solution.py:20
  47.1 11.4 %collective-permute-start.10 = (bf16[4,32,768]{2,1,0:T(8,128)(2,1)S(1)}, bf16[4,32,768]{2,1,0:T(8,128)(2,1)S(1)}, u32[]{:S(2)}, u32[]{:S(2)}) collective-permute-start(bf16[4,32,768]{2,1,0:T(8,128)(2,1)S(1)} %get-tuple-element.61), channel_id=1, source_target_pairs={{0,8},{1,9},{2,10},{3,11},{4,12},{5,13},{6,14},{7,15},{8,0},{9,1},... | collective-permute-start | bytes 589832 | tf_op jit(solution)/shard_map/ppermute | solution.py:20
  58.6 11.1 %collective-permute-start.14 = (bf16[2,128,768]{2,1,0:T(8,128)(2,1)S(1)}, bf16[2,128,768]{2,1,0:T(8,128)(2,1)S(1)}, u32[]{:S(2)}, u32[]{:S(2)}) collective-permute-start(bf16[2,128,768]{2,1,0:T(8,128)(2,1)S(1)} %get-tuple-element.77), channel_id=1, source_target_pairs={{0,1},{1,0},{2,3},{3,2},{4,5},{5,4},{6,7},{7,6},{8,9},{9,8},{10,11... | collective-permute-start | bytes 1179656 | tf_op jit(solution)/shard_map/ppermute | solution.py:20
  62.6 12.8 %collective-permute-start.16 = (bf16[96,768]{1,0:T(8,128)(2,1)S(1)}, bf16[96,768]{1,0:T(8,128)(2,1)S(1)}, u32[]{:S(2)}, u32[]{:S(2)}) collective-permute-start(bf16[96,768]{1,0:T(8,128)(2,1)S(1)} %get-tuple-element.81), channel_id=1, source_target_pairs={{0,8},{1,9},{2,10},{3,11},{4,12},{5,13},{6,14},{7,15},{8,0},{9,1},... | collective-permute-start | bytes 442376 | tf_op jit(solution)/shard_map/ppermute | solution.py:20
  64.1 11.2 %collective-permute-start.17 = (bf16[96,768]{1,0:T(8,128)(2,1)S(1)}, bf16[96,768]{1,0:T(8,128)(2,1)S(1)}, u32[]{:S(2)}, u32[]{:S(2)}) collective-permute-start(bf16[96,768]{1,0:T(8,128)(2,1)S(1)} %get-tuple-element.82), channel_id=1, source_target_pairs={{0,12},{1,13},{2,14},{3,15},{4,8},{5,9},{6,10},{7,11},{8,4},{9,5},... | collective-permute-start | bytes 442376 | tf_op jit(solution)/shard_map/ppermute | solution.py:20
  65.4 10.7 %collective-permute-start.18 = (bf16[96,768]{1,0:T(8,128)(2,1)S(1)}, bf16[96,768]{1,0:T(8,128)(2,1)S(1)}, u32[]{:S(2)}, u32[]{:S(2)}) collective-permute-start(bf16[96,768]{1,0:T(8,128)(2,1)S(1)} %get-tuple-element.76), channel_id=1, source_target_pairs={{0,4},{1,5},{2,6},{3,7},{4,0},{5,1},{6,2},{7,3},{8,12},{9,13},{10,... | collective-permute-start | bytes 442376 | tf_op jit(solution)/shard_map/ppermute | solution.py:20
  69.8 8.7 %collective-permute-start.15 = (bf16[128,768]{1,0:T(8,128)(2,1)S(1)}, bf16[128,768]{1,0:T(8,128)(2,1)S(1)}, u32[]{:S(2)}, u32[]{:S(2)}) collective-permute-start(bf16[128,768]{1,0:T(8,128)(2,1)S(1)} %get-tuple-element.80), channel_id=1, source_target_pairs={{0,3},{1,2},{2,1},{3,0},{4,7},{5,6},{6,5},{7,4},{8,11},{9,10},{10,... | collective-permute-start | bytes 589832 | tf_op jit(solution)/shard_map/ppermute | solution.py:20
  (3 other events, 4.9 us)

commit v8 on v5

--- a/solution.py
+++ b/solution.py
@@ -239,15 +239,16 @@
     far = row_swap(features, 1, 0, 0)
     near_parts = [features] + [row_swap(features, 0, d, 0) for d in (1, 2, 3)]
     blocks, weights = load(blocks, weights)
-    far, blocks, weights, to_plan = lax.optimization_barrier((far, blocks, weights, to_plan))
     tables = plan(*to_plan)
+    far, blocks, weights, tables = lax.optimization_barrier((far, blocks, weights, tables))
+    near_parts[1], weights = lax.optimization_barrier((near_parts[1], weights))
     stage = lambda index, value, total: tile_stage(index, tables, blocks, weights, value, total)
     far_parts = [far] + [row_swap(far, 0, d, 0) for d in (1, 2, 3)]
     near = jnp.concatenate(near_parts, axis=0)
     near_other = row_swap(near, 0, 0, 1)
     (total,) = stage(0, near, None)
     (total,) = stage(1, near_other, total)
-    far_parts[-1], total = lax.optimization_barrier((far_parts[-1], total))
+    far_parts[1:], total = lax.optimization_barrier((far_parts[1:], total))
     rest = jnp.concatenate(far_parts, axis=0)
     rest_other = row_swap(rest, 0, 0, 1)
     (total,) = stage(2, rest, total)

time: 80.2 us -> 82.9 us (1.034)
  waiting for transfers between devices: 30.6 us -> 32 us
  other arithmetic: 0.93 us -> 2.28 us
    ppermute x9, waiting for transfers between devices: 4.43 us -> 5.52 us  [row_swap(): lax.ppermute(value, 'row', [(at, at ^ dz * 8 + dx * 2 + dc) for at in ran...]
    unnamed x22 -> x16, local copies, waits for them, and re-layouts: 4.55 us -> 4.54 us
  transfers between devices with their start and end apart: 19 -> 19, of which waited for: 8 -> 9; matrix products, arithmetic and copies ran while one was open for 1% -> 2% of each run, Pallas kernels for 11% -> 10%
where the time goes in v8:
time: 82.9 us; the launch traced here: 82.4 us
  waiting for transfers between devices  32 us (39%)
  starting transfers between devices  30.7 us (37%)
  Pallas kernels  12.3 us (15%)
  local copies, waits for them, and re-layouts  4.58 us (6%)
  other arithmetic  2.28 us (3%)
    ppermute x10, waiting for transfers between devices, col_swap(): lax.ppermute(value, 'col', [(at, at ^ dz * Y + dy) for at in range(16)])  26.5 us
    ppermute x9, starting transfers between devices, row_swap(): lax.ppermute(value, 'row', [(at, at ^ dz * 8 + dx * 2 + dc) for at in ran...  15.6 us
    ppermute x10, starting transfers between devices, col_swap(): lax.ppermute(value, 'col', [(at, at ^ dz * Y + dy) for at in range(16)])  15.1 us
    pallas_call x4, Pallas kernels, tile_stage(): pl.pallas_call(functools.partial(stage_kernel, group, first, last), out_s...  9.65 us
    ppermute x9, waiting for transfers between devices, row_swap(): lax.ppermute(value, 'row', [(at, at ^ dz * 8 + dx * 2 + dc) for at in ran...  5.52 us
    unnamed x16, local copies, waits for them, and re-layouts  4.54 us
    pallas_call x1, Pallas kernels, plan(): pl.pallas_call(plan_kernel, out_shape=[jax.ShapeDtypeStruct((many,), jnp....  1.68 us
  transfers between devices with their start and end apart: 19, of which 9 were waited for; matrix products, arithmetic and copies ran while one was open for 2% of the time, Pallas kernels for 10%

profile of v8, /device:TPU:4, one launch (start us, length us, event | category | flops | bytes accessed | tf_op | source)
XLA Modules:
  0.0 82.4 jit_solution(5698680415297376552)
XLA Ops:
  0.5 2.7 %collective-permute-start.5 = (bf16[128,768]{1,0:T(8,128)(2,1)}, bf16[128,768]{1,0:T(8,128)(2,1)S(1)}, u32[]{:S(2)}, u32[]{:S(2)}) collective-permute-start(bf16[128,768]{1,0:T(8,128)(2,1)} %param.8), channel_id=1, source_target_pairs={{0,64},{16,80},{32,96},{48,112},{64,0},{80,16},{96,32},{112,48},{1... | collective-permute-start | bytes 589832 | tf_op jit(solution)/shard_map/ppermute | solution.py:16
  4.1 7.2 %collective-permute-start = (bf16[128,768]{1,0:T(8,128)(2,1)}, bf16[128,768]{1,0:T(8,128)(2,1)S(1)}, u32[]{:S(2)}, u32[]{:S(2)}) collective-permute-start(bf16[128,768]{1,0:T(8,128)(2,1)} %param.8), channel_id=1, source_target_pairs={{0,128},{16,144},{32,160},{48,176},{64,192},{80,208},{96,224},{112... | collective-permute-start | bytes 589832 | tf_op jit(solution)/shard_map/ppermute | solution.py:16
  12.7 1.7 %plan.1 = (s32[40]{0:T(128)S(1)}, s32[21]{0:T(128)S(1)}) custom-call(s32[5,8]{1,0:T(8,128)S(1)} %fusion.4.table_ref), custom_call_target="tpu_custom_call" | custom-call | tf_op jit(solution)/shard_map/plan/pallas_call | solution.py:137
  14.4 2.7 %copy-done.1 = bf16[768,5,768]{2,0,1:T(8,128)(2,1)S(1)} copy-done((bf16[768,5,768]{2,0,1:T(8,128)(2,1)S(1)}, bf16[768,5,768]{2,0,1:T(8,128)(2,1)}, u32[]{:S(2)}) %copy-start.1) | copy-done | bytes 5898264
  17.1 1.3 %copy-done.2 = bf16[1,1,5,8,128,128]{5,4,3,2,1,0:T(8,128)(2,1)S(1)} copy-done((bf16[1,1,5,8,128,128]{5,4,3,2,1,0:T(8,128)(2,1)S(1)}, bf16[1,1,5,8,128,128]{5,4,3,2,1,0:T(8,128)(2,1)}, u32[]{:S(2)}) %copy-start.2) | copy-done | bytes 1310744
  20.3 2.8 %collective-permute-start.3 = (bf16[128,768]{1,0:T(8,128)(2,1)S(1)}, bf16[128,768]{1,0:T(8,128)(2,1)S(1)}, u32[]{:S(2)}, u32[]{:S(2)}) collective-permute-start(bf16[128,768]{1,0:T(8,128)(2,1)S(1)} %collective-permute-done), channel_id=1, source_target_pairs={{0,64},{16,80},{32,96},{48,112},{64,0},{80,16},{96,32},{112,48},{1... | collective-permute-start | bytes 589832 | tf_op jit(solution)/shard_map/ppermute | solution.py:16
  23.7 2.3 %tile.4.refs_0_ = f32[2048,768]{1,0:T(8,128)S(1)} custom-call(s32[40]{0:T(128)S(1)} %get-tuple-element.52.codes_ref, s32[21]{0:T(128)S(1)} %get-tuple-element.53.starts_ref, bf16[40,128,128]{2,1,0:T(8,128)(2,1)S(1)} %get-tuple-element.54.blocks_ref, bf16[5,768,768]{2,1,0:T(8,128)(2,1)S(1)} %get-tuple-element.56.weight_ref, ...), custom_call_target="tpu_custom_call" | custom-call | flops 1073741824 | bytes 4194304 | tf_op jit(solution)/shard_map/tile/pallas_call | solution.py:164
  26.0 1.7 %tile.5.refs_0_ = f32[2048,768]{1,0:T(8,128)S(1)} custom-call(s32[40]{0:T(128)S(1)} %get-tuple-element.52.codes_ref, s32[21]{0:T(128)S(1)} %get-tuple-element.53.starts_ref, bf16[40,128,128]{2,1,0:T(8,128)(2,1)S(1)} %get-tuple-element.54.blocks_ref, bf16[5,768,768]{2,1,0:T(8,128)(2,1)S(1)} %get-tuple-element.56.weight_ref, ...), custom_call_target="tpu_custom_call", output_to_operand_aliasing={{}: (5, {})} | custom-call | flops 1073741824 | bytes 4194304 | tf_op jit(solution)/shard_map/tile/pallas_call | solution.py:164
  27.8 3.3 %collective-permute-done.4 = bf16[128,768]{1,0:T(8,128)(2,1)S(1)} collective-permute-done((bf16[128,768]{1,0:T(8,128)(2,1)S(1)}, bf16[128,768]{1,0:T(8,128)(2,1)S(1)}, u32[]{:S(2)}, u32[]{:S(2)}) %collective-permute-start.4) | collective-permute-done | bytes 196640 | tf_op jit(solution)/shard_map/ppermute | solution.py:16
  31.1 1.8 %collective-permute-done.2 = bf16[128,768]{1,0:T(8,128)(2,1)S(1)} collective-permute-done((bf16[128,768]{1,0:T(8,128)(2,1)S(1)}, bf16[128,768]{1,0:T(8,128)(2,1)S(1)}, u32[]{:S(2)}, u32[]{:S(2)}) %collective-permute-start.2) | collective-permute-done | bytes 196640 | tf_op jit(solution)/shard_map/ppermute | solution.py:16
  33.1 1.9 %tile.6.refs_0_ = f32[2048,768]{1,0:T(8,128)S(1)} custom-call(s32[40]{0:T(128)S(1)} %get-tuple-element.52.codes_ref, s32[21]{0:T(128)S(1)} %get-tuple-element.53.starts_ref, bf16[40,128,128]{2,1,0:T(8,128)(2,1)S(1)} %get-tuple-element.54.blocks_ref, bf16[5,768,768]{2,1,0:T(8,128)(2,1)S(1)} %get-tuple-element.56.weight_ref, ...), custom_call_target="tpu_custom_call", output_to_operand_aliasing={{}: (5, {})} | custom-call | flops 1073741824 | bytes 4194304 | tf_op jit(solution)/shard_map/tile/pallas_call | solution.py:164
  35.4 3.7 %tile.7 = (f32[2048,768]{1,0:T(8,128)S(1)}, bf16[3,96,768]{2,1,0:T(8,128)(2,1)S(1)}, bf16[3,96,768]{2,1,0:T(8,128)(2,1)S(1)}, bf16[3,96,768]{2,1,0:T(8,128)(2,1)...) custom-call(s32[40]{0:T(128)S(1)} %get-tuple-element.52.codes_ref, ...), custom_call_target="tpu_custom_call", output_to_operand_aliasing={{0}: (5, {})} | custom-call | flops 1073741824 | bytes 4194304 | tf_op jit(solution)/shard_map/tile/pallas_call | solution.py:164
  39.1 1.4 %collective-permute-start.9 = (bf16[2,4,32,768]{3,2,1,0:T(8,128)(2,1)S(1)}, bf16[2,4,32,768]{3,2,1,0:T(8,128)(2,1)S(1)}, u32[]{:S(2)}, u32[]{:S(2)}) collective-permute-start(bf16[2,4,32,768]{3,2,1,0:T(8,128)(2,1)S(1)} %get-tuple-element.64), channel_id=1, source_target_pairs={{0,4},{1,5},{2,6},{3,7},{4,0},{5,1},{6,2},{7,3},{8,12},{9,13},{10,... | collective-permute-start | bytes 1179656 | tf_op jit(solution)/shard_map/ppermute | solution.py:20
  40.5 4.6 %collective-permute-start.11 = (bf16[3,96,768]{2,1,0:T(8,128)(2,1)S(1)}, bf16[3,96,768]{2,1,0:T(8,128)(2,1)S(1)}, u32[]{:S(2)}, u32[]{:S(2)}) collective-permute-start(bf16[3,96,768]{2,1,0:T(8,128)(2,1)S(1)} %get-tuple-element.73), channel_id=1, source_target_pairs={{0,2},{1,3},{2,0},{3,1},{4,6},{5,7},{6,4},{7,5},{8,10},{9,11},{10,... | collective-permute-start | bytes 1327112 | tf_op jit(solution)/shard_map/ppermute | solution.py:20
  45.7 5.2 %collective-permute-done.9.refs_1_ = bf16[2,4,32,768]{3,2,1,0:T(8,128)(2,1)S(1)} collective-permute-done((bf16[2,4,32,768]{3,2,1,0:T(8,128)(2,1)S(1)}, bf16[2,4,32,768]{3,2,1,0:T(8,128)(2,1)S(1)}, u32[]{:S(2)}, u32[]{:S(2)}) %collective-permute-start.9) | collective-permute-done | bytes 393248 | tf_op jit(solution)/shard_map/ppermute | solution.py:20
  51.0 1.1 %collective-permute-start.10 = (bf16[4,32,768]{2,1,0:T(8,128)(2,1)S(1)}, bf16[4,32,768]{2,1,0:T(8,128)(2,1)S(1)}, u32[]{:S(2)}, u32[]{:S(2)}) collective-permute-start(bf16[4,32,768]{2,1,0:T(8,128)(2,1)S(1)} %get-tuple-element.67), channel_id=1, source_target_pairs={{0,8},{1,9},{2,10},{3,11},{4,12},{5,13},{6,14},{7,15},{8,0},{9,1},... | collective-permute-start | bytes 589832 | tf_op jit(solution)/shard_map/ppermute | solution.py:20
  52.5 10.4 %collective-permute-done.10.refs_1_ = bf16[4,32,768]{2,1,0:T(8,128)(2,1)S(1)} collective-permute-done((bf16[4,32,768]{2,1,0:T(8,128)(2,1)S(1)}, bf16[4,32,768]{2,1,0:T(8,128)(2,1)S(1)}, u32[]{:S(2)}, u32[]{:S(2)}) %collective-permute-start.10) | collective-permute-done | bytes 196640 | tf_op jit(solution)/shard_map/ppermute | solution.py:20
  63.0 1.3 %collective-permute-start.14 = (bf16[2,128,768]{2,1,0:T(8,128)(2,1)S(1)}, bf16[2,128,768]{2,1,0:T(8,128)(2,1)S(1)}, u32[]{:S(2)}, u32[]{:S(2)}) collective-permute-start(bf16[2,128,768]{2,1,0:T(8,128)(2,1)S(1)} %get-tuple-element.83), channel_id=1, source_target_pairs={{0,1},{1,0},{2,3},{3,2},{4,5},{5,4},{6,7},{7,6},{8,9},{9,8},{10,11... | collective-permute-start | bytes 1179656 | tf_op jit(solution)/shard_map/ppermute | solution.py:20
  64.5 1.6 %collective-permute-start.16 = (bf16[96,768]{1,0:T(8,128)(2,1)S(1)}, bf16[96,768]{1,0:T(8,128)(2,1)S(1)}, u32[]{:S(2)}, u32[]{:S(2)}) collective-permute-start(bf16[96,768]{1,0:T(8,128)(2,1)S(1)} %get-tuple-element.87), channel_id=1, source_target_pairs={{0,8},{1,9},{2,10},{3,11},{4,12},{5,13},{6,14},{7,15},{8,0},{9,1},... | collective-permute-start | bytes 442376 | tf_op jit(solution)/shard_map/ppermute | solution.py:20
  66.1 1.9 %collective-permute-start.17 = (bf16[96,768]{1,0:T(8,128)(2,1)S(1)}, bf16[96,768]{1,0:T(8,128)(2,1)S(1)}, u32[]{:S(2)}, u32[]{:S(2)}) collective-permute-start(bf16[96,768]{1,0:T(8,128)(2,1)S(1)} %get-tuple-element.88), channel_id=1, source_target_pairs={{0,12},{1,13},{2,14},{3,15},{4,8},{5,9},{6,10},{7,11},{8,4},{9,5},... | collective-permute-start | bytes 442376 | tf_op jit(solution)/shard_map/ppermute | solution.py:20
  68.1 6.1 %collective-permute-done.14.refs_2_ = bf16[2,128,768]{2,1,0:T(8,128)(2,1)S(1)} collective-permute-done((bf16[2,128,768]{2,1,0:T(8,128)(2,1)S(1)}, bf16[2,128,768]{2,1,0:T(8,128)(2,1)S(1)}, u32[]{:S(2)}, u32[]{:S(2)}) %collective-permute-start.14) | collective-permute-done | bytes 393248 | tf_op jit(solution)/shard_map/ppermute | solution.py:20
  74.2 2.5 %collective-permute-start.15 = (bf16[128,768]{1,0:T(8,128)(2,1)S(1)}, bf16[128,768]{1,0:T(8,128)(2,1)S(1)}, u32[]{:S(2)}, u32[]{:S(2)}) collective-permute-start(bf16[128,768]{1,0:T(8,128)(2,1)S(1)} %get-tuple-element.86), channel_id=1, source_target_pairs={{0,3},{1,2},{2,1},{3,0},{4,7},{5,6},{6,5},{7,4},{8,11},{9,10},{10,... | collective-permute-start | bytes 589832 | tf_op jit(solution)/shard_map/ppermute | solution.py:20
  76.8 1.5 %collective-permute-done.16 = bf16[96,768]{1,0:T(8,128)(2,1)S(1)} collective-permute-done((bf16[96,768]{1,0:T(8,128)(2,1)S(1)}, bf16[96,768]{1,0:T(8,128)(2,1)S(1)}, u32[]{:S(2)}, u32[]{:S(2)}) %collective-permute-start.16) | collective-permute-done | bytes 147488 | tf_op jit(solution)/shard_map/ppermute | solution.py:20
  78.4 3.1 %collective-permute-done.15 = bf16[128,768]{1,0:T(8,128)(2,1)S(1)} collective-permute-done((bf16[128,768]{1,0:T(8,128)(2,1)S(1)}, bf16[128,768]{1,0:T(8,128)(2,1)S(1)}, u32[]{:S(2)}, u32[]{:S(2)}) %collective-permute-start.15) | collective-permute-done | bytes 196640 | tf_op jit(solution)/shard_map/ppermute | solution.py:20
  (50 shorter events, 8.2 us)
Async XLA Ops:
  0.0 52.1 %copy-start = (bf16[768,768]{1,0:T(8,128)(2,1)S(1)}, bf16[768,768]{1,0:T(8,128)(2,1)}, u32[]{:S(2)}) copy-start(bf16[768,768]{1,0:T(8,128)(2,1)} %param.9) | copy-start | bytes 3538948
  0.0 19.4 %collective-permute-start.6 = (bf16[128,768]{1,0:T(8,128)(2,1)}, bf16[128,768]{1,0:T(8,128)(2,1)S(1)}, u32[]{:S(2)}, u32[]{:S(2)}) collective-permute-start(bf16[128,768]{1,0:T(8,128)(2,1)} %param.8), channel_id=1, source_target_pairs={{0,96},{16,112},{32,64},{48,80},{64,32},{80,48},{96,0},{112,16},{1... | collective-permute-start | bytes 589832 | tf_op jit(solution)/shard_map/ppermute | solution.py:16
  0.5 18.8 %collective-permute-start.5 = (bf16[128,768]{1,0:T(8,128)(2,1)}, bf16[128,768]{1,0:T(8,128)(2,1)S(1)}, u32[]{:S(2)}, u32[]{:S(2)}) collective-permute-start(bf16[128,768]{1,0:T(8,128)(2,1)} %param.8), channel_id=1, source_target_pairs={{0,64},{16,80},{32,96},{48,112},{64,0},{80,16},{96,32},{112,48},{1... | collective-permute-start | bytes 589832 | tf_op jit(solution)/shard_map/ppermute | solution.py:16
  3.3 16.1 %collective-permute-start.1 = (bf16[128,768]{1,0:T(8,128)(2,1)}, bf16[128,768]{1,0:T(8,128)(2,1)S(1)}, u32[]{:S(2)}, u32[]{:S(2)}) collective-permute-start(bf16[128,768]{1,0:T(8,128)(2,1)} %param.8), channel_id=1, source_target_pairs={{0,32},{16,48},{32,0},{48,16},{64,96},{80,112},{96,64},{112,80},{1... | collective-permute-start | bytes 589832 | tf_op jit(solution)/shard_map/ppermute | solution.py:16
  4.1 15.2 %collective-permute-start = (bf16[128,768]{1,0:T(8,128)(2,1)}, bf16[128,768]{1,0:T(8,128)(2,1)S(1)}, u32[]{:S(2)}, u32[]{:S(2)}) collective-permute-start(bf16[128,768]{1,0:T(8,128)(2,1)} %param.8), channel_id=1, source_target_pairs={{0,128},{16,144},{32,160},{48,176},{64,192},{80,208},{96,224},{112... | collective-permute-start | bytes 589832 | tf_op jit(solution)/shard_map/ppermute | solution.py:16
  14.4 2.7 %copy-start.1 = (bf16[768,5,768]{2,0,1:T(8,128)(2,1)S(1)}, bf16[768,5,768]{2,0,1:T(8,128)(2,1)}, u32[]{:S(2)}) copy-start(bf16[768,5,768]{2,0,1:T(8,128)(2,1)} %param.10) | copy-start | bytes 17694724
  17.1 1.3 %copy-start.2 = (bf16[1,1,5,8,128,128]{5,4,3,2,1,0:T(8,128)(2,1)S(1)}, bf16[1,1,5,8,128,128]{5,4,3,2,1,0:T(8,128)(2,1)}, u32[]{:S(2)}) copy-start(bf16[1,1,5,8,128,128]{5,4,3,2,1,0:T(8,128)(2,1)} %param.12) | copy-start | bytes 3932164
  18.4 0.9 %copy-start.3 = (bf16[128,768]{1,0:T(8,128)(2,1)S(1)}, bf16[128,768]{1,0:T(8,128)(2,1)}, u32[]{:S(2)}) copy-start(bf16[128,768]{1,0:T(8,128)(2,1)} %param.8) | copy-start | bytes 589828
  19.4 6.6 %collective-permute-start.7 = (bf16[512,768]{1,0:T(8,128)(2,1)S(1)}, bf16[512,768]{1,0:T(8,128)(2,1)S(1)}, u32[]{:S(2)}, u32[]{:S(2)}) collective-permute-start(bf16[512,768]{1,0:T(8,128)(2,1)S(1)} %constant_dynamic-update-slice_fusion.group_ref), channel_id=1, source_target_pairs={{0,16},{16,0},{32,48},{48,32},{64,80},{80,64},{96,112},{112,96},{1... | collective-permute-start | bytes 2359304 | tf_op jit(solution)/shard_map/ppermute | solution.py:16
  19.5 11.5 %collective-permute-start.4 = (bf16[128,768]{1,0:T(8,128)(2,1)S(1)}, bf16[128,768]{1,0:T(8,128)(2,1)S(1)}, u32[]{:S(2)}, u32[]{:S(2)}) collective-permute-start(bf16[128,768]{1,0:T(8,128)(2,1)S(1)} %collective-permute-done), channel_id=1, source_target_pairs={{0,96},{16,112},{32,64},{48,80},{64,32},{80,48},{96,0},{112,16},{1... | collective-permute-start | bytes 589832 | tf_op jit(solution)/shard_map/ppermute | solution.py:16
  20.3 10.8 %collective-permute-start.3 = (bf16[128,768]{1,0:T(8,128)(2,1)S(1)}, bf16[128,768]{1,0:T(8,128)(2,1)S(1)}, u32[]{:S(2)}, u32[]{:S(2)}) collective-permute-start(bf16[128,768]{1,0:T(8,128)(2,1)S(1)} %collective-permute-done), channel_id=1, source_target_pairs={{0,64},{16,80},{32,96},{48,112},{64,0},{80,16},{96,32},{112,48},{1... | collective-permute-start | bytes 589832 | tf_op jit(solution)/shard_map/ppermute | solution.py:16
  23.1 9.8 %collective-permute-start.2 = (bf16[128,768]{1,0:T(8,128)(2,1)S(1)}, bf16[128,768]{1,0:T(8,128)(2,1)S(1)}, u32[]{:S(2)}, u32[]{:S(2)}) collective-permute-start(bf16[128,768]{1,0:T(8,128)(2,1)S(1)} %collective-permute-done), channel_id=1, source_target_pairs={{0,32},{16,48},{32,0},{48,16},{64,96},{80,112},{96,64},{112,80},{1... | collective-permute-start | bytes 589832 | tf_op jit(solution)/shard_map/ppermute | solution.py:16
  33.0 2.4 %collective-permute-start.8 = (bf16[512,768]{1,0:T(8,128)(2,1)S(1)}, bf16[512,768]{1,0:T(8,128)(2,1)S(1)}, u32[]{:S(2)}, u32[]{:S(2)}) collective-permute-start(bf16[512,768]{1,0:T(8,128)(2,1)S(1)} %constant_dynamic-update-slice_fusion.4.group_ref), channel_id=1, source_target_pairs={{0,16},{16,0},{32,48},{48,32},{64,80},{80,64},{96,112},{112,96},{1... | collective-permute-start | bytes 2359304 | tf_op jit(solution)/shard_map/ppermute | solution.py:16
  39.1 42.5 %copy-start.4 = (f32[768]{0:T(1024)S(1)}, f32[768]{0:T(1024)}, u32[]{:S(2)}) copy-start(f32[768]{0:T(1024)} %param.11) | copy-start | bytes 9220
  39.1 11.8 %collective-permute-start.9 = (bf16[2,4,32,768]{3,2,1,0:T(8,128)(2,1)S(1)}, bf16[2,4,32,768]{3,2,1,0:T(8,128)(2,1)S(1)}, u32[]{:S(2)}, u32[]{:S(2)}) collective-permute-start(bf16[2,4,32,768]{3,2,1,0:T(8,128)(2,1)S(1)} %get-tuple-element.64), channel_id=1, source_target_pairs={{0,4},{1,5},{2,6},{3,7},{4,0},{5,1},{6,2},{7,3},{8,12},{9,13},{10,... | collective-permute-start | bytes 1179656 | tf_op jit(solution)/shard_map/ppermute | solution.py:20
  40.5 23.7 %collective-permute-start.11 = (bf16[3,96,768]{2,1,0:T(8,128)(2,1)S(1)}, bf16[3,96,768]{2,1,0:T(8,128)(2,1)S(1)}, u32[]{:S(2)}, u32[]{:S(2)}) collective-permute-start(bf16[3,96,768]{2,1,0:T(8,128)(2,1)S(1)} %get-tuple-element.73), channel_id=1, source_target_pairs={{0,2},{1,3},{2,0},{3,1},{4,6},{5,7},{6,4},{7,5},{8,10},{9,11},{10,... | collective-permute-start | bytes 1327112 | tf_op jit(solution)/shard_map/ppermute | solution.py:20
  45.1 19.2 %collective-permute-start.12 = (bf16[3,96,768]{2,1,0:T(8,128)(2,1)S(1)}, bf16[3,96,768]{2,1,0:T(8,128)(2,1)S(1)}, u32[]{:S(2)}, u32[]{:S(2)}) collective-permute-start(bf16[3,96,768]{2,1,0:T(8,128)(2,1)S(1)} %get-tuple-element.74), channel_id=1, source_target_pairs={{0,1},{1,0},{2,3},{3,2},{4,5},{5,4},{6,7},{7,6},{8,9},{9,8},{10,11... | collective-permute-start | bytes 1327112 | tf_op jit(solution)/shard_map/ppermute | solution.py:20
  45.1 19.2 %collective-permute-start.13 = (bf16[3,96,768]{2,1,0:T(8,128)(2,1)S(1)}, bf16[3,96,768]{2,1,0:T(8,128)(2,1)S(1)}, u32[]{:S(2)}, u32[]{:S(2)}) collective-permute-start(bf16[3,96,768]{2,1,0:T(8,128)(2,1)S(1)} %get-tuple-element.75), channel_id=1, source_target_pairs={{0,3},{1,2},{2,1},{3,0},{4,7},{5,6},{6,5},{7,4},{8,11},{9,10},{10,... | collective-permute-start | bytes 1327112 | tf_op jit(solution)/shard_map/ppermute | solution.py:20
  51.0 11.9 %collective-permute-start.10 = (bf16[4,32,768]{2,1,0:T(8,128)(2,1)S(1)}, bf16[4,32,768]{2,1,0:T(8,128)(2,1)S(1)}, u32[]{:S(2)}, u32[]{:S(2)}) collective-permute-start(bf16[4,32,768]{2,1,0:T(8,128)(2,1)S(1)} %get-tuple-element.67), channel_id=1, source_target_pairs={{0,8},{1,9},{2,10},{3,11},{4,12},{5,13},{6,14},{7,15},{8,0},{9,1},... | collective-permute-start | bytes 589832 | tf_op jit(solution)/shard_map/ppermute | solution.py:20
  63.0 11.2 %collective-permute-start.14 = (bf16[2,128,768]{2,1,0:T(8,128)(2,1)S(1)}, bf16[2,128,768]{2,1,0:T(8,128)(2,1)S(1)}, u32[]{:S(2)}, u32[]{:S(2)}) collective-permute-start(bf16[2,128,768]{2,1,0:T(8,128)(2,1)S(1)} %get-tuple-element.83), channel_id=1, source_target_pairs={{0,1},{1,0},{2,3},{3,2},{4,5},{5,4},{6,7},{7,6},{8,9},{9,8},{10,11... | collective-permute-start | bytes 1179656 | tf_op jit(solution)/shard_map/ppermute | solution.py:20
  64.5 13.8 %collective-permute-start.16 = (bf16[96,768]{1,0:T(8,128)(2,1)S(1)}, bf16[96,768]{1,0:T(8,128)(2,1)S(1)}, u32[]{:S(2)}, u32[]{:S(2)}) collective-permute-start(bf16[96,768]{1,0:T(8,128)(2,1)S(1)} %get-tuple-element.87), channel_id=1, source_target_pairs={{0,8},{1,9},{2,10},{3,11},{4,12},{5,13},{6,14},{7,15},{8,0},{9,1},... | collective-permute-start | bytes 442376 | tf_op jit(solution)/shard_map/ppermute | solution.py:20
  66.1 12.2 %collective-permute-start.17 = (bf16[96,768]{1,0:T(8,128)(2,1)S(1)}, bf16[96,768]{1,0:T(8,128)(2,1)S(1)}, u32[]{:S(2)}, u32[]{:S(2)}) collective-permute-start(bf16[96,768]{1,0:T(8,128)(2,1)S(1)} %get-tuple-element.88), channel_id=1, source_target_pairs={{0,12},{1,13},{2,14},{3,15},{4,8},{5,9},{6,10},{7,11},{8,4},{9,5},... | collective-permute-start | bytes 442376 | tf_op jit(solution)/shard_map/ppermute | solution.py:20
  68.0 10.3 %collective-permute-start.18 = (bf16[96,768]{1,0:T(8,128)(2,1)S(1)}, bf16[96,768]{1,0:T(8,128)(2,1)S(1)}, u32[]{:S(2)}, u32[]{:S(2)}) collective-permute-start(bf16[96,768]{1,0:T(8,128)(2,1)S(1)} %get-tuple-element.82), channel_id=1, source_target_pairs={{0,4},{1,5},{2,6},{3,7},{4,0},{5,1},{6,2},{7,3},{8,12},{9,13},{10,... | collective-permute-start | bytes 442376 | tf_op jit(solution)/shard_map/ppermute | solution.py:20
  74.2 7.3 %collective-permute-start.15 = (bf16[128,768]{1,0:T(8,128)(2,1)S(1)}, bf16[128,768]{1,0:T(8,128)(2,1)S(1)}, u32[]{:S(2)}, u32[]{:S(2)}) collective-permute-start(bf16[128,768]{1,0:T(8,128)(2,1)S(1)} %get-tuple-element.86), channel_id=1, source_target_pairs={{0,3},{1,2},{2,1},{3,0},{4,7},{5,6},{6,5},{7,4},{8,11},{9,10},{10,... | collective-permute-start | bytes 589832 | tf_op jit(solution)/shard_map/ppermute | solution.py:20

commit v9 on v5

--- a/solution.py
+++ b/solution.py
@@ -24,17 +24,14 @@
     return pl.ds(pl.multiple_of(index * size, size), size)
 
 
-def stage_kernel(group, first, last, codes_ref, starts_ref, blocks_ref, weight_ref, group_ref, *refs):
-    if not first:
-        refs = refs[1:]
+def stage_kernel(group, last, codes_ref, starts_ref, blocks_ref, weight_ref, group_ref, *refs):
+    refs = refs[1:]
     total, refs = refs[0], refs[1:]
     if last:
         y_refs, z_refs, own_ref, refs = refs[:Y], refs[Y : Y + 2], refs[Y + 2], refs[Y + 3 :]
     (picked,) = refs
     relations = weight_ref.shape[0]
     size = blocks_ref.shape[-1]
-    if first:
-        total[...] = jnp.zeros_like(total)
     base = starts_ref[group * relations]
     length = starts_ref[(group + 1) * relations] - base
 
@@ -150,7 +147,7 @@
 def tile_stage(group, tables, blocks, weights, value, total):
     many, size, _ = blocks.shape
     width = weights.shape[-1]
-    first, last = group == 0, group == 3
+    last = group == 3
     vmem = pl.BlockSpec(memory_space=pltpu.VMEM)
     smem = pl.BlockSpec(memory_space=pltpu.SMEM)
     out_shape = [jax.ShapeDtypeStruct((Y * Z * size, width), jnp.float32)]
@@ -159,15 +156,14 @@
         out_shape += [jax.ShapeDtypeStruct((Z // 2, Y, FIRST, width), jnp.bfloat16)] * 2
         out_shape += [jax.ShapeDtypeStruct((Y, size - FIRST, width), jnp.bfloat16)]
     args = [*tables, blocks, weights, value]
-    if not first:
-        args.append(total)
+    args.append(total)
     return pl.pallas_call(
-        functools.partial(stage_kernel, group, first, last),
+        functools.partial(stage_kernel, group, last),
         out_shape=out_shape,
         in_specs=[smem] * 2 + [vmem] * (len(args) - 2),
         out_specs=[vmem] * len(out_shape),
         scratch_shapes=[pltpu.VMEM((many * size, width), jnp.bfloat16)],
-        input_output_aliases={} if first else {len(args) - 1: 0},
+        input_output_aliases={len(args) - 1: 0},
         compiler_params=pltpu.CompilerParams(vmem_limit_bytes=14 << 20),
         cost_estimate=pl.CostEstimate(flops=1 << 30, bytes_accessed=4 << 20, transcendentals=0),
         name="tile",
@@ -218,18 +214,21 @@
     outs[1][...] = (across[...] + got[1].astype(jnp.float32)).astype(jnp.bfloat16)
 
 
-def load_kernel(blocks_ref, weights_ref, blocks_out, weights_out):
+def load_kernel(blocks_ref, weights_ref, blocks_out, weights_out, total):
+    total[...] = jnp.zeros_like(total)
     blocks_out[...] = blocks_ref[...]
     weights_out[...] = weights_ref[...]
 
 
 def load(blocks, weights):
+    size, width = blocks.shape[-1], weights.shape[-1]
     vmem = pl.BlockSpec(memory_space=pltpu.VMEM)
     return pl.pallas_call(
         load_kernel,
-        out_shape=[jax.ShapeDtypeStruct(a.shape, a.dtype) for a in (blocks, weights)],
+        out_shape=[jax.ShapeDtypeStruct(a.shape, a.dtype) for a in (blocks, weights)]
+        + [jax.ShapeDtypeStruct((Y * Z * size, width), jnp.float32)],
         in_specs=[vmem] * 2,
-        out_specs=[vmem] * 2,
+        out_specs=[vmem] * 3,
         compiler_params=pltpu.CompilerParams(vmem_limit_bytes=2 << 20),
         name="load",
     )(blocks, weights)
@@ -238,14 +237,14 @@
 def gather_groups(features, to_plan, blocks, weights):
     far = row_swap(features, 1, 0, 0)
     near_parts = [features] + [row_swap(features, 0, d, 0) for d in (1, 2, 3)]
-    blocks, weights = load(blocks, weights)
-    far, blocks, weights, to_plan = lax.optimization_barrier((far, blocks, weights, to_plan))
+    blocks, weights, total = load(blocks, weights)
+    far, blocks, weights, total, to_plan = lax.optimization_barrier((far, blocks, weights, total, to_plan))
     tables = plan(*to_plan)
     stage = lambda index, value, total: tile_stage(index, tables, blocks, weights, value, total)
     far_parts = [far] + [row_swap(far, 0, d, 0) for d in (1, 2, 3)]
     near = jnp.concatenate(near_parts, axis=0)
     near_other = row_swap(near, 0, 0, 1)
-    (total,) = stage(0, near, None)
+    (total,) = stage(0, near, total)
     (total,) = stage(1, near_other, total)
     far_parts[-1], total = lax.optimization_barrier((far_parts[-1], total))
     rest = jnp.concatenate(far_parts, axis=0)

time: 80.2 us -> 80.7 us (level)
  starting transfers between devices: 30.9 us -> 37.2 us
  waiting for transfers between devices: 30.6 us -> 24.3 us
  Pallas kernels: 11.7 us -> 12.7 us
    ppermute x10, starting transfers between devices: 15.2 us -> 21.5 us  [col_swap(): lax.ppermute(value, 'col', [(at, at ^ dz * Y + dy) for at in range(16)])]
    ppermute x10, waiting for transfers between devices: 26.2 us -> 20.7 us  [col_swap(): lax.ppermute(value, 'col', [(at, at ^ dz * Y + dy) for at in range(16)])]
    ppermute x9, waiting for transfers between devices: 4.43 us -> 3.6 us  [row_swap(): lax.ppermute(value, 'row', [(at, at ^ dz * 8 + dx * 2 + dc) for at in ran...]
  transfers between devices with their start and end apart: 19 -> 19, of which waited for: 8 -> 8; matrix products, arithmetic and copies ran while one was open for 1% -> 1% of each run, Pallas kernels for 11% -> 13%
where the time goes in v9:
time: 80.7 us; the launch traced here: 79.9 us
  starting transfers between devices  37.2 us (46%)
  waiting for transfers between devices  24.3 us (30%)
  Pallas kernels  12.7 us (16%)
  local copies, waits for them, and re-layouts  4.18 us (5%)
  other arithmetic  0.92 us (1%)
    ppermute x10, starting transfers between devices, col_swap(): lax.ppermute(value, 'col', [(at, at ^ dz * Y + dy) for at in range(16)])  21.5 us
    ppermute x10, waiting for transfers between devices, col_swap(): lax.ppermute(value, 'col', [(at, at ^ dz * Y + dy) for at in range(16)])  20.7 us
    ppermute x9, starting transfers between devices, row_swap(): lax.ppermute(value, 'row', [(at, at ^ dz * 8 + dx * 2 + dc) for at in ran...  15.7 us
    pallas_call x4, Pallas kernels, tile_stage(): pl.pallas_call(functools.partial(stage_kernel, group, last), out_shape=ou...  9.55 us
    unnamed x22, local copies, waits for them, and re-layouts  4.15 us
    ppermute x9, waiting for transfers between devices, row_swap(): lax.ppermute(value, 'row', [(at, at ^ dz * 8 + dx * 2 + dc) for at in ran...  3.6 us
    pallas_call x1, Pallas kernels, plan(): pl.pallas_call(plan_kernel, out_shape=[jax.ShapeDtypeStruct((many,), jnp....  1.78 us
  transfers between devices with their start and end apart: 19, of which 8 were waited for; matrix products, arithmetic and copies ran while one was open for 1% of the time, Pallas kernels for 13%

profile of v9, /device:TPU:4, one launch (start us, length us, event | category | flops | bytes accessed | tf_op | source)
XLA Modules:
  0.0 79.9 jit_solution(14633636231227403525)
XLA Ops:
  0.0 7.3 %collective-permute-start = (bf16[128,768]{1,0:T(8,128)(2,1)}, bf16[128,768]{1,0:T(8,128)(2,1)S(1)}, u32[]{:S(2)}, u32[]{:S(2)}) collective-permute-start(bf16[128,768]{1,0:T(8,128)(2,1)} %param.8), channel_id=1, source_target_pairs={{0,128},{16,144},{32,160},{48,176},{64,192},{80,208},{96,224},{112... | collective-permute-start | bytes 589832 | tf_op jit(solution)/shard_map/ppermute | solution.py:16
  7.3 1.2 %collective-permute-start.4 = (bf16[128,768]{1,0:T(8,128)(2,1)}, bf16[128,768]{1,0:T(8,128)(2,1)S(1)}, u32[]{:S(2)}, u32[]{:S(2)}) collective-permute-start(bf16[128,768]{1,0:T(8,128)(2,1)} %param.8), channel_id=1, source_target_pairs={{0,32},{16,48},{32,0},{48,16},{64,96},{80,112},{96,64},{112,80},{1... | collective-permute-start | bytes 589832 | tf_op jit(solution)/shard_map/ppermute | solution.py:16
  8.5 2.9 %collective-permute-start.5 = (bf16[128,768]{1,0:T(8,128)(2,1)}, bf16[128,768]{1,0:T(8,128)(2,1)S(1)}, u32[]{:S(2)}, u32[]{:S(2)}) collective-permute-start(bf16[128,768]{1,0:T(8,128)(2,1)} %param.8), channel_id=1, source_target_pairs={{0,64},{16,80},{32,96},{48,112},{64,0},{80,16},{96,32},{112,48},{1... | collective-permute-start | bytes 589832 | tf_op jit(solution)/shard_map/ppermute | solution.py:16
  11.4 2.7 %copy-done.1 = bf16[768,5,768]{2,0,1:T(8,128)(2,1)S(1)} copy-done((bf16[768,5,768]{2,0,1:T(8,128)(2,1)S(1)}, bf16[768,5,768]{2,0,1:T(8,128)(2,1)}, u32[]{:S(2)}) %copy-start.1) | copy-done | bytes 5898264
  14.1 1.3 %copy-done.2 = bf16[1,1,5,8,128,128]{5,4,3,2,1,0:T(8,128)(2,1)S(1)} copy-done((bf16[1,1,5,8,128,128]{5,4,3,2,1,0:T(8,128)(2,1)S(1)}, bf16[1,1,5,8,128,128]{5,4,3,2,1,0:T(8,128)(2,1)}, u32[]{:S(2)}) %copy-start.2) | copy-done | bytes 1310744
  16.9 2.7 %collective-permute-start.2 = (bf16[128,768]{1,0:T(8,128)(2,1)S(1)}, bf16[128,768]{1,0:T(8,128)(2,1)S(1)}, u32[]{:S(2)}, u32[]{:S(2)}) collective-permute-start(bf16[128,768]{1,0:T(8,128)(2,1)S(1)} %collective-permute-done), channel_id=1, source_target_pairs={{0,64},{16,80},{32,96},{48,112},{64,0},{80,16},{96,32},{112,48},{1... | collective-permute-start | bytes 589832 | tf_op jit(solution)/shard_map/ppermute | solution.py:16
  20.6 1.3 %collective-permute-done.6 = bf16[128,768]{1,0:T(8,128)(2,1)S(1)} collective-permute-done((bf16[128,768]{1,0:T(8,128)(2,1)}, bf16[128,768]{1,0:T(8,128)(2,1)S(1)}, u32[]{:S(2)}, u32[]{:S(2)}) %collective-permute-start.6) | collective-permute-done | bytes 196640 | tf_op jit(solution)/shard_map/ppermute | solution.py:16
  22.1 1.8 %plan.1 = (s32[40]{0:T(128)S(1)}, s32[21]{0:T(128)S(1)}) custom-call(s32[5,8]{1,0:T(8,128)S(1)} %fusion.4.table_ref), custom_call_target="tpu_custom_call" | custom-call | tf_op jit(solution)/shard_map/plan/pallas_call | solution.py:134
  23.9 1.8 %tile.4.refs_0_ = f32[2048,768]{1,0:T(8,128)S(1)} custom-call(s32[40]{0:T(128)S(1)} %get-tuple-element.53.codes_ref, s32[21]{0:T(128)S(1)} %get-tuple-element.54.starts_ref, bf16[40,128,128]{2,1,0:T(8,128)(2,1)S(1)} %get-tuple-element.55.blocks_ref, bf16[5,768,768]{2,1,0:T(8,128)(2,1)S(1)} %get-tuple-element.56.weight_ref, ...), custom_call_target="tpu_custom_call", output_to_operand_aliasing={{}: (5, {})} | custom-call | flops 1073741824 | bytes 4194304 | tf_op jit(solution)/shard_map/tile/pallas_call | solution.py:160
  25.8 2.2 %collective-permute-done.1 = bf16[128,768]{1,0:T(8,128)(2,1)S(1)} collective-permute-done((bf16[128,768]{1,0:T(8,128)(2,1)S(1)}, bf16[128,768]{1,0:T(8,128)(2,1)S(1)}, u32[]{:S(2)}, u32[]{:S(2)}) %collective-permute-start.1) | collective-permute-done | bytes 196640 | tf_op jit(solution)/shard_map/ppermute | solution.py:16
  28.0 3.1 %tile.5.refs_0_ = f32[2048,768]{1,0:T(8,128)S(1)} custom-call(s32[40]{0:T(128)S(1)} %get-tuple-element.53.codes_ref, s32[21]{0:T(128)S(1)} %get-tuple-element.54.starts_ref, bf16[40,128,128]{2,1,0:T(8,128)(2,1)S(1)} %get-tuple-element.55.blocks_ref, bf16[5,768,768]{2,1,0:T(8,128)(2,1)S(1)} %get-tuple-element.56.weight_ref, ...), custom_call_target="tpu_custom_call", output_to_operand_aliasing={{}: (5, {})} | custom-call | flops 1073741824 | bytes 4194304 | tf_op jit(solution)/shard_map/tile/pallas_call | solution.py:160
  31.3 2.2 %tile.6.refs_0_ = f32[2048,768]{1,0:T(8,128)S(1)} custom-call(s32[40]{0:T(128)S(1)} %get-tuple-element.53.codes_ref, s32[21]{0:T(128)S(1)} %get-tuple-element.54.starts_ref, bf16[40,128,128]{2,1,0:T(8,128)(2,1)S(1)} %get-tuple-element.55.blocks_ref, bf16[5,768,768]{2,1,0:T(8,128)(2,1)S(1)} %get-tuple-element.56.weight_ref, ...), custom_call_target="tpu_custom_call", output_to_operand_aliasing={{}: (5, {})} | custom-call | flops 1073741824 | bytes 4194304 | tf_op jit(solution)/shard_map/tile/pallas_call | solution.py:160
  33.6 2.4 %tile.7 = (f32[2048,768]{1,0:T(8,128)S(1)}, bf16[3,96,768]{2,1,0:T(8,128)(2,1)S(1)}, bf16[3,96,768]{2,1,0:T(8,128)(2,1)S(1)}, bf16[3,96,768]{2,1,0:T(8,128)(2,1)...) custom-call(s32[40]{0:T(128)S(1)} %get-tuple-element.53.codes_ref, ...), custom_call_target="tpu_custom_call", output_to_operand_aliasing={{0}: (5, {})} | custom-call | flops 1073741824 | bytes 4194304 | tf_op jit(solution)/shard_map/tile/pallas_call | solution.py:160
  36.9 3.7 %collective-permute-start.11 = (bf16[3,96,768]{2,1,0:T(8,128)(2,1)S(1)}, bf16[3,96,768]{2,1,0:T(8,128)(2,1)S(1)}, u32[]{:S(2)}, u32[]{:S(2)}) collective-permute-start(bf16[3,96,768]{2,1,0:T(8,128)(2,1)S(1)} %get-tuple-element.71), channel_id=1, source_target_pairs={{0,2},{1,3},{2,0},{3,1},{4,6},{5,7},{6,4},{7,5},{8,10},{9,11},{10,... | collective-permute-start | bytes 1327112 | tf_op jit(solution)/shard_map/ppermute | solution.py:20
  40.6 1.7 %collective-permute-start.13 = (bf16[3,96,768]{2,1,0:T(8,128)(2,1)S(1)}, bf16[3,96,768]{2,1,0:T(8,128)(2,1)S(1)}, u32[]{:S(2)}, u32[]{:S(2)}) collective-permute-start(bf16[3,96,768]{2,1,0:T(8,128)(2,1)S(1)} %get-tuple-element.73), channel_id=1, source_target_pairs={{0,3},{1,2},{2,1},{3,0},{4,7},{5,6},{6,5},{7,4},{8,11},{9,10},{10,... | collective-permute-start | bytes 1327112 | tf_op jit(solution)/shard_map/ppermute | solution.py:20
  42.3 3.1 %collective-permute-done.9.refs_1_ = bf16[2,4,32,768]{3,2,1,0:T(8,128)(2,1)S(1)} collective-permute-done((bf16[2,4,32,768]{3,2,1,0:T(8,128)(2,1)S(1)}, bf16[2,4,32,768]{3,2,1,0:T(8,128)(2,1)S(1)}, u32[]{:S(2)}, u32[]{:S(2)}) %collective-permute-start.9) | collective-permute-done | bytes 393248 | tf_op jit(solution)/shard_map/ppermute | solution.py:20
  45.5 3.4 %collective-permute-start.10 = (bf16[4,32,768]{2,1,0:T(8,128)(2,1)S(1)}, bf16[4,32,768]{2,1,0:T(8,128)(2,1)S(1)}, u32[]{:S(2)}, u32[]{:S(2)}) collective-permute-start(bf16[4,32,768]{2,1,0:T(8,128)(2,1)S(1)} %get-tuple-element.65), channel_id=1, source_target_pairs={{0,8},{1,9},{2,10},{3,11},{4,12},{5,13},{6,14},{7,15},{8,0},{9,1},... | collective-permute-start | bytes 589832 | tf_op jit(solution)/shard_map/ppermute | solution.py:20
  49.3 8.2 %collective-permute-done.10.refs_1_ = bf16[4,32,768]{2,1,0:T(8,128)(2,1)S(1)} collective-permute-done((bf16[4,32,768]{2,1,0:T(8,128)(2,1)S(1)}, bf16[4,32,768]{2,1,0:T(8,128)(2,1)S(1)}, u32[]{:S(2)}, u32[]{:S(2)}) %collective-permute-start.10) | collective-permute-done | bytes 196640 | tf_op jit(solution)/shard_map/ppermute | solution.py:20
  57.6 5.3 %collective-permute-start.14 = (bf16[2,128,768]{2,1,0:T(8,128)(2,1)S(1)}, bf16[2,128,768]{2,1,0:T(8,128)(2,1)S(1)}, u32[]{:S(2)}, u32[]{:S(2)}) collective-permute-start(bf16[2,128,768]{2,1,0:T(8,128)(2,1)S(1)} %get-tuple-element.81), channel_id=1, source_target_pairs={{0,1},{1,0},{2,3},{3,2},{4,5},{5,4},{6,7},{7,6},{8,9},{9,8},{10,11... | collective-permute-start | bytes 1179656 | tf_op jit(solution)/shard_map/ppermute | solution.py:20
  63.1 1.4 %collective-permute-start.16 = (bf16[96,768]{1,0:T(8,128)(2,1)S(1)}, bf16[96,768]{1,0:T(8,128)(2,1)S(1)}, u32[]{:S(2)}, u32[]{:S(2)}) collective-permute-start(bf16[96,768]{1,0:T(8,128)(2,1)S(1)} %get-tuple-element.85), channel_id=1, source_target_pairs={{0,8},{1,9},{2,10},{3,11},{4,12},{5,13},{6,14},{7,15},{8,0},{9,1},... | collective-permute-start | bytes 442376 | tf_op jit(solution)/shard_map/ppermute | solution.py:20
  66.6 4.8 %collective-permute-done.14.refs_2_ = bf16[2,128,768]{2,1,0:T(8,128)(2,1)S(1)} collective-permute-done((bf16[2,128,768]{2,1,0:T(8,128)(2,1)S(1)}, bf16[2,128,768]{2,1,0:T(8,128)(2,1)S(1)}, u32[]{:S(2)}, u32[]{:S(2)}) %collective-permute-start.14) | collective-permute-done | bytes 393248 | tf_op jit(solution)/shard_map/ppermute | solution.py:20
  71.6 2.9 %collective-permute-start.15 = (bf16[128,768]{1,0:T(8,128)(2,1)S(1)}, bf16[128,768]{1,0:T(8,128)(2,1)S(1)}, u32[]{:S(2)}, u32[]{:S(2)}) collective-permute-start(bf16[128,768]{1,0:T(8,128)(2,1)S(1)} %get-tuple-element.84), channel_id=1, source_target_pairs={{0,3},{1,2},{2,1},{3,0},{4,7},{5,6},{6,5},{7,4},{8,11},{9,10},{10,... | collective-permute-start | bytes 589832 | tf_op jit(solution)/shard_map/ppermute | solution.py:20
  74.5 1.5 %collective-permute-done.16 = bf16[96,768]{1,0:T(8,128)(2,1)S(1)} collective-permute-done((bf16[96,768]{1,0:T(8,128)(2,1)S(1)}, bf16[96,768]{1,0:T(8,128)(2,1)S(1)}, u32[]{:S(2)}, u32[]{:S(2)}) %collective-permute-start.16) | collective-permute-done | bytes 147488 | tf_op jit(solution)/shard_map/ppermute | solution.py:20
  76.6 2.4 %collective-permute-done.15 = bf16[128,768]{1,0:T(8,128)(2,1)S(1)} collective-permute-done((bf16[128,768]{1,0:T(8,128)(2,1)S(1)}, bf16[128,768]{1,0:T(8,128)(2,1)S(1)}, u32[]{:S(2)}, u32[]{:S(2)}) %collective-permute-start.15) | collective-permute-done | bytes 196640 | tf_op jit(solution)/shard_map/ppermute | solution.py:20
  (56 shorter events, 8.2 us)
Async XLA Ops:
  0.0 48.9 %copy-start = (bf16[768,768]{1,0:T(8,128)(2,1)S(1)}, bf16[768,768]{1,0:T(8,128)(2,1)}, u32[]{:S(2)}) copy-start(bf16[768,768]{1,0:T(8,128)(2,1)} %param.9) | copy-start | bytes 3538948
  0.0 22.0 %copy-start.7 = (s32[1,1,5]{2,1,0:T(1,128)S(1)}, s32[1,1,5]{2,1,0:T(1,128)}, u32[]{:S(2)}) copy-start(s32[1,1,5]{2,1,0:T(1,128)} %param.15) | copy-start | bytes 64
  0.0 22.0 %copy-start.5 = (s32[1,1,5,8]{3,1,2,0:T(1,128)S(1)}, s32[1,1,5,8]{3,1,2,0:T(1,128)}, u32[]{:S(2)}) copy-start(s32[1,1,5,8]{3,1,2,0:T(1,128)} %param.13) | copy-start | bytes 484
  0.0 16.3 %collective-permute-start = (bf16[128,768]{1,0:T(8,128)(2,1)}, bf16[128,768]{1,0:T(8,128)(2,1)S(1)}, u32[]{:S(2)}, u32[]{:S(2)}) collective-permute-start(bf16[128,768]{1,0:T(8,128)(2,1)} %param.8), channel_id=1, source_target_pairs={{0,128},{16,144},{32,160},{48,176},{64,192},{80,208},{96,224},{112... | collective-permute-start | bytes 589832 | tf_op jit(solution)/shard_map/ppermute | solution.py:16
  7.3 12.4 %collective-permute-start.4 = (bf16[128,768]{1,0:T(8,128)(2,1)}, bf16[128,768]{1,0:T(8,128)(2,1)S(1)}, u32[]{:S(2)}, u32[]{:S(2)}) collective-permute-start(bf16[128,768]{1,0:T(8,128)(2,1)} %param.8), channel_id=1, source_target_pairs={{0,32},{16,48},{32,0},{48,16},{64,96},{80,112},{96,64},{112,80},{1... | collective-permute-start | bytes 589832 | tf_op jit(solution)/shard_map/ppermute | solution.py:16
  8.5 13.4 %collective-permute-start.6 = (bf16[128,768]{1,0:T(8,128)(2,1)}, bf16[128,768]{1,0:T(8,128)(2,1)S(1)}, u32[]{:S(2)}, u32[]{:S(2)}) collective-permute-start(bf16[128,768]{1,0:T(8,128)(2,1)} %param.8), channel_id=1, source_target_pairs={{0,96},{16,112},{32,64},{48,80},{64,32},{80,48},{96,0},{112,16},{1... | collective-permute-start | bytes 589832 | tf_op jit(solution)/shard_map/ppermute | solution.py:16
  8.5 12.0 %collective-permute-start.5 = (bf16[128,768]{1,0:T(8,128)(2,1)}, bf16[128,768]{1,0:T(8,128)(2,1)S(1)}, u32[]{:S(2)}, u32[]{:S(2)}) collective-permute-start(bf16[128,768]{1,0:T(8,128)(2,1)} %param.8), channel_id=1, source_target_pairs={{0,64},{16,80},{32,96},{48,112},{64,0},{80,16},{96,32},{112,48},{1... | collective-permute-start | bytes 589832 | tf_op jit(solution)/shard_map/ppermute | solution.py:16
  15.4 6.7 %copy-start.6 = (s32[1,1,5,8]{3,1,2,0:T(1,128)S(1)}, s32[1,1,5,8]{3,1,2,0:T(1,128)}, u32[]{:S(2)}) copy-start(s32[1,1,5,8]{3,1,2,0:T(1,128)} %param.14) | copy-start | bytes 484
  16.3 14.8 %collective-permute-start.3 = (bf16[128,768]{1,0:T(8,128)(2,1)S(1)}, bf16[128,768]{1,0:T(8,128)(2,1)S(1)}, u32[]{:S(2)}, u32[]{:S(2)}) collective-permute-start(bf16[128,768]{1,0:T(8,128)(2,1)S(1)} %collective-permute-done), channel_id=1, source_target_pairs={{0,96},{16,112},{32,64},{48,80},{64,32},{80,48},{96,0},{112,16},{1... | collective-permute-start | bytes 589832 | tf_op jit(solution)/shard_map/ppermute | solution.py:16
  16.9 11.1 %collective-permute-start.2 = (bf16[128,768]{1,0:T(8,128)(2,1)S(1)}, bf16[128,768]{1,0:T(8,128)(2,1)S(1)}, u32[]{:S(2)}, u32[]{:S(2)}) collective-permute-start(bf16[128,768]{1,0:T(8,128)(2,1)S(1)} %collective-permute-done), channel_id=1, source_target_pairs={{0,64},{16,80},{32,96},{48,112},{64,0},{80,16},{96,32},{112,48},{1... | collective-permute-start | bytes 589832 | tf_op jit(solution)/shard_map/ppermute | solution.py:16
  19.7 8.3 %collective-permute-start.1 = (bf16[128,768]{1,0:T(8,128)(2,1)S(1)}, bf16[128,768]{1,0:T(8,128)(2,1)S(1)}, u32[]{:S(2)}, u32[]{:S(2)}) collective-permute-start(bf16[128,768]{1,0:T(8,128)(2,1)S(1)} %collective-permute-done), channel_id=1, source_target_pairs={{0,32},{16,48},{32,0},{48,16},{64,96},{80,112},{96,64},{112,80},{1... | collective-permute-start | bytes 589832 | tf_op jit(solution)/shard_map/ppermute | solution.py:16
  21.9 6.1 %collective-permute-start.7 = (bf16[512,768]{1,0:T(8,128)(2,1)S(1)}, bf16[512,768]{1,0:T(8,128)(2,1)S(1)}, u32[]{:S(2)}, u32[]{:S(2)}) collective-permute-start(bf16[512,768]{1,0:T(8,128)(2,1)S(1)} %constant_dynamic-update-slice_fusion.group_ref), channel_id=1, source_target_pairs={{0,16},{16,0},{32,48},{48,32},{64,80},{80,64},{96,112},{112,96},{1... | collective-permute-start | bytes 2359304 | tf_op jit(solution)/shard_map/ppermute | solution.py:16
  31.2 2.4 %collective-permute-start.8 = (bf16[512,768]{1,0:T(8,128)(2,1)S(1)}, bf16[512,768]{1,0:T(8,128)(2,1)S(1)}, u32[]{:S(2)}, u32[]{:S(2)}) collective-permute-start(bf16[512,768]{1,0:T(8,128)(2,1)S(1)} %constant_dynamic-update-slice_fusion.4.group_ref), channel_id=1, source_target_pairs={{0,16},{16,0},{32,48},{48,32},{64,80},{80,64},{96,112},{112,96},{1... | collective-permute-start | bytes 2359304 | tf_op jit(solution)/shard_map/ppermute | solution.py:16
  36.0 43.2 %copy-start.4 = (f32[768]{0:T(1024)S(1)}, f32[768]{0:T(1024)}, u32[]{:S(2)}) copy-start(f32[768]{0:T(1024)} %param.11) | copy-start | bytes 9220
  36.0 9.4 %collective-permute-start.9 = (bf16[2,4,32,768]{3,2,1,0:T(8,128)(2,1)S(1)}, bf16[2,4,32,768]{3,2,1,0:T(8,128)(2,1)S(1)}, u32[]{:S(2)}, u32[]{:S(2)}) collective-permute-start(bf16[2,4,32,768]{3,2,1,0:T(8,128)(2,1)S(1)} %get-tuple-element.62), channel_id=1, source_target_pairs={{0,4},{1,5},{2,6},{3,7},{4,0},{5,1},{6,2},{7,3},{8,12},{9,13},{10,... | collective-permute-start | bytes 1179656 | tf_op jit(solution)/shard_map/ppermute | solution.py:20
  36.9 25.9 %collective-permute-start.11 = (bf16[3,96,768]{2,1,0:T(8,128)(2,1)S(1)}, bf16[3,96,768]{2,1,0:T(8,128)(2,1)S(1)}, u32[]{:S(2)}, u32[]{:S(2)}) collective-permute-start(bf16[3,96,768]{2,1,0:T(8,128)(2,1)S(1)} %get-tuple-element.71), channel_id=1, source_target_pairs={{0,2},{1,3},{2,0},{3,1},{4,6},{5,7},{6,4},{7,5},{8,10},{9,11},{10,... | collective-permute-start | bytes 1327112 | tf_op jit(solution)/shard_map/ppermute | solution.py:20
  40.6 22.2 %collective-permute-start.12 = (bf16[3,96,768]{2,1,0:T(8,128)(2,1)S(1)}, bf16[3,96,768]{2,1,0:T(8,128)(2,1)S(1)}, u32[]{:S(2)}, u32[]{:S(2)}) collective-permute-start(bf16[3,96,768]{2,1,0:T(8,128)(2,1)S(1)} %get-tuple-element.72), channel_id=1, source_target_pairs={{0,1},{1,0},{2,3},{3,2},{4,5},{5,4},{6,7},{7,6},{8,9},{9,8},{10,11... | collective-permute-start | bytes 1327112 | tf_op jit(solution)/shard_map/ppermute | solution.py:20
  40.6 22.2 %collective-permute-start.13 = (bf16[3,96,768]{2,1,0:T(8,128)(2,1)S(1)}, bf16[3,96,768]{2,1,0:T(8,128)(2,1)S(1)}, u32[]{:S(2)}, u32[]{:S(2)}) collective-permute-start(bf16[3,96,768]{2,1,0:T(8,128)(2,1)S(1)} %get-tuple-element.73), channel_id=1, source_target_pairs={{0,3},{1,2},{2,1},{3,0},{4,7},{5,6},{6,5},{7,4},{8,11},{9,10},{10,... | collective-permute-start | bytes 1327112 | tf_op jit(solution)/shard_map/ppermute | solution.py:20
  45.5 12.0 %collective-permute-start.10 = (bf16[4,32,768]{2,1,0:T(8,128)(2,1)S(1)}, bf16[4,32,768]{2,1,0:T(8,128)(2,1)S(1)}, u32[]{:S(2)}, u32[]{:S(2)}) collective-permute-start(bf16[4,32,768]{2,1,0:T(8,128)(2,1)S(1)} %get-tuple-element.65), channel_id=1, source_target_pairs={{0,8},{1,9},{2,10},{3,11},{4,12},{5,13},{6,14},{7,15},{8,0},{9,1},... | collective-permute-start | bytes 589832 | tf_op jit(solution)/shard_map/ppermute | solution.py:20
  57.6 13.9 %collective-permute-start.14 = (bf16[2,128,768]{2,1,0:T(8,128)(2,1)S(1)}, bf16[2,128,768]{2,1,0:T(8,128)(2,1)S(1)}, u32[]{:S(2)}, u32[]{:S(2)}) collective-permute-start(bf16[2,128,768]{2,1,0:T(8,128)(2,1)S(1)} %get-tuple-element.81), channel_id=1, source_target_pairs={{0,1},{1,0},{2,3},{3,2},{4,5},{5,4},{6,7},{7,6},{8,9},{9,8},{10,11... | collective-permute-start | bytes 1179656 | tf_op jit(solution)/shard_map/ppermute | solution.py:20
  63.1 12.9 %collective-permute-start.16 = (bf16[96,768]{1,0:T(8,128)(2,1)S(1)}, bf16[96,768]{1,0:T(8,128)(2,1)S(1)}, u32[]{:S(2)}, u32[]{:S(2)}) collective-permute-start(bf16[96,768]{1,0:T(8,128)(2,1)S(1)} %get-tuple-element.85), channel_id=1, source_target_pairs={{0,8},{1,9},{2,10},{3,11},{4,12},{5,13},{6,14},{7,15},{8,0},{9,1},... | collective-permute-start | bytes 442376 | tf_op jit(solution)/shard_map/ppermute | solution.py:20
  64.5 11.5 %collective-permute-start.17 = (bf16[96,768]{1,0:T(8,128)(2,1)S(1)}, bf16[96,768]{1,0:T(8,128)(2,1)S(1)}, u32[]{:S(2)}, u32[]{:S(2)}) collective-permute-start(bf16[96,768]{1,0:T(8,128)(2,1)S(1)} %get-tuple-element.86), channel_id=1, source_target_pairs={{0,12},{1,13},{2,14},{3,15},{4,8},{5,9},{6,10},{7,11},{8,4},{9,5},... | collective-permute-start | bytes 442376 | tf_op jit(solution)/shard_map/ppermute | solution.py:20
  65.6 10.9 %collective-permute-start.18 = (bf16[96,768]{1,0:T(8,128)(2,1)S(1)}, bf16[96,768]{1,0:T(8,128)(2,1)S(1)}, u32[]{:S(2)}, u32[]{:S(2)}) collective-permute-start(bf16[96,768]{1,0:T(8,128)(2,1)S(1)} %get-tuple-element.80), channel_id=1, source_target_pairs={{0,4},{1,5},{2,6},{3,7},{4,0},{5,1},{6,2},{7,3},{8,12},{9,13},{10,... | collective-permute-start | bytes 442376 | tf_op jit(solution)/shard_map/ppermute | solution.py:20
  71.6 7.5 %collective-permute-start.15 = (bf16[128,768]{1,0:T(8,128)(2,1)S(1)}, bf16[128,768]{1,0:T(8,128)(2,1)S(1)}, u32[]{:S(2)}, u32[]{:S(2)}) collective-permute-start(bf16[128,768]{1,0:T(8,128)(2,1)S(1)} %get-tuple-element.84), channel_id=1, source_target_pairs={{0,3},{1,2},{2,1},{3,0},{4,7},{5,6},{6,5},{7,4},{8,11},{9,10},{10,... | collective-permute-start | bytes 589832 | tf_op jit(solution)/shard_map/ppermute | solution.py:20
  (3 other events, 4.9 us)

commit v10 on v9

--- a/solution.py
+++ b/solution.py
@@ -245,10 +245,10 @@
     near = jnp.concatenate(near_parts, axis=0)
     near_other = row_swap(near, 0, 0, 1)
     (total,) = stage(0, near, total)
-    (total,) = stage(1, near_other, total)
     far_parts[-1], total = lax.optimization_barrier((far_parts[-1], total))
     rest = jnp.concatenate(far_parts, axis=0)
     rest_other = row_swap(rest, 0, 0, 1)
+    (total,) = stage(1, near_other, total)
     (total,) = stage(2, rest, total)
     return stage(3, rest_other, total)[1:]
 

time: 80.7 us -> 80.4 us (level)
  the two profiles are of different devices: /device:TPU:4 before, /device:TPU:1 now
where the time goes in v10:
time: 80.4 us; the launch traced here: 80.9 us
  starting transfers between devices  35.5 us (44%)
  waiting for transfers between devices  28.5 us (35%)
  Pallas kernels  11.2 us (14%)
  local copies, waits for them, and re-layouts  4.18 us (5%)
  other arithmetic  0.93 us (1%)
    ppermute x10, waiting for transfers between devices, col_swap(): lax.ppermute(value, 'col', [(at, at ^ dz * Y + dy) for at in range(16)])  26.8 us
    ppermute x9, starting transfers between devices, row_swap(): lax.ppermute(value, 'row', [(at, at ^ dz * 8 + dx * 2 + dc) for at in ran...  20.4 us
    ppermute x10, starting transfers between devices, col_swap(): lax.ppermute(value, 'col', [(at, at ^ dz * Y + dy) for at in range(16)])  15.2 us
    pallas_call x4, Pallas kernels, tile_stage(): pl.pallas_call(functools.partial(stage_kernel, group, last), out_shape=ou...  8.21 us
    unnamed x22, local copies, waits for them, and re-layouts  4.14 us
    ppermute x9, waiting for transfers between devices, row_swap(): lax.ppermute(value, 'row', [(at, at ^ dz * 8 + dx * 2 + dc) for at in ran...  1.71 us
    pallas_call x1, Pallas kernels, plan(): pl.pallas_call(plan_kernel, out_shape=[jax.ShapeDtypeStruct((many,), jnp....  1.62 us
  transfers between devices with their start and end apart: 19, of which 8 were waited for; matrix products, arithmetic and copies ran while one was open for 1% of the time, Pallas kernels for 11%

profile of v10, /device:TPU:1, one launch (start us, length us, event | category | flops | bytes accessed | tf_op | source)
XLA Modules:
  0.0 80.9 jit_solution(13159676471264667479)
XLA Ops:
  0.0 7.8 %collective-permute-start = (bf16[128,768]{1,0:T(8,128)(2,1)}, bf16[128,768]{1,0:T(8,128)(2,1)S(1)}, u32[]{:S(2)}, u32[]{:S(2)}) collective-permute-start(bf16[128,768]{1,0:T(8,128)(2,1)} %param.8), channel_id=1, source_target_pairs={{0,128},{16,144},{32,160},{48,176},{64,192},{80,208},{96,224},{112... | collective-permute-start | bytes 589832 | tf_op jit(solution)/shard_map/ppermute | solution.py:16
  7.8 1.2 %collective-permute-start.4 = (bf16[128,768]{1,0:T(8,128)(2,1)}, bf16[128,768]{1,0:T(8,128)(2,1)S(1)}, u32[]{:S(2)}, u32[]{:S(2)}) collective-permute-start(bf16[128,768]{1,0:T(8,128)(2,1)} %param.8), channel_id=1, source_target_pairs={{0,32},{16,48},{32,0},{48,16},{64,96},{80,112},{96,64},{112,80},{1... | collective-permute-start | bytes 589832 | tf_op jit(solution)/shard_map/ppermute | solution.py:16
  9.0 1.8 %collective-permute-start.6 = (bf16[128,768]{1,0:T(8,128)(2,1)}, bf16[128,768]{1,0:T(8,128)(2,1)S(1)}, u32[]{:S(2)}, u32[]{:S(2)}) collective-permute-start(bf16[128,768]{1,0:T(8,128)(2,1)} %param.8), channel_id=1, source_target_pairs={{0,96},{16,112},{32,64},{48,80},{64,32},{80,48},{96,0},{112,16},{1... | collective-permute-start | bytes 589832 | tf_op jit(solution)/shard_map/ppermute | solution.py:16
  11.5 2.7 %copy-done.1 = bf16[768,5,768]{2,0,1:T(8,128)(2,1)S(1)} copy-done((bf16[768,5,768]{2,0,1:T(8,128)(2,1)S(1)}, bf16[768,5,768]{2,0,1:T(8,128)(2,1)}, u32[]{:S(2)}) %copy-start.1) | copy-done | bytes 5898264
  14.2 1.3 %copy-done.2 = bf16[1,1,5,8,128,128]{5,4,3,2,1,0:T(8,128)(2,1)S(1)} copy-done((bf16[1,1,5,8,128,128]{5,4,3,2,1,0:T(8,128)(2,1)S(1)}, bf16[1,1,5,8,128,128]{5,4,3,2,1,0:T(8,128)(2,1)}, u32[]{:S(2)}) %copy-start.2) | copy-done | bytes 1310744
  16.4 2.2 %collective-permute-start.3 = (bf16[128,768]{1,0:T(8,128)(2,1)S(1)}, bf16[128,768]{1,0:T(8,128)(2,1)S(1)}, u32[]{:S(2)}, u32[]{:S(2)}) collective-permute-start(bf16[128,768]{1,0:T(8,128)(2,1)S(1)} %collective-permute-done), channel_id=1, source_target_pairs={{0,96},{16,112},{32,64},{48,80},{64,32},{80,48},{96,0},{112,16},{1... | collective-permute-start | bytes 589832 | tf_op jit(solution)/shard_map/ppermute | solution.py:16
  20.0 3.7 %collective-permute-start.8 = (bf16[512,768]{1,0:T(8,128)(2,1)S(1)}, bf16[512,768]{1,0:T(8,128)(2,1)S(1)}, u32[]{:S(2)}, u32[]{:S(2)}) collective-permute-start(bf16[512,768]{1,0:T(8,128)(2,1)S(1)} %constant_dynamic-update-slice_fusion.group_ref), channel_id=1, source_target_pairs={{0,16},{16,0},{32,48},{48,32},{64,80},{80,64},{96,112},{112,96},{1... | collective-permute-start | bytes 2359304 | tf_op jit(solution)/shard_map/ppermute | solution.py:16
  23.7 1.6 %plan.1 = (s32[40]{0:T(128)S(1)}, s32[21]{0:T(128)S(1)}) custom-call(s32[5,8]{1,0:T(8,128)S(1)} %fusion.4.table_ref), custom_call_target="tpu_custom_call" | custom-call | tf_op jit(solution)/shard_map/plan/pallas_call | solution.py:134
  25.4 1.7 %tile.4.refs_0_ = f32[2048,768]{1,0:T(8,128)S(1)} custom-call(s32[40]{0:T(128)S(1)} %get-tuple-element.53.codes_ref, s32[21]{0:T(128)S(1)} %get-tuple-element.54.starts_ref, bf16[40,128,128]{2,1,0:T(8,128)(2,1)S(1)} %get-tuple-element.55.blocks_ref, bf16[5,768,768]{2,1,0:T(8,128)(2,1)S(1)} %get-tuple-element.56.weight_ref, ...), custom_call_target="tpu_custom_call", output_to_operand_aliasing={{}: (5, {})} | custom-call | flops 1073741824 | bytes 4194304 | tf_op jit(solution)/shard_map/tile/pallas_call | solution.py:160
  27.1 1.6 %collective-permute-done.3 = bf16[128,768]{1,0:T(8,128)(2,1)S(1)} collective-permute-done((bf16[128,768]{1,0:T(8,128)(2,1)S(1)}, bf16[128,768]{1,0:T(8,128)(2,1)S(1)}, u32[]{:S(2)}, u32[]{:S(2)}) %collective-permute-start.3) | collective-permute-done | bytes 196640 | tf_op jit(solution)/shard_map/ppermute | solution.py:16
  28.7 1.9 %collective-permute-start.7 = (bf16[512,768]{1,0:T(8,128)(2,1)S(1)}, bf16[512,768]{1,0:T(8,128)(2,1)S(1)}, u32[]{:S(2)}, u32[]{:S(2)}) collective-permute-start(bf16[512,768]{1,0:T(8,128)(2,1)S(1)} %constant_dynamic-update-slice_fusion.4.group_ref), channel_id=1, source_target_pairs={{0,16},{16,0},{32,48},{48,32},{64,80},{80,64},{96,112},{112,96},{1... | collective-permute-start | bytes 2359304 | tf_op jit(solution)/shard_map/ppermute | solution.py:16
  30.6 2.1 %tile.5.refs_0_ = f32[2048,768]{1,0:T(8,128)S(1)} custom-call(s32[40]{0:T(128)S(1)} %get-tuple-element.53.codes_ref, s32[21]{0:T(128)S(1)} %get-tuple-element.54.starts_ref, bf16[40,128,128]{2,1,0:T(8,128)(2,1)S(1)} %get-tuple-element.55.blocks_ref, bf16[5,768,768]{2,1,0:T(8,128)(2,1)S(1)} %get-tuple-element.56.weight_ref, ...), custom_call_target="tpu_custom_call", output_to_operand_aliasing={{}: (5, {})} | custom-call | flops 1073741824 | bytes 4194304 | tf_op jit(solution)/shard_map/tile/pallas_call | solution.py:160
  32.7 2.4 %tile.6.refs_0_ = f32[2048,768]{1,0:T(8,128)S(1)} custom-call(s32[40]{0:T(128)S(1)} %get-tuple-element.53.codes_ref, s32[21]{0:T(128)S(1)} %get-tuple-element.54.starts_ref, bf16[40,128,128]{2,1,0:T(8,128)(2,1)S(1)} %get-tuple-element.55.blocks_ref, bf16[5,768,768]{2,1,0:T(8,128)(2,1)S(1)} %get-tuple-element.56.weight_ref, ...), custom_call_target="tpu_custom_call", output_to_operand_aliasing={{}: (5, {})} | custom-call | flops 1073741824 | bytes 4194304 | tf_op jit(solution)/shard_map/tile/pallas_call | solution.py:160
  35.1 2.0 %tile.7 = (f32[2048,768]{1,0:T(8,128)S(1)}, bf16[3,96,768]{2,1,0:T(8,128)(2,1)S(1)}, bf16[3,96,768]{2,1,0:T(8,128)(2,1)S(1)}, bf16[3,96,768]{2,1,0:T(8,128)(2,1)...) custom-call(s32[40]{0:T(128)S(1)} %get-tuple-element.53.codes_ref, ...), custom_call_target="tpu_custom_call", output_to_operand_aliasing={{0}: (5, {})} | custom-call | flops 1073741824 | bytes 4194304 | tf_op jit(solution)/shard_map/tile/pallas_call | solution.py:160
  37.2 2.2 %collective-permute-start.9 = (bf16[2,4,32,768]{3,2,1,0:T(8,128)(2,1)S(1)}, bf16[2,4,32,768]{3,2,1,0:T(8,128)(2,1)S(1)}, u32[]{:S(2)}, u32[]{:S(2)}) collective-permute-start(bf16[2,4,32,768]{3,2,1,0:T(8,128)(2,1)S(1)} %get-tuple-element.62), channel_id=1, source_target_pairs={{0,4},{1,5},{2,6},{3,7},{4,0},{5,1},{6,2},{7,3},{8,12},{9,13},{10,... | collective-permute-start | bytes 1179656 | tf_op jit(solution)/shard_map/ppermute | solution.py:20
  39.3 2.9 %collective-permute-start.11 = (bf16[3,96,768]{2,1,0:T(8,128)(2,1)S(1)}, bf16[3,96,768]{2,1,0:T(8,128)(2,1)S(1)}, u32[]{:S(2)}, u32[]{:S(2)}) collective-permute-start(bf16[3,96,768]{2,1,0:T(8,128)(2,1)S(1)} %get-tuple-element.71), channel_id=1, source_target_pairs={{0,2},{1,3},{2,0},{3,1},{4,6},{5,7},{6,4},{7,5},{8,10},{9,11},{10,... | collective-permute-start | bytes 1327112 | tf_op jit(solution)/shard_map/ppermute | solution.py:20
  42.3 2.2 %collective-permute-start.12 = (bf16[3,96,768]{2,1,0:T(8,128)(2,1)S(1)}, bf16[3,96,768]{2,1,0:T(8,128)(2,1)S(1)}, u32[]{:S(2)}, u32[]{:S(2)}) collective-permute-start(bf16[3,96,768]{2,1,0:T(8,128)(2,1)S(1)} %get-tuple-element.72), channel_id=1, source_target_pairs={{0,1},{1,0},{2,3},{3,2},{4,5},{5,4},{6,7},{7,6},{8,9},{9,8},{10,11... | collective-permute-start | bytes 1327112 | tf_op jit(solution)/shard_map/ppermute | solution.py:20
  44.6 3.7 %collective-permute-done.9.refs_1_ = bf16[2,4,32,768]{3,2,1,0:T(8,128)(2,1)S(1)} collective-permute-done((bf16[2,4,32,768]{3,2,1,0:T(8,128)(2,1)S(1)}, bf16[2,4,32,768]{3,2,1,0:T(8,128)(2,1)S(1)}, u32[]{:S(2)}, u32[]{:S(2)}) %collective-permute-start.9) | collective-permute-done | bytes 393248 | tf_op jit(solution)/shard_map/ppermute | solution.py:20
  48.9 10.7 %collective-permute-done.10.refs_1_ = bf16[4,32,768]{2,1,0:T(8,128)(2,1)S(1)} collective-permute-done((bf16[4,32,768]{2,1,0:T(8,128)(2,1)S(1)}, bf16[4,32,768]{2,1,0:T(8,128)(2,1)S(1)}, u32[]{:S(2)}, u32[]{:S(2)}) %collective-permute-start.10) | collective-permute-done | bytes 196640 | tf_op jit(solution)/shard_map/ppermute | solution.py:20
  59.6 4.6 %collective-permute-start.14 = (bf16[2,128,768]{2,1,0:T(8,128)(2,1)S(1)}, bf16[2,128,768]{2,1,0:T(8,128)(2,1)S(1)}, u32[]{:S(2)}, u32[]{:S(2)}) collective-permute-start(bf16[2,128,768]{2,1,0:T(8,128)(2,1)S(1)} %get-tuple-element.81), channel_id=1, source_target_pairs={{0,1},{1,0},{2,3},{3,2},{4,5},{5,4},{6,7},{7,6},{8,9},{9,8},{10,11... | collective-permute-start | bytes 1179656 | tf_op jit(solution)/shard_map/ppermute | solution.py:20
  64.5 1.6 %collective-permute-start.17 = (bf16[96,768]{1,0:T(8,128)(2,1)S(1)}, bf16[96,768]{1,0:T(8,128)(2,1)S(1)}, u32[]{:S(2)}, u32[]{:S(2)}) collective-permute-start(bf16[96,768]{1,0:T(8,128)(2,1)S(1)} %get-tuple-element.86), channel_id=1, source_target_pairs={{0,12},{1,13},{2,14},{3,15},{4,8},{5,9},{6,10},{7,11},{8,4},{9,5},... | collective-permute-start | bytes 442376 | tf_op jit(solution)/shard_map/ppermute | solution.py:20
  67.2 6.1 %collective-permute-done.14.refs_2_ = bf16[2,128,768]{2,1,0:T(8,128)(2,1)S(1)} collective-permute-done((bf16[2,128,768]{2,1,0:T(8,128)(2,1)S(1)}, bf16[2,128,768]{2,1,0:T(8,128)(2,1)S(1)}, u32[]{:S(2)}, u32[]{:S(2)}) %collective-permute-start.14) | collective-permute-done | bytes 393248 | tf_op jit(solution)/shard_map/ppermute | solution.py:20
  73.7 3.0 %collective-permute-done.16 = bf16[96,768]{1,0:T(8,128)(2,1)S(1)} collective-permute-done((bf16[96,768]{1,0:T(8,128)(2,1)S(1)}, bf16[96,768]{1,0:T(8,128)(2,1)S(1)}, u32[]{:S(2)}, u32[]{:S(2)}) %collective-permute-start.16) | collective-permute-done | bytes 147488 | tf_op jit(solution)/shard_map/ppermute | solution.py:20
  77.1 3.0 %collective-permute-done.15 = bf16[128,768]{1,0:T(8,128)(2,1)S(1)} collective-permute-done((bf16[128,768]{1,0:T(8,128)(2,1)S(1)}, bf16[128,768]{1,0:T(8,128)(2,1)S(1)}, u32[]{:S(2)}, u32[]{:S(2)}) %collective-permute-start.15) | collective-permute-done | bytes 196640 | tf_op jit(solution)/shard_map/ppermute | solution.py:20
  (56 shorter events, 6.7 us)
Async XLA Ops:
  0.0 48.5 %copy-start = (bf16[768,768]{1,0:T(8,128)(2,1)S(1)}, bf16[768,768]{1,0:T(8,128)(2,1)}, u32[]{:S(2)}) copy-start(bf16[768,768]{1,0:T(8,128)(2,1)} %param.9) | copy-start | bytes 3538948
  0.0 23.7 %copy-start.7 = (s32[1,1,5]{2,1,0:T(1,128)S(1)}, s32[1,1,5]{2,1,0:T(1,128)}, u32[]{:S(2)}) copy-start(s32[1,1,5]{2,1,0:T(1,128)} %param.15) | copy-start | bytes 64
  0.0 23.7 %copy-start.5 = (s32[1,1,5,8]{3,1,2,0:T(1,128)S(1)}, s32[1,1,5,8]{3,1,2,0:T(1,128)}, u32[]{:S(2)}) copy-start(s32[1,1,5,8]{3,1,2,0:T(1,128)} %param.13) | copy-start | bytes 484
  0.0 16.4 %collective-permute-start = (bf16[128,768]{1,0:T(8,128)(2,1)}, bf16[128,768]{1,0:T(8,128)(2,1)S(1)}, u32[]{:S(2)}, u32[]{:S(2)}) collective-permute-start(bf16[128,768]{1,0:T(8,128)(2,1)} %param.8), channel_id=1, source_target_pairs={{0,128},{16,144},{32,160},{48,176},{64,192},{80,208},{96,224},{112... | collective-permute-start | bytes 589832 | tf_op jit(solution)/shard_map/ppermute | solution.py:16
  7.8 11.3 %collective-permute-start.4 = (bf16[128,768]{1,0:T(8,128)(2,1)}, bf16[128,768]{1,0:T(8,128)(2,1)S(1)}, u32[]{:S(2)}, u32[]{:S(2)}) collective-permute-start(bf16[128,768]{1,0:T(8,128)(2,1)} %param.8), channel_id=1, source_target_pairs={{0,32},{16,48},{32,0},{48,16},{64,96},{80,112},{96,64},{112,80},{1... | collective-permute-start | bytes 589832 | tf_op jit(solution)/shard_map/ppermute | solution.py:16
  9.0 10.9 %collective-permute-start.6 = (bf16[128,768]{1,0:T(8,128)(2,1)}, bf16[128,768]{1,0:T(8,128)(2,1)S(1)}, u32[]{:S(2)}, u32[]{:S(2)}) collective-permute-start(bf16[128,768]{1,0:T(8,128)(2,1)} %param.8), channel_id=1, source_target_pairs={{0,96},{16,112},{32,64},{48,80},{64,32},{80,48},{96,0},{112,16},{1... | collective-permute-start | bytes 589832 | tf_op jit(solution)/shard_map/ppermute | solution.py:16
  10.9 9.1 %collective-permute-start.5 = (bf16[128,768]{1,0:T(8,128)(2,1)}, bf16[128,768]{1,0:T(8,128)(2,1)S(1)}, u32[]{:S(2)}, u32[]{:S(2)}) collective-permute-start(bf16[128,768]{1,0:T(8,128)(2,1)} %param.8), channel_id=1, source_target_pairs={{0,64},{16,80},{32,96},{48,112},{64,0},{80,16},{96,32},{112,48},{1... | collective-permute-start | bytes 589832 | tf_op jit(solution)/shard_map/ppermute | solution.py:16
  15.5 8.2 %copy-start.6 = (s32[1,1,5,8]{3,1,2,0:T(1,128)S(1)}, s32[1,1,5,8]{3,1,2,0:T(1,128)}, u32[]{:S(2)}) copy-start(s32[1,1,5,8]{3,1,2,0:T(1,128)} %param.14) | copy-start | bytes 484
  16.4 12.2 %collective-permute-start.3 = (bf16[128,768]{1,0:T(8,128)(2,1)S(1)}, bf16[128,768]{1,0:T(8,128)(2,1)S(1)}, u32[]{:S(2)}, u32[]{:S(2)}) collective-permute-start(bf16[128,768]{1,0:T(8,128)(2,1)S(1)} %collective-permute-done), channel_id=1, source_target_pairs={{0,96},{16,112},{32,64},{48,80},{64,32},{80,48},{96,0},{112,16},{1... | collective-permute-start | bytes 589832 | tf_op jit(solution)/shard_map/ppermute | solution.py:16
  18.6 10.1 %collective-permute-start.2 = (bf16[128,768]{1,0:T(8,128)(2,1)S(1)}, bf16[128,768]{1,0:T(8,128)(2,1)S(1)}, u32[]{:S(2)}, u32[]{:S(2)}) collective-permute-start(bf16[128,768]{1,0:T(8,128)(2,1)S(1)} %collective-permute-done), channel_id=1, source_target_pairs={{0,64},{16,80},{32,96},{48,112},{64,0},{80,16},{96,32},{112,48},{1... | collective-permute-start | bytes 589832 | tf_op jit(solution)/shard_map/ppermute | solution.py:16
  19.1 9.5 %collective-permute-start.1 = (bf16[128,768]{1,0:T(8,128)(2,1)S(1)}, bf16[128,768]{1,0:T(8,128)(2,1)S(1)}, u32[]{:S(2)}, u32[]{:S(2)}) collective-permute-start(bf16[128,768]{1,0:T(8,128)(2,1)S(1)} %collective-permute-done), channel_id=1, source_target_pairs={{0,32},{16,48},{32,0},{48,16},{64,96},{80,112},{96,64},{112,80},{1... | collective-permute-start | bytes 589832 | tf_op jit(solution)/shard_map/ppermute | solution.py:16
  20.0 10.6 %collective-permute-start.8 = (bf16[512,768]{1,0:T(8,128)(2,1)S(1)}, bf16[512,768]{1,0:T(8,128)(2,1)S(1)}, u32[]{:S(2)}, u32[]{:S(2)}) collective-permute-start(bf16[512,768]{1,0:T(8,128)(2,1)S(1)} %constant_dynamic-update-slice_fusion.group_ref), channel_id=1, source_target_pairs={{0,16},{16,0},{32,48},{48,32},{64,80},{80,64},{96,112},{112,96},{1... | collective-permute-start | bytes 2359304 | tf_op jit(solution)/shard_map/ppermute | solution.py:16
  28.7 6.4 %collective-permute-start.7 = (bf16[512,768]{1,0:T(8,128)(2,1)S(1)}, bf16[512,768]{1,0:T(8,128)(2,1)S(1)}, u32[]{:S(2)}, u32[]{:S(2)}) collective-permute-start(bf16[512,768]{1,0:T(8,128)(2,1)S(1)} %constant_dynamic-update-slice_fusion.4.group_ref), channel_id=1, source_target_pairs={{0,16},{16,0},{32,48},{48,32},{64,80},{80,64},{96,112},{112,96},{1... | collective-permute-start | bytes 2359304 | tf_op jit(solution)/shard_map/ppermute | solution.py:16
  37.2 43.0 %copy-start.4 = (f32[768]{0:T(1024)S(1)}, f32[768]{0:T(1024)}, u32[]{:S(2)}) copy-start(f32[768]{0:T(1024)} %param.11) | copy-start | bytes 9220
  37.2 11.2 %collective-permute-start.9 = (bf16[2,4,32,768]{3,2,1,0:T(8,128)(2,1)S(1)}, bf16[2,4,32,768]{3,2,1,0:T(8,128)(2,1)S(1)}, u32[]{:S(2)}, u32[]{:S(2)}) collective-permute-start(bf16[2,4,32,768]{3,2,1,0:T(8,128)(2,1)S(1)} %get-tuple-element.62), channel_id=1, source_target_pairs={{0,4},{1,5},{2,6},{3,7},{4,0},{5,1},{6,2},{7,3},{8,12},{9,13},{10,... | collective-permute-start | bytes 1179656 | tf_op jit(solution)/shard_map/ppermute | solution.py:20
  39.3 24.9 %collective-permute-start.11 = (bf16[3,96,768]{2,1,0:T(8,128)(2,1)S(1)}, bf16[3,96,768]{2,1,0:T(8,128)(2,1)S(1)}, u32[]{:S(2)}, u32[]{:S(2)}) collective-permute-start(bf16[3,96,768]{2,1,0:T(8,128)(2,1)S(1)} %get-tuple-element.71), channel_id=1, source_target_pairs={{0,2},{1,3},{2,0},{3,1},{4,6},{5,7},{6,4},{7,5},{8,10},{9,11},{10,... | collective-permute-start | bytes 1327112 | tf_op jit(solution)/shard_map/ppermute | solution.py:20
  42.3 22.0 %collective-permute-start.12 = (bf16[3,96,768]{2,1,0:T(8,128)(2,1)S(1)}, bf16[3,96,768]{2,1,0:T(8,128)(2,1)S(1)}, u32[]{:S(2)}, u32[]{:S(2)}) collective-permute-start(bf16[3,96,768]{2,1,0:T(8,128)(2,1)S(1)} %get-tuple-element.72), channel_id=1, source_target_pairs={{0,1},{1,0},{2,3},{3,2},{4,5},{5,4},{6,7},{7,6},{8,9},{9,8},{10,11... | collective-permute-start | bytes 1327112 | tf_op jit(solution)/shard_map/ppermute | solution.py:20
  44.5 19.7 %collective-permute-start.13 = (bf16[3,96,768]{2,1,0:T(8,128)(2,1)S(1)}, bf16[3,96,768]{2,1,0:T(8,128)(2,1)S(1)}, u32[]{:S(2)}, u32[]{:S(2)}) collective-permute-start(bf16[3,96,768]{2,1,0:T(8,128)(2,1)S(1)} %get-tuple-element.73), channel_id=1, source_target_pairs={{0,3},{1,2},{2,1},{3,0},{4,7},{5,6},{6,5},{7,4},{8,11},{9,10},{10,... | collective-permute-start | bytes 1327112 | tf_op jit(solution)/shard_map/ppermute | solution.py:20
  48.4 11.1 %collective-permute-start.10 = (bf16[4,32,768]{2,1,0:T(8,128)(2,1)S(1)}, bf16[4,32,768]{2,1,0:T(8,128)(2,1)S(1)}, u32[]{:S(2)}, u32[]{:S(2)}) collective-permute-start(bf16[4,32,768]{2,1,0:T(8,128)(2,1)S(1)} %get-tuple-element.65), channel_id=1, source_target_pairs={{0,8},{1,9},{2,10},{3,11},{4,12},{5,13},{6,14},{7,15},{8,0},{9,1},... | collective-permute-start | bytes 589832 | tf_op jit(solution)/shard_map/ppermute | solution.py:20
  59.6 13.7 %collective-permute-start.14 = (bf16[2,128,768]{2,1,0:T(8,128)(2,1)S(1)}, bf16[2,128,768]{2,1,0:T(8,128)(2,1)S(1)}, u32[]{:S(2)}, u32[]{:S(2)}) collective-permute-start(bf16[2,128,768]{2,1,0:T(8,128)(2,1)S(1)} %get-tuple-element.81), channel_id=1, source_target_pairs={{0,1},{1,0},{2,3},{3,2},{4,5},{5,4},{6,7},{7,6},{8,9},{9,8},{10,11... | collective-permute-start | bytes 1179656 | tf_op jit(solution)/shard_map/ppermute | solution.py:20
  64.4 12.3 %collective-permute-start.16 = (bf16[96,768]{1,0:T(8,128)(2,1)S(1)}, bf16[96,768]{1,0:T(8,128)(2,1)S(1)}, u32[]{:S(2)}, u32[]{:S(2)}) collective-permute-start(bf16[96,768]{1,0:T(8,128)(2,1)S(1)} %get-tuple-element.85), channel_id=1, source_target_pairs={{0,8},{1,9},{2,10},{3,11},{4,12},{5,13},{6,14},{7,15},{8,0},{9,1},... | collective-permute-start | bytes 442376 | tf_op jit(solution)/shard_map/ppermute | solution.py:20
  64.5 12.2 %collective-permute-start.17 = (bf16[96,768]{1,0:T(8,128)(2,1)S(1)}, bf16[96,768]{1,0:T(8,128)(2,1)S(1)}, u32[]{:S(2)}, u32[]{:S(2)}) collective-permute-start(bf16[96,768]{1,0:T(8,128)(2,1)S(1)} %get-tuple-element.86), channel_id=1, source_target_pairs={{0,12},{1,13},{2,14},{3,15},{4,8},{5,9},{6,10},{7,11},{8,4},{9,5},... | collective-permute-start | bytes 442376 | tf_op jit(solution)/shard_map/ppermute | solution.py:20
  66.2 10.8 %collective-permute-start.18 = (bf16[96,768]{1,0:T(8,128)(2,1)S(1)}, bf16[96,768]{1,0:T(8,128)(2,1)S(1)}, u32[]{:S(2)}, u32[]{:S(2)}) collective-permute-start(bf16[96,768]{1,0:T(8,128)(2,1)S(1)} %get-tuple-element.80), channel_id=1, source_target_pairs={{0,4},{1,5},{2,6},{3,7},{4,0},{5,1},{6,2},{7,3},{8,12},{9,13},{10,... | collective-permute-start | bytes 442376 | tf_op jit(solution)/shard_map/ppermute | solution.py:20
  73.4 6.7 %collective-permute-start.15 = (bf16[128,768]{1,0:T(8,128)(2,1)S(1)}, bf16[128,768]{1,0:T(8,128)(2,1)S(1)}, u32[]{:S(2)}, u32[]{:S(2)}) collective-permute-start(bf16[128,768]{1,0:T(8,128)(2,1)S(1)} %get-tuple-element.84), channel_id=1, source_target_pairs={{0,3},{1,2},{2,1},{3,0},{4,7},{5,6},{6,5},{7,4},{8,11},{9,10},{10,... | collective-permute-start | bytes 589832 | tf_op jit(solution)/shard_map/ppermute | solution.py:20
  (3 other events, 4.9 us)

commit v11 on v5

--- a/solution.py
+++ b/solution.py
@@ -274,7 +274,7 @@
     y_in, across = lax.optimization_barrier((y_in, across))
     shapes = [jax.ShapeDtypeStruct(own.shape[1:], bf16)] * (Z - 1)
     y_send = list(small(merge_y, shapes, y_parts[0], *y_in))
-    y_last = [col_swap(y_send[e - 1], e, 0) for e in (2, 3, 1)]
+    y_last = [col_swap(y_send[e - 1], e, 0) for e in (1, 2, 3)]
     y_send[0], got = lax.optimization_barrier((y_send[0], got))
     shapes = [jax.ShapeDtypeStruct(block, f32), jax.ShapeDtypeStruct(block, bf16)]
     here, send = small(merge_z_last, shapes, here, across, got)

time: 80.2 us -> 81.1 us (1.011)
  Pallas kernels: 11.7 us -> 14.1 us
  waiting for transfers between devices: 30.6 us -> 28.7 us
    pallas_call x4, Pallas kernels: 9.11 us -> 11.4 us  [tile_stage(): pl.pallas_call(functools.partial(stage_kernel, group, first, last), out_s...]
    ppermute x9, waiting for transfers between devices: 4.43 us -> 2.89 us  [row_swap(): lax.ppermute(value, 'row', [(at, at ^ dz * 8 + dx * 2 + dc) for at in ran...]
  transfers between devices with their start and end apart: 19 -> 19, of which waited for: 8 -> 9; matrix products, arithmetic and copies ran while one was open for 1% -> 1% of each run, Pallas kernels for 11% -> 13%
where the time goes in v11:
time: 81.1 us; the launch traced here: 80.1 us
  starting transfers between devices  31.1 us (38%)
  waiting for transfers between devices  28.7 us (35%)
  Pallas kernels  14.1 us (17%)
  local copies, waits for them, and re-layouts  4.59 us (6%)
  other arithmetic  0.94 us (1%)
    ppermute x10, waiting for transfers between devices, col_swap(): lax.ppermute(value, 'col', [(at, at ^ dz * Y + dy) for at in range(16)])  25.9 us
    ppermute x9, starting transfers between devices, row_swap(): lax.ppermute(value, 'row', [(at, at ^ dz * 8 + dx * 2 + dc) for at in ran...  15.8 us
    ppermute x10, starting transfers between devices, col_swap(): lax.ppermute(value, 'col', [(at, at ^ dz * Y + dy) for at in range(16)])  15.3 us
    pallas_call x4, Pallas kernels, tile_stage(): pl.pallas_call(functools.partial(stage_kernel, group, first, last), out_s...  11.4 us
    unnamed x22, local copies, waits for them, and re-layouts  4.55 us
    ppermute x9, waiting for transfers between devices, row_swap(): lax.ppermute(value, 'row', [(at, at ^ dz * 8 + dx * 2 + dc) for at in ran...  2.89 us
    pallas_call x1, Pallas kernels, plan(): pl.pallas_call(plan_kernel, out_shape=[jax.ShapeDtypeStruct((many,), jnp....  1.83 us
  transfers between devices with their start and end apart: 19, of which 9 were waited for; matrix products, arithmetic and copies ran while one was open for 1% of the time, Pallas kernels for 13%

profile of v11, /device:TPU:4, one launch (start us, length us, event | category | flops | bytes accessed | tf_op | source)
XLA Modules:
  0.0 80.1 jit_solution(10526615977841333564)
XLA Ops:
  0.0 7.3 %collective-permute-start = (bf16[128,768]{1,0:T(8,128)(2,1)}, bf16[128,768]{1,0:T(8,128)(2,1)S(1)}, u32[]{:S(2)}, u32[]{:S(2)}) collective-permute-start(bf16[128,768]{1,0:T(8,128)(2,1)} %param.8), channel_id=1, source_target_pairs={{0,128},{16,144},{32,160},{48,176},{64,192},{80,208},{96,224},{112... | collective-permute-start | bytes 589832 | tf_op jit(solution)/shard_map/ppermute | solution.py:16
  7.3 1.2 %collective-permute-start.4 = (bf16[128,768]{1,0:T(8,128)(2,1)}, bf16[128,768]{1,0:T(8,128)(2,1)S(1)}, u32[]{:S(2)}, u32[]{:S(2)}) collective-permute-start(bf16[128,768]{1,0:T(8,128)(2,1)} %param.8), channel_id=1, source_target_pairs={{0,32},{16,48},{32,0},{48,16},{64,96},{80,112},{96,64},{112,80},{1... | collective-permute-start | bytes 589832 | tf_op jit(solution)/shard_map/ppermute | solution.py:16
  8.5 2.9 %collective-permute-start.5 = (bf16[128,768]{1,0:T(8,128)(2,1)}, bf16[128,768]{1,0:T(8,128)(2,1)S(1)}, u32[]{:S(2)}, u32[]{:S(2)}) collective-permute-start(bf16[128,768]{1,0:T(8,128)(2,1)} %param.8), channel_id=1, source_target_pairs={{0,64},{16,80},{32,96},{48,112},{64,0},{80,16},{96,32},{112,48},{1... | collective-permute-start | bytes 589832 | tf_op jit(solution)/shard_map/ppermute | solution.py:16
  11.4 2.7 %copy-done.1 = bf16[768,5,768]{2,0,1:T(8,128)(2,1)S(1)} copy-done((bf16[768,5,768]{2,0,1:T(8,128)(2,1)S(1)}, bf16[768,5,768]{2,0,1:T(8,128)(2,1)}, u32[]{:S(2)}) %copy-start.1) | copy-done | bytes 5898264
  14.1 1.3 %copy-done.2 = bf16[1,1,5,8,128,128]{5,4,3,2,1,0:T(8,128)(2,1)S(1)} copy-done((bf16[1,1,5,8,128,128]{5,4,3,2,1,0:T(8,128)(2,1)S(1)}, bf16[1,1,5,8,128,128]{5,4,3,2,1,0:T(8,128)(2,1)}, u32[]{:S(2)}) %copy-start.2) | copy-done | bytes 1310744
  16.9 2.7 %collective-permute-start.2 = (bf16[128,768]{1,0:T(8,128)(2,1)S(1)}, bf16[128,768]{1,0:T(8,128)(2,1)S(1)}, u32[]{:S(2)}, u32[]{:S(2)}) collective-permute-start(bf16[128,768]{1,0:T(8,128)(2,1)S(1)} %collective-permute-done), channel_id=1, source_target_pairs={{0,64},{16,80},{32,96},{48,112},{64,0},{80,16},{96,32},{112,48},{1... | collective-permute-start | bytes 589832 | tf_op jit(solution)/shard_map/ppermute | solution.py:16
  20.6 1.3 %collective-permute-done.6 = bf16[128,768]{1,0:T(8,128)(2,1)S(1)} collective-permute-done((bf16[128,768]{1,0:T(8,128)(2,1)}, bf16[128,768]{1,0:T(8,128)(2,1)S(1)}, u32[]{:S(2)}, u32[]{:S(2)}) %collective-permute-start.6) | collective-permute-done | bytes 196640 | tf_op jit(solution)/shard_map/ppermute | solution.py:16
  22.1 1.8 %plan.1 = (s32[40]{0:T(128)S(1)}, s32[21]{0:T(128)S(1)}) custom-call(s32[5,8]{1,0:T(8,128)S(1)} %fusion.4.table_ref), custom_call_target="tpu_custom_call" | custom-call | tf_op jit(solution)/shard_map/plan/pallas_call | solution.py:137
  24.0 2.5 %tile.4.refs_0_ = f32[2048,768]{1,0:T(8,128)S(1)} custom-call(s32[40]{0:T(128)S(1)} %get-tuple-element.50.codes_ref, s32[21]{0:T(128)S(1)} %get-tuple-element.51.starts_ref, bf16[40,128,128]{2,1,0:T(8,128)(2,1)S(1)} %get-tuple-element.52.blocks_ref, bf16[5,768,768]{2,1,0:T(8,128)(2,1)S(1)} %get-tuple-element.53.weight_ref, ...), custom_call_target="tpu_custom_call" | custom-call | flops 1073741824 | bytes 4194304 | tf_op jit(solution)/shard_map/tile/pallas_call | solution.py:164
  26.4 1.6 %collective-permute-done.1 = bf16[128,768]{1,0:T(8,128)(2,1)S(1)} collective-permute-done((bf16[128,768]{1,0:T(8,128)(2,1)S(1)}, bf16[128,768]{1,0:T(8,128)(2,1)S(1)}, u32[]{:S(2)}, u32[]{:S(2)}) %collective-permute-start.1) | collective-permute-done | bytes 196640 | tf_op jit(solution)/shard_map/ppermute | solution.py:16
  28.0 2.8 %tile.5.refs_0_ = f32[2048,768]{1,0:T(8,128)S(1)} custom-call(s32[40]{0:T(128)S(1)} %get-tuple-element.50.codes_ref, s32[21]{0:T(128)S(1)} %get-tuple-element.51.starts_ref, bf16[40,128,128]{2,1,0:T(8,128)(2,1)S(1)} %get-tuple-element.52.blocks_ref, bf16[5,768,768]{2,1,0:T(8,128)(2,1)S(1)} %get-tuple-element.53.weight_ref, ...), custom_call_target="tpu_custom_call", output_to_operand_aliasing={{}: (5, {})} | custom-call | flops 1073741824 | bytes 4194304 | tf_op jit(solution)/shard_map/tile/pallas_call | solution.py:164
  31.0 2.7 %tile.6.refs_0_ = f32[2048,768]{1,0:T(8,128)S(1)} custom-call(s32[40]{0:T(128)S(1)} %get-tuple-element.50.codes_ref, s32[21]{0:T(128)S(1)} %get-tuple-element.51.starts_ref, bf16[40,128,128]{2,1,0:T(8,128)(2,1)S(1)} %get-tuple-element.52.blocks_ref, bf16[5,768,768]{2,1,0:T(8,128)(2,1)S(1)} %get-tuple-element.53.weight_ref, ...), custom_call_target="tpu_custom_call", output_to_operand_aliasing={{}: (5, {})} | custom-call | flops 1073741824 | bytes 4194304 | tf_op jit(solution)/shard_map/tile/pallas_call | solution.py:164
  33.8 3.4 %tile.7 = (f32[2048,768]{1,0:T(8,128)S(1)}, bf16[3,96,768]{2,1,0:T(8,128)(2,1)S(1)}, bf16[3,96,768]{2,1,0:T(8,128)(2,1)S(1)}, bf16[3,96,768]{2,1,0:T(8,128)(2,1)...) custom-call(s32[40]{0:T(128)S(1)} %get-tuple-element.50.codes_ref, ...), custom_call_target="tpu_custom_call", output_to_operand_aliasing={{0}: (5, {})} | custom-call | flops 1073741824 | bytes 4194304 | tf_op jit(solution)/shard_map/tile/pallas_call | solution.py:164
  37.3 3.1 %collective-permute-start.11 = (bf16[3,96,768]{2,1,0:T(8,128)(2,1)S(1)}, bf16[3,96,768]{2,1,0:T(8,128)(2,1)S(1)}, u32[]{:S(2)}, u32[]{:S(2)}) collective-permute-start(bf16[3,96,768]{2,1,0:T(8,128)(2,1)S(1)} %get-tuple-element.67), channel_id=1, source_target_pairs={{0,2},{1,3},{2,0},{3,1},{4,6},{5,7},{6,4},{7,5},{8,10},{9,11},{10,... | collective-permute-start | bytes 1327112 | tf_op jit(solution)/shard_map/ppermute | solution.py:20
  40.4 1.7 %collective-permute-start.12 = (bf16[3,96,768]{2,1,0:T(8,128)(2,1)S(1)}, bf16[3,96,768]{2,1,0:T(8,128)(2,1)S(1)}, u32[]{:S(2)}, u32[]{:S(2)}) collective-permute-start(bf16[3,96,768]{2,1,0:T(8,128)(2,1)S(1)} %get-tuple-element.68), channel_id=1, source_target_pairs={{0,1},{1,0},{2,3},{3,2},{4,5},{5,4},{6,7},{7,6},{8,9},{9,8},{10,11... | collective-permute-start | bytes 1327112 | tf_op jit(solution)/shard_map/ppermute | solution.py:20
  42.1 5.3 %collective-permute-done.9.refs_1_ = bf16[2,4,32,768]{3,2,1,0:T(8,128)(2,1)S(1)} collective-permute-done((bf16[2,4,32,768]{3,2,1,0:T(8,128)(2,1)S(1)}, bf16[2,4,32,768]{3,2,1,0:T(8,128)(2,1)S(1)}, u32[]{:S(2)}, u32[]{:S(2)}) %collective-permute-start.9) | collective-permute-done | bytes 393248 | tf_op jit(solution)/shard_map/ppermute | solution.py:20
  47.5 2.1 %collective-permute-start.10 = (bf16[4,32,768]{2,1,0:T(8,128)(2,1)S(1)}, bf16[4,32,768]{2,1,0:T(8,128)(2,1)S(1)}, u32[]{:S(2)}, u32[]{:S(2)}) collective-permute-start(bf16[4,32,768]{2,1,0:T(8,128)(2,1)S(1)} %get-tuple-element.61), channel_id=1, source_target_pairs={{0,8},{1,9},{2,10},{3,11},{4,12},{5,13},{6,14},{7,15},{8,0},{9,1},... | collective-permute-start | bytes 589832 | tf_op jit(solution)/shard_map/ppermute | solution.py:20
  50.0 8.7 %collective-permute-done.10.refs_1_ = bf16[4,32,768]{2,1,0:T(8,128)(2,1)S(1)} collective-permute-done((bf16[4,32,768]{2,1,0:T(8,128)(2,1)S(1)}, bf16[4,32,768]{2,1,0:T(8,128)(2,1)S(1)}, u32[]{:S(2)}, u32[]{:S(2)}) %collective-permute-start.10) | collective-permute-done | bytes 196640 | tf_op jit(solution)/shard_map/ppermute | solution.py:20
  59.1 3.5 %collective-permute-done.12.refs_2_ = bf16[3,96,768]{2,1,0:T(8,128)(2,1)S(1)} collective-permute-done((bf16[3,96,768]{2,1,0:T(8,128)(2,1)S(1)}, bf16[3,96,768]{2,1,0:T(8,128)(2,1)S(1)}, u32[]{:S(2)}, u32[]{:S(2)}) %collective-permute-start.12) | collective-permute-done | bytes 442400 | tf_op jit(solution)/shard_map/ppermute | solution.py:20
  62.8 1.1 %collective-permute-start.17 = (bf16[96,768]{1,0:T(8,128)(2,1)S(1)}, bf16[96,768]{1,0:T(8,128)(2,1)S(1)}, u32[]{:S(2)}, u32[]{:S(2)}) collective-permute-start(bf16[96,768]{1,0:T(8,128)(2,1)S(1)} %get-tuple-element.81), channel_id=1, source_target_pairs={{0,8},{1,9},{2,10},{3,11},{4,12},{5,13},{6,14},{7,15},{8,0},{9,1},... | collective-permute-start | bytes 442376 | tf_op jit(solution)/shard_map/ppermute | solution.py:20
  64.5 1.9 %collective-permute-start.16 = (bf16[96,768]{1,0:T(8,128)(2,1)S(1)}, bf16[96,768]{1,0:T(8,128)(2,1)S(1)}, u32[]{:S(2)}, u32[]{:S(2)}) collective-permute-start(bf16[96,768]{1,0:T(8,128)(2,1)S(1)} %get-tuple-element.76), channel_id=1, source_target_pairs={{0,4},{1,5},{2,6},{3,7},{4,0},{5,1},{6,2},{7,3},{8,12},{9,13},{10,... | collective-permute-start | bytes 442376 | tf_op jit(solution)/shard_map/ppermute | solution.py:20
  66.4 4.1 %collective-permute-done.14.refs_2_ = bf16[2,128,768]{2,1,0:T(8,128)(2,1)S(1)} collective-permute-done((bf16[2,128,768]{2,1,0:T(8,128)(2,1)S(1)}, bf16[2,128,768]{2,1,0:T(8,128)(2,1)S(1)}, u32[]{:S(2)}, u32[]{:S(2)}) %collective-permute-start.14) | collective-permute-done | bytes 393248 | tf_op jit(solution)/shard_map/ppermute | solution.py:20
  70.5 4.3 %collective-permute-start.15 = (bf16[128,768]{1,0:T(8,128)(2,1)S(1)}, bf16[128,768]{1,0:T(8,128)(2,1)S(1)}, u32[]{:S(2)}, u32[]{:S(2)}) collective-permute-start(bf16[128,768]{1,0:T(8,128)(2,1)S(1)} %get-tuple-element.80), channel_id=1, source_target_pairs={{0,3},{1,2},{2,1},{3,0},{4,7},{5,6},{6,5},{7,4},{8,11},{9,10},{10,... | collective-permute-start | bytes 589832 | tf_op jit(solution)/shard_map/ppermute | solution.py:20
  76.8 2.5 %collective-permute-done.15 = bf16[128,768]{1,0:T(8,128)(2,1)S(1)} collective-permute-done((bf16[128,768]{1,0:T(8,128)(2,1)S(1)}, bf16[128,768]{1,0:T(8,128)(2,1)S(1)}, u32[]{:S(2)}, u32[]{:S(2)}) %collective-permute-start.15) | collective-permute-done | bytes 196640 | tf_op jit(solution)/shard_map/ppermute | solution.py:20
  (56 shorter events, 7.5 us)
Async XLA Ops:
  0.0 49.6 %copy-start = (bf16[768,768]{1,0:T(8,128)(2,1)S(1)}, bf16[768,768]{1,0:T(8,128)(2,1)}, u32[]{:S(2)}) copy-start(bf16[768,768]{1,0:T(8,128)(2,1)} %param.9) | copy-start | bytes 3538948
  0.0 22.0 %copy-start.7 = (s32[1,1,5]{2,1,0:T(1,128)S(1)}, s32[1,1,5]{2,1,0:T(1,128)}, u32[]{:S(2)}) copy-start(s32[1,1,5]{2,1,0:T(1,128)} %param.15) | copy-start | bytes 64
  0.0 22.0 %copy-start.5 = (s32[1,1,5,8]{3,1,2,0:T(1,128)S(1)}, s32[1,1,5,8]{3,1,2,0:T(1,128)}, u32[]{:S(2)}) copy-start(s32[1,1,5,8]{3,1,2,0:T(1,128)} %param.13) | copy-start | bytes 484
  0.0 16.3 %collective-permute-start = (bf16[128,768]{1,0:T(8,128)(2,1)}, bf16[128,768]{1,0:T(8,128)(2,1)S(1)}, u32[]{:S(2)}, u32[]{:S(2)}) collective-permute-start(bf16[128,768]{1,0:T(8,128)(2,1)} %param.8), channel_id=1, source_target_pairs={{0,128},{16,144},{32,160},{48,176},{64,192},{80,208},{96,224},{112... | collective-permute-start | bytes 589832 | tf_op jit(solution)/shard_map/ppermute | solution.py:16
  7.3 12.4 %collective-permute-start.4 = (bf16[128,768]{1,0:T(8,128)(2,1)}, bf16[128,768]{1,0:T(8,128)(2,1)S(1)}, u32[]{:S(2)}, u32[]{:S(2)}) collective-permute-start(bf16[128,768]{1,0:T(8,128)(2,1)} %param.8), channel_id=1, source_target_pairs={{0,32},{16,48},{32,0},{48,16},{64,96},{80,112},{96,64},{112,80},{1... | collective-permute-start | bytes 589832 | tf_op jit(solution)/shard_map/ppermute | solution.py:16
  8.5 13.4 %collective-permute-start.6 = (bf16[128,768]{1,0:T(8,128)(2,1)}, bf16[128,768]{1,0:T(8,128)(2,1)S(1)}, u32[]{:S(2)}, u32[]{:S(2)}) collective-permute-start(bf16[128,768]{1,0:T(8,128)(2,1)} %param.8), channel_id=1, source_target_pairs={{0,96},{16,112},{32,64},{48,80},{64,32},{80,48},{96,0},{112,16},{1... | collective-permute-start | bytes 589832 | tf_op jit(solution)/shard_map/ppermute | solution.py:16
  8.5 12.0 %collective-permute-start.5 = (bf16[128,768]{1,0:T(8,128)(2,1)}, bf16[128,768]{1,0:T(8,128)(2,1)S(1)}, u32[]{:S(2)}, u32[]{:S(2)}) collective-permute-start(bf16[128,768]{1,0:T(8,128)(2,1)} %param.8), channel_id=1, source_target_pairs={{0,64},{16,80},{32,96},{48,112},{64,0},{80,16},{96,32},{112,48},{1... | collective-permute-start | bytes 589832 | tf_op jit(solution)/shard_map/ppermute | solution.py:16
  15.4 6.7 %copy-start.6 = (s32[1,1,5,8]{3,1,2,0:T(1,128)S(1)}, s32[1,1,5,8]{3,1,2,0:T(1,128)}, u32[]{:S(2)}) copy-start(s32[1,1,5,8]{3,1,2,0:T(1,128)} %param.14) | copy-start | bytes 484
  16.3 14.5 %collective-permute-start.3 = (bf16[128,768]{1,0:T(8,128)(2,1)S(1)}, bf16[128,768]{1,0:T(8,128)(2,1)S(1)}, u32[]{:S(2)}, u32[]{:S(2)}) collective-permute-start(bf16[128,768]{1,0:T(8,128)(2,1)S(1)} %collective-permute-done), channel_id=1, source_target_pairs={{0,96},{16,112},{32,64},{48,80},{64,32},{80,48},{96,0},{112,16},{1... | collective-permute-start | bytes 589832 | tf_op jit(solution)/shard_map/ppermute | solution.py:16
  16.9 11.1 %collective-permute-start.2 = (bf16[128,768]{1,0:T(8,128)(2,1)S(1)}, bf16[128,768]{1,0:T(8,128)(2,1)S(1)}, u32[]{:S(2)}, u32[]{:S(2)}) collective-permute-start(bf16[128,768]{1,0:T(8,128)(2,1)S(1)} %collective-permute-done), channel_id=1, source_target_pairs={{0,64},{16,80},{32,96},{48,112},{64,0},{80,16},{96,32},{112,48},{1... | collective-permute-start | bytes 589832 | tf_op jit(solution)/shard_map/ppermute | solution.py:16
  19.7 8.3 %collective-permute-start.1 = (bf16[128,768]{1,0:T(8,128)(2,1)S(1)}, bf16[128,768]{1,0:T(8,128)(2,1)S(1)}, u32[]{:S(2)}, u32[]{:S(2)}) collective-permute-start(bf16[128,768]{1,0:T(8,128)(2,1)S(1)} %collective-permute-done), channel_id=1, source_target_pairs={{0,32},{16,48},{32,0},{48,16},{64,96},{80,112},{96,64},{112,80},{1... | collective-permute-start | bytes 589832 | tf_op jit(solution)/shard_map/ppermute | solution.py:16
  21.9 6.1 %collective-permute-start.7 = (bf16[512,768]{1,0:T(8,128)(2,1)S(1)}, bf16[512,768]{1,0:T(8,128)(2,1)S(1)}, u32[]{:S(2)}, u32[]{:S(2)}) collective-permute-start(bf16[512,768]{1,0:T(8,128)(2,1)S(1)} %constant_dynamic-update-slice_fusion.group_ref), channel_id=1, source_target_pairs={{0,16},{16,0},{32,48},{48,32},{64,80},{80,64},{96,112},{112,96},{1... | collective-permute-start | bytes 2359304 | tf_op jit(solution)/shard_map/ppermute | solution.py:16
  30.8 2.9 %collective-permute-start.8 = (bf16[512,768]{1,0:T(8,128)(2,1)S(1)}, bf16[512,768]{1,0:T(8,128)(2,1)S(1)}, u32[]{:S(2)}, u32[]{:S(2)}) collective-permute-start(bf16[512,768]{1,0:T(8,128)(2,1)S(1)} %constant_dynamic-update-slice_fusion.4.group_ref), channel_id=1, source_target_pairs={{0,16},{16,0},{32,48},{48,32},{64,80},{80,64},{96,112},{112,96},{1... | collective-permute-start | bytes 2359304 | tf_op jit(solution)/shard_map/ppermute | solution.py:16
  37.2 42.2 %copy-start.4 = (f32[768]{0:T(1024)S(1)}, f32[768]{0:T(1024)}, u32[]{:S(2)}) copy-start(f32[768]{0:T(1024)} %param.11) | copy-start | bytes 9220
  37.2 10.2 %collective-permute-start.9 = (bf16[2,4,32,768]{3,2,1,0:T(8,128)(2,1)S(1)}, bf16[2,4,32,768]{3,2,1,0:T(8,128)(2,1)S(1)}, u32[]{:S(2)}, u32[]{:S(2)}) collective-permute-start(bf16[2,4,32,768]{3,2,1,0:T(8,128)(2,1)S(1)} %get-tuple-element.58), channel_id=1, source_target_pairs={{0,4},{1,5},{2,6},{3,7},{4,0},{5,1},{6,2},{7,3},{8,12},{9,13},{10,... | collective-permute-start | bytes 1179656 | tf_op jit(solution)/shard_map/ppermute | solution.py:20
  37.3 21.8 %collective-permute-start.11 = (bf16[3,96,768]{2,1,0:T(8,128)(2,1)S(1)}, bf16[3,96,768]{2,1,0:T(8,128)(2,1)S(1)}, u32[]{:S(2)}, u32[]{:S(2)}) collective-permute-start(bf16[3,96,768]{2,1,0:T(8,128)(2,1)S(1)} %get-tuple-element.67), channel_id=1, source_target_pairs={{0,2},{1,3},{2,0},{3,1},{4,6},{5,7},{6,4},{7,5},{8,10},{9,11},{10,... | collective-permute-start | bytes 1327112 | tf_op jit(solution)/shard_map/ppermute | solution.py:20
  40.4 22.2 %collective-permute-start.12 = (bf16[3,96,768]{2,1,0:T(8,128)(2,1)S(1)}, bf16[3,96,768]{2,1,0:T(8,128)(2,1)S(1)}, u32[]{:S(2)}, u32[]{:S(2)}) collective-permute-start(bf16[3,96,768]{2,1,0:T(8,128)(2,1)S(1)} %get-tuple-element.68), channel_id=1, source_target_pairs={{0,1},{1,0},{2,3},{3,2},{4,5},{5,4},{6,7},{7,6},{8,9},{9,8},{10,11... | collective-permute-start | bytes 1327112 | tf_op jit(solution)/shard_map/ppermute | solution.py:20
  42.1 20.5 %collective-permute-start.13 = (bf16[3,96,768]{2,1,0:T(8,128)(2,1)S(1)}, bf16[3,96,768]{2,1,0:T(8,128)(2,1)S(1)}, u32[]{:S(2)}, u32[]{:S(2)}) collective-permute-start(bf16[3,96,768]{2,1,0:T(8,128)(2,1)S(1)} %get-tuple-element.69), channel_id=1, source_target_pairs={{0,3},{1,2},{2,1},{3,0},{4,7},{5,6},{6,5},{7,4},{8,11},{9,10},{10,... | collective-permute-start | bytes 1327112 | tf_op jit(solution)/shard_map/ppermute | solution.py:20
  47.5 11.1 %collective-permute-start.10 = (bf16[4,32,768]{2,1,0:T(8,128)(2,1)S(1)}, bf16[4,32,768]{2,1,0:T(8,128)(2,1)S(1)}, u32[]{:S(2)}, u32[]{:S(2)}) collective-permute-start(bf16[4,32,768]{2,1,0:T(8,128)(2,1)S(1)} %get-tuple-element.61), channel_id=1, source_target_pairs={{0,8},{1,9},{2,10},{3,11},{4,12},{5,13},{6,14},{7,15},{8,0},{9,1},... | collective-permute-start | bytes 589832 | tf_op jit(solution)/shard_map/ppermute | solution.py:20
  58.7 11.7 %collective-permute-start.14 = (bf16[2,128,768]{2,1,0:T(8,128)(2,1)S(1)}, bf16[2,128,768]{2,1,0:T(8,128)(2,1)S(1)}, u32[]{:S(2)}, u32[]{:S(2)}) collective-permute-start(bf16[2,128,768]{2,1,0:T(8,128)(2,1)S(1)} %get-tuple-element.77), channel_id=1, source_target_pairs={{0,1},{1,0},{2,3},{3,2},{4,5},{5,4},{6,7},{7,6},{8,9},{9,8},{10,11... | collective-permute-start | bytes 1179656 | tf_op jit(solution)/shard_map/ppermute | solution.py:20
  62.8 12.9 %collective-permute-start.17 = (bf16[96,768]{1,0:T(8,128)(2,1)S(1)}, bf16[96,768]{1,0:T(8,128)(2,1)S(1)}, u32[]{:S(2)}, u32[]{:S(2)}) collective-permute-start(bf16[96,768]{1,0:T(8,128)(2,1)S(1)} %get-tuple-element.81), channel_id=1, source_target_pairs={{0,8},{1,9},{2,10},{3,11},{4,12},{5,13},{6,14},{7,15},{8,0},{9,1},... | collective-permute-start | bytes 442376 | tf_op jit(solution)/shard_map/ppermute | solution.py:20
  63.9 11.9 %collective-permute-start.18 = (bf16[96,768]{1,0:T(8,128)(2,1)S(1)}, bf16[96,768]{1,0:T(8,128)(2,1)S(1)}, u32[]{:S(2)}, u32[]{:S(2)}) collective-permute-start(bf16[96,768]{1,0:T(8,128)(2,1)S(1)} %get-tuple-element.82), channel_id=1, source_target_pairs={{0,12},{1,13},{2,14},{3,15},{4,8},{5,9},{6,10},{7,11},{8,4},{9,5},... | collective-permute-start | bytes 442376 | tf_op jit(solution)/shard_map/ppermute | solution.py:20
  64.5 12.2 %collective-permute-start.16 = (bf16[96,768]{1,0:T(8,128)(2,1)S(1)}, bf16[96,768]{1,0:T(8,128)(2,1)S(1)}, u32[]{:S(2)}, u32[]{:S(2)}) collective-permute-start(bf16[96,768]{1,0:T(8,128)(2,1)S(1)} %get-tuple-element.76), channel_id=1, source_target_pairs={{0,4},{1,5},{2,6},{3,7},{4,0},{5,1},{6,2},{7,3},{8,12},{9,13},{10,... | collective-permute-start | bytes 442376 | tf_op jit(solution)/shard_map/ppermute | solution.py:20
  70.5 8.7 %collective-permute-start.15 = (bf16[128,768]{1,0:T(8,128)(2,1)S(1)}, bf16[128,768]{1,0:T(8,128)(2,1)S(1)}, u32[]{:S(2)}, u32[]{:S(2)}) collective-permute-start(bf16[128,768]{1,0:T(8,128)(2,1)S(1)} %get-tuple-element.80), channel_id=1, source_target_pairs={{0,3},{1,2},{2,1},{3,0},{4,7},{5,6},{6,5},{7,4},{8,11},{9,10},{10,... | collective-permute-start | bytes 589832 | tf_op jit(solution)/shard_map/ppermute | solution.py:20
  (3 other events, 4.9 us)
